TPU v7x, 128 devices: a whole 4x4x4 slice. The times are simulated.
128 devices in a mesh: expert: 32 (over y, x_hi, z), tensor: 4 (over x_lo, core).
Axes of the slice: x: 4 (x_hi: 2, x_lo: 2; x = x_hi * 2 + x_lo), y: 4, z: 4, core: 2. Of those that a mesh axis runs over, the one named last changes fastest.
Arguments:
- hidden_in: bfloat16 [16384, 4096], P(('expert', 'tensor')), may hold values from -20 to 20
- context: bfloat16 [16384, 4096], P('expert', 'tensor'), may hold values from -6 to 6
- w_out: bfloat16 [4096, 4096], P('tensor', 'expert'), may hold values from -0.09375 to 0.09375
- norm_gain: float32 [4096], replicated, may hold values from 0.25 to 1.75
- expert_ids: int32 [16384, 8], P(('expert', 'tensor')), may hold values from 0 to 127, all different within a row; in each aligned block of 128 rows (0 to 127, 128 to 255, ...) at most 9 rows name the same one
- route_weight: float32 [16384, 8], P(('expert', 'tensor')), may hold values from 0.05 to 1
- w_gate_up: bfloat16 [128, 4096, 1536], P(('expert', 'tensor')), may hold values from -0.09375 to 0.09375
- w_down: bfloat16 [128, 768, 4096], P(('expert', 'tensor')), may hold values from -0.21875 to 0.21875
Outputs:
- attended: bfloat16 [16384, 4096], P(('expert', 'tensor'))
- mixed: bfloat16 [16384, 4096], P(('expert', 'tensor'))
Inputs may be any that keep to these rules, and one draw needn't show every extreme that they name: `expert_ids`: each row names 8 different experts. Among the 128 rows of one device no expert is named more than 9 times, and in every draw some expert is named exactly 9 times by the rows of some device.
All inputs are finite; a program needn't handle non-finite values.
Results may differ from a plain program's by a relative error of at most 0.0053.
Values may be sent and summed in bfloat16 or wider, within the bound.
A program may use at most 128 MiB of HBM per device.

v0:
```python
import jax
import jax.numpy as jnp
from jax import lax
from jax.sharding import PartitionSpec as P


def expert_block(received, w_gate_up, w_down):
    block_shape = received.shape
    flattened = received.reshape(-1, block_shape[-1])
    hidden_units = w_down.shape[1]
    gate_and_up = jnp.dot(flattened, w_gate_up[0], preferred_element_type=jnp.float32)
    activated = (jax.nn.silu(gate_and_up[:, :hidden_units]) * gate_and_up[:, hidden_units:]).astype(
        jnp.bfloat16
    )
    result = jnp.dot(activated, w_down[0], preferred_element_type=jnp.float32).astype(jnp.bfloat16)
    return result.reshape(block_shape)


def on_device(hidden_in, context, w_out, norm_gain, expert_ids, route_weight, w_gate_up, w_down):
    tok_count, width = hidden_in.shape
    partial_sums = jnp.dot(
        context,
        lax.all_gather(w_out, "expert", axis=1, tiled=True),
        preferred_element_type=jnp.float32,
    )
    projected = lax.psum_scatter(partial_sums, "tensor", scatter_dimension=0, tiled=True)
    residual = hidden_in.astype(jnp.float32) + projected
    attended = residual.astype(jnp.bfloat16)
    inverse = lax.rsqrt(jnp.mean(residual * residual, axis=1, keepdims=True) + 1e-06)
    normed = (residual * inverse * norm_gain[None, :]).astype(jnp.bfloat16)
    top_count = expert_ids.shape[1]
    expert_count = lax.axis_size("expert")
    tensor_count = lax.axis_size("tensor")
    experts_all = expert_count * tensor_count
    capacity = tok_count * top_count * 9 // (8 * experts_all)
    chosen = expert_ids.reshape(-1)
    onehot = (chosen[:, None] == jnp.arange(experts_all, dtype=jnp.int32)[None, :]).astype(
        jnp.int32
    )
    before = jnp.cumsum(onehot, axis=0) - onehot
    slots = jnp.sum(before * onehot, axis=1)
    target = chosen * capacity + slots
    token_index = jnp.arange(tok_count * top_count, dtype=jnp.int32) // top_count
    send_buffer = (
        jnp.zeros((experts_all * capacity, width), jnp.bfloat16).at[target].set(normed[token_index])
    )
    send_buffer = send_buffer.reshape(experts_all, capacity, width)
    outputs = expert_block(
        lax.all_to_all(send_buffer, ("expert", "tensor"), split_axis=0, concat_axis=0, tiled=True),
        w_gate_up,
        w_down,
    )
    returned = lax.all_to_all(
        outputs, ("expert", "tensor"), split_axis=0, concat_axis=0, tiled=True
    )
    returned = returned.reshape(experts_all * capacity, width)
    picked = returned[target].reshape(tok_count, top_count, width)
    moe_sum = jnp.sum(route_weight[:, :, None] * picked, axis=1)
    mixed = (residual + moe_sum).astype(jnp.bfloat16)
    return (attended, mixed)


def solution(mesh):
    in_specs = (
        P(("expert", "tensor"), None),
        P("expert", "tensor"),
        P("tensor", "expert"),
        P(),
        P(("expert", "tensor"), None),
        P(("expert", "tensor"), None),
        P(("expert", "tensor"), None, None),
        P(("expert", "tensor"), None, None),
    )
    out_specs = (P(("expert", "tensor"), None), P(("expert", "tensor"), None))
    return jax.shard_map(
        on_device, mesh=mesh, in_specs=in_specs, out_specs=out_specs, check_vma=False
    )
```

profile of v0, /device:TPU:54, one launch (start us, length us, event | category | flops | bytes accessed | tf_op | source)
XLA Modules:
  0.0 848.2 jit_solution(2491653852069091634)
XLA Ops:
  7.2 0.0 copy-start
  7.2 0.0 all-gather.2.cloned.1.call-start
  7.2 0.7 all-gather.2.cloned.1.call-update
  7.9 0.0 reduce-scatter.2.cloned.1.call-start
  8.0 132.3 %all-gather.2.cloned.1.call-done = bf16[1024,4096]{1,0:T(8,128)(2,1)} async-done(((bf16[1024,128]{1,0:T(8,128)(2,1)}), bf16[1024,4096]{1,0:T(8,128)(2,1)}) %all-gather.2.cloned.1.call-update) | async-done | bytes 8388624 | tf_op jit(solution)/shard_map/all_gather | solution.py:23
  140.3 0.0 copy-done
  140.3 10.0 %fusion.16 = f32[512,4096]{1,0:T(8,128)} fusion(bf16[512,1024]{1,0:T(8,128)(2,1)S(1)} %copy-done, bf16[1024,4096]{1,0:T(8,128)(2,1)} %all-gather.2.cloned.1.call-done), kind=kOutput, calls=%fused_computation.40 | convolution fusion | flops 4294967296 | bytes 17825792 | tf_op jit(solution)/shard_map/dot_general | solution.py:21
  150.3 0.0 copy-start.5
  150.3 0.0 copy-start.3
  150.3 0.0 copy-start.4
  150.3 0.0 reduce-scatter.2.cloned.1.call-update
  150.3 0.7 copy-done.5
  151.0 0.1 copy.13
  151.1 0.1 eq.29
  151.2 0.1 eq.25
  151.3 0.1 copy.15
  151.4 0.2 fusion.11
  151.7 0.1 copy.16
  151.8 0.1 copy.12
  151.9 0.1 mul.56
  152.0 0.4 fusion.10
  152.4 77.2 %reduce-scatter.2.cloned.1.call-done = f32[128,4096]{1,0:T(8,128)} async-done(((f32[512,4096]{1,0:T(8,128)}), f32[128,4096]{1,0:T(8,128)}) %reduce-scatter.2.cloned.1.call-update) | async-done | bytes 2097168 | tf_op jit(solution)/shard_map/reduce_scatter | solution.py:26
  229.6 0.0 copy-done.3
  229.6 1.9 multiply_reduce_fusion
  231.5 0.0 copy-done.4
  231.5 1.9 multiply_convert_fusion
  233.5 7.7 gather_fusion
  241.2 18.2 %scatter_custom_fusion = bf16[1152,4096]{1,0:T(8,128)(2,1)} fusion(s32[1024]{0:T(1024)S(1)} %bitcast.26, bf16[1024,4096]{1,0:T(8,128)(2,1)} %gather_fusion, bf16[]{:T(256)} %constant.29.clone.1), kind=kCustom, calls=%fused_computation.9 | custom fusion | bytes 9437696 | tf_op jit(solution)/shard_map/scatter | solution.py:45
  259.5 15.1 %reshape.119 = bf16[128,9,4096]{2,1,0:T(8,128)(2,1)} reshape(bf16[1152,4096]{1,0:T(8,128)(2,1)} %scatter_custom_fusion) | data formatting | bytes 18874368 | tf_op jit(solution)/shard_map/reshape | solution.py:47
  274.6 210.0 %all_to_all.10 = bf16[128,9,4096]{2,1,0:T(8,128)(2,1)} all-to-all(bf16[128,9,4096]{2,1,0:T(8,128)(2,1)} %reshape.119), channel_id=1, replica_groups=mesh['expert'=32,'tensor'=4] {'expert','tensor'}, dimensions={0} | all-to-all | bytes 18874368 | tf_op jit(solution)/shard_map/all_to_all | solution.py:49
  484.6 15.8 %reshape.120 = bf16[1152,4096]{1,0:T(8,128)(2,1)} reshape(bf16[128,9,4096]{2,1,0:T(8,128)(2,1)} %all_to_all.10) | data formatting | bytes 18874368 | tf_op jit(solution)/shard_map/reshape | solution.py:9
  500.4 18.2 %fusion.1 = f32[1152,1536]{1,0:T(8,128)S(1)} fusion(bf16[1152,4096]{1,0:T(8,128)(2,1)} %reshape.120, bf16[1,4096,1536]{2,1,0:T(8,128)(2,1)} %param.14), kind=kOutput, calls=%fused_computation.6 | convolution fusion | flops 14495514624 | bytes 29097984 | tf_op jit(solution)/shard_map/dot_general | solution.py:11
  518.7 12.5 %convolution_convert_fusion = bf16[1152,4096]{1,0:T(8,128)(2,1)} fusion(bf16[1,768,4096]{2,1,0:T(8,128)(2,1)} %param.15, f32[1152,1536]{1,0:T(8,128)S(1)} %fusion.1), kind=kOutput, calls=%fused_computation.5 | convolution fusion | flops 7257784320 | bytes 22806528 | tf_op jit(solution)/shard_map/dot_general | solution.py:15
  531.2 15.1 %reshape.121 = bf16[128,9,4096]{2,1,0:T(8,128)(2,1)} reshape(bf16[1152,4096]{1,0:T(8,128)(2,1)} %convolution_convert_fusion) | data formatting | bytes 18874368 | tf_op jit(solution)/shard_map/reshape | solution.py:16
  546.3 0.0 copy-start.6
  546.3 8.2 all-to-all-start.1
  554.5 0.0 copy-done.6
  554.5 0.1 copy.11
  554.6 234.0 %all-to-all-done.1 = bf16[128,9,4096]{2,1,0:T(8,128)(2,1)} async-done(((bf16[128,9,4096]{2,1,0:T(8,128)(2,1)}), bf16[128,9,4096]{2,1,0:T(8,128)(2,1)}, u32[]{:S(2)}, u32[]{:S(2)}) %all-to-all-start.1) | async-done | bytes 9437216 | tf_op jit(solution)/shard_map/all_to_all | solution.py:53
  788.6 15.8 %reshape.122 = bf16[1152,4096]{1,0:T(8,128)(2,1)} reshape(bf16[128,9,4096]{2,1,0:T(8,128)(2,1)} %all-to-all-done.1) | data formatting | bytes 18874368 | tf_op jit(solution)/shard_map/reshape | solution.py:56
  804.4 0.0 copy-start.1
  804.4 20.0 %gather_fusion.1 = bf16[1024,4096]{1,0:T(8,128)(2,1)} fusion(bf16[1152,4096]{1,0:T(8,128)(2,1)} %reshape.122, s32[1024]{0:T(1024)S(1)} %broadcast_clamp_fusion), kind=kCustom, calls=%fused_computation.1 | custom fusion | bytes 16781312 | tf_op jit(solution)/shard_map/gather | solution.py:57
  824.4 0.0 copy-start.2
  824.4 13.3 %fusion = f32[128,4096]{1,0:T(8,128)} fusion(bf16[1024,4096]{1,0:T(8,128)(2,1)} %gather_fusion.1, f32[128,8]{1,0:T(8,128)S(1)} %copy.11), kind=kLoop, calls=%fused_computation.4 | loop fusion | flops 12058624 | bytes 10489856 | tf_op jit(solution)/shard_map/reduce_sum | solution.py:58
  837.8 0.0 copy-done.2
  837.8 3.6 add_convert_fusion
  841.4 0.0 copy-done.1
  (10 shorter events, 0.1 us)
Async XLA Ops:
  7.2 133.1 %copy-start = (bf16[512,1024]{1,0:T(8,128)(2,1)S(1)}, bf16[512,1024]{1,0:T(8,128)(2,1)}, u32[]{:S(2)}) copy-start(bf16[512,1024]{1,0:T(8,128)(2,1)} %param.9) | copy-start | bytes 3145732
  7.2 133.1 %all-gather.2.cloned.1.call-start = ((), (), s32[]{:S(2)}) async-start(), calls=%async_computation.3 | async-start | bytes 8650752 | tf_op jit(solution)/shard_map/all_gather | solution.py:23
  7.9 221.7 %reduce-scatter.2.cloned.1.call-start = ((), (), s32[]{:S(2)}) async-start(), calls=%async_computation.4 | async-start | bytes 10485760 | tf_op jit(solution)/shard_map/reduce_scatter | solution.py:26
  150.3 0.7 copy-start.5
  150.3 79.3 %copy-start.3 = (bf16[128,4096]{1,0:T(8,128)(2,1)S(1)}, bf16[128,4096]{1,0:T(8,128)(2,1)}, u32[]{:S(2)}) copy-start(bf16[128,4096]{1,0:T(8,128)(2,1)} %param.8) | copy-start | bytes 3145732
  150.3 81.2 %copy-start.4 = (f32[4096]{0:T(1024)S(1)}, f32[4096]{0:T(1024)}, u32[]{:S(2)}) copy-start(f32[4096]{0:T(1024)} %param.11) | copy-start | bytes 49156
  546.3 8.2 copy-start.6
  546.3 242.3 %all-to-all-start.1 = ((bf16[128,9,4096]{2,1,0:T(8,128)(2,1)}), bf16[128,9,4096]{2,1,0:T(8,128)(2,1)}, u32[]{:S(2)}, u32[]{:S(2)}) async-start(bf16[128,9,4096]{2,1,0:T(8,128)(2,1)} %reshape.121), calls=%async_computation.2 | async-start | bytes 33554432 | tf_op jit(solution)/shard_map/all_to_all | solution.py:53
  804.4 37.0 %copy-start.1 = (bf16[512,1024]{1,0:T(8,128)(2,1)S(1)}, bf16[512,1024]{1,0:T(8,128)(2,1)}, u32[]{:S(2)}) copy-start(bf16[512,1024]{1,0:T(8,128)(2,1)} %param.9) | copy-start | bytes 3145732
  824.4 13.3 %copy-start.2 = (f32[128,4096]{1,0:T(8,128)S(1)}, f32[128,4096]{1,0:T(8,128)}, u32[]{:S(2)}) copy-start(f32[128,4096]{1,0:T(8,128)} %reduce-scatter.2.cloned.1.call-done) | copy-start | bytes 6291460
Sparse Core Ops, SparseCore 0:
  10.8 129.4 all-gather.1
  150.4 79.0 reduce-scatter.1
where the time goes:
time: 858 us; the launch traced here: 848 us
  waiting for transfers between devices  444 us (52%)
  blocking collectives  210 us (24%)
  local copies, waits for them, and re-layouts  109 us (13%)
  matrix products  40.8 us (5%)
  other arithmetic  21.5 us (3%)
  between operations  14.2 us (2%)
    all_to_all x1, waiting for transfers between devices, on_device(): lax.all_to_all(outputs, ('expert', 'tensor'), split_axis=0, concat_axis=0...  234 us
    all_to_all x1, blocking collectives, on_device(): lax.all_to_all(send_buffer, ('expert', 'tensor'), split_axis=0, concat_ax...  210 us
    all_gather x1, waiting for transfers between devices, on_device(): lax.all_gather(w_out, 'expert', axis=1, tiled=True)  132 us
    reduce_scatter x1, waiting for transfers between devices, on_device(): lax.psum_scatter(partial_sums, 'tensor', scatter_dimension=0, tiled=True)  77.2 us
    gather x1, local copies, waits for them, and re-layouts, on_device(): picked = returned[target].reshape(tok_count, top_count, width)  20 us
    scatter x1, local copies, waits for them, and re-layouts, on_device(): jnp.zeros((experts_all * capacity, width), jnp.bfloat16).at[target]  18.2 us
    dot_general x1, matrix products, expert_block(): jnp.dot(flattened, w_gate_up[0], preferred_element_type=jnp.float32)  18.2 us
  transfers between devices with their start and end apart: 3, of which 3 were waited for; matrix products, arithmetic and copies ran while one was open for 0% of the time, Pallas kernels for 0%

commit v1 on v0

v1 whole, which is shorter than its diff:
```python
import jax
import jax.numpy as jnp
from jax import lax
from jax.sharding import PartitionSpec as P

LANES = 128


def expert_block(received, w_gate_up, w_down):
    hidden_units = w_down.shape[1]
    gate_and_up = jnp.dot(received, w_gate_up[0], preferred_element_type=jnp.float32)
    activated = (jax.nn.silu(gate_and_up[:, :hidden_units]) * gate_and_up[:, hidden_units:]).astype(
        jnp.bfloat16
    )
    return jnp.dot(activated, w_down[0], preferred_element_type=jnp.float32).astype(jnp.bfloat16)


def split_bf16(x):
    hi = x.astype(jnp.bfloat16)
    rest = x - hi.astype(jnp.float32)
    mid = rest.astype(jnp.bfloat16)
    lo = (rest - mid.astype(jnp.float32)).astype(jnp.bfloat16)
    return hi, mid, lo


def on_device(hidden_in, context, w_out, norm_gain, expert_ids, route_weight, w_gate_up, w_down):
    tok_count, width = hidden_in.shape
    chunks = width // LANES
    partial_sums = jnp.dot(
        context,
        lax.all_gather(w_out, "expert", axis=1, tiled=True),
        preferred_element_type=jnp.float32,
    )
    projected = lax.psum_scatter(partial_sums, "tensor", scatter_dimension=0, tiled=True)
    residual = hidden_in.astype(jnp.float32) + projected
    attended = residual.astype(jnp.bfloat16)
    inverse = lax.rsqrt(jnp.mean(residual * residual, axis=1, keepdims=True) + 1e-06)
    normed = (residual * inverse * norm_gain[None, :]).astype(jnp.bfloat16)
    top_count = expert_ids.shape[1]
    expert_count = lax.axis_size("expert")
    tensor_count = lax.axis_size("tensor")
    experts_all = expert_count * tensor_count
    capacity = tok_count * top_count * 9 // (8 * experts_all)
    rows_all = experts_all * capacity
    chosen = expert_ids.reshape(-1)
    onehot = (chosen[:, None] == jnp.arange(experts_all, dtype=jnp.int32)[None, :]).astype(
        jnp.int32
    )
    before = jnp.cumsum(onehot, axis=0) - onehot
    slots = jnp.sum(before * onehot, axis=1)
    target = (chosen * capacity + slots).reshape(tok_count, top_count)
    place = jnp.arange(rows_all, dtype=jnp.int32)[:, None, None] == target[None, :, :]
    dispatch = jnp.any(place, axis=2).astype(jnp.bfloat16)
    normed3 = normed.reshape(tok_count, chunks, LANES)
    send = jnp.einsum(
        "ri,icl->rcl", dispatch, normed3, preferred_element_type=jnp.float32
    ).astype(jnp.bfloat16)
    send = send.reshape(experts_all, capacity * chunks, LANES)
    received = lax.all_to_all(send, ("expert", "tensor"), split_axis=0, concat_axis=0, tiled=True)
    outputs = expert_block(received.reshape(rows_all, width), w_gate_up, w_down)
    outputs = outputs.reshape(experts_all, capacity * chunks, LANES)
    returned = lax.all_to_all(
        outputs, ("expert", "tensor"), split_axis=0, concat_axis=0, tiled=True
    )
    returned = returned.reshape(rows_all, chunks, LANES)
    combine = jnp.sum(
        jnp.where(place, route_weight[None, :, :], 0.0), axis=2
    ).T
    hi, mid, lo = split_bf16(combine)
    stacked = jnp.concatenate([hi, mid, lo], axis=0)
    parts = jnp.einsum("ir,rcl->icl", stacked, returned, preferred_element_type=jnp.float32)
    moe_sum = (parts[:tok_count] + parts[tok_count : 2 * tok_count]) + parts[2 * tok_count :]
    mixed = (residual + moe_sum.reshape(tok_count, width)).astype(jnp.bfloat16)
    return (attended, mixed)


def solution(mesh):
    in_specs = (
        P(("expert", "tensor"), None),
        P("expert", "tensor"),
        P("tensor", "expert"),
        P(),
        P(("expert", "tensor"), None),
        P(("expert", "tensor"), None),
        P(("expert", "tensor"), None, None),
        P(("expert", "tensor"), None, None),
    )
    out_specs = (P(("expert", "tensor"), None), P(("expert", "tensor"), None))
    return jax.shard_map(
        on_device, mesh=mesh, in_specs=in_specs, out_specs=out_specs, check_vma=False
    )
```

time: 858 us -> 609 us (0.71); the launches traced: 848 us -> 608 us
  waiting for transfers between devices: 444 us -> 319 us
  blocking collectives: 210 us -> 121 us
  local copies, waits for them, and re-layouts: 109 us -> 72.7 us
  matrix products: 40.8 us -> 51.8 us
    all_to_all x1, waiting for transfers between devices: 234 us -> 112 us  [on_device(): lax.all_to_all(outputs, ('expert', 'tensor'), split_axis=0, concat_axis=0...]
    all_to_all x1, blocking collectives: 210 us -> 121 us  [on_device(): lax.all_to_all(send, ('expert', 'tensor'), split_axis=0, concat_axis=0, t...]
    gather x2 -> x0, local copies, waits for them, and re-layouts: 27.8 us -> none  [the longest x1 20 us: on_device(): picked = returned[target].reshape(tok_count, top_count, width)]
    convert_element_type x0 -> x1, local copies, waits for them, and re-layouts: none -> 24.2 us  [on_device(): send = jnp.einsum('ri,icl->rcl', dispatch, normed3, preferred_element_typ...]
    scatter x1 -> x0, local copies, waits for them, and re-layouts: 18.2 us -> none  [on_device(): jnp.zeros((experts_all * capacity, width), jnp.bfloat16).at[target]]
    reshape x4, local copies, waits for them, and re-layouts: 61.9 us -> 45.8 us  [the longest x1 15 us: on_device(): outputs = outputs.reshape(experts_all, capacity * chunks, LANES)]
    dot_general x1 -> x2, matrix products: 18.2 us -> 21.2 us  [the longest x1 18.2 us: expert_block(): jnp.dot(received, w_gate_up[0], preferred_element_type=jnp.float32)]
  transfers between devices with their start and end apart: 3 -> 3, of which waited for: 3 -> 3; matrix products, arithmetic and copies ran while one was open for 0% -> 2% of each run, Pallas kernels for 0% -> 0%
where the time goes in v1:
time: 609 us; the launch traced here: 608 us
  waiting for transfers between devices  319 us (52%)
  blocking collectives  121 us (20%)
  local copies, waits for them, and re-layouts  72.7 us (12%)
  matrix products  51.8 us (9%)
  other arithmetic  19.9 us (3%)
  between operations  14.2 us (2%)
  starting transfers between devices  10.1 us (2%)
    all_gather x1, waiting for transfers between devices, on_device(): lax.all_gather(w_out, 'expert', axis=1, tiled=True)  132 us
    all_to_all x1, blocking collectives, on_device(): lax.all_to_all(send, ('expert', 'tensor'), split_axis=0, concat_axis=0, t...  121 us
    all_to_all x1, waiting for transfers between devices, on_device(): lax.all_to_all(outputs, ('expert', 'tensor'), split_axis=0, concat_axis=0...  112 us
    reduce_scatter x1, waiting for transfers between devices, on_device(): lax.psum_scatter(partial_sums, 'tensor', scatter_dimension=0, tiled=True)  73.1 us
    convert_element_type x1, local copies, waits for them, and re-layouts, on_device(): send = jnp.einsum('ri,icl->rcl', dispatch, normed3, preferred_element_typ...  24.2 us
    dot_general x1, matrix products, expert_block(): jnp.dot(received, w_gate_up[0], preferred_element_type=jnp.float32)  18.2 us
    reshape x1, local copies, waits for them, and re-layouts, on_device(): outputs = outputs.reshape(experts_all, capacity * chunks, LANES)  15 us
    reshape x1, local copies, waits for them, and re-layouts, on_device(): outputs = expert_block(received.reshape(rows_all, width), w_gate_up, w_down)  14.8 us
  transfers between devices with their start and end apart: 3, of which 3 were waited for; matrix products, arithmetic and copies ran while one was open for 2% of the time, Pallas kernels for 0%

profile of v1, /device:TPU:54, one launch (start us, length us, event | category | flops | bytes accessed | tf_op | source)
XLA Modules:
  0.0 607.9 jit_solution(6904759618319250274)
XLA Ops:
  7.2 0.0 copy-start
  7.2 0.0 all-gather.2.cloned.1.call-start
  7.2 0.7 all-gather.2.cloned.1.call-update
  7.9 0.0 reduce-scatter.2.cloned.1.call-start
  8.0 132.3 %all-gather.2.cloned.1.call-done = bf16[1024,4096]{1,0:T(8,128)(2,1)} async-done(((bf16[1024,128]{1,0:T(8,128)(2,1)}), bf16[1024,4096]{1,0:T(8,128)(2,1)}) %all-gather.2.cloned.1.call-update) | async-done | bytes 8388624 | tf_op jit(solution)/shard_map/all_gather | solution.py:31
  140.3 0.0 copy-done
  140.3 10.0 %fusion.26 = f32[512,4096]{1,0:T(8,128)} fusion(bf16[512,1024]{1,0:T(8,128)(2,1)S(1)} %copy-done, bf16[1024,4096]{1,0:T(8,128)(2,1)} %all-gather.2.cloned.1.call-done), kind=kOutput, calls=%fused_computation.46 | convolution fusion | flops 4294967296 | bytes 17825792 | tf_op jit(solution)/shard_map/dot_general | solution.py:29
  150.3 0.0 copy-start.6
  150.3 0.0 copy-start.3
  150.3 0.0 reduce-scatter.2.cloned.1.call-update
  150.3 0.7 copy-done.6
  151.0 0.0 copy-start.5
  151.0 0.1 copy.37
  151.1 0.1 eq.43
  151.2 0.1 eq.39
  151.3 0.1 copy.39
  151.4 0.2 fusion.19
  151.7 0.1 copy.40
  151.8 0.4 fusion.18
  152.1 0.1 reduce_sum.30
  152.3 4.2 fusion.3
  156.5 73.1 %reduce-scatter.2.cloned.1.call-done = f32[128,4096]{1,0:T(8,128)} async-done(((f32[512,4096]{1,0:T(8,128)}), f32[128,4096]{1,0:T(8,128)}) %reduce-scatter.2.cloned.1.call-update) | async-done | bytes 2097168 | tf_op jit(solution)/shard_map/reduce_scatter | solution.py:34
  229.6 0.0 copy-done.3
  229.6 0.0 copy-start.2
  229.6 2.1 multiply_reduce_fusion
  231.7 0.0 copy-done.5
  231.7 0.1 copy-done.2
  231.8 2.9 convolution_convert_fusion.1
  234.8 24.2 %copy.44 = bf16[1152,32,128]{2,1,0:T(8,128)(2,1)S(1)} copy(bf16[1152,32,128]{2,0,1:T(8,128)(2,1)S(1)} %convolution_convert_fusion.1) | data formatting | bytes 18874368 | tf_op jit(solution)/shard_map/convert_element_type | solution.py:57
  258.9 120.8 %all_to_all.10 = bf16[128,288,128]{2,1,0:T(8,128)(2,1)} all-to-all(bf16[128,288,128]{2,1,0:T(8,128)(2,1)S(1)} %bitcast.48), channel_id=1, replica_groups=mesh['expert'=32,'tensor'=4] {'expert','tensor'}, dimensions={0} | all-to-all | bytes 18874368 | tf_op jit(solution)/shard_map/all_to_all | solution.py:59
  379.7 14.8 %reshape.59 = bf16[1152,4096]{1,0:T(8,128)(2,1)} reshape(bf16[128,288,128]{2,1,0:T(8,128)(2,1)} %all_to_all.10) | data formatting | bytes 18874368 | tf_op jit(solution)/shard_map/reshape | solution.py:60
  394.6 18.2 %fusion = f32[1152,1536]{1,0:T(8,128)S(1)} fusion(bf16[1152,4096]{1,0:T(8,128)(2,1)} %reshape.59, bf16[1,4096,1536]{2,1,0:T(8,128)(2,1)} %param.14), kind=kOutput, calls=%fused_computation.2 | convolution fusion | flops 14495514624 | bytes 29097984 | tf_op jit(solution)/shard_map/dot_general | solution.py:11
  412.8 12.5 %convolution_convert_fusion = bf16[1152,4096]{1,0:T(8,128)(2,1)} fusion(bf16[1,768,4096]{2,1,0:T(8,128)(2,1)} %param.15, f32[1152,1536]{1,0:T(8,128)S(1)} %fusion), kind=kOutput, calls=%fused_computation | convolution fusion | flops 7257784320 | bytes 22806528 | tf_op jit(solution)/shard_map/dot_general | solution.py:15
  425.3 15.0 %reshape.60 = bf16[128,288,128]{2,1,0:T(8,128)(2,1)} reshape(bf16[1152,4096]{1,0:T(8,128)(2,1)} %convolution_convert_fusion) | data formatting | bytes 18874368 | tf_op jit(solution)/shard_map/reshape | solution.py:61
  440.3 0.0 copy-start.7
  440.3 10.0 %all-to-all-start.1 = ((bf16[128,288,128]{2,1,0:T(8,128)(2,1)}), bf16[128,288,128]{2,1,0:T(8,128)(2,1)}, u32[]{:S(2)}, u32[]{:S(2)}) async-start(bf16[128,288,128]{2,1,0:T(8,128)(2,1)} %reshape.60), calls=%async_computation.2 | async-start | bytes 18874368 | tf_op jit(solution)/shard_map/all_to_all | solution.py:62
  450.3 0.0 copy-done.7
  450.3 6.9 %select_reduce_fusion = f32[1152,128]{1,0:T(8,128)} fusion(f32[128,8]{0,1:T(8,128)S(1)} %copy-done.7, s32[128,8]{0,1:T(8,128)S(1)} %multiply_add_fusion), kind=kLoop, calls=%fused_computation.5 | loop fusion | flops 3391488 | bytes 598016 | tf_op jit(solution)/shard_map/reduce_sum | solution.py:66
  457.2 1.3 copy.42
  458.6 0.8 fusion.21
  459.3 112.5 %all-to-all-done.1 = bf16[128,288,128]{2,1,0:T(8,128)(2,1)} async-done(((bf16[128,288,128]{2,1,0:T(8,128)(2,1)}), bf16[128,288,128]{2,1,0:T(8,128)(2,1)}, u32[]{:S(2)}, u32[]{:S(2)}) %all-to-all-start.1) | async-done | bytes 9437216 | tf_op jit(solution)/shard_map/all_to_all | solution.py:62
  571.8 0.0 copy-start.4
  571.8 13.0 %copy.45 = bf16[1152,32,128]{0,2,1:T(8,128)(2,1)} copy(bf16[1152,32,128]{2,1,0:T(8,128)(2,1)} %bitcast.8) | data formatting | bytes 18874368 | tf_op jit(solution)/shard_map/reshape | solution.py:65
  584.8 0.0 copy-done.4
  584.8 8.0 %fusion.10 = f32[384,4096]{0,1:S(1)} fusion(bf16[1152,4096]{0,1:T(8,128)(2,1)} %bitcast.49, bf16[128,1152]{1,0:T(8,128)(2,1)S(1)} %copy-done.4, bf16[128,1152]{1,0:T(8,128)(2,1)S(1)} %get-tuple-element.4, bf16[128,1152]{1,0:T(8,128)(2,1)S(1)} %bitcast_convert_fusion), kind=kOutput, calls=%fused_computation.20 | convolution fusion | flops 3626532864 | bytes 16613376
  592.9 1.7 slice_add_fusion
  594.5 0.0 copy-start.1
  594.5 3.0 copy.47
  597.5 3.6 add_convert_fusion
  601.1 0.0 copy-done.1
  (8 shorter events, 0.2 us)
Async XLA Ops:
  7.2 133.1 %copy-start = (bf16[512,1024]{1,0:T(8,128)(2,1)S(1)}, bf16[512,1024]{1,0:T(8,128)(2,1)}, u32[]{:S(2)}) copy-start(bf16[512,1024]{1,0:T(8,128)(2,1)} %param.9) | copy-start | bytes 3145732
  7.2 133.1 %all-gather.2.cloned.1.call-start = ((), (), s32[]{:S(2)}) async-start(), calls=%async_computation.3 | async-start | bytes 8650752 | tf_op jit(solution)/shard_map/all_gather | solution.py:31
  7.9 221.7 %reduce-scatter.2.cloned.1.call-start = ((), (), s32[]{:S(2)}) async-start(), calls=%async_computation.4 | async-start | bytes 10485760 | tf_op jit(solution)/shard_map/reduce_scatter | solution.py:34
  150.3 0.7 copy-start.6
  150.3 79.3 %copy-start.3 = (bf16[128,4096]{1,0:T(8,128)(2,1)S(1)}, bf16[128,4096]{1,0:T(8,128)(2,1)}, u32[]{:S(2)}) copy-start(bf16[128,4096]{1,0:T(8,128)(2,1)} %param.8) | copy-start | bytes 3145732
  151.0 80.7 %copy-start.5 = (f32[4096]{0:T(1024)S(1)}, f32[4096]{0:T(1024)}, u32[]{:S(2)}) copy-start(f32[4096]{0:T(1024)} %param.11) | copy-start | bytes 49156
  229.6 2.2 copy-start.2
  440.3 10.0 %copy-start.7 = (f32[128,8]{0,1:T(8,128)S(1)}, f32[128,8]{0,1:T(8,128)}, u32[]{:S(2)}) copy-start(f32[128,8]{0,1:T(8,128)} %param.13) | copy-start | bytes 12292
  440.3 131.5 %all-to-all-start.1 = ((bf16[128,288,128]{2,1,0:T(8,128)(2,1)}), bf16[128,288,128]{2,1,0:T(8,128)(2,1)}, u32[]{:S(2)}, u32[]{:S(2)}) async-start(bf16[128,288,128]{2,1,0:T(8,128)(2,1)} %reshape.60), calls=%async_computation.2 | async-start | bytes 18874368 | tf_op jit(solution)/shard_map/all_to_all | solution.py:62
  571.8 13.0 %copy-start.4 = (bf16[128,1152]{1,0:T(8,128)(2,1)S(1)}, bf16[128,1152]{1,0:T(8,128)(2,1)}, u32[]{:S(2)}) copy-start(bf16[128,1152]{1,0:T(8,128)(2,1)} %get-tuple-element.5) | copy-start | bytes 884740
  594.5 6.6 %copy-start.1 = (bf16[512,1024]{1,0:T(8,128)(2,1)S(1)}, bf16[512,1024]{1,0:T(8,128)(2,1)}, u32[]{:S(2)}) copy-start(bf16[512,1024]{1,0:T(8,128)(2,1)} %param.9) | copy-start | bytes 3145732
Sparse Core Ops, SparseCore 0:
  10.8 129.4 all-gather.1
  150.4 79.0 reduce-scatter.1

commit v2 on v0

v2 whole, which is shorter than its diff:
```python
import jax
import jax.numpy as jnp
import numpy as np
from jax import lax
from jax.sharding import Mesh
from jax.sharding import PartitionSpec as P

LANES = 128
ALL = ("expert", "xlo", "core")


def expert_block(received, w_gate_up, w_down):
    hidden_units = w_down.shape[1]
    gate_and_up = jnp.dot(received, w_gate_up[0], preferred_element_type=jnp.float32)
    activated = (jax.nn.silu(gate_and_up[:, :hidden_units]) * gate_and_up[:, hidden_units:]).astype(
        jnp.bfloat16
    )
    return jnp.dot(activated, w_down[0], preferred_element_type=jnp.float32).astype(jnp.bfloat16)


def project(context, w_out):
    n_x = lax.axis_size("xlo")
    n_c = lax.axis_size("core")
    rows = context.shape[0] // (n_x * n_c)
    context = context.reshape(n_x, n_c, rows, -1).transpose(1, 0, 2, 3).reshape(n_x * n_c * rows, -1)
    partial_sums = jnp.dot(
        context,
        lax.all_gather(w_out, "expert", axis=1, tiled=True),
        preferred_element_type=jnp.float32,
    )
    width = partial_sums.shape[1]
    chip_sums = lax.psum_scatter(partial_sums, "core", scatter_dimension=0, tiled=True)
    chip_sums = chip_sums.reshape(n_x, rows, width)
    me = lax.axis_index("xlo")
    own = lax.dynamic_index_in_dim(chip_sums, me, axis=0, keepdims=False)
    other = lax.dynamic_index_in_dim(chip_sums, 1 - me, axis=0, keepdims=False)
    arrived = lax.ppermute(other.astype(jnp.bfloat16), "xlo", perm=[(0, 1), (1, 0)])
    return own + arrived.astype(jnp.float32)


def on_device(hidden_in, context, w_out, norm_gain, expert_ids, route_weight, w_gate_up, w_down):
    tok_count, width = hidden_in.shape
    chunks = width // LANES
    projected = project(context, w_out)
    residual = hidden_in.astype(jnp.float32) + projected
    attended = residual.astype(jnp.bfloat16)
    inverse = lax.rsqrt(jnp.mean(residual * residual, axis=1, keepdims=True) + 1e-06)
    normed = (residual * inverse * norm_gain[None, :]).astype(jnp.bfloat16)
    top_count = expert_ids.shape[1]
    experts_all = lax.axis_size(ALL)
    capacity = tok_count * top_count * 9 // (8 * experts_all)
    rows_all = experts_all * capacity
    chosen = expert_ids.reshape(-1)
    onehot = (chosen[:, None] == jnp.arange(experts_all, dtype=jnp.int32)[None, :]).astype(
        jnp.int32
    )
    before = jnp.cumsum(onehot, axis=0) - onehot
    slots = jnp.sum(before * onehot, axis=1)
    target = chosen * capacity + slots
    token_index = jnp.arange(tok_count * top_count, dtype=jnp.int32) // top_count
    source = jnp.full((rows_all,), tok_count, jnp.int32).at[target].set(token_index)
    normed3 = jnp.concatenate(
        [normed.reshape(tok_count, chunks, LANES), jnp.zeros((1, chunks, LANES), jnp.bfloat16)],
        axis=0,
    )
    send = jnp.take(normed3, source, axis=0)
    send = send.reshape(experts_all, capacity * chunks, LANES)
    received = lax.all_to_all(send, ALL, split_axis=0, concat_axis=0, tiled=True)
    outputs = expert_block(received.reshape(rows_all, width), w_gate_up, w_down)
    outputs = outputs.reshape(experts_all, capacity * chunks, LANES)
    returned = lax.all_to_all(outputs, ALL, split_axis=0, concat_axis=0, tiled=True)
    returned = returned.reshape(rows_all, chunks, LANES)
    picked = jnp.take(returned, target, axis=0).reshape(tok_count, top_count, chunks, LANES)
    moe_sum = jnp.sum(route_weight[:, :, None, None] * picked.astype(jnp.float32), axis=1)
    mixed = (residual + moe_sum.reshape(tok_count, width)).astype(jnp.bfloat16)
    return (attended, mixed)


def solution(mesh):
    n_expert = mesh.shape["expert"]
    n_tensor = mesh.shape["tensor"]
    n_core = 2 if n_tensor % 2 == 0 else 1
    devices = np.asarray(mesh.devices).reshape(n_expert, n_tensor // n_core, n_core)
    mesh3 = Mesh(devices, ALL)
    tensor = ("xlo", "core")
    in_specs = (
        P(ALL, None),
        P("expert", tensor),
        P(tensor, "expert"),
        P(),
        P(ALL, None),
        P(ALL, None),
        P(ALL, None, None),
        P(ALL, None, None),
    )
    out_specs = (P(ALL, None), P(ALL, None))
    return jax.shard_map(
        on_device, mesh=mesh3, in_specs=in_specs, out_specs=out_specs, check_vma=False
    )
```

time: 858 us -> 562 us (0.66); the launches traced: 848 us -> 561 us
  waiting for transfers between devices: 444 us -> 292 us
  blocking collectives: 210 us -> 120 us
  local copies, waits for them, and re-layouts: 109 us -> 59.4 us
    all_to_all x1, waiting for transfers between devices: 234 us -> 122 us  [on_device(): lax.all_to_all(outputs, ALL, split_axis=0, concat_axis=0, tiled=True)]
    all_to_all x1, blocking collectives: 210 us -> 120 us  [on_device(): lax.all_to_all(send, ALL, split_axis=0, concat_axis=0, tiled=True)]
    reduce_scatter x1, waiting for transfers between devices: 77.2 us -> 19.2 us  [project(): lax.psum_scatter(partial_sums, 'core', scatter_dimension=0, tiled=True)]
    reshape x4 -> x3, local copies, waits for them, and re-layouts: 61.9 us -> 29.9 us  [the longest x1 15 us: on_device(): outputs = outputs.reshape(experts_all, capacity * chunks, LANES)]
    ppermute x0 -> x1, waiting for transfers between devices: none -> 18.9 us  [project(): lax.ppermute(other.astype(jnp.bfloat16), 'xlo', perm=[(0, 1), (1, 0)])]
    scatter x1, local copies, waits for them, and re-layouts: 18.2 us -> 4.32 us  [on_device(): jnp.full((rows_all,), tok_count, jnp.int32).at[target].set(token_index)]
    select_n x2 -> x4, other arithmetic: 0.02 us -> 8.9 us  [the longest x2 8.89 us: on_device(): send = jnp.take(normed3, source, axis=0)]
  transfers between devices with their start and end apart: 3 -> 4, of which waited for: 3 -> 4; matrix products, arithmetic and copies ran while one was open for 0% -> 1% of each run, Pallas kernels for 0% -> 0%
where the time goes in v2:
time: 562 us; the launch traced here: 561 us
  waiting for transfers between devices  292 us (52%)
  blocking collectives  120 us (21%)
  local copies, waits for them, and re-layouts  59.4 us (11%)
  matrix products  40.8 us (7%)
  other arithmetic  23.4 us (4%)
  between operations  14.3 us (3%)
  starting transfers between devices  11 us (2%)
    all_gather x1, waiting for transfers between devices, project(): lax.all_gather(w_out, 'expert', axis=1, tiled=True)  131 us
    all_to_all x1, waiting for transfers between devices, on_device(): lax.all_to_all(outputs, ALL, split_axis=0, concat_axis=0, tiled=True)  122 us
    all_to_all x1, blocking collectives, on_device(): lax.all_to_all(send, ALL, split_axis=0, concat_axis=0, tiled=True)  120 us
    reduce_scatter x1, waiting for transfers between devices, project(): lax.psum_scatter(partial_sums, 'core', scatter_dimension=0, tiled=True)  19.2 us
    ppermute x1, waiting for transfers between devices, project(): lax.ppermute(other.astype(jnp.bfloat16), 'xlo', perm=[(0, 1), (1, 0)])  18.9 us
    dot_general x1, matrix products, expert_block(): jnp.dot(received, w_gate_up[0], preferred_element_type=jnp.float32)  18.2 us
    reshape x1, local copies, waits for them, and re-layouts, on_device(): outputs = outputs.reshape(experts_all, capacity * chunks, LANES)  15 us
    reshape x1, local copies, waits for them, and re-layouts, on_device(): outputs = expert_block(received.reshape(rows_all, width), w_gate_up, w_down)  14.8 us
  transfers between devices with their start and end apart: 4, of which 4 were waited for; matrix products, arithmetic and copies ran while one was open for 1% of the time, Pallas kernels for 0%

profile of v2, /device:TPU:54, one launch (start us, length us, event | category | flops | bytes accessed | tf_op | source)
XLA Modules:
  0.0 561.1 jit_solution(10142530440497520180)
XLA Ops:
  7.2 0.0 all-gather.2.cloned.1.call-start
  7.2 0.7 all-gather.2.cloned.1.call-update
  7.9 0.0 reduce-scatter.2.cloned.1.call-start
  7.9 1.3 copy.29
  9.2 131.0 %all-gather.2.cloned.1.call-done = bf16[1024,4096]{1,0:T(8,128)(2,1)} async-done(((bf16[1024,128]{1,0:T(8,128)(2,1)}), bf16[1024,4096]{1,0:T(8,128)(2,1)}) %all-gather.2.cloned.1.call-update) | async-done | bytes 8388624 | tf_op jit(solution)/shard_map/all_gather | solution.py:28
  140.2 10.0 %fusion.22 = f32[512,4096]{1,0:T(8,128)} fusion(bf16[512,1024]{1,0:T(8,128)(2,1)S(1)} %bitcast.54, bf16[1024,4096]{1,0:T(8,128)(2,1)} %all-gather.2.cloned.1.call-done), kind=kOutput, calls=%fused_computation.50 | convolution fusion | flops 4294967296 | bytes 17825792 | tf_op jit(solution)/shard_map/dot_general | solution.py:26
  150.3 0.0 copy-start
  150.3 0.0 reduce-scatter.2.cloned.1.call-update
  150.3 0.0 copy-start.1
  150.3 0.6 copy-done
  151.0 0.1 copy.31
  151.1 0.1 eq.26
  151.2 0.1 copy.33
  151.3 0.2 fusion.12
  151.6 19.2 %reduce-scatter.2.cloned.1.call-done = f32[256,4096]{1,0:T(8,128)} async-done(((f32[512,4096]{1,0:T(8,128)}), f32[256,4096]{1,0:T(8,128)}) %reduce-scatter.2.cloned.1.call-update) | async-done | bytes 4194320 | tf_op jit(solution)/shard_map/reduce_scatter | solution.py:32
  170.8 1.7 fusion.8
  172.5 0.9 collective-permute-start
  173.5 0.1 reshape.112
  173.5 0.1 copy.34
  173.7 0.1 copy.37
  173.8 0.1 mul.60
  173.9 0.4 fusion.11
  174.2 4.3 scatter_custom_fusion
  178.6 0.2 broadcast_in_dim.39
  178.8 0.1 copy.38
  178.9 0.2 copy.39
  179.1 18.9 %collective-permute-done = bf16[128,4096]{1,0:T(8,128)(2,1)} collective-permute-done((bf16[128,4096]{1,0:T(8,128)(2,1)S(1)}, bf16[128,4096]{1,0:T(8,128)(2,1)}, u32[]{:S(2)}, u32[]{:S(2)}) %collective-permute-start) | collective-permute-done | bytes 1048608 | tf_op jit(solution)/shard_map/ppermute | solution.py:37
  198.0 2.7 multiply_reduce_fusion.1
  200.7 0.0 copy-done.1
  200.7 0.3 fusion.9
  201.1 0.2 copy.40
  201.3 0.2 concatenate.3
  201.5 6.1 %gather_fusion = bf16[1152,32,128]{2,1,0:T(8,128)(2,1)} fusion(bf16[129,32,128]{2,1,0:T(8,128)(2,1)S(1)} %concatenate.3, s32[2048]{0:T(1024)S(1)} %pad_clamp_fusion), kind=kCustom, calls=%fused_computation | custom fusion | bytes 18878976 | tf_op jit(solution)/shard_map/jit(_take)/gather | solution.py:66
  207.6 8.9 %bitcast_select_fusion = bf16[128,288,128]{2,1,0:T(8,128)(2,1)S(1)} fusion(pred[128,288]{1,0:T(8,128)(4,1)S(1)} %copy.39, bf16[128,288,128]{2,1,0:T(8,128)(2,1)} %bitcast.48), kind=kLoop, calls=%fused_computation.7 | loop fusion | flops 4718592 | bytes 18911232 | tf_op jit(solution)/shard_map/jit(_take)/select_n | solution.py:66
  216.5 120.5 %all_to_all.10 = bf16[128,288,128]{2,1,0:T(8,128)(2,1)} all-to-all(bf16[128,288,128]{2,1,0:T(8,128)(2,1)S(1)} %bitcast_select_fusion), channel_id=1, replica_groups=mesh['expert'=32,'xlo'=2,'core'=2] {'expert','xlo','core'}, dimensions={0} | all-to-all | bytes 18874368 | tf_op jit(solution)/shard_map/all_to_all | solution.py:68
  337.0 14.8 %reshape.115 = bf16[1152,4096]{1,0:T(8,128)(2,1)} reshape(bf16[128,288,128]{2,1,0:T(8,128)(2,1)} %all_to_all.10) | data formatting | bytes 18874368 | tf_op jit(solution)/shard_map/reshape | solution.py:69
  351.8 18.2 %fusion = f32[1152,1536]{1,0:T(8,128)S(1)} fusion(bf16[1152,4096]{1,0:T(8,128)(2,1)} %reshape.115, bf16[1,4096,1536]{2,1,0:T(8,128)(2,1)} %param.14), kind=kOutput, calls=%fused_computation.5 | convolution fusion | flops 14495514624 | bytes 29097984 | tf_op jit(solution)/shard_map/dot_general | solution.py:14
  370.1 12.5 %convolution_convert_fusion = bf16[1152,4096]{1,0:T(8,128)(2,1)} fusion(bf16[1,768,4096]{2,1,0:T(8,128)(2,1)} %param.15, f32[1152,1536]{1,0:T(8,128)S(1)} %fusion), kind=kOutput, calls=%fused_computation.4 | convolution fusion | flops 7257784320 | bytes 22806528 | tf_op jit(solution)/shard_map/dot_general | solution.py:18
  382.6 15.0 %reshape.116 = bf16[128,288,128]{2,1,0:T(8,128)(2,1)} reshape(bf16[1152,4096]{1,0:T(8,128)(2,1)} %convolution_convert_fusion) | data formatting | bytes 18874368 | tf_op jit(solution)/shard_map/reshape | solution.py:70
  397.6 0.0 copy-start.2
  397.6 10.0 %all-to-all-start.1 = ((bf16[128,288,128]{2,1,0:T(8,128)(2,1)}), bf16[128,288,128]{2,1,0:T(8,128)(2,1)}, u32[]{:S(2)}, u32[]{:S(2)}) async-start(bf16[128,288,128]{2,1,0:T(8,128)(2,1)} %reshape.116), calls=%async_computation.2 | async-start | bytes 18874368 | tf_op jit(solution)/shard_map/all_to_all | solution.py:71
  407.6 0.1 reduce_sum.32
  407.7 0.1 copy.36
  407.9 0.0 copy-done.2
  407.9 0.1 copy.30
  408.0 121.9 %all-to-all-done.1 = bf16[128,288,128]{2,1,0:T(8,128)(2,1)} async-done(((bf16[128,288,128]{2,1,0:T(8,128)(2,1)}), bf16[128,288,128]{2,1,0:T(8,128)(2,1)}, u32[]{:S(2)}, u32[]{:S(2)}) %all-to-all-start.1) | async-done | bytes 9437216 | tf_op jit(solution)/shard_map/all_to_all | solution.py:71
  529.9 13.5 %gather_fusion.1 = bf16[1024,32,128]{2,1,0:T(8,128)(2,1)} fusion(bf16[1152,32,128]{2,1,0:T(8,128)(2,1)} %bitcast.15, s32[1024]{0:T(1024)S(1)} %broadcast_clamp_fusion), kind=kCustom, calls=%fused_computation.1 | custom fusion | bytes 16781312 | tf_op jit(solution)/shard_map/jit(_take)/gather | solution.py:73
  543.4 8.2 %multiply_reduce_fusion = f32[128,32,128]{2,1,0:T(8,128)S(1)} fusion(f32[128,8]{1,0:T(8,128)S(1)} %copy.30, pred[128,8]{1,0:T(8,128)(4,1)S(1)} %copy.36, bf16[1024,32,128]{2,1,0:T(8,128)(2,1)} %gather_fusion.1), kind=kLoop, calls=%fused_computation.3 | loop fusion | flops 16252928 | bytes 10490880 | tf_op jit(solution)/shard_map/reduce_sum | solution.py:74
  551.6 2.6 fusion.4
  (15 shorter events, 0.2 us)
Async XLA Ops:
  7.2 133.1 %all-gather.2.cloned.1.call-start = ((), (), s32[]{:S(2)}) async-start(), calls=%async_computation.3 | async-start | bytes 8650752 | tf_op jit(solution)/shard_map/all_gather | solution.py:28
  7.9 162.9 %reduce-scatter.2.cloned.1.call-start = ((), (), s32[]{:S(2)}) async-start(), calls=%async_computation.4 | async-start | bytes 12582912 | tf_op jit(solution)/shard_map/reduce_scatter | solution.py:32
  150.3 0.7 copy-start
  150.3 50.4 %copy-start.1 = (f32[4096]{0:T(1024)S(1)}, f32[4096]{0:T(1024)}, u32[]{:S(2)}) copy-start(f32[4096]{0:T(1024)} %param.11) | copy-start | bytes 49156
  172.5 25.5 %collective-permute-start = (bf16[128,4096]{1,0:T(8,128)(2,1)S(1)}, bf16[128,4096]{1,0:T(8,128)(2,1)}, u32[]{:S(2)}, u32[]{:S(2)}) collective-permute-start(bf16[128,4096]{1,0:T(8,128)(2,1)S(1)} %fusion.8), channel_id=1, source_target_pairs={{0,2},{2,0},{1,3},{3,1},{4,6},{6,4},{5,7},{7,5},{8,10},{10,8},{9,1... | collective-permute-start | bytes 3145736 | tf_op jit(solution)/shard_map/ppermute | solution.py:37
  397.6 10.3 %copy-start.2 = (f32[128,8]{0,1:T(8,128)S(1)}, f32[128,8]{0,1:T(8,128)}, u32[]{:S(2)}) copy-start(f32[128,8]{0,1:T(8,128)} %param.13) | copy-start | bytes 12292
  397.6 132.3 %all-to-all-start.1 = ((bf16[128,288,128]{2,1,0:T(8,128)(2,1)}), bf16[128,288,128]{2,1,0:T(8,128)(2,1)}, u32[]{:S(2)}, u32[]{:S(2)}) async-start(bf16[128,288,128]{2,1,0:T(8,128)(2,1)} %reshape.116), calls=%async_computation.2 | async-start | bytes 18874368 | tf_op jit(solution)/shard_map/all_to_all | solution.py:71
Sparse Core Ops, SparseCore 0:
  10.7 129.4 all-gather.1
  150.4 20.3 reduce-scatter.1

commit v3 on v2

--- a/solution.py
+++ b/solution.py
@@ -2,6 +2,8 @@
 import jax.numpy as jnp
 import numpy as np
 from jax import lax
+from jax.experimental import pallas as pl
+from jax.experimental.pallas import tpu as pltpu
 from jax.sharding import Mesh
 from jax.sharding import PartitionSpec as P
 
@@ -18,6 +20,62 @@
     return jnp.dot(activated, w_down[0], preferred_element_type=jnp.float32).astype(jnp.bfloat16)
 
 
+def gather_kernel(n, w_ref, out_ref, send_sem, recv_sem, local_sem):
+    me = lax.axis_index("expert")
+    cols = w_ref.shape[1]
+    barrier = pltpu.get_barrier_semaphore()
+    for step in range(1, n):
+        pl.semaphore_signal(
+            barrier, inc=1, device_id={"expert": lax.rem(me + step, n)},
+            device_id_type=pl.DeviceIdType.MESH,
+        )
+    pl.semaphore_wait(barrier, n - 1)
+    mine = out_ref.at[:, pl.ds(pl.multiple_of(me * cols, cols), cols)]
+    local = pltpu.make_async_copy(w_ref, mine, local_sem)
+    local.start()
+    copies = []
+    for step in range(1, n):
+        copy = pltpu.make_async_remote_copy(
+            src_ref=w_ref,
+            dst_ref=mine,
+            send_sem=send_sem.at[step],
+            recv_sem=recv_sem.at[me],
+            device_id={"expert": lax.rem(me + step, n)},
+            device_id_type=pl.DeviceIdType.MESH,
+        )
+        copy.start()
+        copies.append(copy)
+    local.wait()
+    for step in range(1, n):
+        copies[step - 1].wait_send()
+        source = lax.rem(me + n - step, n)
+        pltpu.make_async_remote_copy(
+            src_ref=w_ref,
+            dst_ref=out_ref.at[:, pl.ds(pl.multiple_of(source * cols, cols), cols)],
+            send_sem=send_sem.at[step],
+            recv_sem=recv_sem.at[source],
+            device_id={"expert": source},
+            device_id_type=pl.DeviceIdType.MESH,
+        ).wait_recv()
+
+
+def gather_columns(w_out):
+    n = lax.axis_size("expert")
+    rows, cols = w_out.shape
+    return pl.pallas_call(
+        lambda *refs: gather_kernel(n, *refs),
+        out_shape=jax.ShapeDtypeStruct((rows, cols * n), w_out.dtype),
+        in_specs=[pl.BlockSpec(memory_space=pl.ANY)],
+        out_specs=pl.BlockSpec(memory_space=pl.ANY),
+        scratch_shapes=[
+            pltpu.SemaphoreType.DMA((n,)),
+            pltpu.SemaphoreType.DMA((n,)),
+            pltpu.SemaphoreType.DMA(()),
+        ],
+        compiler_params=pltpu.CompilerParams(collective_id=0, has_side_effects=True),
+    )(w_out)
+
+
 def project(context, w_out):
     n_x = lax.axis_size("xlo")
     n_c = lax.axis_size("core")
@@ -25,7 +83,7 @@
     context = context.reshape(n_x, n_c, rows, -1).transpose(1, 0, 2, 3).reshape(n_x * n_c * rows, -1)
     partial_sums = jnp.dot(
         context,
-        lax.all_gather(w_out, "expert", axis=1, tiled=True),
+        gather_columns(w_out),
         preferred_element_type=jnp.float32,
     )
     width = partial_sums.shape[1]
@@ -63,14 +121,14 @@
         [normed.reshape(tok_count, chunks, LANES), jnp.zeros((1, chunks, LANES), jnp.bfloat16)],
         axis=0,
     )
-    send = jnp.take(normed3, source, axis=0)
+    send = jnp.take(normed3, source, axis=0, mode="clip")
     send = send.reshape(experts_all, capacity * chunks, LANES)
     received = lax.all_to_all(send, ALL, split_axis=0, concat_axis=0, tiled=True)
     outputs = expert_block(received.reshape(rows_all, width), w_gate_up, w_down)
     outputs = outputs.reshape(experts_all, capacity * chunks, LANES)
     returned = lax.all_to_all(outputs, ALL, split_axis=0, concat_axis=0, tiled=True)
     returned = returned.reshape(rows_all, chunks, LANES)
-    picked = jnp.take(returned, target, axis=0).reshape(tok_count, top_count, chunks, LANES)
+    picked = jnp.take(returned, target, axis=0, mode="clip").reshape(tok_count, top_count, chunks, LANES)
     moe_sum = jnp.sum(route_weight[:, :, None, None] * picked.astype(jnp.float32), axis=1)
     mixed = (residual + moe_sum.reshape(tok_count, width)).astype(jnp.bfloat16)
     return (attended, mixed)

time: 562 us -> 588 us (1.046)
  Pallas kernels: 0 us -> 146 us
  waiting for transfers between devices: 292 us -> 185 us
  other arithmetic: 23.4 us -> 12 us
    pallas_call x0 -> x1, Pallas kernels: none -> 146 us  [gather_columns(): pl.pallas_call(lambda *refs: gather_kernel(n, *refs), out_shape=jax.Shape...]
    all_gather x1 -> x0, waiting for transfers between devices: 131 us -> none  [project(): lax.all_gather(w_out, 'expert', axis=1, tiled=True)]
    reduce_scatter x1, waiting for transfers between devices: 19.2 us -> 43.5 us  [project(): lax.psum_scatter(partial_sums, 'core', scatter_dimension=0, tiled=True)]
    select_n x3 -> x1, other arithmetic: 8.9 us -> 0.01 us  [on_device(): jnp.full((rows_all,), tok_count, jnp.int32).at[target].set(token_index)]
  transfers between devices with their start and end apart: 4 -> 3, of which waited for: 4 -> 3; matrix products, arithmetic and copies ran while one was open for 1% -> 1% of each run, Pallas kernels for 0% -> 0%
where the time goes in v3:
time: 588 us; the launch traced here: 587 us
  waiting for transfers between devices  185 us (31%)
  Pallas kernels  146 us (25%)
  blocking collectives  121 us (21%)
  local copies, waits for them, and re-layouts  57.4 us (10%)
  matrix products  40.9 us (7%)
  between operations  14.2 us (2%)
  other arithmetic  12 us (2%)
  starting transfers between devices  10.9 us (2%)
    pallas_call x1, Pallas kernels, gather_columns(): pl.pallas_call(lambda *refs: gather_kernel(n, *refs), out_shape=jax.Shape...  146 us
    all_to_all x1, waiting for transfers between devices, on_device(): lax.all_to_all(outputs, ALL, split_axis=0, concat_axis=0, tiled=True)  122 us
    all_to_all x1, blocking collectives, on_device(): lax.all_to_all(send, ALL, split_axis=0, concat_axis=0, tiled=True)  121 us
    reduce_scatter x1, waiting for transfers between devices, project(): lax.psum_scatter(partial_sums, 'core', scatter_dimension=0, tiled=True)  43.5 us
    ppermute x1, waiting for transfers between devices, project(): lax.ppermute(other.astype(jnp.bfloat16), 'xlo', perm=[(0, 1), (1, 0)])  19.5 us
    dot_general x1, matrix products, expert_block(): jnp.dot(received, w_gate_up[0], preferred_element_type=jnp.float32)  18.2 us
    reshape x1, local copies, waits for them, and re-layouts, on_device(): outputs = outputs.reshape(experts_all, capacity * chunks, LANES)  15 us
    reshape x1, local copies, waits for them, and re-layouts, on_device(): outputs = expert_block(received.reshape(rows_all, width), w_gate_up, w_down)  14.8 us
  transfers between devices with their start and end apart: 3, of which 3 were waited for; matrix products, arithmetic and copies ran while one was open for 1% of the time, Pallas kernels for 0%

profile of v3, /device:TPU:54, one launch (start us, length us, event | category | flops | bytes accessed | tf_op | source)
XLA Modules:
  0.0 587.2 jit_solution(11938918752904897700)
XLA Ops:
  7.2 0.0 copy-start
  7.2 0.0 reduce-scatter.2.cloned.1.call-start
  7.2 146.0 %shard_map.95 = bf16[1024,4096]{1,0:T(8,128)(2,1)} custom-call(bf16[1024,128]{1,0:T(8,128)(2,1)} %refs_0_.1), custom_call_target="tpu_custom_call" | custom-call | tf_op jit(solution)/shard_map/pallas_call | solution.py:65
  153.2 0.0 copy-done
  153.3 0.1 copy.17
  153.3 10.1 %fusion.23 = f32[512,4096]{1,0:T(8,128)} fusion(bf16[512,1024]{1,0:T(8,128)(2,1)S(1)} %bitcast.53, bf16[1024,4096]{1,0:T(8,128)(2,1)} %shard_map.95), kind=kOutput, calls=%fused_computation.46 | convolution fusion | flops 4294967296 | bytes 17825792 | tf_op jit(solution)/shard_map/dot_general | solution.py:84
  163.4 0.0 copy-start.2
  163.4 0.0 reduce-scatter.2.cloned.1.call-update
  163.5 0.0 copy-start.1
  163.5 0.6 copy-done.2
  164.1 0.1 copy.20
  164.2 0.1 eq.29
  164.3 0.1 eq.25
  164.4 0.1 copy.22
  164.5 0.2 fusion.13
  164.8 43.5 %reduce-scatter.2.cloned.1.call-done = f32[256,4096]{1,0:T(8,128)} async-done(((f32[512,4096]{1,0:T(8,128)}), f32[256,4096]{1,0:T(8,128)}) %reduce-scatter.2.cloned.1.call-update) | async-done | bytes 4194320 | tf_op jit(solution)/shard_map/reduce_scatter | solution.py:90
  208.3 1.7 fusion.9
  210.0 0.9 collective-permute-start
  210.9 0.1 copy.23
  211.1 0.1 copy.19
  211.2 0.1 mul.65
  211.3 0.4 fusion.12
  211.7 4.3 scatter_custom_fusion
  216.0 19.5 %collective-permute-done = bf16[128,4096]{1,0:T(8,128)(2,1)} collective-permute-done((bf16[128,4096]{1,0:T(8,128)(2,1)S(1)}, bf16[128,4096]{1,0:T(8,128)(2,1)}, u32[]{:S(2)}, u32[]{:S(2)}) %collective-permute-start) | collective-permute-done | bytes 1048608 | tf_op jit(solution)/shard_map/ppermute | solution.py:95
  235.5 2.7 multiply_reduce_fusion
  238.2 0.0 copy-done.1
  238.2 0.4 fusion.10
  238.5 0.2 copy.24
  238.8 0.2 concatenate.3
  239.0 6.0 %gather_fusion = bf16[1152,32,128]{2,1,0:T(8,128)(2,1)} fusion(bf16[129,32,128]{2,1,0:T(8,128)(2,1)S(1)} %concatenate.3, s32[2048]{0:T(1024)S(1)} %pad_clamp_fusion), kind=kCustom, calls=%fused_computation | custom fusion | bytes 18878976 | tf_op jit(solution)/shard_map/jit(_take)/gather | solution.py:124
  245.0 120.7 %all_to_all.10 = bf16[128,288,128]{2,1,0:T(8,128)(2,1)} all-to-all(bf16[128,288,128]{2,1,0:T(8,128)(2,1)} %bitcast.47), channel_id=1, replica_groups=mesh['expert'=32,'xlo'=2,'core'=2] {'expert','xlo','core'}, dimensions={0} | all-to-all | bytes 18874368 | tf_op jit(solution)/shard_map/all_to_all | solution.py:126
  365.7 14.8 %reshape.105 = bf16[1152,4096]{1,0:T(8,128)(2,1)} reshape(bf16[128,288,128]{2,1,0:T(8,128)(2,1)} %all_to_all.10) | data formatting | bytes 18874368 | tf_op jit(solution)/shard_map/reshape | solution.py:127
  380.5 18.2 %fusion.1 = f32[1152,1536]{1,0:T(8,128)S(1)} fusion(bf16[1152,4096]{1,0:T(8,128)(2,1)} %reshape.105, bf16[1,4096,1536]{2,1,0:T(8,128)(2,1)} %param.14), kind=kOutput, calls=%fused_computation.6 | convolution fusion | flops 14495514624 | bytes 29097984 | tf_op jit(solution)/shard_map/dot_general | solution.py:16
  398.7 12.5 %convolution_convert_fusion = bf16[1152,4096]{1,0:T(8,128)(2,1)} fusion(bf16[1,768,4096]{2,1,0:T(8,128)(2,1)} %param.15, f32[1152,1536]{1,0:T(8,128)S(1)} %fusion.1), kind=kOutput, calls=%fused_computation.5 | convolution fusion | flops 7257784320 | bytes 22806528 | tf_op jit(solution)/shard_map/dot_general | solution.py:20
  411.2 15.0 %reshape.106 = bf16[128,288,128]{2,1,0:T(8,128)(2,1)} reshape(bf16[1152,4096]{1,0:T(8,128)(2,1)} %convolution_convert_fusion) | data formatting | bytes 18874368 | tf_op jit(solution)/shard_map/reshape | solution.py:128
  426.3 0.0 copy-start.3
  426.3 9.9 %all-to-all-start.1 = ((bf16[128,288,128]{2,1,0:T(8,128)(2,1)}), bf16[128,288,128]{2,1,0:T(8,128)(2,1)}, u32[]{:S(2)}, u32[]{:S(2)}) async-start(bf16[128,288,128]{2,1,0:T(8,128)(2,1)} %reshape.106), calls=%async_computation.2 | async-start | bytes 18874368 | tf_op jit(solution)/shard_map/all_to_all | solution.py:129
  436.2 0.0 copy-done.3
  436.2 0.1 copy.18
  436.3 122.2 %all-to-all-done.1 = bf16[128,288,128]{2,1,0:T(8,128)(2,1)} async-done(((bf16[128,288,128]{2,1,0:T(8,128)(2,1)}), bf16[128,288,128]{2,1,0:T(8,128)(2,1)}, u32[]{:S(2)}, u32[]{:S(2)}) %all-to-all-start.1) | async-done | bytes 9437216 | tf_op jit(solution)/shard_map/all_to_all | solution.py:129
  558.5 13.5 %gather_fusion.1 = bf16[1024,32,128]{2,1,0:T(8,128)(2,1)} fusion(bf16[1152,32,128]{2,1,0:T(8,128)(2,1)} %bitcast.14, s32[1024]{0:T(1024)S(1)} %broadcast_clamp_fusion), kind=kCustom, calls=%fused_computation.1 | custom fusion | bytes 16781312 | tf_op jit(solution)/shard_map/jit(_take)/gather | solution.py:131
  572.0 5.7 fusion
  577.7 2.6 fusion.5
  (10 shorter events, 0.1 us)
Async XLA Ops:
  7.2 146.1 %copy-start = (bf16[512,1024]{1,0:T(8,128)(2,1)S(1)}, bf16[512,1024]{1,0:T(8,128)(2,1)}, u32[]{:S(2)}) copy-start(bf16[512,1024]{1,0:T(8,128)(2,1)} %param.9) | copy-start | bytes 3145732
  7.2 201.1 %reduce-scatter.2.cloned.1.call-start = ((), (), s32[]{:S(2)}) async-start(), calls=%async_computation.3 | async-start | bytes 12582912 | tf_op jit(solution)/shard_map/reduce_scatter | solution.py:90
  163.4 0.7 copy-start.2
  163.5 74.7 %copy-start.1 = (f32[4096]{0:T(1024)S(1)}, f32[4096]{0:T(1024)}, u32[]{:S(2)}) copy-start(f32[4096]{0:T(1024)} %param.11) | copy-start | bytes 49156
  210.0 25.5 %collective-permute-start = (bf16[128,4096]{1,0:T(8,128)(2,1)S(1)}, bf16[128,4096]{1,0:T(8,128)(2,1)}, u32[]{:S(2)}, u32[]{:S(2)}) collective-permute-start(bf16[128,4096]{1,0:T(8,128)(2,1)S(1)} %fusion.9), channel_id=1, source_target_pairs={{0,2},{2,0},{1,3},{3,1},{4,6},{6,4},{5,7},{7,5},{8,10},{10,8},{9,1... | collective-permute-start | bytes 3145736 | tf_op jit(solution)/shard_map/ppermute | solution.py:95
  426.3 9.9 %copy-start.3 = (f32[128,8]{0,1:T(8,128)S(1)}, f32[128,8]{0,1:T(8,128)}, u32[]{:S(2)}) copy-start(f32[128,8]{0,1:T(8,128)} %param.13) | copy-start | bytes 12292
  426.3 132.2 %all-to-all-start.1 = ((bf16[128,288,128]{2,1,0:T(8,128)(2,1)}), bf16[128,288,128]{2,1,0:T(8,128)(2,1)}, u32[]{:S(2)}, u32[]{:S(2)}) async-start(bf16[128,288,128]{2,1,0:T(8,128)(2,1)} %reshape.106), calls=%async_computation.2 | async-start | bytes 18874368 | tf_op jit(solution)/shard_map/all_to_all | solution.py:129
Sparse Core Ops, SparseCore 0:
  163.6 44.6 reduce-scatter.1

commit v4 on v2

--- a/solution.py
+++ b/solution.py
@@ -2,11 +2,14 @@
 import jax.numpy as jnp
 import numpy as np
 from jax import lax
+from jax.experimental import pallas as pl
+from jax.experimental.pallas import tpu as pltpu
 from jax.sharding import Mesh
 from jax.sharding import PartitionSpec as P
 
 LANES = 128
-ALL = ("expert", "xlo", "core")
+EXPERT = ("y", "xhi", "z")
+ALL = EXPERT + ("xlo", "core")
 
 
 def expert_block(received, w_gate_up, w_down):
@@ -18,6 +21,14 @@
     return jnp.dot(activated, w_down[0], preferred_element_type=jnp.float32).astype(jnp.bfloat16)
 
 
+def gather_columns(w_out):
+    rows, cols = w_out.shape
+    staged = lax.all_gather(w_out, "xhi", axis=0)
+    staged = lax.all_gather(staged, "z", axis=0)
+    staged = lax.all_gather(staged, "y", axis=0)
+    return staged.transpose(3, 0, 2, 1, 4).reshape(rows, -1)
+
+
 def project(context, w_out):
     n_x = lax.axis_size("xlo")
     n_c = lax.axis_size("core")
@@ -25,7 +36,7 @@
     context = context.reshape(n_x, n_c, rows, -1).transpose(1, 0, 2, 3).reshape(n_x * n_c * rows, -1)
     partial_sums = jnp.dot(
         context,
-        lax.all_gather(w_out, "expert", axis=1, tiled=True),
+        gather_columns(w_out),
         preferred_element_type=jnp.float32,
     )
     width = partial_sums.shape[1]
@@ -63,14 +74,14 @@
         [normed.reshape(tok_count, chunks, LANES), jnp.zeros((1, chunks, LANES), jnp.bfloat16)],
         axis=0,
     )
-    send = jnp.take(normed3, source, axis=0)
+    send = jnp.take(normed3, source, axis=0, mode="clip")
     send = send.reshape(experts_all, capacity * chunks, LANES)
     received = lax.all_to_all(send, ALL, split_axis=0, concat_axis=0, tiled=True)
     outputs = expert_block(received.reshape(rows_all, width), w_gate_up, w_down)
     outputs = outputs.reshape(experts_all, capacity * chunks, LANES)
     returned = lax.all_to_all(outputs, ALL, split_axis=0, concat_axis=0, tiled=True)
     returned = returned.reshape(rows_all, chunks, LANES)
-    picked = jnp.take(returned, target, axis=0).reshape(tok_count, top_count, chunks, LANES)
+    picked = jnp.take(returned, target, axis=0, mode="clip").reshape(tok_count, top_count, chunks, LANES)
     moe_sum = jnp.sum(route_weight[:, :, None, None] * picked.astype(jnp.float32), axis=1)
     mixed = (residual + moe_sum.reshape(tok_count, width)).astype(jnp.bfloat16)
     return (attended, mixed)
@@ -80,13 +91,15 @@
     n_expert = mesh.shape["expert"]
     n_tensor = mesh.shape["tensor"]
     n_core = 2 if n_tensor % 2 == 0 else 1
-    devices = np.asarray(mesh.devices).reshape(n_expert, n_tensor // n_core, n_core)
-    mesh3 = Mesh(devices, ALL)
+    n_xhi = 2 if n_expert % 32 == 0 else 1
+    n_z = 4 if n_expert % 4 == 0 else 1
+    shape = (n_expert // (n_xhi * n_z), n_xhi, n_z, n_tensor // n_core, n_core)
+    mesh3 = Mesh(np.asarray(mesh.devices).reshape(shape), ALL)
     tensor = ("xlo", "core")
     in_specs = (
         P(ALL, None),
-        P("expert", tensor),
-        P(tensor, "expert"),
+        P(EXPERT, tensor),
+        P(tensor, EXPERT),
         P(),
         P(ALL, None),
         P(ALL, None),

time: 562 us -> 558 us (level)
  waiting for transfers between devices: 292 us -> 277 us
  other arithmetic: 23.4 us -> 12 us
  blocking collectives: 120 us -> 131 us
  local copies, waits for them, and re-layouts: 59.4 us -> 70 us
    all_gather x1 -> x2, waiting for transfers between devices: 131 us -> 116 us  [the longest x1 84.1 us: gather_columns(): staged = lax.all_gather(staged, 'y', axis=0)]
    transpose x0 -> x1, local copies, waits for them, and re-layouts: none -> 11.4 us  [gather_columns(): return staged.transpose(3, 0, 2, 1, 4).reshape(rows, -1)]
    all_gather x0 -> x1, blocking collectives: none -> 10.5 us  [gather_columns(): staged = lax.all_gather(w_out, 'xhi', axis=0)]
    select_n x3 -> x1, other arithmetic: 8.9 us -> 0.01 us  [on_device(): jnp.full((rows_all,), tok_count, jnp.int32).at[target].set(token_index)]
  transfers between devices with their start and end apart: 4 -> 5, of which waited for: 4 -> 5; matrix products, arithmetic and copies ran while one was open for 1% -> 1% of each run, Pallas kernels for 0% -> 0%
where the time goes in v4:
time: 558 us; the launch traced here: 556 us
  waiting for transfers between devices  277 us (50%)
  blocking collectives  131 us (23%)
  local copies, waits for them, and re-layouts  70 us (13%)
  matrix products  40.8 us (7%)
  between operations  13.9 us (2%)
  other arithmetic  12 us (2%)
  starting transfers between devices  11 us (2%)
    all_to_all x1, waiting for transfers between devices, on_device(): lax.all_to_all(outputs, ALL, split_axis=0, concat_axis=0, tiled=True)  122 us
    all_to_all x1, blocking collectives, on_device(): lax.all_to_all(send, ALL, split_axis=0, concat_axis=0, tiled=True)  121 us
    all_gather x1, waiting for transfers between devices, gather_columns(): staged = lax.all_gather(staged, 'y', axis=0)  84.1 us
    all_gather x1, waiting for transfers between devices, gather_columns(): staged = lax.all_gather(staged, 'z', axis=0)  31.8 us
    reduce_scatter x1, waiting for transfers between devices, project(): lax.psum_scatter(partial_sums, 'core', scatter_dimension=0, tiled=True)  19.8 us
    ppermute x1, waiting for transfers between devices, project(): lax.ppermute(other.astype(jnp.bfloat16), 'xlo', perm=[(0, 1), (1, 0)])  19.4 us
    dot_general x1, matrix products, expert_block(): jnp.dot(received, w_gate_up[0], preferred_element_type=jnp.float32)  18.2 us
    reshape x1, local copies, waits for them, and re-layouts, on_device(): outputs = outputs.reshape(experts_all, capacity * chunks, LANES)  15 us
  transfers between devices with their start and end apart: 5, of which 5 were waited for; matrix products, arithmetic and copies ran while one was open for 1% of the time, Pallas kernels for 0%

profile of v4, /device:TPU:54, one launch (start us, length us, event | category | flops | bytes accessed | tf_op | source)
XLA Modules:
  0.0 556.4 jit_solution(10019403710016031345)
XLA Ops:
  7.2 0.0 all-gather.6.cloned.1.call-start
  7.2 10.5 %all-gather = bf16[2048,128]{1,0:T(8,128)(2,1)} all-gather(bf16[1024,128]{1,0:T(8,128)(2,1)} %param.10), channel_id=2, replica_groups=mesh['y'=4,'xhi'=2,'z'=4,'xlo'=2,'core'=2] {'xhi'}, dimensions={0}, use_global_device_ids=true | all-gather | bytes 786432 | tf_op jit(solution)/shard_map/all_gather | solution.py:26
  17.8 0.0 all-gather.6.cloned.1.call-update
  17.8 0.0 all-gather.8.cloned.1.call-start
  17.8 31.8 %all-gather.6.cloned.1.call-done = bf16[8,1024,128]{2,1,0:T(8,128)(2,1)} async-done(((bf16[2,1024,128]{2,1,0:T(8,128)(2,1)}), bf16[8,1024,128]{2,1,0:T(8,128)(2,1)}) %all-gather.6.cloned.1.call-update) | async-done | bytes 2097168 | tf_op jit(solution)/shard_map/all_gather | solution.py:27
  49.7 0.0 all-gather.8.cloned.1.call-update
  49.7 0.0 reduce-scatter.2.cloned.1.call-start
  49.7 1.3 copy.25
  51.0 84.1 %all-gather.8.cloned.1.call-done = bf16[16,2,1024,128]{3,2,1,0:T(8,128)(2,1)} async-done(((bf16[4,2,1024,128]{3,2,1,0:T(8,128)(2,1)}), bf16[16,2,1024,128]{3,2,1,0:T(8,128)(2,1)}) %all-gather.8.cloned.1.call-update) | async-done | bytes 8388624 | tf_op jit(solution)/shard_map/all_gather | solution.py:28
  135.1 11.4 %copy.26 = bf16[1024,4,2,4,128]{0,4,3,2,1:T(8,128)(2,1)} copy(bf16[1024,4,2,4,128]{4,0,2,3,1:T(8,128)(2,1)} %bitcast.55) | data formatting | bytes 16777216 | tf_op jit(solution)/shard_map/transpose | solution.py:29
  146.6 10.1 %fusion.23 = f32[512,4096]{1,0:T(8,128)} fusion(bf16[512,1024]{1,0:T(8,128)(2,1)S(1)} %bitcast.63, bf16[1024,4096]{0,1:T(8,128)(2,1)} %bitcast.56), kind=kOutput, calls=%fused_computation.46 | convolution fusion | flops 4294967296 | bytes 17825792 | tf_op jit(solution)/shard_map/dot_general | solution.py:37
  156.7 0.0 copy-start.1
  156.7 0.0 reduce-scatter.2.cloned.1.call-update
  156.7 0.0 copy-start
  156.7 0.6 copy-done.1
  157.4 0.1 copy.29
  157.5 0.1 eq.29
  157.6 0.1 eq.25
  157.6 0.1 copy.31
  157.7 0.2 fusion.13
  158.0 19.8 %reduce-scatter.2.cloned.1.call-done = f32[256,4096]{1,0:T(8,128)} async-done(((f32[512,4096]{1,0:T(8,128)}), f32[256,4096]{1,0:T(8,128)}) %reduce-scatter.2.cloned.1.call-update) | async-done | bytes 4194320 | tf_op jit(solution)/shard_map/reduce_scatter | solution.py:43
  177.8 1.7 fusion.9
  179.5 1.0 collective-permute-start
  180.5 0.1 copy.32
  180.6 0.1 copy.28
  180.7 0.1 mul.65
  180.8 0.4 fusion.12
  181.2 4.3 scatter_custom_fusion
  185.6 19.4 %collective-permute-done = bf16[128,4096]{1,0:T(8,128)(2,1)} collective-permute-done((bf16[128,4096]{1,0:T(8,128)(2,1)S(1)}, bf16[128,4096]{1,0:T(8,128)(2,1)}, u32[]{:S(2)}, u32[]{:S(2)}) %collective-permute-start) | collective-permute-done | bytes 1048608 | tf_op jit(solution)/shard_map/ppermute | solution.py:48
  204.9 2.7 multiply_reduce_fusion
  207.7 0.0 copy-done
  207.7 0.4 fusion.10
  208.0 0.2 copy.33
  208.3 0.2 concatenate.3
  208.5 6.0 %gather_fusion = bf16[1152,32,128]{2,1,0:T(8,128)(2,1)} fusion(bf16[129,32,128]{2,1,0:T(8,128)(2,1)S(1)} %concatenate.3, s32[2048]{0:T(1024)S(1)} %pad_clamp_fusion), kind=kCustom, calls=%fused_computation | custom fusion | bytes 18878976 | tf_op jit(solution)/shard_map/jit(_take)/gather | solution.py:77
  214.5 120.7 %all_to_all.10 = bf16[128,288,128]{2,1,0:T(8,128)(2,1)} all-to-all(bf16[128,288,128]{2,1,0:T(8,128)(2,1)} %bitcast.53), channel_id=1, replica_groups=mesh['y'=4,'xhi'=2,'z'=4,'xlo'=2,'core'=2] {'y','xhi','z','xlo','core'}, dimensions={0} | all-to-all | bytes 18874368 | tf_op jit(solution)/shard_map/all_to_all | solution.py:79
  335.2 14.8 %reshape.109 = bf16[1152,4096]{1,0:T(8,128)(2,1)} reshape(bf16[128,288,128]{2,1,0:T(8,128)(2,1)} %all_to_all.10) | data formatting | bytes 18874368 | tf_op jit(solution)/shard_map/reshape | solution.py:80
  350.0 18.2 %fusion.1 = f32[1152,1536]{1,0:T(8,128)S(1)} fusion(bf16[1152,4096]{1,0:T(8,128)(2,1)} %reshape.109, bf16[1,4096,1536]{2,1,0:T(8,128)(2,1)} %param.14), kind=kOutput, calls=%fused_computation.6 | convolution fusion | flops 14495514624 | bytes 29097984 | tf_op jit(solution)/shard_map/dot_general | solution.py:17
  368.3 12.5 %convolution_convert_fusion = bf16[1152,4096]{1,0:T(8,128)(2,1)} fusion(bf16[1,768,4096]{2,1,0:T(8,128)(2,1)} %param.15, f32[1152,1536]{1,0:T(8,128)S(1)} %fusion.1), kind=kOutput, calls=%fused_computation.5 | convolution fusion | flops 7257784320 | bytes 22806528 | tf_op jit(solution)/shard_map/dot_general | solution.py:21
  380.8 15.0 %reshape.110 = bf16[128,288,128]{2,1,0:T(8,128)(2,1)} reshape(bf16[1152,4096]{1,0:T(8,128)(2,1)} %convolution_convert_fusion) | data formatting | bytes 18874368 | tf_op jit(solution)/shard_map/reshape | solution.py:81
  395.8 0.0 copy-start.2
  395.8 9.9 %all-to-all-start.1 = ((bf16[128,288,128]{2,1,0:T(8,128)(2,1)}), bf16[128,288,128]{2,1,0:T(8,128)(2,1)}, u32[]{:S(2)}, u32[]{:S(2)}) async-start(bf16[128,288,128]{2,1,0:T(8,128)(2,1)} %reshape.110), calls=%async_computation.2 | async-start | bytes 18874368 | tf_op jit(solution)/shard_map/all_to_all | solution.py:82
  405.7 0.0 copy-done.2
  405.7 0.1 copy.27
  405.8 122.2 %all-to-all-done.1 = bf16[128,288,128]{2,1,0:T(8,128)(2,1)} async-done(((bf16[128,288,128]{2,1,0:T(8,128)(2,1)}), bf16[128,288,128]{2,1,0:T(8,128)(2,1)}, u32[]{:S(2)}, u32[]{:S(2)}) %all-to-all-start.1) | async-done | bytes 9437216 | tf_op jit(solution)/shard_map/all_to_all | solution.py:82
  528.0 13.5 %gather_fusion.1 = bf16[1024,32,128]{2,1,0:T(8,128)(2,1)} fusion(bf16[1152,32,128]{2,1,0:T(8,128)(2,1)} %bitcast.19, s32[1024]{0:T(1024)S(1)} %broadcast_clamp_fusion), kind=kCustom, calls=%fused_computation.1 | custom fusion | bytes 16781312 | tf_op jit(solution)/shard_map/jit(_take)/gather | solution.py:84
  541.5 5.7 %fusion = f32[128,32,128]{2,1,0:T(8,128)S(1)} fusion(f32[128,8]{1,0:T(8,128)S(1)} %copy.27, bf16[1024,32,128]{2,1,0:T(8,128)(2,1)} %gather_fusion.1), kind=kLoop, calls=%fused_computation.4 | loop fusion | flops 12058624 | bytes 10489856 | tf_op jit(solution)/shard_map/reduce_sum | solution.py:85
  547.2 2.6 fusion.5
  (10 shorter events, 0.1 us)
Async XLA Ops:
  7.2 42.5 %all-gather.6.cloned.1.call-start = ((), (), s32[]{:S(2)}) async-start(), calls=%async_computation.4 | async-start | bytes 2621440 | tf_op jit(solution)/shard_map/all_gather | solution.py:27
  17.8 117.4 %all-gather.8.cloned.1.call-start = ((), (), s32[]{:S(2)}) async-start(), calls=%async_computation.5 | async-start | bytes 10485760 | tf_op jit(solution)/shard_map/all_gather | solution.py:28
  49.7 128.1 %reduce-scatter.2.cloned.1.call-start = ((), (), s32[]{:S(2)}) async-start(), calls=%async_computation.3 | async-start | bytes 12582912 | tf_op jit(solution)/shard_map/reduce_scatter | solution.py:43
  156.7 0.7 copy-start.1
  156.7 51.0 %copy-start = (f32[4096]{0:T(1024)S(1)}, f32[4096]{0:T(1024)}, u32[]{:S(2)}) copy-start(f32[4096]{0:T(1024)} %param.11) | copy-start | bytes 49156
  179.5 25.4 %collective-permute-start = (bf16[128,4096]{1,0:T(8,128)(2,1)S(1)}, bf16[128,4096]{1,0:T(8,128)(2,1)}, u32[]{:S(2)}, u32[]{:S(2)}) collective-permute-start(bf16[128,4096]{1,0:T(8,128)(2,1)S(1)} %fusion.9), channel_id=1, source_target_pairs={{0,2},{2,0},{1,3},{3,1},{4,6},{6,4},{5,7},{7,5},{8,10},{10,8},{9,1... | collective-permute-start | bytes 3145736 | tf_op jit(solution)/shard_map/ppermute | solution.py:48
  395.8 9.9 %copy-start.2 = (f32[128,8]{0,1:T(8,128)S(1)}, f32[128,8]{0,1:T(8,128)}, u32[]{:S(2)}) copy-start(f32[128,8]{0,1:T(8,128)} %param.13) | copy-start | bytes 12292
  395.8 132.2 %all-to-all-start.1 = ((bf16[128,288,128]{2,1,0:T(8,128)(2,1)}), bf16[128,288,128]{2,1,0:T(8,128)(2,1)}, u32[]{:S(2)}, u32[]{:S(2)}) async-start(bf16[128,288,128]{2,1,0:T(8,128)(2,1)} %reshape.110), calls=%async_computation.2 | async-start | bytes 18874368 | tf_op jit(solution)/shard_map/all_to_all | solution.py:82
Sparse Core Ops, SparseCore 0:
  17.9 31.7 all-gather.5
  51.3 83.7 all-gather.7
  156.8 20.9 reduce-scatter.1

commit v5 on v4

--- a/solution.py
+++ b/solution.py
@@ -76,11 +76,17 @@
     )
     send = jnp.take(normed3, source, axis=0, mode="clip")
     send = send.reshape(experts_all, capacity * chunks, LANES)
-    received = lax.all_to_all(send, ALL, split_axis=0, concat_axis=0, tiled=True)
-    outputs = expert_block(received.reshape(rows_all, width), w_gate_up, w_down)
-    outputs = outputs.reshape(experts_all, capacity * chunks, LANES)
-    returned = lax.all_to_all(outputs, ALL, split_axis=0, concat_axis=0, tiled=True)
-    returned = returned.reshape(rows_all, chunks, LANES)
+    first = (capacity + 1) // 2
+    returned = []
+    for lo, hi in ((0, first), (first, capacity)):
+        part = send[:, lo * chunks : hi * chunks]
+        received = lax.all_to_all(part, ALL, split_axis=0, concat_axis=0, tiled=True)
+        outputs = expert_block(
+            received.reshape(experts_all * (hi - lo), width), w_gate_up, w_down
+        )
+        outputs = outputs.reshape(experts_all, (hi - lo) * chunks, LANES)
+        returned.append(lax.all_to_all(outputs, ALL, split_axis=0, concat_axis=0, tiled=True))
+    returned = jnp.concatenate(returned, axis=1).reshape(rows_all, chunks, LANES)
     picked = jnp.take(returned, target, axis=0, mode="clip").reshape(tok_count, top_count, chunks, LANES)
     moe_sum = jnp.sum(route_weight[:, :, None, None] * picked.astype(jnp.float32), axis=1)
     mixed = (residual + moe_sum.reshape(tok_count, width)).astype(jnp.bfloat16)

time: 558 us -> 528 us (0.946)
  blocking collectives: 131 us -> 10.5 us
  waiting for transfers between devices: 277 us -> 311 us
  starting transfers between devices: 11 us -> 35.8 us
  local copies, waits for them, and re-layouts: 70 us -> 82.6 us
  other arithmetic: 12 us -> 21.1 us
  matrix products: 40.8 us -> 49.8 us
    all_to_all x1 -> x0, blocking collectives: 121 us -> none  [on_device(): lax.all_to_all(send, ALL, split_axis=0, concat_axis=0, tiled=True)]
    all_to_all x0 -> x2, waiting for transfers between devices: none -> 78.1 us  [on_device(): lax.all_to_all(part, ALL, split_axis=0, concat_axis=0, tiled=True)]
    all_to_all x1 -> x2, waiting for transfers between devices: 122 us -> 77.4 us  [on_device(): lax.all_to_all(outputs, ALL, split_axis=0, concat_axis=0, tiled=True)]
    all_to_all x0 -> x2, starting transfers between devices: none -> 18.2 us  [on_device(): lax.all_to_all(part, ALL, split_axis=0, concat_axis=0, tiled=True)]
    slice x0 -> x2, local copies, waits for them, and re-layouts: none -> 10.1 us  [on_device(): part = send[:, lo * chunks:hi * chunks]]
    concatenate x0 -> x1, other arithmetic: none -> 9.06 us  [on_device(): jnp.concatenate(returned, axis=1).reshape(rows_all, chunks, LANES)]
    all_to_all x1 -> x2, starting transfers between devices: 9.92 us -> 16.6 us  [on_device(): lax.all_to_all(outputs, ALL, split_axis=0, concat_axis=0, tiled=True)]
    dot_general x1 -> x2, matrix products: 18.2 us -> 22.9 us  [expert_block(): jnp.dot(received, w_gate_up[0], preferred_element_type=jnp.float32)]
  transfers between devices with their start and end apart: 5 -> 8, of which waited for: 5 -> 8; matrix products, arithmetic and copies ran while one was open for 1% -> 16% of each run, Pallas kernels for 0% -> 0%
where the time goes in v5:
time: 528 us; the launch traced here: 525 us
  waiting for transfers between devices  311 us (59%)
  local copies, waits for them, and re-layouts  82.6 us (16%)
  matrix products  49.8 us (9%)
  starting transfers between devices  35.8 us (7%)
  other arithmetic  21.1 us (4%)
  between operations  14 us (3%)
  blocking collectives  10.5 us (2%)
    all_gather x1, waiting for transfers between devices, gather_columns(): staged = lax.all_gather(staged, 'y', axis=0)  84.1 us
    all_to_all x2, waiting for transfers between devices, on_device(): lax.all_to_all(part, ALL, split_axis=0, concat_axis=0, tiled=True)  78.1 us
    all_to_all x2, waiting for transfers between devices, on_device(): lax.all_to_all(outputs, ALL, split_axis=0, concat_axis=0, tiled=True)  77.4 us
    all_gather x1, waiting for transfers between devices, gather_columns(): staged = lax.all_gather(staged, 'z', axis=0)  31.8 us
    dot_general x2, matrix products, expert_block(): jnp.dot(received, w_gate_up[0], preferred_element_type=jnp.float32)  22.9 us
    reduce_scatter x1, waiting for transfers between devices, project(): lax.psum_scatter(partial_sums, 'core', scatter_dimension=0, tiled=True)  19.6 us
    ppermute x1, waiting for transfers between devices, project(): lax.ppermute(other.astype(jnp.bfloat16), 'xlo', perm=[(0, 1), (1, 0)])  19.6 us
    all_to_all x2, starting transfers between devices, on_device(): lax.all_to_all(part, ALL, split_axis=0, concat_axis=0, tiled=True)  18.2 us
  transfers between devices with their start and end apart: 8, of which 8 were waited for; matrix products, arithmetic and copies ran while one was open for 16% of the time, Pallas kernels for 0%

profile of v5, /device:TPU:54, one launch (start us, length us, event | category | flops | bytes accessed | tf_op | source)
XLA Modules:
  0.0 524.6 jit_solution(11217123719934472340)
XLA Ops:
  7.2 0.0 all-gather.6.cloned.1.call-start
  7.2 10.5 %all-gather = bf16[2048,128]{1,0:T(8,128)(2,1)} all-gather(bf16[1024,128]{1,0:T(8,128)(2,1)} %param.10), channel_id=2, replica_groups=mesh['y'=4,'xhi'=2,'z'=4,'xlo'=2,'core'=2] {'xhi'}, dimensions={0}, use_global_device_ids=true | all-gather | bytes 786432 | tf_op jit(solution)/shard_map/all_gather | solution.py:26
  17.8 0.0 all-gather.6.cloned.1.call-update
  17.8 0.0 all-gather.8.cloned.1.call-start
  17.8 31.8 %all-gather.6.cloned.1.call-done = bf16[8,1024,128]{2,1,0:T(8,128)(2,1)} async-done(((bf16[2,1024,128]{2,1,0:T(8,128)(2,1)}), bf16[8,1024,128]{2,1,0:T(8,128)(2,1)}) %all-gather.6.cloned.1.call-update) | async-done | bytes 2097168 | tf_op jit(solution)/shard_map/all_gather | solution.py:27
  49.7 0.0 all-gather.8.cloned.1.call-update
  49.7 0.0 reduce-scatter.2.cloned.1.call-start
  49.7 1.3 copy.25
  51.0 84.1 %all-gather.8.cloned.1.call-done = bf16[16,2,1024,128]{3,2,1,0:T(8,128)(2,1)} async-done(((bf16[4,2,1024,128]{3,2,1,0:T(8,128)(2,1)}), bf16[16,2,1024,128]{3,2,1,0:T(8,128)(2,1)}) %all-gather.8.cloned.1.call-update) | async-done | bytes 8388624 | tf_op jit(solution)/shard_map/all_gather | solution.py:28
  135.1 11.4 %copy.26 = bf16[1024,4,2,4,128]{0,4,3,2,1:T(8,128)(2,1)} copy(bf16[1024,4,2,4,128]{4,0,2,3,1:T(8,128)(2,1)} %bitcast.65) | data formatting | bytes 16777216 | tf_op jit(solution)/shard_map/transpose | solution.py:29
  146.6 10.1 %fusion.34 = f32[512,4096]{1,0:T(8,128)} fusion(bf16[512,1024]{1,0:T(8,128)(2,1)S(1)} %bitcast.73, bf16[1024,4096]{0,1:T(8,128)(2,1)} %bitcast.66), kind=kOutput, calls=%fused_computation.56 | convolution fusion | flops 4294967296 | bytes 17825792 | tf_op jit(solution)/shard_map/dot_general | solution.py:37
  156.7 0.0 copy-start.1
  156.7 0.0 reduce-scatter.2.cloned.1.call-update
  156.7 0.7 copy-done.1
  157.4 0.1 copy.29
  157.5 0.1 eq.29
  157.5 0.1 eq.25
  157.7 0.1 copy.28
  157.8 0.1 mul.72
  157.9 0.1 copy.31
  158.0 0.2 fusion.23
  158.2 19.6 %reduce-scatter.2.cloned.1.call-done = f32[256,4096]{1,0:T(8,128)} async-done(((f32[512,4096]{1,0:T(8,128)}), f32[256,4096]{1,0:T(8,128)}) %reduce-scatter.2.cloned.1.call-update) | async-done | bytes 4194320 | tf_op jit(solution)/shard_map/reduce_scatter | solution.py:43
  177.8 1.7 fusion.15
  179.5 1.0 collective-permute-start
  180.5 0.0 copy-start
  180.5 0.1 copy.32
  180.7 0.4 fusion.22
  181.1 4.3 scatter_custom_fusion
  185.4 19.6 %collective-permute-done = bf16[128,4096]{1,0:T(8,128)(2,1)} collective-permute-done((bf16[128,4096]{1,0:T(8,128)(2,1)S(1)}, bf16[128,4096]{1,0:T(8,128)(2,1)}, u32[]{:S(2)}, u32[]{:S(2)}) %collective-permute-start) | collective-permute-done | bytes 1048608 | tf_op jit(solution)/shard_map/ppermute | solution.py:48
  204.9 2.7 multiply_reduce_fusion
  207.6 0.0 copy-done
  207.7 0.4 fusion.16
  208.0 0.2 copy.33
  208.3 0.2 concatenate.6
  208.5 6.1 %gather_fusion = bf16[1152,32,128]{2,1,0:T(8,128)(2,1)} fusion(bf16[129,32,128]{2,1,0:T(8,128)(2,1)S(1)} %concatenate.6, s32[2048]{0:T(1024)S(1)} %pad_clamp_fusion), kind=kCustom, calls=%fused_computation | custom fusion | bytes 18878976 | tf_op jit(solution)/shard_map/jit(_take)/gather | solution.py:77
  214.5 4.8 slice.41
  219.3 10.1 %all-to-all-start.2 = ((bf16[128,128,128]{2,1,0:T(8,128)(2,1)}), bf16[128,128,128]{2,1,0:T(8,128)(2,1)}, u32[]{:S(2)}, u32[]{:S(2)}) async-start(bf16[128,128,128]{2,1,0:T(8,128)(2,1)} %slice.41), calls=%async_computation.3 | async-start | bytes 8388608 | tf_op jit(solution)/shard_map/all_to_all | solution.py:83
  229.4 5.2 slice.38
  234.6 46.7 %all-to-all-done.2 = bf16[128,128,128]{2,1,0:T(8,128)(2,1)} async-done(((bf16[128,128,128]{2,1,0:T(8,128)(2,1)}), bf16[128,128,128]{2,1,0:T(8,128)(2,1)}, u32[]{:S(2)}, u32[]{:S(2)}) %all-to-all-start.2) | async-done | bytes 4194336 | tf_op jit(solution)/shard_map/all_to_all | solution.py:83
  281.4 8.1 %all-to-all-start = ((bf16[128,160,128]{2,1,0:T(8,128)(2,1)}), bf16[128,160,128]{2,1,0:T(8,128)(2,1)}, u32[]{:S(2)}, u32[]{:S(2)}) async-start(bf16[128,160,128]{2,1,0:T(8,128)(2,1)} %slice.38), calls=%async_computation.1 | async-start | bytes 10485760 | tf_op jit(solution)/shard_map/all_to_all | solution.py:83
  289.5 7.3 %reshape.117 = bf16[512,4096]{1,0:T(8,128)(2,1)} reshape(bf16[128,128,128]{2,1,0:T(8,128)(2,1)} %all-to-all-done.2) | data formatting | bytes 8388608 | tf_op jit(solution)/shard_map/reshape | solution.py:85
  296.8 10.5 %fusion.1 = f32[512,1536]{1,0:T(8,128)S(1)} fusion(bf16[512,4096]{1,0:T(8,128)(2,1)} %reshape.117, bf16[1,4096,1536]{2,1,0:T(8,128)(2,1)} %param.14), kind=kOutput, calls=%fused_computation.5 | convolution fusion | flops 6442450944 | bytes 19922944 | tf_op jit(solution)/shard_map/dot_general | solution.py:17
  307.3 7.9 %fusion.8 = bf16[512,4096]{1,0:T(8,128)(2,1)} fusion(bf16[1,768,4096]{2,1,0:T(8,128)(2,1)} %param.15, f32[512,1536]{1,0:T(8,128)S(1)} %fusion.1), kind=kOutput, calls=%fused_computation.14 | convolution fusion | flops 3225681920 | bytes 13631488 | tf_op jit(solution)/shard_map/dot_general | solution.py:21
  315.2 7.4 %reshape.118 = bf16[128,128,128]{2,1,0:T(8,128)(2,1)} reshape(bf16[512,4096]{1,0:T(8,128)(2,1)} %fusion.8) | data formatting | bytes 8388608 | tf_op jit(solution)/shard_map/reshape | solution.py:87
  322.6 31.4 %all-to-all-done = bf16[128,160,128]{2,1,0:T(8,128)(2,1)} async-done(((bf16[128,160,128]{2,1,0:T(8,128)(2,1)}), bf16[128,160,128]{2,1,0:T(8,128)(2,1)}, u32[]{:S(2)}, u32[]{:S(2)}) %all-to-all-start) | async-done | bytes 5242912 | tf_op jit(solution)/shard_map/all_to_all | solution.py:83
  354.1 8.5 %all-to-all-start.3 = ((bf16[128,128,128]{2,1,0:T(8,128)(2,1)}), bf16[128,128,128]{2,1,0:T(8,128)(2,1)}, u32[]{:S(2)}, u32[]{:S(2)}) async-start(bf16[128,128,128]{2,1,0:T(8,128)(2,1)} %reshape.118), calls=%async_computation.4 | async-start | bytes 8388608 | tf_op jit(solution)/shard_map/all_to_all | solution.py:88
  362.5 8.8 %reshape.115 = bf16[640,4096]{1,0:T(8,128)(2,1)} reshape(bf16[128,160,128]{2,1,0:T(8,128)(2,1)} %all-to-all-done) | data formatting | bytes 10485760 | tf_op jit(solution)/shard_map/reshape | solution.py:85
  371.4 12.4 %fusion.3 = f32[640,1536]{1,0:T(8,128)S(1)} fusion(bf16[640,4096]{1,0:T(8,128)(2,1)} %reshape.115, bf16[1,4096,1536]{2,1,0:T(8,128)(2,1)} %param.14), kind=kOutput, calls=%fused_computation.7 | convolution fusion | flops 8053063680 | bytes 21757952 | tf_op jit(solution)/shard_map/dot_general | solution.py:17
  383.8 8.9 %convolution_convert_fusion = bf16[640,4096]{1,0:T(8,128)(2,1)} fusion(bf16[1,768,4096]{2,1,0:T(8,128)(2,1)} %param.15, f32[640,1536]{1,0:T(8,128)S(1)} %fusion.3), kind=kOutput, calls=%fused_computation.10 | convolution fusion | flops 4032102400 | bytes 15466496 | tf_op jit(solution)/shard_map/dot_general | solution.py:21
  392.7 8.9 %reshape.116 = bf16[128,160,128]{2,1,0:T(8,128)(2,1)} reshape(bf16[640,4096]{1,0:T(8,128)(2,1)} %convolution_convert_fusion) | data formatting | bytes 10485760 | tf_op jit(solution)/shard_map/reshape | solution.py:87
  401.6 0.0 copy-start.2
  401.6 12.9 %all-to-all-done.3 = bf16[128,128,128]{2,1,0:T(8,128)(2,1)} async-done(((bf16[128,128,128]{2,1,0:T(8,128)(2,1)}), bf16[128,128,128]{2,1,0:T(8,128)(2,1)}, u32[]{:S(2)}, u32[]{:S(2)}) %all-to-all-start.3) | async-done | bytes 4194336 | tf_op jit(solution)/shard_map/all_to_all | solution.py:88
  414.5 8.1 %all-to-all-start.1 = ((bf16[128,160,128]{2,1,0:T(8,128)(2,1)}), bf16[128,160,128]{2,1,0:T(8,128)(2,1)}, u32[]{:S(2)}, u32[]{:S(2)}) async-start(bf16[128,160,128]{2,1,0:T(8,128)(2,1)} %reshape.116), calls=%async_computation.2 | async-start | bytes 10485760 | tf_op jit(solution)/shard_map/all_to_all | solution.py:88
  422.6 0.0 copy-done.2
  422.6 0.1 copy.27
  422.7 64.5 %all-to-all-done.1 = bf16[128,160,128]{2,1,0:T(8,128)(2,1)} async-done(((bf16[128,160,128]{2,1,0:T(8,128)(2,1)}), bf16[128,160,128]{2,1,0:T(8,128)(2,1)}, u32[]{:S(2)}, u32[]{:S(2)}) %all-to-all-start.1) | async-done | bytes 5242912 | tf_op jit(solution)/shard_map/all_to_all | solution.py:88
  487.2 9.1 %pad_maximum_fusion = bf16[128,288,128]{2,1,0:T(8,128)(2,1)} fusion(bf16[128,128,128]{2,1,0:T(8,128)(2,1)} %all-to-all-done.3, bf16[128,160,128]{2,1,0:T(8,128)(2,1)} %all-to-all-done.1), kind=kLoop, calls=%fused_computation.9 | loop fusion | flops 18874368 | bytes 18874368 | tf_op jit(solution)/shard_map/concatenate | solution.py:89
  496.3 13.4 %gather_fusion.1 = bf16[1024,32,128]{2,1,0:T(8,128)(2,1)} fusion(bf16[1152,32,128]{2,1,0:T(8,128)(2,1)} %bitcast.63, s32[1024]{0:T(1024)S(1)} %broadcast_clamp_fusion), kind=kCustom, calls=%fused_computation.1 | custom fusion | bytes 16781312 | tf_op jit(solution)/shard_map/jit(_take)/gather | solution.py:90
  509.7 5.7 %fusion = f32[128,32,128]{2,1,0:T(8,128)S(1)} fusion(f32[128,8]{1,0:T(8,128)S(1)} %copy.27, bf16[1024,32,128]{2,1,0:T(8,128)(2,1)} %gather_fusion.1), kind=kLoop, calls=%fused_computation.4 | loop fusion | flops 12058624 | bytes 10489856 | tf_op jit(solution)/shard_map/reduce_sum | solution.py:91
  515.4 2.6 fusion.11
  (10 shorter events, 0.1 us)
Async XLA Ops:
  7.2 42.5 %all-gather.6.cloned.1.call-start = ((), (), s32[]{:S(2)}) async-start(), calls=%async_computation.6 | async-start | bytes 2621440 | tf_op jit(solution)/shard_map/all_gather | solution.py:27
  17.8 117.4 %all-gather.8.cloned.1.call-start = ((), (), s32[]{:S(2)}) async-start(), calls=%async_computation.7 | async-start | bytes 10485760 | tf_op jit(solution)/shard_map/all_gather | solution.py:28
  49.7 128.1 %reduce-scatter.2.cloned.1.call-start = ((), (), s32[]{:S(2)}) async-start(), calls=%async_computation.5 | async-start | bytes 12582912 | tf_op jit(solution)/shard_map/reduce_scatter | solution.py:43
  156.7 0.7 copy-start.1
  179.5 25.4 %collective-permute-start = (bf16[128,4096]{1,0:T(8,128)(2,1)S(1)}, bf16[128,4096]{1,0:T(8,128)(2,1)}, u32[]{:S(2)}, u32[]{:S(2)}) collective-permute-start(bf16[128,4096]{1,0:T(8,128)(2,1)S(1)} %fusion.15), channel_id=1, source_target_pairs={{0,2},{2,0},{1,3},{3,1},{4,6},{6,4},{5,7},{7,5},{8,10},{10,8},{9,1... | collective-permute-start | bytes 3145736 | tf_op jit(solution)/shard_map/ppermute | solution.py:48
  180.5 27.1 %copy-start = (f32[4096]{0:T(1024)S(1)}, f32[4096]{0:T(1024)}, u32[]{:S(2)}) copy-start(f32[4096]{0:T(1024)} %param.11) | copy-start | bytes 49156
  219.3 62.0 %all-to-all-start.2 = ((bf16[128,128,128]{2,1,0:T(8,128)(2,1)}), bf16[128,128,128]{2,1,0:T(8,128)(2,1)}, u32[]{:S(2)}, u32[]{:S(2)}) async-start(bf16[128,128,128]{2,1,0:T(8,128)(2,1)} %slice.41), calls=%async_computation.3 | async-start | bytes 8388608 | tf_op jit(solution)/shard_map/all_to_all | solution.py:83
  281.4 72.7 %all-to-all-start = ((bf16[128,160,128]{2,1,0:T(8,128)(2,1)}), bf16[128,160,128]{2,1,0:T(8,128)(2,1)}, u32[]{:S(2)}, u32[]{:S(2)}) async-start(bf16[128,160,128]{2,1,0:T(8,128)(2,1)} %slice.38), calls=%async_computation.1 | async-start | bytes 10485760 | tf_op jit(solution)/shard_map/all_to_all | solution.py:83
  354.1 60.4 %all-to-all-start.3 = ((bf16[128,128,128]{2,1,0:T(8,128)(2,1)}), bf16[128,128,128]{2,1,0:T(8,128)(2,1)}, u32[]{:S(2)}, u32[]{:S(2)}) async-start(bf16[128,128,128]{2,1,0:T(8,128)(2,1)} %reshape.118), calls=%async_computation.4 | async-start | bytes 8388608 | tf_op jit(solution)/shard_map/all_to_all | solution.py:88
  401.6 21.0 %copy-start.2 = (f32[128,8]{0,1:T(8,128)S(1)}, f32[128,8]{0,1:T(8,128)}, u32[]{:S(2)}) copy-start(f32[128,8]{0,1:T(8,128)} %param.13) | copy-start | bytes 12292
  414.5 72.7 %all-to-all-start.1 = ((bf16[128,160,128]{2,1,0:T(8,128)(2,1)}), bf16[128,160,128]{2,1,0:T(8,128)(2,1)}, u32[]{:S(2)}, u32[]{:S(2)}) async-start(bf16[128,160,128]{2,1,0:T(8,128)(2,1)} %reshape.116), calls=%async_computation.2 | async-start | bytes 10485760 | tf_op jit(solution)/shard_map/all_to_all | solution.py:88
Sparse Core Ops, SparseCore 0:
  17.9 31.7 all-gather.5
  51.3 83.7 all-gather.7
  156.8 20.9 reduce-scatter.1

commit v6 on v4

--- a/solution.py
+++ b/solution.py
@@ -70,19 +70,29 @@
     target = chosen * capacity + slots
     token_index = jnp.arange(tok_count * top_count, dtype=jnp.int32) // top_count
     source = jnp.full((rows_all,), tok_count, jnp.int32).at[target].set(token_index)
+    source = source.reshape(experts_all, capacity)
     normed3 = jnp.concatenate(
         [normed.reshape(tok_count, chunks, LANES), jnp.zeros((1, chunks, LANES), jnp.bfloat16)],
         axis=0,
     )
-    send = jnp.take(normed3, source, axis=0, mode="clip")
-    send = send.reshape(experts_all, capacity * chunks, LANES)
-    received = lax.all_to_all(send, ALL, split_axis=0, concat_axis=0, tiled=True)
-    outputs = expert_block(received.reshape(rows_all, width), w_gate_up, w_down)
-    outputs = outputs.reshape(experts_all, capacity * chunks, LANES)
-    returned = lax.all_to_all(outputs, ALL, split_axis=0, concat_axis=0, tiled=True)
-    returned = returned.reshape(rows_all, chunks, LANES)
-    picked = jnp.take(returned, target, axis=0, mode="clip").reshape(tok_count, top_count, chunks, LANES)
-    moe_sum = jnp.sum(route_weight[:, :, None, None] * picked.astype(jnp.float32), axis=1)
+    weights = route_weight.reshape(-1)
+    groups = 3 if capacity % 3 == 0 else 2
+    bounds = [capacity * g // groups for g in range(groups + 1)]
+    moe_sum = None
+    for lo, hi in zip(bounds[:-1], bounds[1:]):
+        size = hi - lo
+        send = jnp.take(normed3, source[:, lo:hi].reshape(-1), axis=0, mode="clip")
+        send = send.reshape(experts_all, size * chunks, LANES)
+        received = lax.all_to_all(send, ALL, split_axis=0, concat_axis=0, tiled=True)
+        outputs = expert_block(received.reshape(experts_all * size, width), w_gate_up, w_down)
+        outputs = outputs.reshape(experts_all, size * chunks, LANES)
+        returned = lax.all_to_all(outputs, ALL, split_axis=0, concat_axis=0, tiled=True)
+        returned = returned.reshape(experts_all * size, chunks, LANES)
+        inside = (slots >= lo) & (slots < hi)
+        picked = jnp.take(returned, chosen * size + slots - lo, axis=0, mode="clip")
+        scaled = jnp.where(inside, weights, 0.0)[:, None, None] * picked.astype(jnp.float32)
+        part = jnp.sum(scaled.reshape(tok_count, top_count, chunks, LANES), axis=1)
+        moe_sum = part if moe_sum is None else moe_sum + part
     mixed = (residual + moe_sum.reshape(tok_count, width)).astype(jnp.bfloat16)
     return (attended, mixed)
 

time: 558 us -> 540 us (0.968)
  blocking collectives: 131 us -> 10.7 us
  starting transfers between devices: 11 us -> 50.8 us
  local copies, waits for them, and re-layouts: 70 us -> 102 us
  matrix products: 40.8 us -> 57.6 us
  other arithmetic: 12 us -> 20 us
    all_to_all x1 -> x0, blocking collectives: 121 us -> none  [on_device(): lax.all_to_all(send, ALL, split_axis=0, concat_axis=0, tiled=True)]
    all_to_all x0 -> x3, waiting for transfers between devices: none -> 83.4 us  [on_device(): lax.all_to_all(send, ALL, split_axis=0, concat_axis=0, tiled=True)]
    all_to_all x1 -> x3, waiting for transfers between devices: 122 us -> 40.5 us  [on_device(): lax.all_to_all(outputs, ALL, split_axis=0, concat_axis=0, tiled=True)]
    all_to_all x0 -> x3, starting transfers between devices: none -> 25.8 us  [on_device(): lax.all_to_all(send, ALL, split_axis=0, concat_axis=0, tiled=True)]
    gather x2 -> x6, local copies, waits for them, and re-layouts: 19.5 us -> 42.9 us  [the longest x3 33.4 us: on_device(): picked = jnp.take(returned, chosen * size + slots - lo, axis=0, mode='clip')]
    all_to_all x1 -> x3, starting transfers between devices: 9.92 us -> 23.9 us  [on_device(): lax.all_to_all(outputs, ALL, split_axis=0, concat_axis=0, tiled=True)]
    dot_general x1 -> x3, matrix products: 18.2 us -> 26.8 us  [expert_block(): jnp.dot(received, w_gate_up[0], preferred_element_type=jnp.float32)]
    dot_general x1 -> x3, matrix products: 12.5 us -> 20.7 us  [expert_block(): jnp.dot(activated, w_down[0], preferred_element_type=jnp.float32)]
  transfers between devices with their start and end apart: 5 -> 10, of which waited for: 5 -> 10; matrix products, arithmetic and copies ran while one was open for 1% -> 22% of each run, Pallas kernels for 0% -> 0%
where the time goes in v6:
time: 540 us; the launch traced here: 535 us
  waiting for transfers between devices  280 us (52%)
  local copies, waits for them, and re-layouts  102 us (19%)
  matrix products  57.6 us (11%)
  starting transfers between devices  50.8 us (9%)
  other arithmetic  20 us (4%)
  between operations  14.1 us (3%)
  blocking collectives  10.7 us (2%)
    all_gather x1, waiting for transfers between devices, gather_columns(): staged = lax.all_gather(staged, 'y', axis=0)  85.3 us
    all_to_all x3, waiting for transfers between devices, on_device(): lax.all_to_all(send, ALL, split_axis=0, concat_axis=0, tiled=True)  83.4 us
    all_to_all x3, waiting for transfers between devices, on_device(): lax.all_to_all(outputs, ALL, split_axis=0, concat_axis=0, tiled=True)  40.5 us
    gather x3, local copies, waits for them, and re-layouts, on_device(): picked = jnp.take(returned, chosen * size + slots - lo, axis=0, mode='clip')  33.4 us
    all_gather x1, waiting for transfers between devices, gather_columns(): staged = lax.all_gather(staged, 'z', axis=0)  31.8 us
    dot_general x3, matrix products, expert_block(): jnp.dot(received, w_gate_up[0], preferred_element_type=jnp.float32)  26.8 us
    all_to_all x3, starting transfers between devices, on_device(): lax.all_to_all(send, ALL, split_axis=0, concat_axis=0, tiled=True)  25.8 us
    all_to_all x3, starting transfers between devices, on_device(): lax.all_to_all(outputs, ALL, split_axis=0, concat_axis=0, tiled=True)  23.9 us
  transfers between devices with their start and end apart: 10, of which 10 were waited for; matrix products, arithmetic and copies ran while one was open for 22% of the time, Pallas kernels for 0%

profile of v6, /device:TPU:54, one launch (start us, length us, event | category | flops | bytes accessed | tf_op | source)
XLA Modules:
  0.0 534.8 jit_solution(10658965795359366968)
XLA Ops:
  7.2 10.7 %all-gather = bf16[2048,128]{1,0:T(8,128)(2,1)} all-gather(bf16[1024,128]{1,0:T(8,128)(2,1)} %param.10), channel_id=2, replica_groups=mesh['y'=4,'xhi'=2,'z'=4,'xlo'=2,'core'=2] {'xhi'}, dimensions={0}, use_global_device_ids=true | all-gather | bytes 786432 | tf_op jit(solution)/shard_map/all_gather | solution.py:26
  18.0 31.8 %all-gather.6.cloned.1.call-done = bf16[8,1024,128]{2,1,0:T(8,128)(2,1)} async-done(((bf16[2,1024,128]{2,1,0:T(8,128)(2,1)}), bf16[8,1024,128]{2,1,0:T(8,128)(2,1)}) %all-gather.6.cloned.1.call-update) | async-done | bytes 2097168 | tf_op jit(solution)/shard_map/all_gather | solution.py:27
  50.0 85.3 %all-gather.8.cloned.1.call-done = bf16[16,2,1024,128]{3,2,1,0:T(8,128)(2,1)} async-done(((bf16[4,2,1024,128]{3,2,1,0:T(8,128)(2,1)}), bf16[16,2,1024,128]{3,2,1,0:T(8,128)(2,1)}) %all-gather.8.cloned.1.call-update) | async-done | bytes 8388624 | tf_op jit(solution)/shard_map/all_gather | solution.py:28
  135.3 11.4 %copy.34 = bf16[1024,4,2,4,128]{0,4,3,2,1:T(8,128)(2,1)} copy(bf16[1024,4,2,4,128]{4,0,2,3,1:T(8,128)(2,1)} %bitcast.85) | data formatting | bytes 16777216 | tf_op jit(solution)/shard_map/transpose | solution.py:29
  146.7 10.1 %fusion.52 = f32[512,4096]{1,0:T(8,128)} fusion(bf16[512,1024]{1,0:T(8,128)(2,1)S(1)} %bitcast.94, bf16[1024,4096]{0,1:T(8,128)(2,1)} %bitcast.86), kind=kOutput, calls=%fused_computation.88 | convolution fusion | flops 4294967296 | bytes 17825792 | tf_op jit(solution)/shard_map/dot_general | solution.py:37
  156.9 0.7 copy-done.7
  157.5 0.1 copy.35
  157.7 0.1 copy.37
  157.8 0.2 fusion.39
  158.1 19.9 %reduce-scatter.2.cloned.1.call-done = f32[256,4096]{1,0:T(8,128)} async-done(((f32[512,4096]{1,0:T(8,128)}), f32[256,4096]{1,0:T(8,128)}) %reduce-scatter.2.cloned.1.call-update) | async-done | bytes 4194320 | tf_op jit(solution)/shard_map/reduce_scatter | solution.py:43
  178.0 1.7 fusion.29
  179.7 0.9 collective-permute-start
  180.8 0.1 copy.38
  180.9 0.1 copy.40
  181.1 0.1 copy.41
  181.3 0.4 fusion.38
  181.7 4.3 scatter_custom_fusion
  186.0 0.2 reshape.237
  186.3 0.2 reshape.287
  186.5 18.6 %collective-permute-done = bf16[128,4096]{1,0:T(8,128)(2,1)} collective-permute-done((bf16[128,4096]{1,0:T(8,128)(2,1)S(1)}, bf16[128,4096]{1,0:T(8,128)(2,1)}, u32[]{:S(2)}, u32[]{:S(2)}) %collective-permute-start) | collective-permute-done | bytes 1048608 | tf_op jit(solution)/shard_map/ppermute | solution.py:48
  205.1 2.4 multiply_reduce_fusion
  207.6 0.3 fusion.30
  208.0 0.2 copy.44
  208.2 0.8 copy-done.1
  209.0 0.2 concatenate.3
  209.2 3.1 gather_fusion.4
  212.4 10.0 %all-to-all-start.4 = ((bf16[128,96,128]{2,1,0:T(8,128)(2,1)}), bf16[128,96,128]{2,1,0:T(8,128)(2,1)}, u32[]{:S(2)}, u32[]{:S(2)}) async-start(bf16[128,96,128]{2,1,0:T(8,128)(2,1)} %bitcast.84), calls=%async_computation.5 | async-start | bytes 6291456 | tf_op jit(solution)/shard_map/all_to_all | solution.py:86
  222.3 0.2 reshape.271
  222.6 3.2 gather_fusion.2
  225.7 35.7 %all-to-all-done.4 = bf16[128,96,128]{2,1,0:T(8,128)(2,1)} async-done(((bf16[128,96,128]{2,1,0:T(8,128)(2,1)}), bf16[128,96,128]{2,1,0:T(8,128)(2,1)}, u32[]{:S(2)}, u32[]{:S(2)}) %all-to-all-start.4) | async-done | bytes 3145760 | tf_op jit(solution)/shard_map/all_to_all | solution.py:86
  261.5 8.1 %all-to-all-start.2 = ((bf16[128,96,128]{2,1,0:T(8,128)(2,1)}), bf16[128,96,128]{2,1,0:T(8,128)(2,1)}, u32[]{:S(2)}, u32[]{:S(2)}) async-start(bf16[128,96,128]{2,1,0:T(8,128)(2,1)} %bitcast.83), calls=%async_computation.3 | async-start | bytes 6291456 | tf_op jit(solution)/shard_map/all_to_all | solution.py:86
  269.6 0.2 reshape.255
  269.8 3.2 gather_fusion
  273.0 35.7 %all-to-all-done.2 = bf16[128,96,128]{2,1,0:T(8,128)(2,1)} async-done(((bf16[128,96,128]{2,1,0:T(8,128)(2,1)}), bf16[128,96,128]{2,1,0:T(8,128)(2,1)}, u32[]{:S(2)}, u32[]{:S(2)}) %all-to-all-start.2) | async-done | bytes 3145760 | tf_op jit(solution)/shard_map/all_to_all | solution.py:86
  308.7 7.7 %all-to-all-start = ((bf16[128,96,128]{2,1,0:T(8,128)(2,1)}), bf16[128,96,128]{2,1,0:T(8,128)(2,1)S(1)}, u32[]{:S(2)}, u32[]{:S(2)}) async-start(bf16[128,96,128]{2,1,0:T(8,128)(2,1)} %bitcast.82), calls=%async_computation.1 | async-start | bytes 6291456 | tf_op jit(solution)/shard_map/all_to_all | solution.py:86
  316.5 5.8 %reshape.247 = bf16[384,4096]{1,0:T(8,128)(2,1)} reshape(bf16[128,96,128]{2,1,0:T(8,128)(2,1)} %all-to-all-done.4) | data formatting | bytes 6291456 | tf_op jit(solution)/shard_map/reshape | solution.py:87
  322.2 8.9 %fusion.3 = f32[384,1536]{1,0:T(8,128)S(1)} fusion(bf16[384,4096]{1,0:T(8,128)(2,1)} %reshape.247, bf16[1,4096,1536]{2,1,0:T(8,128)(2,1)} %param.14), kind=kOutput, calls=%fused_computation.13 | convolution fusion | flops 4831838208 | bytes 18087936 | tf_op jit(solution)/shard_map/dot_general | solution.py:17
  331.2 6.9 %fusion.21 = bf16[384,4096]{1,0:T(8,128)(2,1)} fusion(bf16[1,768,4096]{2,1,0:T(8,128)(2,1)} %param.15, f32[384,1536]{1,0:T(8,128)S(1)} %fusion.3), kind=kOutput, calls=%fused_computation.27 | convolution fusion | flops 2419261440 | bytes 11796480 | tf_op jit(solution)/shard_map/dot_general | solution.py:21
  338.1 5.9 %reshape.248 = bf16[128,96,128]{2,1,0:T(8,128)(2,1)} reshape(bf16[384,4096]{1,0:T(8,128)(2,1)} %fusion.21) | data formatting | bytes 6291456 | tf_op jit(solution)/shard_map/reshape | solution.py:88
  343.9 11.9 %all-to-all-done = bf16[128,96,128]{2,1,0:T(8,128)(2,1)S(1)} async-done(((bf16[128,96,128]{2,1,0:T(8,128)(2,1)}), bf16[128,96,128]{2,1,0:T(8,128)(2,1)S(1)}, u32[]{:S(2)}, u32[]{:S(2)}) %all-to-all-start) | async-done | bytes 3145760 | tf_op jit(solution)/shard_map/all_to_all | solution.py:86
  355.9 1.7 copy-done.3
  357.6 7.7 %all-to-all-start.5 = ((bf16[128,96,128]{2,1,0:T(8,128)(2,1)}), bf16[128,96,128]{2,1,0:T(8,128)(2,1)S(1)}, u32[]{:S(2)}, u32[]{:S(2)}) async-start(bf16[128,96,128]{2,1,0:T(8,128)(2,1)} %reshape.248), calls=%async_computation.6 | async-start | bytes 6291456 | tf_op jit(solution)/shard_map/all_to_all | solution.py:89
  365.3 5.8 %reshape.243 = bf16[384,4096]{1,0:T(8,128)(2,1)} reshape(bf16[128,96,128]{2,1,0:T(8,128)(2,1)} %all-to-all-done.2) | data formatting | bytes 6291456 | tf_op jit(solution)/shard_map/reshape | solution.py:87
  371.1 8.9 %fusion.5 = f32[384,1536]{1,0:T(8,128)S(1)} fusion(bf16[384,4096]{1,0:T(8,128)(2,1)} %reshape.243, bf16[1,4096,1536]{2,1,0:T(8,128)(2,1)} %param.14), kind=kOutput, calls=%fused_computation.15 | convolution fusion | flops 4831838208 | bytes 18087936 | tf_op jit(solution)/shard_map/dot_general | solution.py:17
  380.0 6.9 %fusion.18 = bf16[384,4096]{1,0:T(8,128)(2,1)} fusion(bf16[1,768,4096]{2,1,0:T(8,128)(2,1)} %param.15, f32[384,1536]{1,0:T(8,128)S(1)} %fusion.5), kind=kOutput, calls=%fused_computation.26 | convolution fusion | flops 2419261440 | bytes 11796480 | tf_op jit(solution)/shard_map/dot_general | solution.py:21
  386.9 5.9 %reshape.244 = bf16[128,96,128]{2,1,0:T(8,128)(2,1)} reshape(bf16[384,4096]{1,0:T(8,128)(2,1)} %fusion.18) | data formatting | bytes 6291456 | tf_op jit(solution)/shard_map/reshape | solution.py:88
  392.8 11.9 %all-to-all-done.5 = bf16[128,96,128]{2,1,0:T(8,128)(2,1)S(1)} async-done(((bf16[128,96,128]{2,1,0:T(8,128)(2,1)}), bf16[128,96,128]{2,1,0:T(8,128)(2,1)S(1)}, u32[]{:S(2)}, u32[]{:S(2)}) %all-to-all-start.5) | async-done | bytes 3145760 | tf_op jit(solution)/shard_map/all_to_all | solution.py:89
  404.7 8.1 %all-to-all-start.3 = ((bf16[128,96,128]{2,1,0:T(8,128)(2,1)}), bf16[128,96,128]{2,1,0:T(8,128)(2,1)}, u32[]{:S(2)}, u32[]{:S(2)}) async-start(bf16[128,96,128]{2,1,0:T(8,128)(2,1)} %reshape.244), calls=%async_computation.4 | async-start | bytes 6291456 | tf_op jit(solution)/shard_map/all_to_all | solution.py:89
  412.9 5.8 %reshape.239 = bf16[384,4096]{1,0:T(8,128)(2,1)} reshape(bf16[128,96,128]{2,1,0:T(8,128)(2,1)} %copy-done.3) | data formatting | bytes 6291456 | tf_op jit(solution)/shard_map/reshape | solution.py:87
  418.7 8.9 %fusion.7 = f32[384,1536]{1,0:T(8,128)S(1)} fusion(bf16[384,4096]{1,0:T(8,128)(2,1)} %reshape.239, bf16[1,4096,1536]{2,1,0:T(8,128)(2,1)} %param.14), kind=kOutput, calls=%fused_computation.17 | convolution fusion | flops 4831838208 | bytes 18087936 | tf_op jit(solution)/shard_map/dot_general | solution.py:17
  427.6 6.9 %fusion.15 = bf16[384,4096]{1,0:T(8,128)(2,1)} fusion(bf16[1,768,4096]{2,1,0:T(8,128)(2,1)} %param.15, f32[384,1536]{1,0:T(8,128)S(1)} %fusion.7), kind=kOutput, calls=%fused_computation.25 | convolution fusion | flops 2419261440 | bytes 11796480 | tf_op jit(solution)/shard_map/dot_general | solution.py:21
  434.5 5.8 %reshape.240 = bf16[128,96,128]{2,1,0:T(8,128)(2,1)} reshape(bf16[384,4096]{1,0:T(8,128)(2,1)} %fusion.15) | data formatting | bytes 6291456 | tf_op jit(solution)/shard_map/reshape | solution.py:88
  440.3 11.7 %all-to-all-done.3 = bf16[128,96,128]{2,1,0:T(8,128)(2,1)} async-done(((bf16[128,96,128]{2,1,0:T(8,128)(2,1)}), bf16[128,96,128]{2,1,0:T(8,128)(2,1)}, u32[]{:S(2)}, u32[]{:S(2)}) %all-to-all-start.3) | async-done | bytes 3145760 | tf_op jit(solution)/shard_map/all_to_all | solution.py:89
  452.0 8.1 %all-to-all-start.1 = ((bf16[128,96,128]{2,1,0:T(8,128)(2,1)}), bf16[128,96,128]{2,1,0:T(8,128)(2,1)}, u32[]{:S(2)}, u32[]{:S(2)}) async-start(bf16[128,96,128]{2,1,0:T(8,128)(2,1)} %reshape.240), calls=%async_computation.2 | async-start | bytes 6291456 | tf_op jit(solution)/shard_map/all_to_all | solution.py:89
  460.4 0.1 copy.39
  460.6 9.8 %gather_fusion.5 = bf16[1024,32,128]{2,1,0:T(8,128)(2,1)} fusion(bf16[384,32,128]{2,1,0:T(8,128)(2,1)S(1)} %bitcast.81, s32[1024]{0:T(1024)S(1)} %broadcast_clamp_fusion), kind=kCustom, calls=%fused_computation.5 | custom fusion | bytes 16781312 | tf_op jit(solution)/shard_map/jit(_take)/gather | solution.py:92
  470.4 11.8 %gather_fusion.3 = bf16[1024,32,128]{2,1,0:T(8,128)(2,1)} fusion(bf16[384,32,128]{2,1,0:T(8,128)(2,1)} %bitcast.23, s32[1024]{0:T(1024)S(1)} %broadcast_clamp_fusion.1), kind=kCustom, calls=%fused_computation.3 | custom fusion | bytes 16781312 | tf_op jit(solution)/shard_map/jit(_take)/gather | solution.py:92
  482.3 17.0 %all-to-all-done.1 = bf16[128,96,128]{2,1,0:T(8,128)(2,1)} async-done(((bf16[128,96,128]{2,1,0:T(8,128)(2,1)}), bf16[128,96,128]{2,1,0:T(8,128)(2,1)}, u32[]{:S(2)}, u32[]{:S(2)}) %all-to-all-start.1) | async-done | bytes 3145760 | tf_op jit(solution)/shard_map/all_to_all | solution.py:89
  499.2 11.7 %gather_fusion.1 = bf16[1024,32,128]{2,1,0:T(8,128)(2,1)} fusion(bf16[384,32,128]{2,1,0:T(8,128)(2,1)} %bitcast.19, s32[1024]{0:T(1024)S(1)} %broadcast_clamp_fusion.2), kind=kCustom, calls=%fused_computation.1 | custom fusion | bytes 16781312 | tf_op jit(solution)/shard_map/jit(_take)/gather | solution.py:92
  511.0 6.0 %fusion.2 = f32[128,32,128]{2,1,0:T(8,128)S(1)} fusion(f32[128,8]{1,0:T(8,128)S(1)} %get-tuple-element.13, bf16[1024,32,128]{2,1,0:T(8,128)(2,1)} %gather_fusion.1), kind=kLoop, calls=%fused_computation.12 | loop fusion | flops 12058624 | bytes 10489856 | tf_op jit(solution)/shard_map/reduce_sum | solution.py:94
  517.0 7.1 %fusion = (f32[128,32,128]{2,1,0:T(8,128)S(1)}, f32[128,32,128]{2,1,0:T(8,128)S(1)}) fusion(f32[128,8]{1,0:T(8,128)S(1)} %get-tuple-element.12, bf16[1024,32,128]{2,1,0:T(8,128)(2,1)} %gather_fusion.5, bf16[1024,32,128]{2,1,0:T(8,128)(2,1)S(1)} %copy-done, f32[128,8]{1,0:T(8,128)S(1)} %get-tuple-element.11), kind=kLoop, calls=%fused_computation.8 | loop fusion | flops 24117248 | bytes 20979712 | tf_op jit(solution)/shard_map/reduce_sum | solution.py:94
  524.1 0.8 add_add_fusion
  524.9 0.8 copy-done.2
  525.7 2.6 fusion.24
  (46 shorter events, 1.2 us)
Async XLA Ops:
  7.2 42.7 %copy-start.4 = (bf16[512,1024]{1,0:T(8,128)(2,1)S(1)}, bf16[512,1024]{1,0:T(8,128)(2,1)}, u32[]{:S(2)}) copy-start(bf16[512,1024]{1,0:T(8,128)(2,1)} %param.9) | copy-start | bytes 3145732
  7.2 42.6 %all-gather.6.cloned.1.call-start = ((), (), s32[]{:S(2)}) async-start(), calls=%async_computation.8 | async-start | bytes 2621440 | tf_op jit(solution)/shard_map/all_gather | solution.py:27
  17.9 117.4 %all-gather.8.cloned.1.call-start = ((), (), s32[]{:S(2)}) async-start(), calls=%async_computation.9 | async-start | bytes 10485760 | tf_op jit(solution)/shard_map/all_gather | solution.py:28
  49.8 128.2 %reduce-scatter.2.cloned.1.call-start = ((), (), s32[]{:S(2)}) async-start(), calls=%async_computation.7 | async-start | bytes 12582912 | tf_op jit(solution)/shard_map/reduce_scatter | solution.py:43
  156.8 0.7 copy-start.7
  157.8 47.3 %copy-start.5 = (bf16[128,4096]{1,0:T(8,128)(2,1)S(1)}, bf16[128,4096]{1,0:T(8,128)(2,1)}, u32[]{:S(2)}) copy-start(bf16[128,4096]{1,0:T(8,128)(2,1)} %param.8) | copy-start | bytes 3145732
  179.7 25.4 %collective-permute-start = (bf16[128,4096]{1,0:T(8,128)(2,1)S(1)}, bf16[128,4096]{1,0:T(8,128)(2,1)}, u32[]{:S(2)}, u32[]{:S(2)}) collective-permute-start(bf16[128,4096]{1,0:T(8,128)(2,1)S(1)} %fusion.29), channel_id=1, source_target_pairs={{0,2},{2,0},{1,3},{3,1},{4,6},{6,4},{5,7},{7,5},{8,10},{10,8},{9,1... | collective-permute-start | bytes 3145736 | tf_op jit(solution)/shard_map/ppermute | solution.py:48
  186.5 21.1 %copy-start.6 = (f32[4096]{0:T(1024)S(1)}, f32[4096]{0:T(1024)}, u32[]{:S(2)}) copy-start(f32[4096]{0:T(1024)} %param.11) | copy-start | bytes 49156
  207.6 1.5 copy-start.1
  212.4 49.1 %all-to-all-start.4 = ((bf16[128,96,128]{2,1,0:T(8,128)(2,1)}), bf16[128,96,128]{2,1,0:T(8,128)(2,1)}, u32[]{:S(2)}, u32[]{:S(2)}) async-start(bf16[128,96,128]{2,1,0:T(8,128)(2,1)} %bitcast.84), calls=%async_computation.5 | async-start | bytes 6291456 | tf_op jit(solution)/shard_map/all_to_all | solution.py:86
  261.5 47.2 %all-to-all-start.2 = ((bf16[128,96,128]{2,1,0:T(8,128)(2,1)}), bf16[128,96,128]{2,1,0:T(8,128)(2,1)}, u32[]{:S(2)}, u32[]{:S(2)}) async-start(bf16[128,96,128]{2,1,0:T(8,128)(2,1)} %bitcast.83), calls=%async_computation.3 | async-start | bytes 6291456 | tf_op jit(solution)/shard_map/all_to_all | solution.py:86
  308.7 47.1 %all-to-all-start = ((bf16[128,96,128]{2,1,0:T(8,128)(2,1)}), bf16[128,96,128]{2,1,0:T(8,128)(2,1)S(1)}, u32[]{:S(2)}, u32[]{:S(2)}) async-start(bf16[128,96,128]{2,1,0:T(8,128)(2,1)} %bitcast.82), calls=%async_computation.1 | async-start | bytes 6291456 | tf_op jit(solution)/shard_map/all_to_all | solution.py:86
  355.9 1.7 copy-start.3
  357.6 47.1 %all-to-all-start.5 = ((bf16[128,96,128]{2,1,0:T(8,128)(2,1)}), bf16[128,96,128]{2,1,0:T(8,128)(2,1)S(1)}, u32[]{:S(2)}, u32[]{:S(2)}) async-start(bf16[128,96,128]{2,1,0:T(8,128)(2,1)} %reshape.248), calls=%async_computation.6 | async-start | bytes 6291456 | tf_op jit(solution)/shard_map/all_to_all | solution.py:89
  404.7 47.2 %all-to-all-start.3 = ((bf16[128,96,128]{2,1,0:T(8,128)(2,1)}), bf16[128,96,128]{2,1,0:T(8,128)(2,1)}, u32[]{:S(2)}, u32[]{:S(2)}) async-start(bf16[128,96,128]{2,1,0:T(8,128)(2,1)} %reshape.244), calls=%async_computation.4 | async-start | bytes 6291456 | tf_op jit(solution)/shard_map/all_to_all | solution.py:89
  440.3 20.1 %copy-start.8 = (f32[128,8]{0,1:T(8,128)S(1)}, f32[128,8]{0,1:T(8,128)}, u32[]{:S(2)}) copy-start(f32[128,8]{0,1:T(8,128)} %param.13) | copy-start | bytes 12292
  452.0 47.2 %all-to-all-start.1 = ((bf16[128,96,128]{2,1,0:T(8,128)(2,1)}), bf16[128,96,128]{2,1,0:T(8,128)(2,1)}, u32[]{:S(2)}, u32[]{:S(2)}) async-start(bf16[128,96,128]{2,1,0:T(8,128)(2,1)} %reshape.240), calls=%async_computation.2 | async-start | bytes 6291456 | tf_op jit(solution)/shard_map/all_to_all | solution.py:89
  511.0 6.0 %copy-start = (bf16[1024,32,128]{2,1,0:T(8,128)(2,1)S(1)}, bf16[1024,32,128]{2,1,0:T(8,128)(2,1)}, u32[]{:S(2)}) copy-start(bf16[1024,32,128]{2,1,0:T(8,128)(2,1)} %gather_fusion.3) | copy-start | bytes 25165828
  524.1 1.6 copy-start.2
Sparse Core Ops, SparseCore 0:
  18.0 31.7 all-gather.5
  51.5 83.7 all-gather.7
  157.0 20.9 reduce-scatter.1

commit v7 on v5

--- a/solution.py
+++ b/solution.py
@@ -23,10 +23,9 @@
 
 def gather_columns(w_out):
     rows, cols = w_out.shape
-    staged = lax.all_gather(w_out, "xhi", axis=0)
-    staged = lax.all_gather(staged, "z", axis=0)
-    staged = lax.all_gather(staged, "y", axis=0)
-    return staged.transpose(3, 0, 2, 1, 4).reshape(rows, -1)
+    staged = lax.all_gather(w_out, "xhi", axis=1, tiled=True)
+    staged = lax.all_gather(staged, "z", axis=1, tiled=True)
+    return lax.all_gather(staged, "y", axis=1, tiled=True)
 
 
 def project(context, w_out):
@@ -46,7 +45,10 @@
     own = lax.dynamic_index_in_dim(chip_sums, me, axis=0, keepdims=False)
     other = lax.dynamic_index_in_dim(chip_sums, 1 - me, axis=0, keepdims=False)
     arrived = lax.ppermute(other.astype(jnp.bfloat16), "xlo", perm=[(0, 1), (1, 0)])
-    return own + arrived.astype(jnp.float32)
+    summed = own + arrived.astype(jnp.float32)
+    n_y, n_z, n_xhi = (lax.axis_size(name) for name in ("y", "z", "xhi"))
+    summed = summed.reshape(rows, n_y, n_z, n_xhi, -1).transpose(0, 1, 3, 2, 4)
+    return summed.reshape(rows, width)
 
 
 def on_device(hidden_in, context, w_out, norm_gain, expert_ids, route_weight, w_gate_up, w_down):

time: 528 us -> 529 us (level)
    transpose x1 -> x0, local copies, waits for them, and re-layouts: 11.4 us -> none  [gather_columns(): return staged.transpose(3, 0, 2, 1, 4).reshape(rows, -1)]
    reshape x0 -> x3, local copies, waits for them, and re-layouts: none -> 8.47 us  [the longest x2 6.35 us: project(): summed = summed.reshape(rows, n_y, n_z, n_xhi, -1).transpose(0, 1, 3, 2, 4)]
where the time goes in v7:
time: 529 us; the launch traced here: 526 us
  waiting for transfers between devices  315 us (60%)
  local copies, waits for them, and re-layouts  79.7 us (15%)
  matrix products  49.7 us (9%)
  starting transfers between devices  35.8 us (7%)
  other arithmetic  20.8 us (4%)
  between operations  14 us (3%)
  blocking collectives  10.6 us (2%)
    all_gather x1, waiting for transfers between devices, gather_columns(): return lax.all_gather(staged, 'y', axis=1, tiled=True)  84.8 us
    all_to_all x2, waiting for transfers between devices, on_device(): lax.all_to_all(part, ALL, split_axis=0, concat_axis=0, tiled=True)  78.2 us
    all_to_all x2, waiting for transfers between devices, on_device(): lax.all_to_all(outputs, ALL, split_axis=0, concat_axis=0, tiled=True)  77.4 us
    all_gather x1, waiting for transfers between devices, gather_columns(): staged = lax.all_gather(staged, 'z', axis=1, tiled=True)  35.8 us
    dot_general x2, matrix products, expert_block(): jnp.dot(received, w_gate_up[0], preferred_element_type=jnp.float32)  22.9 us
    reduce_scatter x1, waiting for transfers between devices, project(): lax.psum_scatter(partial_sums, 'core', scatter_dimension=0, tiled=True)  19.6 us
    ppermute x1, waiting for transfers between devices, project(): lax.ppermute(other.astype(jnp.bfloat16), 'xlo', perm=[(0, 1), (1, 0)])  19.5 us
    all_to_all x2, starting transfers between devices, on_device(): lax.all_to_all(part, ALL, split_axis=0, concat_axis=0, tiled=True)  18.1 us
  transfers between devices with their start and end apart: 8, of which 8 were waited for; matrix products, arithmetic and copies ran while one was open for 16% of the time, Pallas kernels for 0%

profile of v7, /device:TPU:54, one launch (start us, length us, event | category | flops | bytes accessed | tf_op | source)
XLA Modules:
  0.0 525.8 jit_solution(12330672209196159523)
XLA Ops:
  7.2 0.0 all-gather.3.cloned.1.call-start
  7.2 10.6 %all_gather.9 = bf16[1024,256]{1,0:T(8,128)(2,1)} all-gather(bf16[1024,128]{1,0:T(8,128)(2,1)} %param.10), channel_id=1, replica_groups=mesh['y'=4,'xhi'=2,'z'=4,'xlo'=2,'core'=2] {'xhi'}, dimensions={1}, use_global_device_ids=true | all-gather | bytes 786432 | tf_op jit(solution)/shard_map/all_gather | solution.py:26
  17.8 0.0 all-gather.3.cloned.1.call-update
  17.8 0.0 all-gather.5.cloned.1.call-start
  17.8 35.8 %all-gather.3.cloned.1.call-done = bf16[1024,1024]{1,0:T(8,128)(2,1)} async-done(((bf16[1024,256]{1,0:T(8,128)(2,1)}), bf16[1024,1024]{1,0:T(8,128)(2,1)}) %all-gather.3.cloned.1.call-update) | async-done | bytes 2097168 | tf_op jit(solution)/shard_map/all_gather | solution.py:27
  53.6 0.0 all-gather.5.cloned.1.call-update
  53.6 0.0 reduce-scatter.2.cloned.1.call-start
  53.7 1.3 copy.19
  55.0 84.8 %all-gather.5.cloned.1.call-done = bf16[1024,4096]{1,0:T(8,128)(2,1)} async-done(((bf16[1024,1024]{1,0:T(8,128)(2,1)}), bf16[1024,4096]{1,0:T(8,128)(2,1)}) %all-gather.5.cloned.1.call-update) | async-done | bytes 8388624 | tf_op jit(solution)/shard_map/all_gather | solution.py:28
  139.8 10.0 %fusion.33 = f32[512,4096]{1,0:T(8,128)} fusion(bf16[512,1024]{1,0:T(8,128)(2,1)S(1)} %bitcast.64, bf16[1024,4096]{1,0:T(8,128)(2,1)} %all-gather.5.cloned.1.call-done), kind=kOutput, calls=%fused_computation.58 | convolution fusion | flops 4294967296 | bytes 17825792 | tf_op jit(solution)/shard_map/dot_general | solution.py:36
  149.8 0.0 copy-start.3
  149.8 0.0 reduce-scatter.2.cloned.1.call-update
  149.8 0.7 copy-done.3
  150.5 0.1 copy.23
  150.6 0.1 eq.29
  150.7 0.1 eq.25
  150.8 0.1 copy.22
  150.9 0.1 mul.72
  151.0 0.1 copy.25
  151.1 0.2 fusion.22
  151.3 19.6 %reduce-scatter.2.cloned.1.call-done = f32[256,4096]{1,0:T(8,128)} async-done(((f32[512,4096]{1,0:T(8,128)}), f32[256,4096]{1,0:T(8,128)}) %reduce-scatter.2.cloned.1.call-update) | async-done | bytes 4194320 | tf_op jit(solution)/shard_map/reduce_scatter | solution.py:42
  170.9 1.7 fusion.14
  172.6 0.9 collective-permute-start
  173.6 0.1 copy.26
  173.8 0.4 fusion.21
  174.2 4.3 scatter_custom_fusion
  178.5 19.5 %collective-permute-done = bf16[128,4096]{1,0:T(8,128)(2,1)S(1)} collective-permute-done((bf16[128,4096]{1,0:T(8,128)(2,1)S(1)}, bf16[128,4096]{1,0:T(8,128)(2,1)S(1)}, u32[]{:S(2)}, u32[]{:S(2)}) %collective-permute-start) | collective-permute-done | bytes 1048608 | tf_op jit(solution)/shard_map/ppermute | solution.py:47
  198.0 1.8 bitcast_add_fusion.1
  199.8 2.8 reshape.114
  202.6 0.0 copy-start
  202.6 3.5 copy.31
  206.1 2.1 reshape.115
  208.3 0.0 copy-done
  208.3 0.4 multiply_reduce_fusion
  208.7 0.0 copy-done.2
  208.7 0.4 fusion.15
  209.1 0.2 copy.27
  209.3 0.2 concatenate.6
  209.5 6.1 %gather_fusion = bf16[1152,32,128]{2,1,0:T(8,128)(2,1)} fusion(bf16[129,32,128]{2,1,0:T(8,128)(2,1)S(1)} %concatenate.6, s32[2048]{0:T(1024)S(1)} %pad_clamp_fusion), kind=kCustom, calls=%fused_computation | custom fusion | bytes 18878976 | tf_op jit(solution)/shard_map/jit(_take)/gather | solution.py:79
  215.6 4.8 slice.41
  220.4 10.0 %all-to-all-start.2 = ((bf16[128,128,128]{2,1,0:T(8,128)(2,1)}), bf16[128,128,128]{2,1,0:T(8,128)(2,1)}, u32[]{:S(2)}, u32[]{:S(2)}) async-start(bf16[128,128,128]{2,1,0:T(8,128)(2,1)} %slice.41), calls=%async_computation.3 | async-start | bytes 8388608 | tf_op jit(solution)/shard_map/all_to_all | solution.py:85
  230.4 5.2 slice.38
  235.7 46.7 %all-to-all-done.2 = bf16[128,128,128]{2,1,0:T(8,128)(2,1)} async-done(((bf16[128,128,128]{2,1,0:T(8,128)(2,1)}), bf16[128,128,128]{2,1,0:T(8,128)(2,1)}, u32[]{:S(2)}, u32[]{:S(2)}) %all-to-all-start.2) | async-done | bytes 4194336 | tf_op jit(solution)/shard_map/all_to_all | solution.py:85
  282.4 8.1 %all-to-all-start = ((bf16[128,160,128]{2,1,0:T(8,128)(2,1)}), bf16[128,160,128]{2,1,0:T(8,128)(2,1)}, u32[]{:S(2)}, u32[]{:S(2)}) async-start(bf16[128,160,128]{2,1,0:T(8,128)(2,1)} %slice.38), calls=%async_computation.1 | async-start | bytes 10485760 | tf_op jit(solution)/shard_map/all_to_all | solution.py:85
  290.5 7.3 %reshape.121 = bf16[512,4096]{1,0:T(8,128)(2,1)} reshape(bf16[128,128,128]{2,1,0:T(8,128)(2,1)} %all-to-all-done.2) | data formatting | bytes 8388608 | tf_op jit(solution)/shard_map/reshape | solution.py:87
  297.8 10.5 %fusion.1 = f32[512,1536]{1,0:T(8,128)S(1)} fusion(bf16[512,4096]{1,0:T(8,128)(2,1)} %reshape.121, bf16[1,4096,1536]{2,1,0:T(8,128)(2,1)} %param.14), kind=kOutput, calls=%fused_computation.5 | convolution fusion | flops 6442450944 | bytes 19922944 | tf_op jit(solution)/shard_map/dot_general | solution.py:17
  308.3 7.9 %fusion.8 = bf16[512,4096]{1,0:T(8,128)(2,1)} fusion(bf16[1,768,4096]{2,1,0:T(8,128)(2,1)} %param.15, f32[512,1536]{1,0:T(8,128)S(1)} %fusion.1), kind=kOutput, calls=%fused_computation.14 | convolution fusion | flops 3225681920 | bytes 13631488 | tf_op jit(solution)/shard_map/dot_general | solution.py:21
  316.3 7.4 %reshape.122 = bf16[128,128,128]{2,1,0:T(8,128)(2,1)} reshape(bf16[512,4096]{1,0:T(8,128)(2,1)} %fusion.8) | data formatting | bytes 8388608 | tf_op jit(solution)/shard_map/reshape | solution.py:89
  323.6 31.5 %all-to-all-done = bf16[128,160,128]{2,1,0:T(8,128)(2,1)} async-done(((bf16[128,160,128]{2,1,0:T(8,128)(2,1)}), bf16[128,160,128]{2,1,0:T(8,128)(2,1)}, u32[]{:S(2)}, u32[]{:S(2)}) %all-to-all-start) | async-done | bytes 5242912 | tf_op jit(solution)/shard_map/all_to_all | solution.py:85
  355.1 8.5 %all-to-all-start.3 = ((bf16[128,128,128]{2,1,0:T(8,128)(2,1)}), bf16[128,128,128]{2,1,0:T(8,128)(2,1)}, u32[]{:S(2)}, u32[]{:S(2)}) async-start(bf16[128,128,128]{2,1,0:T(8,128)(2,1)} %reshape.122), calls=%async_computation.4 | async-start | bytes 8388608 | tf_op jit(solution)/shard_map/all_to_all | solution.py:90
  363.6 8.8 %reshape.119 = bf16[640,4096]{1,0:T(8,128)(2,1)} reshape(bf16[128,160,128]{2,1,0:T(8,128)(2,1)} %all-to-all-done) | data formatting | bytes 10485760 | tf_op jit(solution)/shard_map/reshape | solution.py:87
  372.4 12.4 %fusion.3 = f32[640,1536]{1,0:T(8,128)S(1)} fusion(bf16[640,4096]{1,0:T(8,128)(2,1)} %reshape.119, bf16[1,4096,1536]{2,1,0:T(8,128)(2,1)} %param.14), kind=kOutput, calls=%fused_computation.7 | convolution fusion | flops 8053063680 | bytes 21757952 | tf_op jit(solution)/shard_map/dot_general | solution.py:17
  384.8 8.9 %convolution_convert_fusion = bf16[640,4096]{1,0:T(8,128)(2,1)} fusion(bf16[1,768,4096]{2,1,0:T(8,128)(2,1)} %param.15, f32[640,1536]{1,0:T(8,128)S(1)} %fusion.3), kind=kOutput, calls=%fused_computation.10 | convolution fusion | flops 4032102400 | bytes 15466496 | tf_op jit(solution)/shard_map/dot_general | solution.py:21
  393.7 8.9 %reshape.120 = bf16[128,160,128]{2,1,0:T(8,128)(2,1)} reshape(bf16[640,4096]{1,0:T(8,128)(2,1)} %convolution_convert_fusion) | data formatting | bytes 10485760 | tf_op jit(solution)/shard_map/reshape | solution.py:89
  402.6 12.9 %all-to-all-done.3 = bf16[128,128,128]{2,1,0:T(8,128)(2,1)} async-done(((bf16[128,128,128]{2,1,0:T(8,128)(2,1)}), bf16[128,128,128]{2,1,0:T(8,128)(2,1)}, u32[]{:S(2)}, u32[]{:S(2)}) %all-to-all-start.3) | async-done | bytes 4194336 | tf_op jit(solution)/shard_map/all_to_all | solution.py:90
  415.5 8.1 %all-to-all-start.1 = ((bf16[128,160,128]{2,1,0:T(8,128)(2,1)}), bf16[128,160,128]{2,1,0:T(8,128)(2,1)}, u32[]{:S(2)}, u32[]{:S(2)}) async-start(bf16[128,160,128]{2,1,0:T(8,128)(2,1)} %reshape.120), calls=%async_computation.2 | async-start | bytes 10485760 | tf_op jit(solution)/shard_map/all_to_all | solution.py:90
  423.6 0.0 copy-done.4
  423.7 0.1 copy.21
  423.8 64.5 %all-to-all-done.1 = bf16[128,160,128]{2,1,0:T(8,128)(2,1)} async-done(((bf16[128,160,128]{2,1,0:T(8,128)(2,1)}), bf16[128,160,128]{2,1,0:T(8,128)(2,1)}, u32[]{:S(2)}, u32[]{:S(2)}) %all-to-all-start.1) | async-done | bytes 5242912 | tf_op jit(solution)/shard_map/all_to_all | solution.py:90
  488.2 9.1 %pad_maximum_fusion = bf16[128,288,128]{2,1,0:T(8,128)(2,1)} fusion(bf16[128,128,128]{2,1,0:T(8,128)(2,1)} %all-to-all-done.3, bf16[128,160,128]{2,1,0:T(8,128)(2,1)} %all-to-all-done.1), kind=kLoop, calls=%fused_computation.9 | loop fusion | flops 18874368 | bytes 18874368 | tf_op jit(solution)/shard_map/concatenate | solution.py:91
  497.3 13.5 %gather_fusion.1 = bf16[1024,32,128]{2,1,0:T(8,128)(2,1)} fusion(bf16[1152,32,128]{2,1,0:T(8,128)(2,1)} %bitcast.57, s32[1024]{0:T(1024)S(1)} %broadcast_clamp_fusion), kind=kCustom, calls=%fused_computation.1 | custom fusion | bytes 16781312 | tf_op jit(solution)/shard_map/jit(_take)/gather | solution.py:92
  510.8 5.7 %fusion = f32[128,32,128]{2,1,0:T(8,128)S(1)} fusion(f32[128,8]{1,0:T(8,128)S(1)} %copy.21, bf16[1024,32,128]{2,1,0:T(8,128)(2,1)} %gather_fusion.1), kind=kLoop, calls=%fused_computation.4 | loop fusion | flops 12058624 | bytes 10489856 | tf_op jit(solution)/shard_map/reduce_sum | solution.py:93
  516.5 0.0 copy-done.1
  516.5 2.8 fusion.11
  (13 shorter events, 0.1 us)
Async XLA Ops:
  7.2 46.4 %all-gather.3.cloned.1.call-start = ((), (), s32[]{:S(2)}) async-start(), calls=%async_computation.5 | async-start | bytes 2621440 | tf_op jit(solution)/shard_map/all_gather | solution.py:27
  17.8 122.0 %all-gather.5.cloned.1.call-start = ((), (), s32[]{:S(2)}) async-start(), calls=%async_computation.6 | async-start | bytes 10485760 | tf_op jit(solution)/shard_map/all_gather | solution.py:28
  53.6 117.3 %reduce-scatter.2.cloned.1.call-start = ((), (), s32[]{:S(2)}) async-start(), calls=%async_computation.7 | async-start | bytes 12582912 | tf_op jit(solution)/shard_map/reduce_scatter | solution.py:42
  149.8 0.7 copy-start.3
  172.6 25.3 %collective-permute-start = (bf16[128,4096]{1,0:T(8,128)(2,1)S(1)}, bf16[128,4096]{1,0:T(8,128)(2,1)S(1)}, u32[]{:S(2)}, u32[]{:S(2)}) collective-permute-start(bf16[128,4096]{1,0:T(8,128)(2,1)S(1)} %fusion.14), channel_id=1, source_target_pairs={{0,2},{2,0},{1,3},{3,1},{4,6},{6,4},{5,7},{7,5},{8,10},{10,8},{9,1... | collective-permute-start | bytes 3145736 | tf_op jit(solution)/shard_map/ppermute | solution.py:47
  202.6 5.7 %copy-start = (bf16[128,4096]{1,0:T(8,128)(2,1)S(1)}, bf16[128,4096]{1,0:T(8,128)(2,1)}, u32[]{:S(2)}) copy-start(bf16[128,4096]{1,0:T(8,128)(2,1)} %param.8) | copy-start | bytes 3145732
  206.1 2.5 copy-start.2
  220.4 62.0 %all-to-all-start.2 = ((bf16[128,128,128]{2,1,0:T(8,128)(2,1)}), bf16[128,128,128]{2,1,0:T(8,128)(2,1)}, u32[]{:S(2)}, u32[]{:S(2)}) async-start(bf16[128,128,128]{2,1,0:T(8,128)(2,1)} %slice.41), calls=%async_computation.3 | async-start | bytes 8388608 | tf_op jit(solution)/shard_map/all_to_all | solution.py:85
  282.4 72.7 %all-to-all-start = ((bf16[128,160,128]{2,1,0:T(8,128)(2,1)}), bf16[128,160,128]{2,1,0:T(8,128)(2,1)}, u32[]{:S(2)}, u32[]{:S(2)}) async-start(bf16[128,160,128]{2,1,0:T(8,128)(2,1)} %slice.38), calls=%async_computation.1 | async-start | bytes 10485760 | tf_op jit(solution)/shard_map/all_to_all | solution.py:85
  355.1 60.4 %all-to-all-start.3 = ((bf16[128,128,128]{2,1,0:T(8,128)(2,1)}), bf16[128,128,128]{2,1,0:T(8,128)(2,1)}, u32[]{:S(2)}, u32[]{:S(2)}) async-start(bf16[128,128,128]{2,1,0:T(8,128)(2,1)} %reshape.122), calls=%async_computation.4 | async-start | bytes 8388608 | tf_op jit(solution)/shard_map/all_to_all | solution.py:90
  402.6 21.1 %copy-start.4 = (f32[128,8]{0,1:T(8,128)S(1)}, f32[128,8]{0,1:T(8,128)}, u32[]{:S(2)}) copy-start(f32[128,8]{0,1:T(8,128)} %param.13) | copy-start | bytes 12292
  415.5 72.7 %all-to-all-start.1 = ((bf16[128,160,128]{2,1,0:T(8,128)(2,1)}), bf16[128,160,128]{2,1,0:T(8,128)(2,1)}, u32[]{:S(2)}, u32[]{:S(2)}) async-start(bf16[128,160,128]{2,1,0:T(8,128)(2,1)} %reshape.120), calls=%async_computation.2 | async-start | bytes 10485760 | tf_op jit(solution)/shard_map/all_to_all | solution.py:90
  510.8 5.7 %copy-start.1 = (bf16[128,4096]{1,0:T(8,128)(2,1)S(1)}, bf16[128,4096]{1,0:T(8,128)(2,1)}, u32[]{:S(2)}) copy-start(bf16[128,4096]{1,0:T(8,128)(2,1)} %param.8) | copy-start | bytes 3145732
Sparse Core Ops, SparseCore 0:
  17.9 35.6 all-gather.2
  55.3 84.4 all-gather.4
  149.9 20.9 reduce-scatter.1

commit v8 on v7

--- a/solution.py
+++ b/solution.py
@@ -21,11 +21,35 @@
     return jnp.dot(activated, w_down[0], preferred_element_type=jnp.float32).astype(jnp.bfloat16)
 
 
+def ring_gather(block, axis):
+    n = lax.axis_size(axis)
+    me = lax.axis_index(axis)
+    plus = [(i, (i + 1) % n) for i in range(n)]
+    minus = [(i, (i - 1) % n) for i in range(n)]
+    from_left = lax.ppermute(block, axis, perm=plus)
+    from_right = lax.ppermute(block, axis, perm=minus)
+    half = block.shape[-1] // 2
+    far = jnp.concatenate(
+        [
+            lax.ppermute(from_left[..., :half], axis, perm=plus),
+            lax.ppermute(from_right[..., half:], axis, perm=minus),
+        ],
+        axis=-1,
+    )
+    by_step = jnp.stack([block, from_right, far, from_left])
+    order = (jnp.arange(n, dtype=jnp.int32) - me) % n
+    return jnp.take(by_step, order, axis=0)
+
+
 def gather_columns(w_out):
-    rows, cols = w_out.shape
-    staged = lax.all_gather(w_out, "xhi", axis=1, tiled=True)
-    staged = lax.all_gather(staged, "z", axis=1, tiled=True)
-    return lax.all_gather(staged, "y", axis=1, tiled=True)
+    staged = lax.all_gather(w_out, "xhi", axis=0)
+    first = lax.all_gather(staged[0], "z", axis=1, tiled=True)
+    first = lax.all_gather(first, "y", axis=1, tiled=True)
+    if staged.shape[0] == 1:
+        return first, None
+    second = ring_gather(staged[1], "y")
+    second = ring_gather(second, "z")
+    return first, second
 
 
 def project(context, w_out):
@@ -33,11 +57,13 @@
     n_c = lax.axis_size("core")
     rows = context.shape[0] // (n_x * n_c)
     context = context.reshape(n_x, n_c, rows, -1).transpose(1, 0, 2, 3).reshape(n_x * n_c * rows, -1)
-    partial_sums = jnp.dot(
-        context,
-        gather_columns(w_out),
-        preferred_element_type=jnp.float32,
-    )
+    first, second = gather_columns(w_out)
+    partial_sums = jnp.dot(context, first, preferred_element_type=jnp.float32)
+    if second is not None:
+        other = jnp.einsum("th,zyhl->tyzl", context, second, preferred_element_type=jnp.float32)
+        partial_sums = jnp.concatenate(
+            [partial_sums, other.reshape(other.shape[0], -1)], axis=1
+        )
     width = partial_sums.shape[1]
     chip_sums = lax.psum_scatter(partial_sums, "core", scatter_dimension=0, tiled=True)
     chip_sums = chip_sums.reshape(n_x, rows, width)
@@ -46,8 +72,8 @@
     other = lax.dynamic_index_in_dim(chip_sums, 1 - me, axis=0, keepdims=False)
     arrived = lax.ppermute(other.astype(jnp.bfloat16), "xlo", perm=[(0, 1), (1, 0)])
     summed = own + arrived.astype(jnp.float32)
-    n_y, n_z, n_xhi = (lax.axis_size(name) for name in ("y", "z", "xhi"))
-    summed = summed.reshape(rows, n_y, n_z, n_xhi, -1).transpose(0, 1, 3, 2, 4)
+    n_y, n_xhi = lax.axis_size("y"), lax.axis_size("xhi")
+    summed = summed.reshape(rows, n_xhi, n_y, -1).transpose(0, 2, 1, 3)
     return summed.reshape(rows, width)
 
 

time: 529 us -> 522 us (0.987)
  waiting for transfers between devices: 315 us -> 262 us
  local copies, waits for them, and re-layouts: 79.7 us -> 106 us
  other arithmetic: 20.8 us -> 30.2 us
  starting transfers between devices: 35.8 us -> 45.1 us
    all_gather x2, waiting for transfers between devices: 121 us -> 27.1 us  [the longest x1 27.1 us: gather_columns(): first = lax.all_gather(staged[0], 'z', axis=1, tiled=True)]
    ppermute x0 -> x8, waiting for transfers between devices: none -> 36.2 us  [the longest x2 25.3 us: ring_gather(): from_left = lax.ppermute(block, axis, perm=plus)]
    ppermute x0 -> x8, starting transfers between devices: none -> 8.74 us  [the longest x2 3.21 us: ring_gather(): from_left = lax.ppermute(block, axis, perm=plus)]
    gather x0 -> x2, local copies, waits for them, and re-layouts: none -> 6.09 us  [ring_gather(): return jnp.take(by_step, order, axis=0)]
    reshape x2 -> x3, local copies, waits for them, and re-layouts: 6.35 us -> 12 us  [the longest x2 6.51 us: project(): summed = summed.reshape(rows, n_xhi, n_y, -1).transpose(0, 2, 1, 3)]
    transpose x0 -> x1, local copies, waits for them, and re-layouts: none -> 5.47 us  [project(): jnp.einsum('th,zyhl->tyzl', context, second, preferred_element_type=jnp.f...]
    dot_general x1 -> x2, matrix products: 10 us -> 11.5 us  [the longest x1 6.78 us: project(): jnp.einsum('th,zyhl->tyzl', context, second, preferred_element_type=jnp.f...]
  transfers between devices with their start and end apart: 8 -> 16, of which waited for: 8 -> 13; matrix products, arithmetic and copies ran while one was open for 16% -> 23% of each run, Pallas kernels for 0% -> 0%
where the time goes in v8:
time: 522 us; the launch traced here: 519 us
  waiting for transfers between devices  262 us (50%)
  local copies, waits for them, and re-layouts  106 us (20%)
  matrix products  51.2 us (10%)
  starting transfers between devices  45.1 us (9%)
  other arithmetic  30.2 us (6%)
  between operations  14.1 us (3%)
  blocking collectives  10.4 us (2%)
    all_to_all x2, waiting for transfers between devices, on_device(): lax.all_to_all(part, ALL, split_axis=0, concat_axis=0, tiled=True)  78.2 us
    all_to_all x2, waiting for transfers between devices, on_device(): lax.all_to_all(outputs, ALL, split_axis=0, concat_axis=0, tiled=True)  77.3 us
    all_gather x1, waiting for transfers between devices, gather_columns(): first = lax.all_gather(staged[0], 'z', axis=1, tiled=True)  27.1 us
    ppermute x2, waiting for transfers between devices, ring_gather(): from_left = lax.ppermute(block, axis, perm=plus)  25.3 us
    reduce_scatter x1, waiting for transfers between devices, project(): lax.psum_scatter(partial_sums, 'core', scatter_dimension=0, tiled=True)  24.1 us
    dot_general x2, matrix products, expert_block(): jnp.dot(received, w_gate_up[0], preferred_element_type=jnp.float32)  22.9 us
    ppermute x1, waiting for transfers between devices, project(): lax.ppermute(other.astype(jnp.bfloat16), 'xlo', perm=[(0, 1), (1, 0)])  19.3 us
    all_to_all x2, starting transfers between devices, on_device(): lax.all_to_all(part, ALL, split_axis=0, concat_axis=0, tiled=True)  18.2 us
  transfers between devices with their start and end apart: 16, of which 13 were waited for; matrix products, arithmetic and copies ran while one was open for 23% of the time, Pallas kernels for 0%

profile of v8, /device:TPU:54, one launch (start us, length us, event | category | flops | bytes accessed | tf_op | source)
XLA Modules:
  0.0 519.0 jit_solution(11553820015273941815)
XLA Ops:
  7.2 10.4 %all-gather = bf16[2048,128]{1,0:T(8,128)(2,1)S(1)} all-gather(bf16[1024,128]{1,0:T(8,128)(2,1)} %param.10), channel_id=2, replica_groups=mesh['y'=4,'xhi'=2,'z'=4,'xlo'=2,'core'=2] {'xhi'}, dimensions={0}, use_global_device_ids=true | all-gather | bytes 786432 | tf_op jit(solution)/shard_map/all_gather | solution.py:45
  17.6 0.8 fusion.47
  18.5 27.1 %all-gather.8.cloned.1.call-done = bf16[1024,512]{1,0:T(8,128)(2,1)} async-done(((bf16[1024,128]{1,0:T(8,128)(2,1)}), bf16[1024,512]{1,0:T(8,128)(2,1)}) %all-gather.8.cloned.1.call-update) | async-done | bytes 1048592 | tf_op jit(solution)/shard_map/all_gather | solution.py:46
  45.7 1.3 collective-permute-start.1
  47.0 0.8 collective-permute-start
  47.8 5.1 collective-permute-done.1
  53.0 1.2 collective-permute-start.2
  54.3 0.9 collective-permute-start.3
  55.2 4.1 collective-permute-done.2
  59.3 1.4 collective-permute-done.3
  61.0 0.7 gather_fusion
  61.8 1.1 broadcast_select_fusion
  62.9 1.9 collective-permute-start.5
  64.9 20.2 %collective-permute-done.5 = bf16[4,1024,128]{2,1,0:T(8,128)(2,1)S(1)} collective-permute-done((bf16[4,1024,128]{2,1,0:T(8,128)(2,1)}, bf16[4,1024,128]{2,1,0:T(8,128)(2,1)S(1)}, u32[]{:S(2)}, u32[]{:S(2)}) %collective-permute-start.5) | collective-permute-done | bytes 1048608 | tf_op jit(solution)/shard_map/ppermute | solution.py:29
  85.1 1.1 copy.35
  86.3 1.9 collective-permute-start.6
  88.6 1.1 copy.36
  89.7 0.6 collective-permute-start.7
  90.3 2.3 copy.34
  92.7 4.4 collective-permute-done.6
  97.2 1.5 copy.37
  98.7 1.0 collective-permute-done.7
  99.6 1.5 copy.38
  101.2 0.6 maximum_bitcast_fusion
  101.8 3.4 pad_maximum_fusion.2
  105.2 5.3 %gather_fusion.1 = bf16[4,4,1024,128]{3,2,1,0:T(8,128)(2,1)} fusion(bf16[4,4,1024,128]{3,2,1,0:T(8,128)(2,1)} %pad_maximum_fusion.2, s32[1024]{0:T(1024)S(1)} %pad_clamp_fusion.1), kind=kCustom, calls=%fused_computation.1 | custom fusion | bytes 8388624 | tf_op jit(solution)/shard_map/jit(_take)/gather | solution.py:41
  110.5 6.8 %fusion.14 = f32[512,4,4,128]{0,3,1,2:T(8,128)} fusion(bf16[512,1024,1,1]{1,0,3,2:T(8,128)(2,1)S(1)} %bitcast.92, bf16[4,4,1024,128]{3,2,1,0:T(8,128)(2,1)} %gather_fusion.1, pred[4]{0:T(512)(128)(4,1)S(1)} %get-tuple-element.10), kind=kOutput, calls=%fused_computation.22 | convolution fusion | flops 2149580800 | bytes 9437188 | tf_op jit(solution)/shard_map/th,zyhl->tyzl/dot_general | solution.py:63
  117.3 5.5 %copy.40 = f32[512,4,4,128]{3,2,1,0:T(4,128)} copy(f32[512,4,4,128]{0,3,1,2:T(8,128)} %fusion.14) | data formatting | bytes 8388608 | tf_op jit(solution)/shard_map/th,zyhl->tyzl/transpose | solution.py:63
  122.8 5.5 %reshape.231 = f32[512,2048]{1,0:T(8,128)} reshape(f32[512,4,4,128]{3,2,1,0:T(4,128)} %copy.40) | data formatting | bytes 8388608 | tf_op jit(solution)/shard_map/reshape | solution.py:65
  128.3 4.7 fusion.48
  133.0 3.8 pad_maximum_fusion.1
  136.8 0.7 copy-done.7
  138.3 24.1 %reduce-scatter.2.cloned.1.call-done = f32[256,4096]{1,0:T(8,128)} async-done(((f32[512,4096]{1,0:T(8,128)}), f32[256,4096]{1,0:T(8,128)}) %reduce-scatter.2.cloned.1.call-update) | async-done | bytes 4194320 | tf_op jit(solution)/shard_map/reduce_scatter | solution.py:68
  162.4 1.7 fusion.21
  164.1 0.9 collective-permute-start.8
  165.6 4.5 scatter_custom_fusion
  170.2 19.3 %collective-permute-done.8 = bf16[128,4096]{1,0:T(8,128)(2,1)S(1)} collective-permute-done((bf16[128,4096]{1,0:T(8,128)(2,1)S(1)}, bf16[128,4096]{1,0:T(8,128)(2,1)S(1)}, u32[]{:S(2)}, u32[]{:S(2)}) %collective-permute-start.8) | collective-permute-done | bytes 1048608 | tf_op jit(solution)/shard_map/ppermute | solution.py:73
  189.5 1.8 bitcast_add_fusion.1
  191.3 2.4 reshape.233
  193.7 4.1 copy.54
  197.8 3.1 reshape.234
  202.1 6.1 %gather_fusion.2 = bf16[1152,32,128]{2,1,0:T(8,128)(2,1)} fusion(bf16[129,32,128]{2,1,0:T(8,128)(2,1)S(1)} %concatenate.18, s32[2048]{0:T(1024)S(1)} %pad_clamp_fusion), kind=kCustom, calls=%fused_computation.2 | custom fusion | bytes 18878976 | tf_op jit(solution)/shard_map/jit(_take)/gather | solution.py:105
  208.2 4.8 slice.77
  213.1 10.1 %all-to-all-start.2 = ((bf16[128,128,128]{2,1,0:T(8,128)(2,1)}), bf16[128,128,128]{2,1,0:T(8,128)(2,1)}, u32[]{:S(2)}, u32[]{:S(2)}) async-start(bf16[128,128,128]{2,1,0:T(8,128)(2,1)} %slice.77), calls=%async_computation.3 | async-start | bytes 8388608 | tf_op jit(solution)/shard_map/all_to_all | solution.py:111
  223.1 5.2 %slice.74 = bf16[128,160,128]{2,1,0:T(8,128)(2,1)} slice(bf16[128,288,128]{2,1,0:T(8,128)(2,1)} %bitcast.81), slice={[0:128], [0:160], [0:128]} | slice | bytes 10485760 | tf_op jit(solution)/shard_map/slice | solution.py:110
  228.4 46.7 %all-to-all-done.2 = bf16[128,128,128]{2,1,0:T(8,128)(2,1)} async-done(((bf16[128,128,128]{2,1,0:T(8,128)(2,1)}), bf16[128,128,128]{2,1,0:T(8,128)(2,1)}, u32[]{:S(2)}, u32[]{:S(2)}) %all-to-all-start.2) | async-done | bytes 4194336 | tf_op jit(solution)/shard_map/all_to_all | solution.py:111
  275.1 8.1 %all-to-all-start = ((bf16[128,160,128]{2,1,0:T(8,128)(2,1)}), bf16[128,160,128]{2,1,0:T(8,128)(2,1)}, u32[]{:S(2)}, u32[]{:S(2)}) async-start(bf16[128,160,128]{2,1,0:T(8,128)(2,1)} %slice.74), calls=%async_computation.1 | async-start | bytes 10485760 | tf_op jit(solution)/shard_map/all_to_all | solution.py:111
  283.2 7.3 %reshape.240 = bf16[512,4096]{1,0:T(8,128)(2,1)} reshape(bf16[128,128,128]{2,1,0:T(8,128)(2,1)} %all-to-all-done.2) | data formatting | bytes 8388608 | tf_op jit(solution)/shard_map/reshape | solution.py:113
  290.5 10.5 %fusion.1 = f32[512,1536]{1,0:T(8,128)S(1)} fusion(bf16[512,4096]{1,0:T(8,128)(2,1)} %reshape.240, bf16[1,4096,1536]{2,1,0:T(8,128)(2,1)} %param.14), kind=kOutput, calls=%fused_computation.7 | convolution fusion | flops 6442450944 | bytes 19922944 | tf_op jit(solution)/shard_map/dot_general | solution.py:17
  301.0 7.9 %fusion.8 = bf16[512,4096]{1,0:T(8,128)(2,1)} fusion(bf16[1,768,4096]{2,1,0:T(8,128)(2,1)} %param.15, f32[512,1536]{1,0:T(8,128)S(1)} %fusion.1), kind=kOutput, calls=%fused_computation.17 | convolution fusion | flops 3225681920 | bytes 13631488 | tf_op jit(solution)/shard_map/dot_general | solution.py:21
  308.9 7.4 %reshape.241 = bf16[128,128,128]{2,1,0:T(8,128)(2,1)} reshape(bf16[512,4096]{1,0:T(8,128)(2,1)} %fusion.8) | data formatting | bytes 8388608 | tf_op jit(solution)/shard_map/reshape | solution.py:115
  316.3 31.5 %all-to-all-done = bf16[128,160,128]{2,1,0:T(8,128)(2,1)} async-done(((bf16[128,160,128]{2,1,0:T(8,128)(2,1)}), bf16[128,160,128]{2,1,0:T(8,128)(2,1)}, u32[]{:S(2)}, u32[]{:S(2)}) %all-to-all-start) | async-done | bytes 5242912 | tf_op jit(solution)/shard_map/all_to_all | solution.py:111
  347.8 9.0 %all-to-all-start.3 = ((bf16[128,128,128]{2,1,0:T(8,128)(2,1)}), bf16[128,128,128]{2,1,0:T(8,128)(2,1)}, u32[]{:S(2)}, u32[]{:S(2)}) async-start(bf16[128,128,128]{2,1,0:T(8,128)(2,1)} %reshape.241), calls=%async_computation.4 | async-start | bytes 8388608 | tf_op jit(solution)/shard_map/all_to_all | solution.py:116
  356.8 8.8 %reshape.238 = bf16[640,4096]{1,0:T(8,128)(2,1)} reshape(bf16[128,160,128]{2,1,0:T(8,128)(2,1)} %all-to-all-done) | data formatting | bytes 10485760 | tf_op jit(solution)/shard_map/reshape | solution.py:113
  365.7 12.4 %fusion.3 = f32[640,1536]{1,0:T(8,128)S(1)} fusion(bf16[640,4096]{1,0:T(8,128)(2,1)} %reshape.238, bf16[1,4096,1536]{2,1,0:T(8,128)(2,1)} %param.14), kind=kOutput, calls=%fused_computation.9 | convolution fusion | flops 8053063680 | bytes 21757952 | tf_op jit(solution)/shard_map/dot_general | solution.py:17
  378.1 8.9 %convolution_convert_fusion = bf16[640,4096]{1,0:T(8,128)(2,1)} fusion(bf16[1,768,4096]{2,1,0:T(8,128)(2,1)} %param.15, f32[640,1536]{1,0:T(8,128)S(1)} %fusion.3), kind=kOutput, calls=%fused_computation.13 | convolution fusion | flops 4032102400 | bytes 15466496 | tf_op jit(solution)/shard_map/dot_general | solution.py:21
  387.0 8.9 %reshape.239 = bf16[128,160,128]{2,1,0:T(8,128)(2,1)} reshape(bf16[640,4096]{1,0:T(8,128)(2,1)} %convolution_convert_fusion) | data formatting | bytes 10485760 | tf_op jit(solution)/shard_map/reshape | solution.py:115
  395.9 12.8 %all-to-all-done.3 = bf16[128,128,128]{2,1,0:T(8,128)(2,1)} async-done(((bf16[128,128,128]{2,1,0:T(8,128)(2,1)}), bf16[128,128,128]{2,1,0:T(8,128)(2,1)}, u32[]{:S(2)}, u32[]{:S(2)}) %all-to-all-start.3) | async-done | bytes 4194336 | tf_op jit(solution)/shard_map/all_to_all | solution.py:116
  408.7 8.1 %all-to-all-start.1 = ((bf16[128,160,128]{2,1,0:T(8,128)(2,1)}), bf16[128,160,128]{2,1,0:T(8,128)(2,1)}, u32[]{:S(2)}, u32[]{:S(2)}) async-start(bf16[128,160,128]{2,1,0:T(8,128)(2,1)} %reshape.239), calls=%async_computation.2 | async-start | bytes 10485760 | tf_op jit(solution)/shard_map/all_to_all | solution.py:116
  417.0 64.5 %all-to-all-done.1 = bf16[128,160,128]{2,1,0:T(8,128)(2,1)} async-done(((bf16[128,160,128]{2,1,0:T(8,128)(2,1)}), bf16[128,160,128]{2,1,0:T(8,128)(2,1)}, u32[]{:S(2)}, u32[]{:S(2)}) %all-to-all-start.1) | async-done | bytes 5242912 | tf_op jit(solution)/shard_map/all_to_all | solution.py:116
  481.4 9.1 %pad_maximum_fusion = bf16[128,288,128]{2,1,0:T(8,128)(2,1)} fusion(bf16[128,128,128]{2,1,0:T(8,128)(2,1)} %all-to-all-done.3, bf16[128,160,128]{2,1,0:T(8,128)(2,1)} %all-to-all-done.1), kind=kLoop, calls=%fused_computation.11 | loop fusion | flops 18874368 | bytes 18874368 | tf_op jit(solution)/shard_map/concatenate | solution.py:117
  490.5 13.5 %gather_fusion.3 = bf16[1024,32,128]{2,1,0:T(8,128)(2,1)} fusion(bf16[1152,32,128]{2,1,0:T(8,128)(2,1)} %bitcast.82, s32[1024]{0:T(1024)S(1)} %broadcast_clamp_fusion), kind=kCustom, calls=%fused_computation.3 | custom fusion | bytes 16781312 | tf_op jit(solution)/shard_map/jit(_take)/gather | solution.py:118
  504.0 5.7 %fusion = f32[128,32,128]{2,1,0:T(8,128)S(1)} fusion(f32[128,8]{1,0:T(8,128)S(1)} %copy.42, bf16[1024,32,128]{2,1,0:T(8,128)(2,1)} %gather_fusion.3), kind=kLoop, calls=%fused_computation.6 | loop fusion | flops 12058624 | bytes 10489856 | tf_op jit(solution)/shard_map/reduce_sum | solution.py:119
  509.7 2.8 fusion.17
  (61 shorter events, 3.9 us)
Async XLA Ops:
  7.2 38.5 %all-gather.8.cloned.1.call-start = ((), (), s32[]{:S(2)}) async-start(), calls=%async_computation.6 | async-start | bytes 1310720 | tf_op jit(solution)/shard_map/all_gather | solution.py:46
  18.5 109.8 %all-gather.10.cloned.1.call-start = ((), (), s32[]{:S(2)}) async-start(), calls=%async_computation.7 | async-start | bytes 5242880 | tf_op jit(solution)/shard_map/all_gather | solution.py:47
  45.7 116.7 %reduce-scatter.2.cloned.1.call-start = ((), (), s32[]{:S(2)}) async-start(), calls=%async_computation.5 | async-start | bytes 12582912 | tf_op jit(solution)/shard_map/reduce_scatter | solution.py:68
  45.7 7.2 %collective-permute-start.1 = (bf16[1024,128]{1,0:T(8,128)(2,1)S(1)}, bf16[1024,128]{1,0:T(8,128)(2,1)S(1)}, u32[]{:S(2)}, u32[]{:S(2)}) collective-permute-start(bf16[1024,128]{1,0:T(8,128)(2,1)S(1)} %get-tuple-element.8), channel_id=1, source_target_pairs={{0,32},{32,64},{64,96},{96,0},{1,33},{33,65},{65,97},{97,1},{2,34}... | collective-permute-start | bytes 786440 | tf_op jit(solution)/shard_map/ppermute | solution.py:29
  47.0 7.2 %collective-permute-start = (bf16[1024,128]{1,0:T(8,128)(2,1)S(1)}, bf16[1024,128]{1,0:T(8,128)(2,1)S(1)}, u32[]{:S(2)}, u32[]{:S(2)}) collective-permute-start(bf16[1024,128]{1,0:T(8,128)(2,1)S(1)} %get-tuple-element.8), channel_id=1, source_target_pairs={{0,96},{32,0},{64,32},{96,64},{1,97},{33,1},{65,33},{97,65},{2,98}... | collective-permute-start | bytes 786440 | tf_op jit(solution)/shard_map/ppermute | solution.py:30
  53.0 6.4 %collective-permute-start.2 = (bf16[1024,64]{1,0:T(8,128)(2,1)S(1)}, bf16[1024,64]{1,0:T(8,128)(2,1)S(1)}, u32[]{:S(2)}, u32[]{:S(2)}) collective-permute-start(bf16[1024,64]{1,0:T(8,128)(2,1)S(1)} %bitcast.95), channel_id=1, source_target_pairs={{0,32},{32,64},{64,96},{96,0},{1,33},{33,65},{65,97},{97,1},{2,34}... | collective-permute-start | bytes 393224 | tf_op jit(solution)/shard_map/ppermute | solution.py:34
  54.3 6.4 %collective-permute-start.3 = (bf16[1024,64]{1,0:T(8,128)(2,1)S(1)}, bf16[1024,64]{1,0:T(8,128)(2,1)S(1)}, u32[]{:S(2)}, u32[]{:S(2)}) collective-permute-start(bf16[1024,64]{1,0:T(8,128)(2,1)S(1)} %slice.69), channel_id=1, source_target_pairs={{0,96},{32,0},{64,32},{96,64},{1,97},{33,1},{65,33},{97,65},{2,98}... | collective-permute-start | bytes 393224 | tf_op jit(solution)/shard_map/ppermute | solution.py:35
  62.9 22.2 %collective-permute-start.5 = (bf16[4,1024,128]{2,1,0:T(8,128)(2,1)}, bf16[4,1024,128]{2,1,0:T(8,128)(2,1)S(1)}, u32[]{:S(2)}, u32[]{:S(2)}) collective-permute-start(bf16[4,1024,128]{2,1,0:T(8,128)(2,1)} %broadcast_select_fusion), channel_id=1, source_target_pairs={{0,4},{4,8},{8,12},{12,0},{1,5},{5,9},{9,13},{13,1},{2,6},{6,10},{... | collective-permute-start | bytes 3145736 | tf_op jit(solution)/shard_map/ppermute | solution.py:29
  64.9 23.3 %collective-permute-start.4 = (bf16[4,1024,128]{2,1,0:T(8,128)(2,1)}, bf16[4,1024,128]{2,1,0:T(8,128)(2,1)S(1)}, u32[]{:S(2)}, u32[]{:S(2)}) collective-permute-start(bf16[4,1024,128]{2,1,0:T(8,128)(2,1)} %broadcast_select_fusion), channel_id=1, source_target_pairs={{0,12},{4,0},{8,4},{12,8},{1,13},{5,1},{9,5},{13,9},{2,14},{6,2},{... | collective-permute-start | bytes 3145736 | tf_op jit(solution)/shard_map/ppermute | solution.py:30
  85.1 3.1 copy-start.3
  86.3 10.9 %collective-permute-start.6 = (bf16[4,1024,64]{1,2,0:T(8,128)(2,1)}, bf16[4,1024,64]{1,2,0:T(8,128)(2,1)}, u32[]{:S(2)}, u32[]{:S(2)}) collective-permute-start(bf16[4,1024,64]{1,2,0:T(8,128)(2,1)} %copy.35), channel_id=1, source_target_pairs={{0,4},{4,8},{8,12},{12,0},{1,5},{5,9},{9,13},{13,1},{2,6},{6,10},{... | collective-permute-start | bytes 1572872 | tf_op jit(solution)/shard_map/ppermute | solution.py:34
  88.2 4.3 copy-start.4
  89.7 10.0 %collective-permute-start.7 = (bf16[4,1024,64]{1,2,0:T(8,128)(2,1)}, bf16[4,1024,64]{1,2,0:T(8,128)(2,1)}, u32[]{:S(2)}, u32[]{:S(2)}) collective-permute-start(bf16[4,1024,64]{1,2,0:T(8,128)(2,1)} %copy.36), channel_id=1, source_target_pairs={{0,12},{4,0},{8,4},{12,8},{1,13},{5,1},{9,5},{13,9},{2,14},{6,2},{... | collective-permute-start | bytes 1572872 | tf_op jit(solution)/shard_map/ppermute | solution.py:35
  105.2 5.3 %copy-start.5 = (bf16[2,2,128,1024]{3,2,1,0:T(8,128)(2,1)S(1)}, bf16[2,2,128,1024]{3,2,1,0:T(8,128)(2,1)}, u32[]{:S(2)}) copy-start(bf16[2,2,128,1024]{3,2,1,0:T(8,128)(2,1)} %copy.34) | copy-start | bytes 3145732
  128.3 4.7 copy-start
  136.8 0.7 copy-start.7
  164.1 25.4 %collective-permute-start.8 = (bf16[128,4096]{1,0:T(8,128)(2,1)S(1)}, bf16[128,4096]{1,0:T(8,128)(2,1)S(1)}, u32[]{:S(2)}, u32[]{:S(2)}) collective-permute-start(bf16[128,4096]{1,0:T(8,128)(2,1)S(1)} %fusion.21), channel_id=1, source_target_pairs={{0,2},{2,0},{1,3},{3,1},{4,6},{6,4},{5,7},{7,5},{8,10},{10,8},{9,1... | collective-permute-start | bytes 3145736 | tf_op jit(solution)/shard_map/ppermute | solution.py:73
  193.7 7.2 %copy-start.1 = (bf16[128,4096]{1,0:T(8,128)(2,1)S(1)}, bf16[128,4096]{1,0:T(8,128)(2,1)}, u32[]{:S(2)}) copy-start(bf16[128,4096]{1,0:T(8,128)(2,1)} %param.8) | copy-start | bytes 3145732
  197.8 3.5 copy-start.6
  213.1 62.0 %all-to-all-start.2 = ((bf16[128,128,128]{2,1,0:T(8,128)(2,1)}), bf16[128,128,128]{2,1,0:T(8,128)(2,1)}, u32[]{:S(2)}, u32[]{:S(2)}) async-start(bf16[128,128,128]{2,1,0:T(8,128)(2,1)} %slice.77), calls=%async_computation.3 | async-start | bytes 8388608 | tf_op jit(solution)/shard_map/all_to_all | solution.py:111
  275.1 72.7 %all-to-all-start = ((bf16[128,160,128]{2,1,0:T(8,128)(2,1)}), bf16[128,160,128]{2,1,0:T(8,128)(2,1)}, u32[]{:S(2)}, u32[]{:S(2)}) async-start(bf16[128,160,128]{2,1,0:T(8,128)(2,1)} %slice.74), calls=%async_computation.1 | async-start | bytes 10485760 | tf_op jit(solution)/shard_map/all_to_all | solution.py:111
  347.8 61.0 %all-to-all-start.3 = ((bf16[128,128,128]{2,1,0:T(8,128)(2,1)}), bf16[128,128,128]{2,1,0:T(8,128)(2,1)}, u32[]{:S(2)}, u32[]{:S(2)}) async-start(bf16[128,128,128]{2,1,0:T(8,128)(2,1)} %reshape.241), calls=%async_computation.4 | async-start | bytes 8388608 | tf_op jit(solution)/shard_map/all_to_all | solution.py:116
  395.9 20.9 %copy-start.8 = (f32[128,8]{0,1:T(8,128)S(1)}, f32[128,8]{0,1:T(8,128)}, u32[]{:S(2)}) copy-start(f32[128,8]{0,1:T(8,128)} %param.13) | copy-start | bytes 12292
  408.7 72.7 %all-to-all-start.1 = ((bf16[128,160,128]{2,1,0:T(8,128)(2,1)}), bf16[128,160,128]{2,1,0:T(8,128)(2,1)}, u32[]{:S(2)}, u32[]{:S(2)}) async-start(bf16[128,160,128]{2,1,0:T(8,128)(2,1)} %reshape.239), calls=%async_computation.2 | async-start | bytes 10485760 | tf_op jit(solution)/shard_map/all_to_all | solution.py:116
  504.0 5.7 %copy-start.2 = (bf16[128,4096]{1,0:T(8,128)(2,1)S(1)}, bf16[128,4096]{1,0:T(8,128)(2,1)}, u32[]{:S(2)}) copy-start(bf16[128,4096]{1,0:T(8,128)(2,1)} %param.8) | copy-start | bytes 3145732
Sparse Core Ops, SparseCore 0:
  18.6 27.0 all-gather.7
  47.3 48.9 all-gather.9
  136.9 25.4 reduce-scatter.1

commit v9 on v5

--- a/solution.py
+++ b/solution.py
@@ -21,12 +21,24 @@
     return jnp.dot(activated, w_down[0], preferred_element_type=jnp.float32).astype(jnp.bfloat16)
 
 
+def ring_gather(block, axis):
+    n = lax.axis_size(axis)
+    plus = [(i, (i + 1) % n) for i in range(n)]
+    minus = [(i, (i - 1) % n) for i in range(n)]
+    from_left = lax.ppermute(block, axis, perm=plus)
+    from_right = lax.ppermute(block, axis, perm=minus)
+    half = block.shape[-1] // 2
+    far_first = lax.ppermute(from_left[:, :half], axis, perm=plus)
+    far_second = lax.ppermute(from_right[:, half:], axis, perm=minus)
+    return [block, from_right, far_first, far_second, from_left]
+
+
 def gather_columns(w_out):
-    rows, cols = w_out.shape
     staged = lax.all_gather(w_out, "xhi", axis=0)
-    staged = lax.all_gather(staged, "z", axis=0)
-    staged = lax.all_gather(staged, "y", axis=0)
-    return staged.transpose(3, 0, 2, 1, 4).reshape(rows, -1)
+    first = lax.all_gather(staged[0], "z", axis=1, tiled=True)
+    first = lax.all_gather(first, "y", axis=1, tiled=True)
+    second = jnp.concatenate(ring_gather(staged[1], "y"), axis=1)
+    return jnp.concatenate([first] + ring_gather(second, "z"), axis=1)
 
 
 def project(context, w_out):
@@ -34,11 +46,7 @@
     n_c = lax.axis_size("core")
     rows = context.shape[0] // (n_x * n_c)
     context = context.reshape(n_x, n_c, rows, -1).transpose(1, 0, 2, 3).reshape(n_x * n_c * rows, -1)
-    partial_sums = jnp.dot(
-        context,
-        gather_columns(w_out),
-        preferred_element_type=jnp.float32,
-    )
+    partial_sums = jnp.dot(context, gather_columns(w_out), preferred_element_type=jnp.float32)
     width = partial_sums.shape[1]
     chip_sums = lax.psum_scatter(partial_sums, "core", scatter_dimension=0, tiled=True)
     chip_sums = chip_sums.reshape(n_x, rows, width)
@@ -46,7 +54,16 @@
     own = lax.dynamic_index_in_dim(chip_sums, me, axis=0, keepdims=False)
     other = lax.dynamic_index_in_dim(chip_sums, 1 - me, axis=0, keepdims=False)
     arrived = lax.ppermute(other.astype(jnp.bfloat16), "xlo", perm=[(0, 1), (1, 0)])
-    return own + arrived.astype(jnp.float32)
+    summed = own + arrived.astype(jnp.float32)
+    n_y, n_z = lax.axis_size("y"), lax.axis_size("z")
+    summed = summed.reshape(rows, 2, n_y * n_z, -1)
+    by_rings = summed[:, 1].reshape(rows, n_z, n_y, -1)
+    z_order = (jnp.arange(n_z, dtype=jnp.int32) - lax.axis_index("z")) % n_z
+    y_order = (jnp.arange(n_y, dtype=jnp.int32) - lax.axis_index("y")) % n_y
+    by_rings = jnp.take(jnp.take(by_rings, z_order, axis=1), y_order, axis=2)
+    by_rings = by_rings.transpose(0, 2, 1, 3).reshape(rows, n_y * n_z, -1)
+    summed = jnp.stack([summed[:, 0], by_rings], axis=1).reshape(rows, 2, n_y, n_z, -1)
+    return summed.transpose(0, 2, 1, 3, 4).reshape(rows, width)
 
 
 def on_device(hidden_in, context, w_out, norm_gain, expert_ids, route_weight, w_gate_up, w_down):

time: 528 us -> 534 us (1.011)
  waiting for transfers between devices: 311 us -> 255 us
  local copies, waits for them, and re-layouts: 82.6 us -> 127 us
  starting transfers between devices: 35.8 us -> 45 us
  other arithmetic: 21.1 us -> 26.7 us
    all_gather x2, waiting for transfers between devices: 116 us -> 27.1 us  [the longest x1 27.1 us: gather_columns(): first = lax.all_gather(staged[0], 'z', axis=1, tiled=True)]
    ppermute x0 -> x8, waiting for transfers between devices: none -> 39 us  [the longest x2 26 us: ring_gather(): from_left = lax.ppermute(block, axis, perm=plus)]
    concatenate x0 -> x2, local copies, waits for them, and re-layouts: none -> 15.3 us  [the longest x1 12.6 us: gather_columns(): return jnp.concatenate([first] + ring_gather(second, 'z'), axis=1)]
    dynamic_slice x0 -> x3, local copies, waits for them, and re-layouts: none -> 13.7 us  [the longest x2 9.74 us: project(): own = lax.dynamic_index_in_dim(chip_sums, me, axis=0, keepdims=False)]
    reshape x0 -> x3, local copies, waits for them, and re-layouts: none -> 11.5 us  [the longest x1 5.81 us: project(): chip_sums = chip_sums.reshape(n_x, rows, width)]
    unnamed x9 -> x21, local copies, waits for them, and re-layouts: 1.11 us -> 11.9 us
    transpose x1, local copies, waits for them, and re-layouts: 11.4 us -> 1.94 us  [project(): return summed.transpose(0, 2, 1, 3, 4).reshape(rows, width)]
    ppermute x1, waiting for transfers between devices: 19.6 us -> 10.6 us  [project(): lax.ppermute(other.astype(jnp.bfloat16), 'xlo', perm=[(0, 1), (1, 0)])]
  transfers between devices with their start and end apart: 8 -> 16, of which waited for: 8 -> 13; matrix products, arithmetic and copies ran while one was open for 16% -> 19% of each run, Pallas kernels for 0% -> 0%
where the time goes in v9:
time: 534 us; the launch traced here: 530 us
  waiting for transfers between devices  255 us (48%)
  local copies, waits for them, and re-layouts  127 us (24%)
  matrix products  51.2 us (10%)
  starting transfers between devices  45 us (8%)
  other arithmetic  26.7 us (5%)
  between operations  14.1 us (3%)
  blocking collectives  10.4 us (2%)
    all_to_all x2, waiting for transfers between devices, on_device(): lax.all_to_all(part, ALL, split_axis=0, concat_axis=0, tiled=True)  78.2 us
    all_to_all x2, waiting for transfers between devices, on_device(): lax.all_to_all(outputs, ALL, split_axis=0, concat_axis=0, tiled=True)  77.3 us
    all_gather x1, waiting for transfers between devices, gather_columns(): first = lax.all_gather(staged[0], 'z', axis=1, tiled=True)  27.1 us
    ppermute x2, waiting for transfers between devices, ring_gather(): from_left = lax.ppermute(block, axis, perm=plus)  26 us
    reduce_scatter x1, waiting for transfers between devices, project(): lax.psum_scatter(partial_sums, 'core', scatter_dimension=0, tiled=True)  23 us
    dot_general x2, matrix products, expert_block(): jnp.dot(received, w_gate_up[0], preferred_element_type=jnp.float32)  22.9 us
    all_to_all x2, starting transfers between devices, on_device(): lax.all_to_all(part, ALL, split_axis=0, concat_axis=0, tiled=True)  18.2 us
    all_to_all x2, starting transfers between devices, on_device(): lax.all_to_all(outputs, ALL, split_axis=0, concat_axis=0, tiled=True)  17.1 us
  transfers between devices with their start and end apart: 16, of which 13 were waited for; matrix products, arithmetic and copies ran while one was open for 19% of the time, Pallas kernels for 0%

profile of v9, /device:TPU:54, one launch (start us, length us, event | category | flops | bytes accessed | tf_op | source)
XLA Modules:
  0.0 530.0 jit_solution(11261560750475088884)
XLA Ops:
  7.2 10.4 %all-gather = bf16[2048,128]{1,0:T(8,128)(2,1)S(1)} all-gather(bf16[1024,128]{1,0:T(8,128)(2,1)} %param.10), channel_id=2, replica_groups=mesh['y'=4,'xhi'=2,'z'=4,'xlo'=2,'core'=2] {'xhi'}, dimensions={0}, use_global_device_ids=true | all-gather | bytes 786432 | tf_op jit(solution)/shard_map/all_gather | solution.py:37
  17.6 0.7 fusion.39
  18.5 27.1 %all-gather.8.cloned.1.call-done = bf16[1024,512]{1,0:T(8,128)(2,1)} async-done(((bf16[1024,128]{1,0:T(8,128)(2,1)}), bf16[1024,512]{1,0:T(8,128)(2,1)}) %all-gather.8.cloned.1.call-update) | async-done | bytes 1048592 | tf_op jit(solution)/shard_map/all_gather | solution.py:38
  45.7 1.3 collective-permute-start.1
  46.9 0.8 collective-permute-start
  47.8 5.2 collective-permute-done.1
  52.9 1.2 collective-permute-start.2
  54.2 0.9 collective-permute-start.3
  55.1 4.1 collective-permute-done.2
  59.3 1.4 collective-permute-done.3
  60.7 2.6 concatenate.14
  63.3 1.9 collective-permute-start.5
  65.3 20.9 %collective-permute-done.5 = bf16[1024,512]{1,0:T(8,128)(2,1)S(1)} collective-permute-done((bf16[1024,512]{1,0:T(8,128)(2,1)}, bf16[1024,512]{1,0:T(8,128)(2,1)S(1)}, u32[]{:S(2)}, u32[]{:S(2)}) %collective-permute-start.5) | collective-permute-done | bytes 1048608 | tf_op jit(solution)/shard_map/ppermute | solution.py:28
  86.2 2.4 collective-permute-start.6
  88.8 2.3 copy.55
  91.1 5.8 %collective-permute-done.6 = bf16[1024,256]{1,0:T(8,128)(2,1)} collective-permute-done((bf16[1024,256]{1,0:T(8,128)(2,1)S(1)}, bf16[1024,256]{1,0:T(8,128)(2,1)}, u32[]{:S(2)}, u32[]{:S(2)}) %collective-permute-start.6) | collective-permute-done | bytes 524320 | tf_op jit(solution)/shard_map/ppermute | solution.py:31
  96.8 1.7 collective-permute-done.7
  98.5 12.6 %concatenate.15 = bf16[1024,4096]{1,0:T(8,128)(2,1)} concatenate(bf16[1024,2048]{1,0:T(8,128)(2,1)} %all-gather.10.cloned.1.call-done, bf16[1024,128]{1,0:T(8,128)(2,1)S(1)} %get-tuple-element.14, bf16[1024,128]{1,0:T(8,128)(2,1)S(1)} %collective-permute-done, bf16[1024,64]{1,0:T(8,128)(2,1)S(1)} %collective-permute-done.2, bf16[1024,64]{1,0:T(8,128)(2,1)S(1)} %collective-permute-done.3, ...), dimensions={1} | concatenate | bytes 16777216 | tf_op jit(solution)/shard_map/concatenate | solution.py:41
  111.1 11.4 %convolution_bitcast_fusion = f32[512,4096]{0,1:T(8,128)} fusion(bf16[1024,4096]{1,0:T(8,128)(2,1)} %concatenate.15, bf16[512,1024]{1,0:T(8,128)(2,1)} %bitcast.94), kind=kOutput, calls=%fused_computation.12 | convolution fusion | flops 4294967296 | bytes 17825792 | tf_op jit(solution)/shard_map/dot_general | solution.py:49
  122.6 0.7 copy-done.4
  124.3 0.7 copy.54
  125.3 23.0 %reduce-scatter.2.cloned.1.call-done = f32[256,4096]{0,1:T(8,128)} async-done(((f32[512,4096]{0,1:T(8,128)}), f32[256,4096]{0,1:T(8,128)}) %reduce-scatter.2.cloned.1.call-update) | async-done | bytes 4194320 | tf_op jit(solution)/shard_map/reduce_scatter | solution.py:51
  148.4 5.8 %reshape.225 = f32[2,128,4096]{1,0,2:T(2,128)} reshape(f32[256,4096]{0,1:T(8,128)} %reduce-scatter.2.cloned.1.call-done) | data formatting | bytes 8388608 | tf_op jit(solution)/shard_map/reshape | solution.py:52
  154.2 4.0 constant_dynamic-slice_fusion
  158.2 3.8 copy.73
  162.0 0.8 collective-permute-start.8
  162.8 4.3 scatter_custom_fusion
  167.2 5.1 constant_dynamic-slice_fusion.1
  172.3 4.7 copy.56
  177.0 10.6 %collective-permute-done.8 = bf16[128,4096]{1,0:T(8,128)(2,1)} collective-permute-done((bf16[128,4096]{1,0:T(8,128)(2,1)}, bf16[128,4096]{1,0:T(8,128)(2,1)}, u32[]{:S(2)}, u32[]{:S(2)}) %collective-permute-start.8) | collective-permute-done | bytes 1048608 | tf_op jit(solution)/shard_map/ppermute | solution.py:56
  187.6 1.4 fusion.12
  189.5 1.3 copy.74
  191.2 0.6 gather_fusion
  192.8 2.7 maximum_bitcast_fusion
  195.5 1.9 copy.60
  198.0 1.6 multiply_convert_fusion
  199.7 2.6 copy.71
  202.3 1.4 concatenate.16
  203.7 6.1 %gather_fusion.2 = bf16[1152,32,128]{2,1,0:T(8,128)(2,1)} fusion(bf16[129,32,128]{2,1,0:T(8,128)(2,1)S(1)} %concatenate.16, s32[2048]{0:T(1024)S(1)} %pad_clamp_fusion), kind=kCustom, calls=%fused_computation.2 | custom fusion | bytes 18878976 | tf_op jit(solution)/shard_map/jit(_take)/gather | solution.py:94
  209.8 4.8 slice.87
  214.7 10.1 %all-to-all-start.2 = ((bf16[128,128,128]{2,1,0:T(8,128)(2,1)}), bf16[128,128,128]{2,1,0:T(8,128)(2,1)}, u32[]{:S(2)}, u32[]{:S(2)}) async-start(bf16[128,128,128]{2,1,0:T(8,128)(2,1)} %slice.87), calls=%async_computation.3 | async-start | bytes 8388608 | tf_op jit(solution)/shard_map/all_to_all | solution.py:100
  224.7 5.2 slice.84
  230.0 46.7 %all-to-all-done.2 = bf16[128,128,128]{2,1,0:T(8,128)(2,1)} async-done(((bf16[128,128,128]{2,1,0:T(8,128)(2,1)}), bf16[128,128,128]{2,1,0:T(8,128)(2,1)}, u32[]{:S(2)}, u32[]{:S(2)}) %all-to-all-start.2) | async-done | bytes 4194336 | tf_op jit(solution)/shard_map/all_to_all | solution.py:100
  276.7 8.1 %all-to-all-start = ((bf16[128,160,128]{2,1,0:T(8,128)(2,1)}), bf16[128,160,128]{2,1,0:T(8,128)(2,1)}, u32[]{:S(2)}, u32[]{:S(2)}) async-start(bf16[128,160,128]{2,1,0:T(8,128)(2,1)} %slice.84), calls=%async_computation.1 | async-start | bytes 10485760 | tf_op jit(solution)/shard_map/all_to_all | solution.py:100
  284.8 7.3 %reshape.233 = bf16[512,4096]{1,0:T(8,128)(2,1)} reshape(bf16[128,128,128]{2,1,0:T(8,128)(2,1)} %all-to-all-done.2) | data formatting | bytes 8388608 | tf_op jit(solution)/shard_map/reshape | solution.py:102
  292.1 10.5 %fusion.1 = f32[512,1536]{1,0:T(8,128)S(1)} fusion(bf16[512,4096]{1,0:T(8,128)(2,1)} %reshape.233, bf16[1,4096,1536]{2,1,0:T(8,128)(2,1)} %param.14), kind=kOutput, calls=%fused_computation.7 | convolution fusion | flops 6442450944 | bytes 19922944 | tf_op jit(solution)/shard_map/dot_general | solution.py:17
  302.6 7.9 %fusion.8 = bf16[512,4096]{1,0:T(8,128)(2,1)} fusion(bf16[1,768,4096]{2,1,0:T(8,128)(2,1)} %param.15, f32[512,1536]{1,0:T(8,128)S(1)} %fusion.1), kind=kOutput, calls=%fused_computation.17 | convolution fusion | flops 3225681920 | bytes 13631488 | tf_op jit(solution)/shard_map/dot_general | solution.py:21
  310.5 7.4 %reshape.234 = bf16[128,128,128]{2,1,0:T(8,128)(2,1)} reshape(bf16[512,4096]{1,0:T(8,128)(2,1)} %fusion.8) | data formatting | bytes 8388608 | tf_op jit(solution)/shard_map/reshape | solution.py:104
  317.9 31.5 %all-to-all-done = bf16[128,160,128]{2,1,0:T(8,128)(2,1)} async-done(((bf16[128,160,128]{2,1,0:T(8,128)(2,1)}), bf16[128,160,128]{2,1,0:T(8,128)(2,1)}, u32[]{:S(2)}, u32[]{:S(2)}) %all-to-all-start) | async-done | bytes 5242912 | tf_op jit(solution)/shard_map/all_to_all | solution.py:100
  349.4 9.0 %all-to-all-start.3 = ((bf16[128,128,128]{2,1,0:T(8,128)(2,1)}), bf16[128,128,128]{2,1,0:T(8,128)(2,1)}, u32[]{:S(2)}, u32[]{:S(2)}) async-start(bf16[128,128,128]{2,1,0:T(8,128)(2,1)} %reshape.234), calls=%async_computation.4 | async-start | bytes 8388608 | tf_op jit(solution)/shard_map/all_to_all | solution.py:105
  358.4 8.8 %reshape.231 = bf16[640,4096]{1,0:T(8,128)(2,1)} reshape(bf16[128,160,128]{2,1,0:T(8,128)(2,1)} %all-to-all-done) | data formatting | bytes 10485760 | tf_op jit(solution)/shard_map/reshape | solution.py:102
  367.2 12.4 %fusion.3 = f32[640,1536]{1,0:T(8,128)S(1)} fusion(bf16[640,4096]{1,0:T(8,128)(2,1)} %reshape.231, bf16[1,4096,1536]{2,1,0:T(8,128)(2,1)} %param.14), kind=kOutput, calls=%fused_computation.9 | convolution fusion | flops 8053063680 | bytes 21757952 | tf_op jit(solution)/shard_map/dot_general | solution.py:17
  379.7 8.9 %convolution_convert_fusion = bf16[640,4096]{1,0:T(8,128)(2,1)} fusion(bf16[1,768,4096]{2,1,0:T(8,128)(2,1)} %param.15, f32[640,1536]{1,0:T(8,128)S(1)} %fusion.3), kind=kOutput, calls=%fused_computation.13 | convolution fusion | flops 4032102400 | bytes 15466496 | tf_op jit(solution)/shard_map/dot_general | solution.py:21
  388.6 8.9 %reshape.232 = bf16[128,160,128]{2,1,0:T(8,128)(2,1)} reshape(bf16[640,4096]{1,0:T(8,128)(2,1)} %convolution_convert_fusion) | data formatting | bytes 10485760 | tf_op jit(solution)/shard_map/reshape | solution.py:104
  397.5 12.8 %all-to-all-done.3 = bf16[128,128,128]{2,1,0:T(8,128)(2,1)} async-done(((bf16[128,128,128]{2,1,0:T(8,128)(2,1)}), bf16[128,128,128]{2,1,0:T(8,128)(2,1)}, u32[]{:S(2)}, u32[]{:S(2)}) %all-to-all-start.3) | async-done | bytes 4194336 | tf_op jit(solution)/shard_map/all_to_all | solution.py:105
  410.4 8.1 %all-to-all-start.1 = ((bf16[128,160,128]{2,1,0:T(8,128)(2,1)}), bf16[128,160,128]{2,1,0:T(8,128)(2,1)}, u32[]{:S(2)}, u32[]{:S(2)}) async-start(bf16[128,160,128]{2,1,0:T(8,128)(2,1)} %reshape.232), calls=%async_computation.2 | async-start | bytes 10485760 | tf_op jit(solution)/shard_map/all_to_all | solution.py:105
  418.6 64.5 %all-to-all-done.1 = bf16[128,160,128]{2,1,0:T(8,128)(2,1)} async-done(((bf16[128,160,128]{2,1,0:T(8,128)(2,1)}), bf16[128,160,128]{2,1,0:T(8,128)(2,1)}, u32[]{:S(2)}, u32[]{:S(2)}) %all-to-all-start.1) | async-done | bytes 5242912 | tf_op jit(solution)/shard_map/all_to_all | solution.py:105
  483.1 9.1 %pad_maximum_fusion = bf16[128,288,128]{2,1,0:T(8,128)(2,1)} fusion(bf16[128,128,128]{2,1,0:T(8,128)(2,1)} %all-to-all-done.3, bf16[128,160,128]{2,1,0:T(8,128)(2,1)} %all-to-all-done.1), kind=kLoop, calls=%fused_computation.11 | loop fusion | flops 18874368 | bytes 18874368 | tf_op jit(solution)/shard_map/concatenate | solution.py:106
  492.1 13.5 %gather_fusion.3 = bf16[1024,32,128]{2,1,0:T(8,128)(2,1)} fusion(bf16[1152,32,128]{2,1,0:T(8,128)(2,1)} %bitcast.86, s32[1024]{0:T(1024)S(1)} %broadcast_clamp_fusion), kind=kCustom, calls=%fused_computation.3 | custom fusion | bytes 16781312 | tf_op jit(solution)/shard_map/jit(_take)/gather | solution.py:107
  505.6 7.0 %fusion = f32[128,32,128]{2,1,0:T(8,128)} fusion(f32[128,8]{1,0:T(8,128)S(1)} %copy.61, bf16[1024,32,128]{2,1,0:T(8,128)(2,1)} %gather_fusion.3), kind=kLoop, calls=%fused_computation.6 | loop fusion | flops 12058624 | bytes 10489856 | tf_op jit(solution)/shard_map/reduce_sum | solution.py:108
  512.6 3.1 copy.72
  515.7 3.2 fusion.11
  518.9 2.3 copy.70
  521.2 2.3 copy.69
  (56 shorter events, 4.4 us)
Async XLA Ops:
  7.2 38.4 %all-gather.8.cloned.1.call-start = ((), (), s32[]{:S(2)}) async-start(), calls=%async_computation.6 | async-start | bytes 1310720 | tf_op jit(solution)/shard_map/all_gather | solution.py:38
  18.4 80.1 %all-gather.10.cloned.1.call-start = ((), (), s32[]{:S(2)}) async-start(), calls=%async_computation.7 | async-start | bytes 5242880 | tf_op jit(solution)/shard_map/all_gather | solution.py:39
  45.6 102.8 %reduce-scatter.2.cloned.1.call-start = ((), (), s32[]{:S(2)}) async-start(), calls=%async_computation.5 | async-start | bytes 12582912 | tf_op jit(solution)/shard_map/reduce_scatter | solution.py:51
  45.7 7.2 %collective-permute-start.1 = (bf16[1024,128]{1,0:T(8,128)(2,1)S(1)}, bf16[1024,128]{1,0:T(8,128)(2,1)S(1)}, u32[]{:S(2)}, u32[]{:S(2)}) collective-permute-start(bf16[1024,128]{1,0:T(8,128)(2,1)S(1)} %get-tuple-element.14), channel_id=1, source_target_pairs={{0,32},{32,64},{64,96},{96,0},{1,33},{33,65},{65,97},{97,1},{2,34}... | collective-permute-start | bytes 786440 | tf_op jit(solution)/shard_map/ppermute | solution.py:28
  46.9 7.2 %collective-permute-start = (bf16[1024,128]{1,0:T(8,128)(2,1)S(1)}, bf16[1024,128]{1,0:T(8,128)(2,1)S(1)}, u32[]{:S(2)}, u32[]{:S(2)}) collective-permute-start(bf16[1024,128]{1,0:T(8,128)(2,1)S(1)} %get-tuple-element.14), channel_id=1, source_target_pairs={{0,96},{32,0},{64,32},{96,64},{1,97},{33,1},{65,33},{97,65},{2,98}... | collective-permute-start | bytes 786440 | tf_op jit(solution)/shard_map/ppermute | solution.py:29
  52.9 6.4 %collective-permute-start.2 = (bf16[1024,64]{1,0:T(8,128)(2,1)S(1)}, bf16[1024,64]{1,0:T(8,128)(2,1)S(1)}, u32[]{:S(2)}, u32[]{:S(2)}) collective-permute-start(bf16[1024,64]{1,0:T(8,128)(2,1)S(1)} %bitcast.91), channel_id=1, source_target_pairs={{0,32},{32,64},{64,96},{96,0},{1,33},{33,65},{65,97},{97,1},{2,34}... | collective-permute-start | bytes 393224 | tf_op jit(solution)/shard_map/ppermute | solution.py:31
  54.2 6.4 %collective-permute-start.3 = (bf16[1024,64]{1,0:T(8,128)(2,1)S(1)}, bf16[1024,64]{1,0:T(8,128)(2,1)S(1)}, u32[]{:S(2)}, u32[]{:S(2)}) collective-permute-start(bf16[1024,64]{1,0:T(8,128)(2,1)S(1)} %slice.77), channel_id=1, source_target_pairs={{0,96},{32,0},{64,32},{96,64},{1,97},{33,1},{65,33},{97,65},{2,98}... | collective-permute-start | bytes 393224 | tf_op jit(solution)/shard_map/ppermute | solution.py:32
  63.3 22.9 %collective-permute-start.5 = (bf16[1024,512]{1,0:T(8,128)(2,1)}, bf16[1024,512]{1,0:T(8,128)(2,1)S(1)}, u32[]{:S(2)}, u32[]{:S(2)}) collective-permute-start(bf16[1024,512]{1,0:T(8,128)(2,1)} %concatenate.14), channel_id=1, source_target_pairs={{0,4},{4,8},{8,12},{12,0},{1,5},{5,9},{9,13},{13,1},{2,6},{6,10},{... | collective-permute-start | bytes 3145736 | tf_op jit(solution)/shard_map/ppermute | solution.py:28
  65.3 23.4 %collective-permute-start.4 = (bf16[1024,512]{1,0:T(8,128)(2,1)}, bf16[1024,512]{1,0:T(8,128)(2,1)S(1)}, u32[]{:S(2)}, u32[]{:S(2)}) collective-permute-start(bf16[1024,512]{1,0:T(8,128)(2,1)} %concatenate.14), channel_id=1, source_target_pairs={{0,12},{4,0},{8,4},{12,8},{1,13},{5,1},{9,5},{13,9},{2,14},{6,2},{... | collective-permute-start | bytes 3145736 | tf_op jit(solution)/shard_map/ppermute | solution.py:29
  86.2 10.6 %collective-permute-start.6 = (bf16[1024,256]{1,0:T(8,128)(2,1)S(1)}, bf16[1024,256]{1,0:T(8,128)(2,1)}, u32[]{:S(2)}, u32[]{:S(2)}) collective-permute-start(bf16[1024,256]{1,0:T(8,128)(2,1)S(1)} %slice.78), channel_id=1, source_target_pairs={{0,4},{4,8},{8,12},{12,0},{1,5},{5,9},{9,13},{13,1},{2,6},{6,10},{... | collective-permute-start | bytes 1572872 | tf_op jit(solution)/shard_map/ppermute | solution.py:31
  88.7 9.8 %collective-permute-start.7 = (bf16[1024,256]{1,0:T(8,128)(2,1)S(1)}, bf16[1024,256]{1,0:T(8,128)(2,1)}, u32[]{:S(2)}, u32[]{:S(2)}) collective-permute-start(bf16[1024,256]{1,0:T(8,128)(2,1)S(1)} %slice.79), channel_id=1, source_target_pairs={{0,12},{4,0},{8,4},{12,8},{1,13},{5,1},{9,5},{13,9},{2,14},{6,2},{... | collective-permute-start | bytes 1572872 | tf_op jit(solution)/shard_map/ppermute | solution.py:32
  122.6 0.7 copy-start.4
  122.6 1.7 copy-start.2
  125.0 73.1 %copy-start = (bf16[128,4096]{0,1:T(8,128)(2,1)}, bf16[128,4096]{0,1:T(8,128)(2,1)S(1)}, u32[]{:S(2)}) copy-start(bf16[128,4096]{0,1:T(8,128)(2,1)S(1)} %copy.54) | copy-start | bytes 3145732
  162.0 25.6 %collective-permute-start.8 = (bf16[128,4096]{1,0:T(8,128)(2,1)}, bf16[128,4096]{1,0:T(8,128)(2,1)}, u32[]{:S(2)}, u32[]{:S(2)}) collective-permute-start(bf16[128,4096]{1,0:T(8,128)(2,1)} %bitcast.92), channel_id=1, source_target_pairs={{0,2},{2,0},{1,3},{3,1},{4,6},{6,4},{5,7},{7,5},{8,10},{10,8},{9,1... | collective-permute-start | bytes 3145736 | tf_op jit(solution)/shard_map/ppermute | solution.py:56
  195.5 2.5 copy-start.3
  214.7 62.0 %all-to-all-start.2 = ((bf16[128,128,128]{2,1,0:T(8,128)(2,1)}), bf16[128,128,128]{2,1,0:T(8,128)(2,1)}, u32[]{:S(2)}, u32[]{:S(2)}) async-start(bf16[128,128,128]{2,1,0:T(8,128)(2,1)} %slice.87), calls=%async_computation.3 | async-start | bytes 8388608 | tf_op jit(solution)/shard_map/all_to_all | solution.py:100
  276.7 72.7 %all-to-all-start = ((bf16[128,160,128]{2,1,0:T(8,128)(2,1)}), bf16[128,160,128]{2,1,0:T(8,128)(2,1)}, u32[]{:S(2)}, u32[]{:S(2)}) async-start(bf16[128,160,128]{2,1,0:T(8,128)(2,1)} %slice.84), calls=%async_computation.1 | async-start | bytes 10485760 | tf_op jit(solution)/shard_map/all_to_all | solution.py:100
  349.4 61.0 %all-to-all-start.3 = ((bf16[128,128,128]{2,1,0:T(8,128)(2,1)}), bf16[128,128,128]{2,1,0:T(8,128)(2,1)}, u32[]{:S(2)}, u32[]{:S(2)}) async-start(bf16[128,128,128]{2,1,0:T(8,128)(2,1)} %reshape.234), calls=%async_computation.4 | async-start | bytes 8388608 | tf_op jit(solution)/shard_map/all_to_all | solution.py:105
  397.5 21.0 %copy-start.5 = (f32[128,8]{0,1:T(8,128)S(1)}, f32[128,8]{0,1:T(8,128)}, u32[]{:S(2)}) copy-start(f32[128,8]{0,1:T(8,128)} %param.13) | copy-start | bytes 12292
  410.4 72.7 %all-to-all-start.1 = ((bf16[128,160,128]{2,1,0:T(8,128)(2,1)}), bf16[128,160,128]{2,1,0:T(8,128)(2,1)}, u32[]{:S(2)}, u32[]{:S(2)}) async-start(bf16[128,160,128]{2,1,0:T(8,128)(2,1)} %reshape.232), calls=%async_computation.2 | async-start | bytes 10485760 | tf_op jit(solution)/shard_map/all_to_all | solution.py:105
  512.6 3.1 copy-start.1
Sparse Core Ops, SparseCore 0:
  18.5 27.0 all-gather.7
  47.2 48.9 all-gather.9
  122.7 25.5 reduce-scatter.1

commit v10 on v8

--- a/solution.py
+++ b/solution.py
@@ -98,25 +98,29 @@
     target = chosen * capacity + slots
     token_index = jnp.arange(tok_count * top_count, dtype=jnp.int32) // top_count
     source = jnp.full((rows_all,), tok_count, jnp.int32).at[target].set(token_index)
+    source = source.reshape(experts_all, capacity)
     normed3 = jnp.concatenate(
         [normed.reshape(tok_count, chunks, LANES), jnp.zeros((1, chunks, LANES), jnp.bfloat16)],
         axis=0,
     )
-    send = jnp.take(normed3, source, axis=0, mode="clip")
-    send = send.reshape(experts_all, capacity * chunks, LANES)
-    first = (capacity + 1) // 2
-    returned = []
-    for lo, hi in ((0, first), (first, capacity)):
-        part = send[:, lo * chunks : hi * chunks]
-        received = lax.all_to_all(part, ALL, split_axis=0, concat_axis=0, tiled=True)
-        outputs = expert_block(
-            received.reshape(experts_all * (hi - lo), width), w_gate_up, w_down
-        )
-        outputs = outputs.reshape(experts_all, (hi - lo) * chunks, LANES)
-        returned.append(lax.all_to_all(outputs, ALL, split_axis=0, concat_axis=0, tiled=True))
-    returned = jnp.concatenate(returned, axis=1).reshape(rows_all, chunks, LANES)
-    picked = jnp.take(returned, target, axis=0, mode="clip").reshape(tok_count, top_count, chunks, LANES)
-    moe_sum = jnp.sum(route_weight[:, :, None, None] * picked.astype(jnp.float32), axis=1)
+    weights = route_weight.reshape(-1)
+    groups = 2
+    bounds = [capacity * g // groups for g in range(groups + 1)]
+    moe_sum = None
+    for lo, hi in zip(bounds[:-1], bounds[1:]):
+        size = hi - lo
+        send = jnp.take(normed3, source[:, lo:hi].reshape(-1), axis=0, mode="clip")
+        send = send.reshape(experts_all, size * chunks, LANES)
+        received = lax.all_to_all(send, ALL, split_axis=0, concat_axis=0, tiled=True)
+        outputs = expert_block(received.reshape(experts_all * size, width), w_gate_up, w_down)
+        outputs = outputs.reshape(experts_all, size * chunks, LANES)
+        returned = lax.all_to_all(outputs, ALL, split_axis=0, concat_axis=0, tiled=True)
+        returned = returned.reshape(experts_all * size, chunks, LANES)
+        inside = (slots >= lo) & (slots < hi)
+        picked = jnp.take(returned, chosen * size + slots - lo, axis=0, mode="clip")
+        scaled = jnp.where(inside, weights, 0.0)[:, None, None] * picked.astype(jnp.float32)
+        part = jnp.sum(scaled.reshape(tok_count, top_count, chunks, LANES), axis=1)
+        moe_sum = part if moe_sum is None else moe_sum + part
     mixed = (residual + moe_sum.reshape(tok_count, width)).astype(jnp.bfloat16)
     return (attended, mixed)
 

time: 522 us -> 503 us (0.964)
  waiting for transfers between devices: 262 us -> 241 us
    ppermute x2, waiting for transfers between devices: 0.01 us -> 26 us  [ring_gather(): from_right = lax.ppermute(block, axis, perm=minus)]
    ppermute x2, waiting for transfers between devices: 25.3 us -> 0.01 us  [ring_gather(): from_left = lax.ppermute(block, axis, perm=plus)]
    all_to_all x2, waiting for transfers between devices: 77.3 us -> 58 us  [on_device(): lax.all_to_all(outputs, ALL, split_axis=0, concat_axis=0, tiled=True)]
    gather x2 -> x4, local copies, waits for them, and re-layouts: 19.6 us -> 32 us  [the longest x2 24.4 us: on_device(): picked = jnp.take(returned, chosen * size + slots - lo, axis=0, mode='clip')]
    slice x2 -> x1, local copies, waits for them, and re-layouts: 10.1 us -> 0.08 us  [on_device(): send = jnp.take(normed3, source[:, lo:hi].reshape(-1), axis=0, mode='clip')]
    concatenate x1 -> x0, other arithmetic: 9.08 us -> none  [on_device(): jnp.concatenate(returned, axis=1).reshape(rows_all, chunks, LANES)]
    ppermute x2, waiting for transfers between devices: 2.37 us -> 10.1 us  [ring_gather(): lax.ppermute(from_right[..., half:], axis, perm=minus)]
    reduce_sum x1 -> x2, other arithmetic: 5.71 us -> 12.8 us  [on_device(): part = jnp.sum(scaled.reshape(tok_count, top_count, chunks, LANES), axis=1)]
  transfers between devices with their start and end apart: 16 -> 16, of which waited for: 13 -> 12; matrix products, arithmetic and copies ran while one was open for 23% -> 28% of each run, Pallas kernels for 0% -> 0%
where the time goes in v10:
time: 503 us; the launch traced here: 500 us
  waiting for transfers between devices  241 us (48%)
  local copies, waits for them, and re-layouts  109 us (22%)
  matrix products  51.1 us (10%)
  starting transfers between devices  45.3 us (9%)
  other arithmetic  28.7 us (6%)
  between operations  14.2 us (3%)
  blocking collectives  10.4 us (2%)
    all_to_all x2, waiting for transfers between devices, on_device(): lax.all_to_all(send, ALL, split_axis=0, concat_axis=0, tiled=True)  79.1 us
    all_to_all x2, waiting for transfers between devices, on_device(): lax.all_to_all(outputs, ALL, split_axis=0, concat_axis=0, tiled=True)  58 us
    all_gather x1, waiting for transfers between devices, gather_columns(): first = lax.all_gather(staged[0], 'z', axis=1, tiled=True)  27.1 us
    ppermute x2, waiting for transfers between devices, ring_gather(): from_right = lax.ppermute(block, axis, perm=minus)  26 us
    gather x2, local copies, waits for them, and re-layouts, on_device(): picked = jnp.take(returned, chosen * size + slots - lo, axis=0, mode='clip')  24.4 us
    dot_general x2, matrix products, expert_block(): jnp.dot(received, w_gate_up[0], preferred_element_type=jnp.float32)  22.9 us
    reduce_scatter x1, waiting for transfers between devices, project(): lax.psum_scatter(partial_sums, 'core', scatter_dimension=0, tiled=True)  20.6 us
    ppermute x1, waiting for transfers between devices, project(): lax.ppermute(other.astype(jnp.bfloat16), 'xlo', perm=[(0, 1), (1, 0)])  18.4 us
  transfers between devices with their start and end apart: 16, of which 12 were waited for; matrix products, arithmetic and copies ran while one was open for 28% of the time, Pallas kernels for 0%

profile of v10, /device:TPU:54, one launch (start us, length us, event | category | flops | bytes accessed | tf_op | source)
XLA Modules:
  0.0 500.3 jit_solution(580083638200808364)
XLA Ops:
  7.2 10.4 %all-gather = bf16[2048,128]{1,0:T(8,128)(2,1)S(1)} all-gather(bf16[1024,128]{1,0:T(8,128)(2,1)} %param.10), channel_id=2, replica_groups=mesh['y'=4,'xhi'=2,'z'=4,'xlo'=2,'core'=2] {'xhi'}, dimensions={0}, use_global_device_ids=true | all-gather | bytes 786432 | tf_op jit(solution)/shard_map/all_gather | solution.py:45
  17.6 0.8 fusion.48
  18.5 27.1 %all-gather.8.cloned.1.call-done = bf16[1024,512]{1,0:T(8,128)(2,1)} async-done(((bf16[1024,128]{1,0:T(8,128)(2,1)}), bf16[1024,512]{1,0:T(8,128)(2,1)}) %all-gather.8.cloned.1.call-update) | async-done | bytes 1048592 | tf_op jit(solution)/shard_map/all_gather | solution.py:46
  45.7 0.6 collective-permute-start
  46.3 1.5 collective-permute-start.1
  47.8 5.1 %collective-permute-done = bf16[1024,128]{1,0:T(8,128)(2,1)S(1)} collective-permute-done((bf16[1024,128]{1,0:T(8,128)(2,1)S(1)}, bf16[1024,128]{1,0:T(8,128)(2,1)S(1)}, u32[]{:S(2)}, u32[]{:S(2)}) %collective-permute-start) | collective-permute-done | bytes 262176 | tf_op jit(solution)/shard_map/ppermute | solution.py:30
  53.1 0.6 collective-permute-start.3
  53.7 2.0 collective-permute-start.2
  55.7 4.4 collective-permute-done.3
  60.4 0.7 gather_fusion
  61.1 1.1 broadcast_select_fusion
  62.3 1.4 collective-permute-start.4
  63.7 0.6 collective-permute-start.5
  64.3 20.9 %collective-permute-done.4 = bf16[4,1024,128]{2,1,0:T(8,128)(2,1)S(1)} collective-permute-done((bf16[4,1024,128]{2,1,0:T(8,128)(2,1)}, bf16[4,1024,128]{2,1,0:T(8,128)(2,1)S(1)}, u32[]{:S(2)}, u32[]{:S(2)}) %collective-permute-start.4) | collective-permute-done | bytes 1048608 | tf_op jit(solution)/shard_map/ppermute | solution.py:30
  85.2 1.1 copy-done.4
  86.6 1.1 copy.43
  87.7 1.1 collective-permute-start.7
  89.2 1.2 collective-permute-start.6
  90.3 2.3 copy.41
  92.8 5.7 %collective-permute-done.7 = bf16[4,1024,64]{1,2,0:T(8,128)(2,1)S(1)} collective-permute-done((bf16[4,1024,64]{1,2,0:T(8,128)(2,1)}, bf16[4,1024,64]{1,2,0:T(8,128)(2,1)S(1)}, u32[]{:S(2)}, u32[]{:S(2)}) %collective-permute-start.7) | collective-permute-done | bytes 524320 | tf_op jit(solution)/shard_map/ppermute | solution.py:35
  99.0 2.0 collective-permute-done.6
  101.0 1.5 copy.44
  102.5 0.6 maximum_bitcast_fusion
  103.1 3.4 pad_maximum_fusion.1
  106.5 5.3 %gather_fusion.1 = bf16[4,4,1024,128]{3,2,1,0:T(8,128)(2,1)} fusion(bf16[4,4,1024,128]{3,2,1,0:T(8,128)(2,1)} %pad_maximum_fusion.1, s32[1024]{0:T(1024)S(1)} %pad_clamp_fusion.2), kind=kCustom, calls=%fused_computation.1 | custom fusion | bytes 8388624 | tf_op jit(solution)/shard_map/jit(_take)/gather | solution.py:41
  111.9 6.8 %fusion.15 = f32[512,4,4,128]{0,3,1,2:T(8,128)} fusion(bf16[512,1024,1,1]{1,0,3,2:T(8,128)(2,1)S(1)} %bitcast.97, bf16[4,4,1024,128]{3,2,1,0:T(8,128)(2,1)} %gather_fusion.1, pred[4]{0:T(512)(128)(4,1)S(1)} %get-tuple-element.18), kind=kOutput, calls=%fused_computation.25 | convolution fusion | flops 2149580800 | bytes 9437188 | tf_op jit(solution)/shard_map/th,zyhl->tyzl/dot_general | solution.py:63
  118.6 5.5 %copy.47 = f32[512,4,4,128]{3,2,1,0:T(4,128)} copy(f32[512,4,4,128]{0,3,1,2:T(8,128)} %fusion.15) | data formatting | bytes 8388608 | tf_op jit(solution)/shard_map/th,zyhl->tyzl/transpose | solution.py:63
  124.1 5.5 %reshape.317 = f32[512,2048]{1,0:T(8,128)} reshape(f32[512,4,4,128]{3,2,1,0:T(4,128)} %copy.47) | data formatting | bytes 8388608 | tf_op jit(solution)/shard_map/reshape | solution.py:65
  129.6 4.7 fusion.49
  134.3 3.8 pad_maximum_fusion
  138.1 0.7 copy-done.8
  139.4 20.6 %reduce-scatter.2.cloned.1.call-done = f32[256,4096]{1,0:T(8,128)} async-done(((f32[512,4096]{1,0:T(8,128)}), f32[256,4096]{1,0:T(8,128)}) %reduce-scatter.2.cloned.1.call-update) | async-done | bytes 4194320 | tf_op jit(solution)/shard_map/reduce_scatter | solution.py:68
  160.0 1.7 fusion.22
  161.8 0.9 collective-permute-start.8
  163.9 4.5 scatter_custom_fusion
  168.7 18.4 %collective-permute-done.8 = bf16[128,4096]{1,0:T(8,128)(2,1)S(1)} collective-permute-done((bf16[128,4096]{1,0:T(8,128)(2,1)S(1)}, bf16[128,4096]{1,0:T(8,128)(2,1)S(1)}, u32[]{:S(2)}, u32[]{:S(2)}) %collective-permute-start.8) | collective-permute-done | bytes 1048608 | tf_op jit(solution)/shard_map/ppermute | solution.py:73
  187.1 1.8 bitcast_add_fusion.1
  188.9 2.4 reshape.319
  191.3 4.1 copy.64
  195.4 3.1 reshape.320
  199.8 3.5 gather_fusion.2
  203.2 10.0 %all-to-all-start = ((bf16[128,128,128]{2,1,0:T(8,128)(2,1)}), bf16[128,128,128]{2,1,0:T(8,128)(2,1)}, u32[]{:S(2)}, u32[]{:S(2)}) async-start(bf16[128,128,128]{2,1,0:T(8,128)(2,1)} %bitcast.87), calls=%async_computation.1 | async-start | bytes 8388608 | tf_op jit(solution)/shard_map/all_to_all | solution.py:114
  213.6 4.1 gather_fusion.4
  217.7 47.5 %all-to-all-done = bf16[128,128,128]{2,1,0:T(8,128)(2,1)} async-done(((bf16[128,128,128]{2,1,0:T(8,128)(2,1)}), bf16[128,128,128]{2,1,0:T(8,128)(2,1)}, u32[]{:S(2)}, u32[]{:S(2)}) %all-to-all-start) | async-done | bytes 4194336 | tf_op jit(solution)/shard_map/all_to_all | solution.py:114
  265.2 8.1 %all-to-all-start.2 = ((bf16[128,160,128]{2,1,0:T(8,128)(2,1)}), bf16[128,160,128]{2,1,0:T(8,128)(2,1)}, u32[]{:S(2)}, u32[]{:S(2)}) async-start(bf16[128,160,128]{2,1,0:T(8,128)(2,1)} %bitcast.86), calls=%async_computation.3 | async-start | bytes 10485760 | tf_op jit(solution)/shard_map/all_to_all | solution.py:114
  273.3 7.3 %reshape.325 = bf16[512,4096]{1,0:T(8,128)(2,1)} reshape(bf16[128,128,128]{2,1,0:T(8,128)(2,1)} %all-to-all-done) | data formatting | bytes 8388608 | tf_op jit(solution)/shard_map/reshape | solution.py:115
  280.6 10.5 %fusion.4 = f32[512,1536]{1,0:T(8,128)S(1)} fusion(bf16[512,4096]{1,0:T(8,128)(2,1)} %reshape.325, bf16[1,4096,1536]{2,1,0:T(8,128)(2,1)} %param.14), kind=kOutput, calls=%fused_computation.13 | convolution fusion | flops 6442450944 | bytes 19922944 | tf_op jit(solution)/shard_map/dot_general | solution.py:17
  291.1 7.9 %fusion.9 = bf16[512,4096]{1,0:T(8,128)(2,1)} fusion(bf16[1,768,4096]{2,1,0:T(8,128)(2,1)} %param.15, f32[512,1536]{1,0:T(8,128)S(1)} %fusion.4), kind=kOutput, calls=%fused_computation.20 | convolution fusion | flops 3225681920 | bytes 13631488 | tf_op jit(solution)/shard_map/dot_general | solution.py:21
  299.0 7.4 %reshape.326 = bf16[128,128,128]{2,1,0:T(8,128)(2,1)} reshape(bf16[512,4096]{1,0:T(8,128)(2,1)} %fusion.9) | data formatting | bytes 8388608 | tf_op jit(solution)/shard_map/reshape | solution.py:116
  306.4 31.5 %all-to-all-done.2 = bf16[128,160,128]{2,1,0:T(8,128)(2,1)} async-done(((bf16[128,160,128]{2,1,0:T(8,128)(2,1)}), bf16[128,160,128]{2,1,0:T(8,128)(2,1)}, u32[]{:S(2)}, u32[]{:S(2)}) %all-to-all-start.2) | async-done | bytes 5242912 | tf_op jit(solution)/shard_map/all_to_all | solution.py:114
  337.9 9.0 %all-to-all-start.1 = ((bf16[128,128,128]{2,1,0:T(8,128)(2,1)}), bf16[128,128,128]{2,1,0:T(8,128)(2,1)}, u32[]{:S(2)}, u32[]{:S(2)}) async-start(bf16[128,128,128]{2,1,0:T(8,128)(2,1)} %reshape.326), calls=%async_computation.2 | async-start | bytes 8388608 | tf_op jit(solution)/shard_map/all_to_all | solution.py:117
  347.0 8.9 %reshape.329 = bf16[640,4096]{1,0:T(8,128)(2,1)} reshape(bf16[128,160,128]{2,1,0:T(8,128)(2,1)} %all-to-all-done.2) | data formatting | bytes 10485760 | tf_op jit(solution)/shard_map/reshape | solution.py:115
  355.8 12.4 %fusion.2 = f32[640,1536]{1,0:T(8,128)S(1)} fusion(bf16[640,4096]{1,0:T(8,128)(2,1)} %reshape.329, bf16[1,4096,1536]{2,1,0:T(8,128)(2,1)} %param.14), kind=kOutput, calls=%fused_computation.11 | convolution fusion | flops 8053063680 | bytes 21757952 | tf_op jit(solution)/shard_map/dot_general | solution.py:17
  368.3 8.9 %convolution_convert_fusion = bf16[640,4096]{1,0:T(8,128)(2,1)} fusion(bf16[1,768,4096]{2,1,0:T(8,128)(2,1)} %param.15, f32[640,1536]{1,0:T(8,128)S(1)} %fusion.2), kind=kOutput, calls=%fused_computation.16 | convolution fusion | flops 4032102400 | bytes 15466496 | tf_op jit(solution)/shard_map/dot_general | solution.py:21
  377.1 8.9 %reshape.330 = bf16[128,160,128]{2,1,0:T(8,128)(2,1)} reshape(bf16[640,4096]{1,0:T(8,128)(2,1)} %convolution_convert_fusion) | data formatting | bytes 10485760 | tf_op jit(solution)/shard_map/reshape | solution.py:116
  386.0 12.8 %all-to-all-done.1 = bf16[128,128,128]{2,1,0:T(8,128)(2,1)} async-done(((bf16[128,128,128]{2,1,0:T(8,128)(2,1)}), bf16[128,128,128]{2,1,0:T(8,128)(2,1)}, u32[]{:S(2)}, u32[]{:S(2)}) %all-to-all-start.1) | async-done | bytes 4194336 | tf_op jit(solution)/shard_map/all_to_all | solution.py:117
  398.9 8.1 %all-to-all-start.3 = ((bf16[128,160,128]{2,1,0:T(8,128)(2,1)}), bf16[128,160,128]{2,1,0:T(8,128)(2,1)}, u32[]{:S(2)}, u32[]{:S(2)}) async-start(bf16[128,160,128]{2,1,0:T(8,128)(2,1)} %reshape.330), calls=%async_computation.4 | async-start | bytes 10485760 | tf_op jit(solution)/shard_map/all_to_all | solution.py:117
  407.4 12.1 %gather_fusion.3 = bf16[1024,32,128]{2,1,0:T(8,128)(2,1)} fusion(bf16[512,32,128]{2,1,0:T(8,128)(2,1)} %bitcast.28, s32[1024]{0:T(1024)S(1)} %broadcast_clamp_fusion.1), kind=kCustom, calls=%fused_computation.3 | custom fusion | bytes 16781312 | tf_op jit(solution)/shard_map/jit(_take)/gather | solution.py:120
  419.4 6.9 %fusion.1 = f32[128,32,128]{2,1,0:T(8,128)} fusion(f32[128,8]{1,0:T(8,128)S(1)} %get-tuple-element.8, bf16[1024,32,128]{2,1,0:T(8,128)(2,1)} %gather_fusion.3), kind=kLoop, calls=%fused_computation.10 | loop fusion | flops 12058624 | bytes 10489856 | tf_op jit(solution)/shard_map/reduce_sum | solution.py:122
  426.4 45.2 %all-to-all-done.3 = bf16[128,160,128]{2,1,0:T(8,128)(2,1)} async-done(((bf16[128,160,128]{2,1,0:T(8,128)(2,1)}), bf16[128,160,128]{2,1,0:T(8,128)(2,1)}, u32[]{:S(2)}, u32[]{:S(2)}) %all-to-all-start.3) | async-done | bytes 5242912 | tf_op jit(solution)/shard_map/all_to_all | solution.py:117
  471.6 12.3 %gather_fusion.5 = bf16[1024,32,128]{2,1,0:T(8,128)(2,1)} fusion(bf16[640,32,128]{2,1,0:T(8,128)(2,1)} %bitcast.32, s32[1024]{0:T(1024)S(1)} %broadcast_clamp_fusion), kind=kCustom, calls=%fused_computation.5 | custom fusion | bytes 16781312 | tf_op jit(solution)/shard_map/jit(_take)/gather | solution.py:120
  483.9 5.8 %fusion = f32[128,32,128]{2,1,0:T(8,128)S(1)} fusion(f32[128,8]{1,0:T(8,128)S(1)} %get-tuple-element.7, bf16[1024,32,128]{2,1,0:T(8,128)(2,1)} %gather_fusion.5), kind=kLoop, calls=%fused_computation.8 | loop fusion | flops 12058624 | bytes 10489856 | tf_op jit(solution)/shard_map/reduce_sum | solution.py:122
  490.3 0.7 copy-done.2
  491.0 2.8 fusion.18
  (78 shorter events, 6.4 us)
Async XLA Ops:
  7.2 38.5 %all-gather.8.cloned.1.call-start = ((), (), s32[]{:S(2)}) async-start(), calls=%async_computation.6 | async-start | bytes 1310720 | tf_op jit(solution)/shard_map/all_gather | solution.py:46
  18.5 111.2 %all-gather.10.cloned.1.call-start = ((), (), s32[]{:S(2)}) async-start(), calls=%async_computation.7 | async-start | bytes 5242880 | tf_op jit(solution)/shard_map/all_gather | solution.py:47
  45.7 114.4 %reduce-scatter.2.cloned.1.call-start = ((), (), s32[]{:S(2)}) async-start(), calls=%async_computation.5 | async-start | bytes 12582912 | tf_op jit(solution)/shard_map/reduce_scatter | solution.py:68
  45.7 7.2 %collective-permute-start = (bf16[1024,128]{1,0:T(8,128)(2,1)S(1)}, bf16[1024,128]{1,0:T(8,128)(2,1)S(1)}, u32[]{:S(2)}, u32[]{:S(2)}) collective-permute-start(bf16[1024,128]{1,0:T(8,128)(2,1)S(1)} %get-tuple-element.6), channel_id=1, source_target_pairs={{0,96},{32,0},{64,32},{96,64},{1,97},{33,1},{65,33},{97,65},{2,98}... | collective-permute-start | bytes 786440 | tf_op jit(solution)/shard_map/ppermute | solution.py:30
  46.3 7.4 %collective-permute-start.1 = (bf16[1024,128]{1,0:T(8,128)(2,1)S(1)}, bf16[1024,128]{1,0:T(8,128)(2,1)S(1)}, u32[]{:S(2)}, u32[]{:S(2)}) collective-permute-start(bf16[1024,128]{1,0:T(8,128)(2,1)S(1)} %get-tuple-element.6), channel_id=1, source_target_pairs={{0,32},{32,64},{64,96},{96,0},{1,33},{33,65},{65,97},{97,1},{2,34}... | collective-permute-start | bytes 786440 | tf_op jit(solution)/shard_map/ppermute | solution.py:29
  53.1 7.0 %collective-permute-start.3 = (bf16[1024,64]{1,0:T(8,128)(2,1)S(1)}, bf16[1024,64]{1,0:T(8,128)(2,1)S(1)}, u32[]{:S(2)}, u32[]{:S(2)}) collective-permute-start(bf16[1024,64]{1,0:T(8,128)(2,1)S(1)} %slice.73), channel_id=1, source_target_pairs={{0,96},{32,0},{64,32},{96,64},{1,97},{33,1},{65,33},{97,65},{2,98}... | collective-permute-start | bytes 393224 | tf_op jit(solution)/shard_map/ppermute | solution.py:35
  53.7 6.4 %collective-permute-start.2 = (bf16[1024,64]{1,0:T(8,128)(2,1)S(1)}, bf16[1024,64]{1,0:T(8,128)(2,1)S(1)}, u32[]{:S(2)}, u32[]{:S(2)}) collective-permute-start(bf16[1024,64]{1,0:T(8,128)(2,1)S(1)} %bitcast.101), channel_id=1, source_target_pairs={{0,32},{32,64},{64,96},{96,0},{1,33},{33,65},{65,97},{97,1},{2,34}... | collective-permute-start | bytes 393224 | tf_op jit(solution)/shard_map/ppermute | solution.py:34
  62.3 22.9 %collective-permute-start.4 = (bf16[4,1024,128]{2,1,0:T(8,128)(2,1)}, bf16[4,1024,128]{2,1,0:T(8,128)(2,1)S(1)}, u32[]{:S(2)}, u32[]{:S(2)}) collective-permute-start(bf16[4,1024,128]{2,1,0:T(8,128)(2,1)} %broadcast_select_fusion), channel_id=1, source_target_pairs={{0,12},{4,0},{8,4},{12,8},{1,13},{5,1},{9,5},{13,9},{2,14},{6,2},{... | collective-permute-start | bytes 3145736 | tf_op jit(solution)/shard_map/ppermute | solution.py:30
  63.7 25.1 %collective-permute-start.5 = (bf16[4,1024,128]{2,1,0:T(8,128)(2,1)}, bf16[4,1024,128]{2,1,0:T(8,128)(2,1)S(1)}, u32[]{:S(2)}, u32[]{:S(2)}) collective-permute-start(bf16[4,1024,128]{2,1,0:T(8,128)(2,1)} %broadcast_select_fusion), channel_id=1, source_target_pairs={{0,4},{4,8},{8,12},{12,0},{1,5},{5,9},{9,13},{13,1},{2,6},{6,10},{... | collective-permute-start | bytes 3145736 | tf_op jit(solution)/shard_map/ppermute | solution.py:29
  85.2 1.1 copy-start.4
  87.7 10.8 %collective-permute-start.7 = (bf16[4,1024,64]{1,2,0:T(8,128)(2,1)}, bf16[4,1024,64]{1,2,0:T(8,128)(2,1)S(1)}, u32[]{:S(2)}, u32[]{:S(2)}) collective-permute-start(bf16[4,1024,64]{1,2,0:T(8,128)(2,1)} %copy.43), channel_id=1, source_target_pairs={{0,12},{4,0},{8,4},{12,8},{1,13},{5,1},{9,5},{13,9},{2,14},{6,2},{... | collective-permute-start | bytes 1572872 | tf_op jit(solution)/shard_map/ppermute | solution.py:35
  88.8 3.8 copy-start.5
  89.2 11.8 %collective-permute-start.6 = (bf16[4,1024,64]{1,2,0:T(8,128)(2,1)S(1)}, bf16[4,1024,64]{1,2,0:T(8,128)(2,1)}, u32[]{:S(2)}, u32[]{:S(2)}) collective-permute-start(bf16[4,1024,64]{1,2,0:T(8,128)(2,1)S(1)} %copy.42), channel_id=1, source_target_pairs={{0,4},{4,8},{8,12},{12,0},{1,5},{5,9},{9,13},{13,1},{2,6},{6,10},{... | collective-permute-start | bytes 1572872 | tf_op jit(solution)/shard_map/ppermute | solution.py:34
  106.5 5.3 %copy-start.6 = (bf16[2,2,128,1024]{3,2,1,0:T(8,128)(2,1)S(1)}, bf16[2,2,128,1024]{3,2,1,0:T(8,128)(2,1)}, u32[]{:S(2)}) copy-start(bf16[2,2,128,1024]{3,2,1,0:T(8,128)(2,1)} %copy.41) | copy-start | bytes 3145732
  129.6 4.7 copy-start
  138.1 0.7 copy-start.8
  161.8 25.4 %collective-permute-start.8 = (bf16[128,4096]{1,0:T(8,128)(2,1)S(1)}, bf16[128,4096]{1,0:T(8,128)(2,1)S(1)}, u32[]{:S(2)}, u32[]{:S(2)}) collective-permute-start(bf16[128,4096]{1,0:T(8,128)(2,1)S(1)} %fusion.22), channel_id=1, source_target_pairs={{0,2},{2,0},{1,3},{3,1},{4,6},{6,4},{5,7},{7,5},{8,10},{10,8},{9,1... | collective-permute-start | bytes 3145736 | tf_op jit(solution)/shard_map/ppermute | solution.py:73
  191.3 7.1 %copy-start.1 = (bf16[128,4096]{1,0:T(8,128)(2,1)S(1)}, bf16[128,4096]{1,0:T(8,128)(2,1)}, u32[]{:S(2)}) copy-start(bf16[128,4096]{1,0:T(8,128)(2,1)} %param.8) | copy-start | bytes 3145732
  195.4 3.5 copy-start.7
  203.2 62.0 %all-to-all-start = ((bf16[128,128,128]{2,1,0:T(8,128)(2,1)}), bf16[128,128,128]{2,1,0:T(8,128)(2,1)}, u32[]{:S(2)}, u32[]{:S(2)}) async-start(bf16[128,128,128]{2,1,0:T(8,128)(2,1)} %bitcast.87), calls=%async_computation.1 | async-start | bytes 8388608 | tf_op jit(solution)/shard_map/all_to_all | solution.py:114
  265.2 72.7 %all-to-all-start.2 = ((bf16[128,160,128]{2,1,0:T(8,128)(2,1)}), bf16[128,160,128]{2,1,0:T(8,128)(2,1)}, u32[]{:S(2)}, u32[]{:S(2)}) async-start(bf16[128,160,128]{2,1,0:T(8,128)(2,1)} %bitcast.86), calls=%async_computation.3 | async-start | bytes 10485760 | tf_op jit(solution)/shard_map/all_to_all | solution.py:114
  337.9 61.0 %all-to-all-start.1 = ((bf16[128,128,128]{2,1,0:T(8,128)(2,1)}), bf16[128,128,128]{2,1,0:T(8,128)(2,1)}, u32[]{:S(2)}, u32[]{:S(2)}) async-start(bf16[128,128,128]{2,1,0:T(8,128)(2,1)} %reshape.326), calls=%async_computation.2 | async-start | bytes 8388608 | tf_op jit(solution)/shard_map/all_to_all | solution.py:117
  386.0 21.2 %copy-start.9 = (f32[128,8]{0,1:T(8,128)S(1)}, f32[128,8]{0,1:T(8,128)}, u32[]{:S(2)}) copy-start(f32[128,8]{0,1:T(8,128)} %param.13) | copy-start | bytes 12292
  398.9 72.7 %all-to-all-start.3 = ((bf16[128,160,128]{2,1,0:T(8,128)(2,1)}), bf16[128,160,128]{2,1,0:T(8,128)(2,1)}, u32[]{:S(2)}, u32[]{:S(2)}) async-start(bf16[128,160,128]{2,1,0:T(8,128)(2,1)} %reshape.330), calls=%async_computation.4 | async-start | bytes 10485760 | tf_op jit(solution)/shard_map/all_to_all | solution.py:117
  483.9 5.8 %copy-start.3 = (f32[128,32,128]{2,1,0:T(8,128)S(1)}, f32[128,32,128]{2,1,0:T(8,128)}, u32[]{:S(2)}) copy-start(f32[128,32,128]{2,1,0:T(8,128)} %fusion.1) | copy-start | bytes 6291460
  489.8 1.2 copy-start.2
Sparse Core Ops, SparseCore 0:
  18.6 27.0 all-gather.7
  47.3 48.9 all-gather.9
  138.2 21.7 reduce-scatter.1

commit v11 on v10

--- a/solution.py
+++ b/solution.py
@@ -43,12 +43,10 @@
 
 def gather_columns(w_out):
     staged = lax.all_gather(w_out, "xhi", axis=0)
-    first = lax.all_gather(staged[0], "z", axis=1, tiled=True)
-    first = lax.all_gather(first, "y", axis=1, tiled=True)
-    if staged.shape[0] == 1:
-        return first, None
-    second = ring_gather(staged[1], "y")
-    second = ring_gather(second, "z")
+    first = lax.all_gather(staged[0], "y", axis=1, tiled=True)
+    first = lax.all_gather(first, "z", axis=1, tiled=True)
+    second = ring_gather(staged[1], "z")
+    second = ring_gather(second, "y")
     return first, second
 
 
@@ -59,11 +57,8 @@
     context = context.reshape(n_x, n_c, rows, -1).transpose(1, 0, 2, 3).reshape(n_x * n_c * rows, -1)
     first, second = gather_columns(w_out)
     partial_sums = jnp.dot(context, first, preferred_element_type=jnp.float32)
-    if second is not None:
-        other = jnp.einsum("th,zyhl->tyzl", context, second, preferred_element_type=jnp.float32)
-        partial_sums = jnp.concatenate(
-            [partial_sums, other.reshape(other.shape[0], -1)], axis=1
-        )
+    other = jnp.einsum("th,yzhl->tyzl", context, second, preferred_element_type=jnp.float32)
+    partial_sums = jnp.concatenate([partial_sums, other.reshape(other.shape[0], -1)], axis=1)
     width = partial_sums.shape[1]
     chip_sums = lax.psum_scatter(partial_sums, "core", scatter_dimension=0, tiled=True)
     chip_sums = chip_sums.reshape(n_x, rows, width)
@@ -72,9 +67,10 @@
     other = lax.dynamic_index_in_dim(chip_sums, 1 - me, axis=0, keepdims=False)
     arrived = lax.ppermute(other.astype(jnp.bfloat16), "xlo", perm=[(0, 1), (1, 0)])
     summed = own + arrived.astype(jnp.float32)
-    n_y, n_xhi = lax.axis_size("y"), lax.axis_size("xhi")
-    summed = summed.reshape(rows, n_xhi, n_y, -1).transpose(0, 2, 1, 3)
-    return summed.reshape(rows, width)
+    n_y, n_z = lax.axis_size("y"), lax.axis_size("z")
+    first = summed[:, : width // 2].reshape(rows, n_z, n_y, -1).transpose(0, 2, 1, 3)
+    second = summed[:, width // 2 :].reshape(rows, n_y, n_z, -1)
+    return jnp.stack([first, second], axis=2).reshape(rows, width)
 
 
 def on_device(hidden_in, context, w_out, norm_gain, expert_ids, route_weight, w_gate_up, w_down):

time: 503 us -> 496 us (0.986)
  local copies, waits for them, and re-layouts: 109 us -> 98.8 us
    reshape x3, local copies, waits for them, and re-layouts: 9.56 us -> 4.07 us  [the longest x1 2.12 us: project(): return jnp.stack([first, second], axis=2).reshape(rows, width)]
    transpose x1 -> x0, local copies, waits for them, and re-layouts: 5.46 us -> none  [project(): jnp.einsum('th,zyhl->tyzl', context, second, preferred_element_type=jnp.f...]
  transfers between devices with their start and end apart: 16 -> 16, of which waited for: 12 -> 14; matrix products, arithmetic and copies ran while one was open for 28% -> 27% of each run, Pallas kernels for 0% -> 0%
where the time goes in v11:
time: 496 us; the launch traced here: 493 us
  waiting for transfers between devices  242 us (49%)
  local copies, waits for them, and re-layouts  98.8 us (20%)
  matrix products  51.1 us (10%)
  starting transfers between devices  44.6 us (9%)
  other arithmetic  31.9 us (6%)
  between operations  14.2 us (3%)
  blocking collectives  10.4 us (2%)
    all_to_all x2, waiting for transfers between devices, on_device(): lax.all_to_all(send, ALL, split_axis=0, concat_axis=0, tiled=True)  79 us
    all_to_all x2, waiting for transfers between devices, on_device(): lax.all_to_all(outputs, ALL, split_axis=0, concat_axis=0, tiled=True)  58.1 us
    all_gather x1, waiting for transfers between devices, gather_columns(): first = lax.all_gather(staged[0], 'y', axis=1, tiled=True)  27.4 us
    gather x2, local copies, waits for them, and re-layouts, on_device(): picked = jnp.take(returned, chosen * size + slots - lo, axis=0, mode='clip')  24.3 us
    dot_general x2, matrix products, expert_block(): jnp.dot(received, w_gate_up[0], preferred_element_type=jnp.float32)  22.9 us
    ppermute x2, waiting for transfers between devices, ring_gather(): from_right = lax.ppermute(block, axis, perm=minus)  22.7 us
    reduce_scatter x1, waiting for transfers between devices, project(): lax.psum_scatter(partial_sums, 'core', scatter_dimension=0, tiled=True)  20.8 us
    ppermute x1, waiting for transfers between devices, project(): lax.ppermute(other.astype(jnp.bfloat16), 'xlo', perm=[(0, 1), (1, 0)])  18.4 us
  transfers between devices with their start and end apart: 16, of which 14 were waited for; matrix products, arithmetic and copies ran while one was open for 27% of the time, Pallas kernels for 0%

profile of v11, /device:TPU:54, one launch (start us, length us, event | category | flops | bytes accessed | tf_op | source)
XLA Modules:
  0.0 493.4 jit_solution(14860032323693692762)
XLA Ops:
  7.2 10.4 %all-gather = bf16[2048,128]{1,0:T(8,128)(2,1)S(1)} all-gather(bf16[1024,128]{1,0:T(8,128)(2,1)} %param.10), channel_id=2, replica_groups=mesh['y'=4,'xhi'=2,'z'=4,'xlo'=2,'core'=2] {'xhi'}, dimensions={0}, use_global_device_ids=true | all-gather | bytes 786432 | tf_op jit(solution)/shard_map/all_gather | solution.py:45
  17.6 0.8 fusion.46
  18.5 27.4 %all-gather.8.cloned.1.call-done = bf16[1024,512]{1,0:T(8,128)(2,1)} async-done(((bf16[1024,128]{1,0:T(8,128)(2,1)}), bf16[1024,512]{1,0:T(8,128)(2,1)}) %all-gather.8.cloned.1.call-update) | async-done | bytes 1048592 | tf_op jit(solution)/shard_map/all_gather | solution.py:46
  46.6 1.6 collective-permute-start.1
  48.1 5.1 %collective-permute-done = bf16[1024,128]{1,0:T(8,128)(2,1)S(1)} collective-permute-done((bf16[1024,128]{1,0:T(8,128)(2,1)S(1)}, bf16[1024,128]{1,0:T(8,128)(2,1)S(1)}, u32[]{:S(2)}, u32[]{:S(2)}) %collective-permute-start) | collective-permute-done | bytes 262176 | tf_op jit(solution)/shard_map/ppermute | solution.py:30
  53.4 1.0 collective-permute-start.3
  54.7 0.8 collective-permute-start.2
  55.5 4.3 collective-permute-done.3
  59.9 5.8 %collective-permute-done.2 = bf16[1024,64]{1,0:T(8,128)(2,1)S(1)} collective-permute-done((bf16[1024,64]{1,0:T(8,128)(2,1)S(1)}, bf16[1024,64]{1,0:T(8,128)(2,1)S(1)}, u32[]{:S(2)}, u32[]{:S(2)}) %collective-permute-start.2) | collective-permute-done | bytes 131104 | tf_op jit(solution)/shard_map/ppermute | solution.py:34
  66.0 0.7 gather_fusion
  66.7 1.1 broadcast_select_fusion
  67.9 2.0 collective-permute-start.5
  69.9 17.6 %collective-permute-done.4 = bf16[4,1024,128]{2,1,0:T(8,128)(2,1)S(1)} collective-permute-done((bf16[4,1024,128]{2,1,0:T(8,128)(2,1)}, bf16[4,1024,128]{2,1,0:T(8,128)(2,1)S(1)}, u32[]{:S(2)}, u32[]{:S(2)}) %collective-permute-start.4) | collective-permute-done | bytes 1048608 | tf_op jit(solution)/shard_map/ppermute | solution.py:30
  87.5 1.1 copy-done.4
  88.9 1.1 copy.46
  90.1 1.0 collective-permute-start.7
  91.4 1.2 collective-permute-start.6
  92.7 2.3 copy.44
  95.2 4.3 collective-permute-done.7
  99.9 1.0 collective-permute-done.6
  101.0 1.5 copy.47
  102.5 0.6 maximum_bitcast_fusion
  103.1 3.4 pad_maximum_fusion.1
  106.5 5.3 %gather_fusion.1 = bf16[4,4,1024,128]{3,2,1,0:T(8,128)(2,1)} fusion(bf16[4,4,1024,128]{3,2,1,0:T(8,128)(2,1)} %pad_maximum_fusion.1, s32[1024]{0:T(1024)S(1)} %pad_clamp_fusion.2), kind=kCustom, calls=%fused_computation.1 | custom fusion | bytes 8388624 | tf_op jit(solution)/shard_map/jit(_take)/gather | solution.py:41
  111.9 6.7 %fusion.12 = f32[4,4,128,512]{3,2,1,0:T(8,128)} fusion(bf16[512,1024,1,1]{1,0,3,2:T(8,128)(2,1)S(1)} %bitcast.103, bf16[4,4,1024,128]{3,2,1,0:T(8,128)(2,1)} %gather_fusion.1, pred[4]{0:T(512)(128)(4,1)S(1)} %get-tuple-element.20), kind=kOutput, calls=%fused_computation.22 | convolution fusion | flops 2149580800 | bytes 9437188 | tf_op jit(solution)/shard_map/th,yzhl->tyzl/dot_general | solution.py:60
  118.6 5.4 %copy.64 = f32[512,2048]{1,0:T(8,128)} copy(f32[512,2048]{0,1:T(8,128)} %bitcast.94) | data formatting | bytes 8388608 | tf_op jit(solution)/shard_map/reshape | solution.py:61
  124.0 4.7 fusion.47
  128.7 3.8 pad_maximum_fusion
  132.5 0.7 copy-done.8
  133.8 20.8 %reduce-scatter.2.cloned.1.call-done = f32[256,4096]{1,0:T(8,128)} async-done(((f32[512,4096]{1,0:T(8,128)}), f32[256,4096]{1,0:T(8,128)}) %reduce-scatter.2.cloned.1.call-update) | async-done | bytes 4194320 | tf_op jit(solution)/shard_map/reduce_scatter | solution.py:63
  154.6 1.7 fusion.19
  156.3 0.9 collective-permute-start.8
  158.4 4.5 scatter_custom_fusion
  163.3 18.4 %collective-permute-done.8 = bf16[128,4096]{1,0:T(8,128)(2,1)S(1)} collective-permute-done((bf16[128,4096]{1,0:T(8,128)(2,1)S(1)}, bf16[128,4096]{1,0:T(8,128)(2,1)S(1)}, u32[]{:S(2)}, u32[]{:S(2)}) %collective-permute-start.8) | collective-permute-done | bytes 1048608 | tf_op jit(solution)/shard_map/ppermute | solution.py:68
  181.7 1.8 bitcast_add_fusion.1
  183.6 0.7 reshape.319
  184.4 1.2 copy.69
  185.6 0.7 stack_reshape.3
  186.3 3.2 pad_maximum_fusion.2
  189.5 2.1 reshape.320
  192.9 3.5 gather_fusion.2
  196.4 10.1 %all-to-all-start = ((bf16[128,128,128]{2,1,0:T(8,128)(2,1)}), bf16[128,128,128]{2,1,0:T(8,128)(2,1)}, u32[]{:S(2)}, u32[]{:S(2)}) async-start(bf16[128,128,128]{2,1,0:T(8,128)(2,1)} %bitcast.91), calls=%async_computation.1 | async-start | bytes 8388608 | tf_op jit(solution)/shard_map/all_to_all | solution.py:110
  206.7 4.1 gather_fusion.4
  210.9 47.5 %all-to-all-done = bf16[128,128,128]{2,1,0:T(8,128)(2,1)} async-done(((bf16[128,128,128]{2,1,0:T(8,128)(2,1)}), bf16[128,128,128]{2,1,0:T(8,128)(2,1)}, u32[]{:S(2)}, u32[]{:S(2)}) %all-to-all-start) | async-done | bytes 4194336 | tf_op jit(solution)/shard_map/all_to_all | solution.py:110
  258.4 8.1 %all-to-all-start.2 = ((bf16[128,160,128]{2,1,0:T(8,128)(2,1)}), bf16[128,160,128]{2,1,0:T(8,128)(2,1)}, u32[]{:S(2)}, u32[]{:S(2)}) async-start(bf16[128,160,128]{2,1,0:T(8,128)(2,1)} %bitcast.90), calls=%async_computation.3 | async-start | bytes 10485760 | tf_op jit(solution)/shard_map/all_to_all | solution.py:110
  266.5 7.3 %reshape.325 = bf16[512,4096]{1,0:T(8,128)(2,1)} reshape(bf16[128,128,128]{2,1,0:T(8,128)(2,1)} %all-to-all-done) | data formatting | bytes 8388608 | tf_op jit(solution)/shard_map/reshape | solution.py:111
  273.8 10.5 %fusion.4 = f32[512,1536]{1,0:T(8,128)S(1)} fusion(bf16[512,4096]{1,0:T(8,128)(2,1)} %reshape.325, bf16[1,4096,1536]{2,1,0:T(8,128)(2,1)} %param.14), kind=kOutput, calls=%fused_computation.13 | convolution fusion | flops 6442450944 | bytes 19922944 | tf_op jit(solution)/shard_map/dot_general | solution.py:17
  284.3 7.9 %fusion.9 = bf16[512,4096]{1,0:T(8,128)(2,1)} fusion(bf16[1,768,4096]{2,1,0:T(8,128)(2,1)} %param.15, f32[512,1536]{1,0:T(8,128)S(1)} %fusion.4), kind=kOutput, calls=%fused_computation.20 | convolution fusion | flops 3225681920 | bytes 13631488 | tf_op jit(solution)/shard_map/dot_general | solution.py:21
  292.2 7.4 %reshape.326 = bf16[128,128,128]{2,1,0:T(8,128)(2,1)} reshape(bf16[512,4096]{1,0:T(8,128)(2,1)} %fusion.9) | data formatting | bytes 8388608 | tf_op jit(solution)/shard_map/reshape | solution.py:112
  299.6 31.5 %all-to-all-done.2 = bf16[128,160,128]{2,1,0:T(8,128)(2,1)} async-done(((bf16[128,160,128]{2,1,0:T(8,128)(2,1)}), bf16[128,160,128]{2,1,0:T(8,128)(2,1)}, u32[]{:S(2)}, u32[]{:S(2)}) %all-to-all-start.2) | async-done | bytes 5242912 | tf_op jit(solution)/shard_map/all_to_all | solution.py:110
  331.1 9.0 %all-to-all-start.1 = ((bf16[128,128,128]{2,1,0:T(8,128)(2,1)}), bf16[128,128,128]{2,1,0:T(8,128)(2,1)}, u32[]{:S(2)}, u32[]{:S(2)}) async-start(bf16[128,128,128]{2,1,0:T(8,128)(2,1)} %reshape.326), calls=%async_computation.2 | async-start | bytes 8388608 | tf_op jit(solution)/shard_map/all_to_all | solution.py:113
  340.1 8.9 %reshape.329 = bf16[640,4096]{1,0:T(8,128)(2,1)} reshape(bf16[128,160,128]{2,1,0:T(8,128)(2,1)} %all-to-all-done.2) | data formatting | bytes 10485760 | tf_op jit(solution)/shard_map/reshape | solution.py:111
  349.0 12.4 %fusion.2 = f32[640,1536]{1,0:T(8,128)S(1)} fusion(bf16[640,4096]{1,0:T(8,128)(2,1)} %reshape.329, bf16[1,4096,1536]{2,1,0:T(8,128)(2,1)} %param.14), kind=kOutput, calls=%fused_computation.11 | convolution fusion | flops 8053063680 | bytes 21757952 | tf_op jit(solution)/shard_map/dot_general | solution.py:17
  361.4 8.9 %convolution_convert_fusion = bf16[640,4096]{1,0:T(8,128)(2,1)} fusion(bf16[1,768,4096]{2,1,0:T(8,128)(2,1)} %param.15, f32[640,1536]{1,0:T(8,128)S(1)} %fusion.2), kind=kOutput, calls=%fused_computation.16 | convolution fusion | flops 4032102400 | bytes 15466496 | tf_op jit(solution)/shard_map/dot_general | solution.py:21
  370.3 8.9 %reshape.330 = bf16[128,160,128]{2,1,0:T(8,128)(2,1)} reshape(bf16[640,4096]{1,0:T(8,128)(2,1)} %convolution_convert_fusion) | data formatting | bytes 10485760 | tf_op jit(solution)/shard_map/reshape | solution.py:112
  379.2 12.9 %all-to-all-done.1 = bf16[128,128,128]{2,1,0:T(8,128)(2,1)} async-done(((bf16[128,128,128]{2,1,0:T(8,128)(2,1)}), bf16[128,128,128]{2,1,0:T(8,128)(2,1)}, u32[]{:S(2)}, u32[]{:S(2)}) %all-to-all-start.1) | async-done | bytes 4194336 | tf_op jit(solution)/shard_map/all_to_all | solution.py:113
  392.1 8.1 %all-to-all-start.3 = ((bf16[128,160,128]{2,1,0:T(8,128)(2,1)}), bf16[128,160,128]{2,1,0:T(8,128)(2,1)}, u32[]{:S(2)}, u32[]{:S(2)}) async-start(bf16[128,160,128]{2,1,0:T(8,128)(2,1)} %reshape.330), calls=%async_computation.4 | async-start | bytes 10485760 | tf_op jit(solution)/shard_map/all_to_all | solution.py:113
  400.5 12.0 %gather_fusion.3 = bf16[1024,32,128]{2,1,0:T(8,128)(2,1)} fusion(bf16[512,32,128]{2,1,0:T(8,128)(2,1)} %bitcast.31, s32[1024]{0:T(1024)S(1)} %broadcast_clamp_fusion.1), kind=kCustom, calls=%fused_computation.3 | custom fusion | bytes 16781312 | tf_op jit(solution)/shard_map/jit(_take)/gather | solution.py:116
  412.6 6.9 %fusion.1 = f32[128,32,128]{2,1,0:T(8,128)} fusion(f32[128,8]{1,0:T(8,128)S(1)} %get-tuple-element.10, bf16[1024,32,128]{2,1,0:T(8,128)(2,1)} %gather_fusion.3), kind=kLoop, calls=%fused_computation.10 | loop fusion | flops 12058624 | bytes 10489856 | tf_op jit(solution)/shard_map/reduce_sum | solution.py:118
  419.5 45.3 %all-to-all-done.3 = bf16[128,160,128]{2,1,0:T(8,128)(2,1)} async-done(((bf16[128,160,128]{2,1,0:T(8,128)(2,1)}), bf16[128,160,128]{2,1,0:T(8,128)(2,1)}, u32[]{:S(2)}, u32[]{:S(2)}) %all-to-all-start.3) | async-done | bytes 5242912 | tf_op jit(solution)/shard_map/all_to_all | solution.py:113
  464.8 12.3 %gather_fusion.5 = bf16[1024,32,128]{2,1,0:T(8,128)(2,1)} fusion(bf16[640,32,128]{2,1,0:T(8,128)(2,1)} %bitcast.35, s32[1024]{0:T(1024)S(1)} %broadcast_clamp_fusion), kind=kCustom, calls=%fused_computation.5 | custom fusion | bytes 16781312 | tf_op jit(solution)/shard_map/jit(_take)/gather | solution.py:116
  477.1 5.8 %fusion = f32[128,32,128]{2,1,0:T(8,128)S(1)} fusion(f32[128,8]{1,0:T(8,128)S(1)} %get-tuple-element.9, bf16[1024,32,128]{2,1,0:T(8,128)(2,1)} %gather_fusion.5), kind=kLoop, calls=%fused_computation.8 | loop fusion | flops 12058624 | bytes 10489856 | tf_op jit(solution)/shard_map/reduce_sum | solution.py:118
  483.4 0.7 copy-done.2
  484.1 2.8 fusion.15
  (80 shorter events, 7.3 us)
Async XLA Ops:
  7.2 38.8 %all-gather.8.cloned.1.call-start = ((), (), s32[]{:S(2)}) async-start(), calls=%async_computation.6 | async-start | bytes 1310720 | tf_op jit(solution)/shard_map/all_gather | solution.py:46
  18.5 105.5 %all-gather.10.cloned.1.call-start = ((), (), s32[]{:S(2)}) async-start(), calls=%async_computation.7 | async-start | bytes 5242880 | tf_op jit(solution)/shard_map/all_gather | solution.py:47
  46.0 108.6 %reduce-scatter.2.cloned.1.call-start = ((), (), s32[]{:S(2)}) async-start(), calls=%async_computation.5 | async-start | bytes 12582912 | tf_op jit(solution)/shard_map/reduce_scatter | solution.py:63
  46.0 7.2 %collective-permute-start = (bf16[1024,128]{1,0:T(8,128)(2,1)S(1)}, bf16[1024,128]{1,0:T(8,128)(2,1)S(1)}, u32[]{:S(2)}, u32[]{:S(2)}) collective-permute-start(bf16[1024,128]{1,0:T(8,128)(2,1)S(1)} %get-tuple-element.8), channel_id=1, source_target_pairs={{0,12},{4,0},{8,4},{12,8},{1,13},{5,1},{9,5},{13,9},{2,14},{6,2},{... | collective-permute-start | bytes 786440 | tf_op jit(solution)/shard_map/ppermute | solution.py:30
  46.6 8.1 %collective-permute-start.1 = (bf16[1024,128]{1,0:T(8,128)(2,1)S(1)}, bf16[1024,128]{1,0:T(8,128)(2,1)S(1)}, u32[]{:S(2)}, u32[]{:S(2)}) collective-permute-start(bf16[1024,128]{1,0:T(8,128)(2,1)S(1)} %get-tuple-element.8), channel_id=1, source_target_pairs={{0,4},{4,8},{8,12},{12,0},{1,5},{5,9},{9,13},{13,1},{2,6},{6,10},{... | collective-permute-start | bytes 786440 | tf_op jit(solution)/shard_map/ppermute | solution.py:29
  53.4 6.4 %collective-permute-start.3 = (bf16[1024,64]{1,0:T(8,128)(2,1)S(1)}, bf16[1024,64]{1,0:T(8,128)(2,1)S(1)}, u32[]{:S(2)}, u32[]{:S(2)}) collective-permute-start(bf16[1024,64]{1,0:T(8,128)(2,1)S(1)} %slice.81), channel_id=1, source_target_pairs={{0,12},{4,0},{8,4},{12,8},{1,13},{5,1},{9,5},{13,9},{2,14},{6,2},{... | collective-permute-start | bytes 393224 | tf_op jit(solution)/shard_map/ppermute | solution.py:35
  54.7 11.0 %collective-permute-start.2 = (bf16[1024,64]{1,0:T(8,128)(2,1)S(1)}, bf16[1024,64]{1,0:T(8,128)(2,1)S(1)}, u32[]{:S(2)}, u32[]{:S(2)}) collective-permute-start(bf16[1024,64]{1,0:T(8,128)(2,1)S(1)} %bitcast.107), channel_id=1, source_target_pairs={{0,4},{4,8},{8,12},{12,0},{1,5},{5,9},{9,13},{13,1},{2,6},{6,10},{... | collective-permute-start | bytes 393224 | tf_op jit(solution)/shard_map/ppermute | solution.py:34
  67.9 19.6 %collective-permute-start.4 = (bf16[4,1024,128]{2,1,0:T(8,128)(2,1)}, bf16[4,1024,128]{2,1,0:T(8,128)(2,1)S(1)}, u32[]{:S(2)}, u32[]{:S(2)}) collective-permute-start(bf16[4,1024,128]{2,1,0:T(8,128)(2,1)} %broadcast_select_fusion), channel_id=1, source_target_pairs={{0,96},{32,0},{64,32},{96,64},{1,97},{33,1},{65,33},{97,65},{2,98}... | collective-permute-start | bytes 3145736 | tf_op jit(solution)/shard_map/ppermute | solution.py:30
  67.9 23.2 %collective-permute-start.5 = (bf16[4,1024,128]{2,1,0:T(8,128)(2,1)}, bf16[4,1024,128]{2,1,0:T(8,128)(2,1)S(1)}, u32[]{:S(2)}, u32[]{:S(2)}) collective-permute-start(bf16[4,1024,128]{2,1,0:T(8,128)(2,1)} %broadcast_select_fusion), channel_id=1, source_target_pairs={{0,32},{32,64},{64,96},{96,0},{1,33},{33,65},{65,97},{97,1},{2,34}... | collective-permute-start | bytes 3145736 | tf_op jit(solution)/shard_map/ppermute | solution.py:29
  87.5 1.1 copy-start.4
  90.1 9.4 %collective-permute-start.7 = (bf16[4,1024,64]{1,2,0:T(8,128)(2,1)}, bf16[4,1024,64]{1,2,0:T(8,128)(2,1)S(1)}, u32[]{:S(2)}, u32[]{:S(2)}) collective-permute-start(bf16[4,1024,64]{1,2,0:T(8,128)(2,1)} %copy.46), channel_id=1, source_target_pairs={{0,96},{32,0},{64,32},{96,64},{1,97},{33,1},{65,33},{97,65},{2,98}... | collective-permute-start | bytes 1572872 | tf_op jit(solution)/shard_map/ppermute | solution.py:35
  91.1 3.9 copy-start.5
  91.4 9.5 %collective-permute-start.6 = (bf16[4,1024,64]{1,2,0:T(8,128)(2,1)S(1)}, bf16[4,1024,64]{1,2,0:T(8,128)(2,1)}, u32[]{:S(2)}, u32[]{:S(2)}) collective-permute-start(bf16[4,1024,64]{1,2,0:T(8,128)(2,1)S(1)} %copy.45), channel_id=1, source_target_pairs={{0,32},{32,64},{64,96},{96,0},{1,33},{33,65},{65,97},{97,1},{2,34}... | collective-permute-start | bytes 1572872 | tf_op jit(solution)/shard_map/ppermute | solution.py:34
  106.5 5.3 %copy-start.6 = (bf16[2,2,128,1024]{3,2,1,0:T(8,128)(2,1)S(1)}, bf16[2,2,128,1024]{3,2,1,0:T(8,128)(2,1)}, u32[]{:S(2)}) copy-start(bf16[2,2,128,1024]{3,2,1,0:T(8,128)(2,1)} %copy.44) | copy-start | bytes 3145732
  124.0 4.7 copy-start
  132.5 0.7 copy-start.8
  156.3 25.4 %collective-permute-start.8 = (bf16[128,4096]{1,0:T(8,128)(2,1)S(1)}, bf16[128,4096]{1,0:T(8,128)(2,1)S(1)}, u32[]{:S(2)}, u32[]{:S(2)}) collective-permute-start(bf16[128,4096]{1,0:T(8,128)(2,1)S(1)} %fusion.19), channel_id=1, source_target_pairs={{0,2},{2,0},{1,3},{3,1},{4,6},{6,4},{5,7},{7,5},{8,10},{10,8},{9,1... | collective-permute-start | bytes 3145736 | tf_op jit(solution)/shard_map/ppermute | solution.py:68
  186.3 5.3 %copy-start.1 = (bf16[128,4096]{1,0:T(8,128)(2,1)S(1)}, bf16[128,4096]{1,0:T(8,128)(2,1)}, u32[]{:S(2)}) copy-start(bf16[128,4096]{1,0:T(8,128)(2,1)} %param.8) | copy-start | bytes 3145732
  189.5 2.5 copy-start.7
  196.4 62.0 %all-to-all-start = ((bf16[128,128,128]{2,1,0:T(8,128)(2,1)}), bf16[128,128,128]{2,1,0:T(8,128)(2,1)}, u32[]{:S(2)}, u32[]{:S(2)}) async-start(bf16[128,128,128]{2,1,0:T(8,128)(2,1)} %bitcast.91), calls=%async_computation.1 | async-start | bytes 8388608 | tf_op jit(solution)/shard_map/all_to_all | solution.py:110
  258.4 72.7 %all-to-all-start.2 = ((bf16[128,160,128]{2,1,0:T(8,128)(2,1)}), bf16[128,160,128]{2,1,0:T(8,128)(2,1)}, u32[]{:S(2)}, u32[]{:S(2)}) async-start(bf16[128,160,128]{2,1,0:T(8,128)(2,1)} %bitcast.90), calls=%async_computation.3 | async-start | bytes 10485760 | tf_op jit(solution)/shard_map/all_to_all | solution.py:110
  331.1 61.0 %all-to-all-start.1 = ((bf16[128,128,128]{2,1,0:T(8,128)(2,1)}), bf16[128,128,128]{2,1,0:T(8,128)(2,1)}, u32[]{:S(2)}, u32[]{:S(2)}) async-start(bf16[128,128,128]{2,1,0:T(8,128)(2,1)} %reshape.326), calls=%async_computation.2 | async-start | bytes 8388608 | tf_op jit(solution)/shard_map/all_to_all | solution.py:113
  379.2 21.2 %copy-start.9 = (f32[128,8]{0,1:T(8,128)S(1)}, f32[128,8]{0,1:T(8,128)}, u32[]{:S(2)}) copy-start(f32[128,8]{0,1:T(8,128)} %param.13) | copy-start | bytes 12292
  392.1 72.7 %all-to-all-start.3 = ((bf16[128,160,128]{2,1,0:T(8,128)(2,1)}), bf16[128,160,128]{2,1,0:T(8,128)(2,1)}, u32[]{:S(2)}, u32[]{:S(2)}) async-start(bf16[128,160,128]{2,1,0:T(8,128)(2,1)} %reshape.330), calls=%async_computation.4 | async-start | bytes 10485760 | tf_op jit(solution)/shard_map/all_to_all | solution.py:113
  477.1 5.8 %copy-start.3 = (f32[128,32,128]{2,1,0:T(8,128)S(1)}, f32[128,32,128]{2,1,0:T(8,128)}, u32[]{:S(2)}) copy-start(f32[128,32,128]{2,1,0:T(8,128)} %fusion.1) | copy-start | bytes 6291460
  482.9 1.2 copy-start.2
Sparse Core Ops, SparseCore 0:
  18.6 27.3 all-gather.7
  47.6 48.9 all-gather.9
  132.6 21.9 reduce-scatter.1

commit v12 on v11

--- a/solution.py
+++ b/solution.py
@@ -57,8 +57,9 @@
     context = context.reshape(n_x, n_c, rows, -1).transpose(1, 0, 2, 3).reshape(n_x * n_c * rows, -1)
     first, second = gather_columns(w_out)
     partial_sums = jnp.dot(context, first, preferred_element_type=jnp.float32)
-    other = jnp.einsum("th,yzhl->tyzl", context, second, preferred_element_type=jnp.float32)
-    partial_sums = jnp.concatenate([partial_sums, other.reshape(other.shape[0], -1)], axis=1)
+    second = second.transpose(2, 0, 1, 3).reshape(second.shape[2], -1)
+    other = jnp.dot(context, second, preferred_element_type=jnp.float32)
+    partial_sums = jnp.concatenate([partial_sums, other], axis=1)
     width = partial_sums.shape[1]
     chip_sums = lax.psum_scatter(partial_sums, "core", scatter_dimension=0, tiled=True)
     chip_sums = chip_sums.reshape(n_x, rows, width)

time: 496 us -> 502 us (1.012)
    select_n x0 -> x1, local copies, waits for them, and re-layouts: none -> 6.4 us  [ring_gather(): return jnp.take(by_step, order, axis=0)]
    reshape x1 -> x0, local copies, waits for them, and re-layouts: 5.41 us -> none  [project(): other.reshape(other.shape[0], -1)]
  transfers between devices with their start and end apart: 16 -> 16, of which waited for: 14 -> 14; matrix products, arithmetic and copies ran while one was open for 27% -> 28% of each run, Pallas kernels for 0% -> 0%
where the time goes in v12:
time: 502 us; the launch traced here: 499 us
  waiting for transfers between devices  242 us (48%)
  local copies, waits for them, and re-layouts  99.7 us (20%)
  matrix products  50.9 us (10%)
  starting transfers between devices  44.6 us (9%)
  other arithmetic  36.5 us (7%)
  between operations  14.2 us (3%)
  blocking collectives  10.4 us (2%)
    all_to_all x2, waiting for transfers between devices, on_device(): lax.all_to_all(send, ALL, split_axis=0, concat_axis=0, tiled=True)  79 us
    all_to_all x2, waiting for transfers between devices, on_device(): lax.all_to_all(outputs, ALL, split_axis=0, concat_axis=0, tiled=True)  58.1 us
    all_gather x1, waiting for transfers between devices, gather_columns(): first = lax.all_gather(staged[0], 'y', axis=1, tiled=True)  27.4 us
    gather x2, local copies, waits for them, and re-layouts, on_device(): picked = jnp.take(returned, chosen * size + slots - lo, axis=0, mode='clip')  24.3 us
    dot_general x2, matrix products, expert_block(): jnp.dot(received, w_gate_up[0], preferred_element_type=jnp.float32)  22.9 us
    ppermute x2, waiting for transfers between devices, ring_gather(): from_right = lax.ppermute(block, axis, perm=minus)  22.8 us
    reduce_scatter x1, waiting for transfers between devices, project(): lax.psum_scatter(partial_sums, 'core', scatter_dimension=0, tiled=True)  20.8 us
    ppermute x1, waiting for transfers between devices, project(): lax.ppermute(other.astype(jnp.bfloat16), 'xlo', perm=[(0, 1), (1, 0)])  18.4 us
  transfers between devices with their start and end apart: 16, of which 14 were waited for; matrix products, arithmetic and copies ran while one was open for 28% of the time, Pallas kernels for 0%

profile of v12, /device:TPU:54, one launch (start us, length us, event | category | flops | bytes accessed | tf_op | source)
XLA Modules:
  0.0 498.8 jit_solution(7991283262463616799)
XLA Ops:
  7.2 10.4 %all-gather = bf16[2048,128]{1,0:T(8,128)(2,1)S(1)} all-gather(bf16[1024,128]{1,0:T(8,128)(2,1)} %param.10), channel_id=2, replica_groups=mesh['y'=4,'xhi'=2,'z'=4,'xlo'=2,'core'=2] {'xhi'}, dimensions={0}, use_global_device_ids=true | all-gather | bytes 786432 | tf_op jit(solution)/shard_map/all_gather | solution.py:45
  17.6 0.8 fusion.41
  18.5 27.4 %all-gather.8.cloned.1.call-done = bf16[1024,512]{1,0:T(8,128)(2,1)} async-done(((bf16[1024,128]{1,0:T(8,128)(2,1)}), bf16[1024,512]{1,0:T(8,128)(2,1)}) %all-gather.8.cloned.1.call-update) | async-done | bytes 1048592 | tf_op jit(solution)/shard_map/all_gather | solution.py:46
  46.6 1.6 collective-permute-start.1
  48.1 5.1 %collective-permute-done = bf16[1024,128]{1,0:T(8,128)(2,1)S(1)} collective-permute-done((bf16[1024,128]{1,0:T(8,128)(2,1)S(1)}, bf16[1024,128]{1,0:T(8,128)(2,1)S(1)}, u32[]{:S(2)}, u32[]{:S(2)}) %collective-permute-start) | collective-permute-done | bytes 262176 | tf_op jit(solution)/shard_map/ppermute | solution.py:30
  53.4 1.0 collective-permute-start.3
  54.7 0.8 collective-permute-start.2
  55.5 4.3 collective-permute-done.3
  59.9 5.8 %collective-permute-done.2 = bf16[1024,64]{1,0:T(8,128)(2,1)S(1)} collective-permute-done((bf16[1024,64]{1,0:T(8,128)(2,1)S(1)}, bf16[1024,64]{1,0:T(8,128)(2,1)S(1)}, u32[]{:S(2)}, u32[]{:S(2)}) %collective-permute-start.2) | collective-permute-done | bytes 131104 | tf_op jit(solution)/shard_map/ppermute | solution.py:34
  66.0 0.7 gather_fusion
  66.7 1.1 broadcast_select_fusion
  67.9 2.0 collective-permute-start.5
  69.9 17.7 %collective-permute-done.4 = bf16[4,1024,128]{2,1,0:T(8,128)(2,1)S(1)} collective-permute-done((bf16[4,1024,128]{2,1,0:T(8,128)(2,1)}, bf16[4,1024,128]{2,1,0:T(8,128)(2,1)S(1)}, u32[]{:S(2)}, u32[]{:S(2)}) %collective-permute-start.4) | collective-permute-done | bytes 1048608 | tf_op jit(solution)/shard_map/ppermute | solution.py:30
  87.6 1.0 copy-done.4
  88.9 1.1 copy.43
  90.1 1.0 collective-permute-start.7
  91.4 1.2 collective-permute-start.6
  92.7 2.3 copy.41
  95.2 4.3 collective-permute-done.7
  99.9 1.0 collective-permute-done.6
  101.0 1.5 copy.44
  103.1 3.4 pad_maximum_fusion.1
  106.5 5.2 %gather_fusion.1 = bf16[4,4,1024,128]{3,2,1,0:T(8,128)(2,1)} fusion(bf16[4,4,1024,128]{3,2,1,0:T(8,128)(2,1)} %pad_maximum_fusion.1, s32[1024]{0:T(1024)S(1)} %pad_clamp_fusion.2), kind=kCustom, calls=%fused_computation.1 | custom fusion | bytes 8388624 | tf_op jit(solution)/shard_map/jit(_take)/gather | solution.py:41
  111.8 4.6 select_bitcast_fusion
  116.4 6.4 %copy.46 = bf16[1024,4,4,128]{0,3,2,1:T(8,128)(2,1)} copy(bf16[1024,4,4,128]{3,0,2,1:T(8,128)(2,1)} %select_bitcast_fusion) | data formatting | bytes 8388608 | tf_op jit(solution)/shard_map/jit(_take)/select_n | solution.py:41
  122.8 6.5 %convolution_bitcast_fusion = f32[512,2048]{1,0:T(8,128)} fusion(bf16[1024,2048]{0,1:T(8,128)(2,1)} %bitcast.93, bf16[512,1024]{1,0:T(8,128)(2,1)S(1)} %bitcast.102), kind=kOutput, calls=%fused_computation.23 | convolution fusion | flops 2147483648 | bytes 9437184 | tf_op jit(solution)/shard_map/dot_general | solution.py:61
  129.3 4.7 fusion.42
  134.0 3.8 pad_maximum_fusion
  137.8 0.7 copy-done.8
  139.1 20.8 %reduce-scatter.2.cloned.1.call-done = f32[256,4096]{1,0:T(8,128)} async-done(((f32[512,4096]{1,0:T(8,128)}), f32[256,4096]{1,0:T(8,128)}) %reduce-scatter.2.cloned.1.call-update) | async-done | bytes 4194320 | tf_op jit(solution)/shard_map/reduce_scatter | solution.py:64
  159.9 1.7 fusion.15
  161.7 0.9 collective-permute-start.8
  163.7 4.5 scatter_custom_fusion
  168.6 18.4 %collective-permute-done.8 = bf16[128,4096]{1,0:T(8,128)(2,1)S(1)} collective-permute-done((bf16[128,4096]{1,0:T(8,128)(2,1)S(1)}, bf16[128,4096]{1,0:T(8,128)(2,1)S(1)}, u32[]{:S(2)}, u32[]{:S(2)}) %collective-permute-start.8) | collective-permute-done | bytes 1048608 | tf_op jit(solution)/shard_map/ppermute | solution.py:69
  187.0 1.8 bitcast_add_fusion.1
  188.9 0.7 reshape.319
  189.7 1.2 copy.64
  190.9 0.7 stack_reshape.3
  191.6 3.2 pad_maximum_fusion.2
  194.8 2.1 reshape.320
  198.2 3.5 gather_fusion.2
  201.7 10.1 %all-to-all-start = ((bf16[128,128,128]{2,1,0:T(8,128)(2,1)}), bf16[128,128,128]{2,1,0:T(8,128)(2,1)}, u32[]{:S(2)}, u32[]{:S(2)}) async-start(bf16[128,128,128]{2,1,0:T(8,128)(2,1)} %bitcast.90), calls=%async_computation.1 | async-start | bytes 8388608 | tf_op jit(solution)/shard_map/all_to_all | solution.py:111
  212.1 4.1 gather_fusion.4
  216.2 47.5 %all-to-all-done = bf16[128,128,128]{2,1,0:T(8,128)(2,1)} async-done(((bf16[128,128,128]{2,1,0:T(8,128)(2,1)}), bf16[128,128,128]{2,1,0:T(8,128)(2,1)}, u32[]{:S(2)}, u32[]{:S(2)}) %all-to-all-start) | async-done | bytes 4194336 | tf_op jit(solution)/shard_map/all_to_all | solution.py:111
  263.7 8.1 %all-to-all-start.2 = ((bf16[128,160,128]{2,1,0:T(8,128)(2,1)}), bf16[128,160,128]{2,1,0:T(8,128)(2,1)}, u32[]{:S(2)}, u32[]{:S(2)}) async-start(bf16[128,160,128]{2,1,0:T(8,128)(2,1)} %bitcast.89), calls=%async_computation.3 | async-start | bytes 10485760 | tf_op jit(solution)/shard_map/all_to_all | solution.py:111
  271.8 7.3 %reshape.325 = bf16[512,4096]{1,0:T(8,128)(2,1)} reshape(bf16[128,128,128]{2,1,0:T(8,128)(2,1)} %all-to-all-done) | data formatting | bytes 8388608 | tf_op jit(solution)/shard_map/reshape | solution.py:112
  279.1 10.5 %fusion.4 = f32[512,1536]{1,0:T(8,128)S(1)} fusion(bf16[512,4096]{1,0:T(8,128)(2,1)} %reshape.325, bf16[1,4096,1536]{2,1,0:T(8,128)(2,1)} %param.14), kind=kOutput, calls=%fused_computation.13 | convolution fusion | flops 6442450944 | bytes 19922944 | tf_op jit(solution)/shard_map/dot_general | solution.py:17
  289.7 7.9 %fusion.9 = bf16[512,4096]{1,0:T(8,128)(2,1)} fusion(bf16[1,768,4096]{2,1,0:T(8,128)(2,1)} %param.15, f32[512,1536]{1,0:T(8,128)S(1)} %fusion.4), kind=kOutput, calls=%fused_computation.20 | convolution fusion | flops 3225681920 | bytes 13631488 | tf_op jit(solution)/shard_map/dot_general | solution.py:21
  297.6 7.4 %reshape.326 = bf16[128,128,128]{2,1,0:T(8,128)(2,1)} reshape(bf16[512,4096]{1,0:T(8,128)(2,1)} %fusion.9) | data formatting | bytes 8388608 | tf_op jit(solution)/shard_map/reshape | solution.py:113
  304.9 31.5 %all-to-all-done.2 = bf16[128,160,128]{2,1,0:T(8,128)(2,1)} async-done(((bf16[128,160,128]{2,1,0:T(8,128)(2,1)}), bf16[128,160,128]{2,1,0:T(8,128)(2,1)}, u32[]{:S(2)}, u32[]{:S(2)}) %all-to-all-start.2) | async-done | bytes 5242912 | tf_op jit(solution)/shard_map/all_to_all | solution.py:111
  336.4 9.0 %all-to-all-start.1 = ((bf16[128,128,128]{2,1,0:T(8,128)(2,1)}), bf16[128,128,128]{2,1,0:T(8,128)(2,1)}, u32[]{:S(2)}, u32[]{:S(2)}) async-start(bf16[128,128,128]{2,1,0:T(8,128)(2,1)} %reshape.326), calls=%async_computation.2 | async-start | bytes 8388608 | tf_op jit(solution)/shard_map/all_to_all | solution.py:114
  345.5 8.9 %reshape.329 = bf16[640,4096]{1,0:T(8,128)(2,1)} reshape(bf16[128,160,128]{2,1,0:T(8,128)(2,1)} %all-to-all-done.2) | data formatting | bytes 10485760 | tf_op jit(solution)/shard_map/reshape | solution.py:112
  354.3 12.4 %fusion.2 = f32[640,1536]{1,0:T(8,128)S(1)} fusion(bf16[640,4096]{1,0:T(8,128)(2,1)} %reshape.329, bf16[1,4096,1536]{2,1,0:T(8,128)(2,1)} %param.14), kind=kOutput, calls=%fused_computation.11 | convolution fusion | flops 8053063680 | bytes 21757952 | tf_op jit(solution)/shard_map/dot_general | solution.py:17
  366.7 8.9 %convolution_convert_fusion = bf16[640,4096]{1,0:T(8,128)(2,1)} fusion(bf16[1,768,4096]{2,1,0:T(8,128)(2,1)} %param.15, f32[640,1536]{1,0:T(8,128)S(1)} %fusion.2), kind=kOutput, calls=%fused_computation.16 | convolution fusion | flops 4032102400 | bytes 15466496 | tf_op jit(solution)/shard_map/dot_general | solution.py:21
  375.6 8.9 %reshape.330 = bf16[128,160,128]{2,1,0:T(8,128)(2,1)} reshape(bf16[640,4096]{1,0:T(8,128)(2,1)} %convolution_convert_fusion) | data formatting | bytes 10485760 | tf_op jit(solution)/shard_map/reshape | solution.py:113
  384.5 12.9 %all-to-all-done.1 = bf16[128,128,128]{2,1,0:T(8,128)(2,1)} async-done(((bf16[128,128,128]{2,1,0:T(8,128)(2,1)}), bf16[128,128,128]{2,1,0:T(8,128)(2,1)}, u32[]{:S(2)}, u32[]{:S(2)}) %all-to-all-start.1) | async-done | bytes 4194336 | tf_op jit(solution)/shard_map/all_to_all | solution.py:114
  397.4 8.1 %all-to-all-start.3 = ((bf16[128,160,128]{2,1,0:T(8,128)(2,1)}), bf16[128,160,128]{2,1,0:T(8,128)(2,1)}, u32[]{:S(2)}, u32[]{:S(2)}) async-start(bf16[128,160,128]{2,1,0:T(8,128)(2,1)} %reshape.330), calls=%async_computation.4 | async-start | bytes 10485760 | tf_op jit(solution)/shard_map/all_to_all | solution.py:114
  405.9 12.0 %gather_fusion.3 = bf16[1024,32,128]{2,1,0:T(8,128)(2,1)} fusion(bf16[512,32,128]{2,1,0:T(8,128)(2,1)} %bitcast.30, s32[1024]{0:T(1024)S(1)} %broadcast_clamp_fusion.1), kind=kCustom, calls=%fused_computation.3 | custom fusion | bytes 16781312 | tf_op jit(solution)/shard_map/jit(_take)/gather | solution.py:117
  417.9 6.9 %fusion.1 = f32[128,32,128]{2,1,0:T(8,128)} fusion(f32[128,8]{1,0:T(8,128)S(1)} %get-tuple-element.10, bf16[1024,32,128]{2,1,0:T(8,128)(2,1)} %gather_fusion.3), kind=kLoop, calls=%fused_computation.10 | loop fusion | flops 12058624 | bytes 10489856 | tf_op jit(solution)/shard_map/reduce_sum | solution.py:119
  424.8 45.3 %all-to-all-done.3 = bf16[128,160,128]{2,1,0:T(8,128)(2,1)} async-done(((bf16[128,160,128]{2,1,0:T(8,128)(2,1)}), bf16[128,160,128]{2,1,0:T(8,128)(2,1)}, u32[]{:S(2)}, u32[]{:S(2)}) %all-to-all-start.3) | async-done | bytes 5242912 | tf_op jit(solution)/shard_map/all_to_all | solution.py:114
  470.1 12.3 %gather_fusion.5 = bf16[1024,32,128]{2,1,0:T(8,128)(2,1)} fusion(bf16[640,32,128]{2,1,0:T(8,128)(2,1)} %bitcast.34, s32[1024]{0:T(1024)S(1)} %broadcast_clamp_fusion), kind=kCustom, calls=%fused_computation.5 | custom fusion | bytes 16781312 | tf_op jit(solution)/shard_map/jit(_take)/gather | solution.py:117
  482.4 5.8 %fusion = f32[128,32,128]{2,1,0:T(8,128)S(1)} fusion(f32[128,8]{1,0:T(8,128)S(1)} %get-tuple-element.9, bf16[1024,32,128]{2,1,0:T(8,128)(2,1)} %gather_fusion.5), kind=kLoop, calls=%fused_computation.8 | loop fusion | flops 12058624 | bytes 10489856 | tf_op jit(solution)/shard_map/reduce_sum | solution.py:119
  488.7 0.7 copy-done.1
  489.4 2.8 fusion.12
  (81 shorter events, 7.9 us)
Async XLA Ops:
  7.2 38.8 %all-gather.8.cloned.1.call-start = ((), (), s32[]{:S(2)}) async-start(), calls=%async_computation.6 | async-start | bytes 1310720 | tf_op jit(solution)/shard_map/all_gather | solution.py:46
  18.5 110.9 %all-gather.10.cloned.1.call-start = ((), (), s32[]{:S(2)}) async-start(), calls=%async_computation.7 | async-start | bytes 5242880 | tf_op jit(solution)/shard_map/all_gather | solution.py:47
  46.0 113.9 %reduce-scatter.2.cloned.1.call-start = ((), (), s32[]{:S(2)}) async-start(), calls=%async_computation.5 | async-start | bytes 12582912 | tf_op jit(solution)/shard_map/reduce_scatter | solution.py:64
  46.0 7.2 %collective-permute-start = (bf16[1024,128]{1,0:T(8,128)(2,1)S(1)}, bf16[1024,128]{1,0:T(8,128)(2,1)S(1)}, u32[]{:S(2)}, u32[]{:S(2)}) collective-permute-start(bf16[1024,128]{1,0:T(8,128)(2,1)S(1)} %get-tuple-element.8), channel_id=1, source_target_pairs={{0,12},{4,0},{8,4},{12,8},{1,13},{5,1},{9,5},{13,9},{2,14},{6,2},{... | collective-permute-start | bytes 786440 | tf_op jit(solution)/shard_map/ppermute | solution.py:30
  46.6 8.1 %collective-permute-start.1 = (bf16[1024,128]{1,0:T(8,128)(2,1)S(1)}, bf16[1024,128]{1,0:T(8,128)(2,1)S(1)}, u32[]{:S(2)}, u32[]{:S(2)}) collective-permute-start(bf16[1024,128]{1,0:T(8,128)(2,1)S(1)} %get-tuple-element.8), channel_id=1, source_target_pairs={{0,4},{4,8},{8,12},{12,0},{1,5},{5,9},{9,13},{13,1},{2,6},{6,10},{... | collective-permute-start | bytes 786440 | tf_op jit(solution)/shard_map/ppermute | solution.py:29
  53.4 6.4 %collective-permute-start.3 = (bf16[1024,64]{1,0:T(8,128)(2,1)S(1)}, bf16[1024,64]{1,0:T(8,128)(2,1)S(1)}, u32[]{:S(2)}, u32[]{:S(2)}) collective-permute-start(bf16[1024,64]{1,0:T(8,128)(2,1)S(1)} %slice.81), channel_id=1, source_target_pairs={{0,12},{4,0},{8,4},{12,8},{1,13},{5,1},{9,5},{13,9},{2,14},{6,2},{... | collective-permute-start | bytes 393224 | tf_op jit(solution)/shard_map/ppermute | solution.py:35
  54.7 11.0 %collective-permute-start.2 = (bf16[1024,64]{1,0:T(8,128)(2,1)S(1)}, bf16[1024,64]{1,0:T(8,128)(2,1)S(1)}, u32[]{:S(2)}, u32[]{:S(2)}) collective-permute-start(bf16[1024,64]{1,0:T(8,128)(2,1)S(1)} %bitcast.106), channel_id=1, source_target_pairs={{0,4},{4,8},{8,12},{12,0},{1,5},{5,9},{9,13},{13,1},{2,6},{6,10},{... | collective-permute-start | bytes 393224 | tf_op jit(solution)/shard_map/ppermute | solution.py:34
  67.9 19.7 %collective-permute-start.4 = (bf16[4,1024,128]{2,1,0:T(8,128)(2,1)}, bf16[4,1024,128]{2,1,0:T(8,128)(2,1)S(1)}, u32[]{:S(2)}, u32[]{:S(2)}) collective-permute-start(bf16[4,1024,128]{2,1,0:T(8,128)(2,1)} %broadcast_select_fusion), channel_id=1, source_target_pairs={{0,96},{32,0},{64,32},{96,64},{1,97},{33,1},{65,33},{97,65},{2,98}... | collective-permute-start | bytes 3145736 | tf_op jit(solution)/shard_map/ppermute | solution.py:30
  67.9 23.2 %collective-permute-start.5 = (bf16[4,1024,128]{2,1,0:T(8,128)(2,1)}, bf16[4,1024,128]{2,1,0:T(8,128)(2,1)S(1)}, u32[]{:S(2)}, u32[]{:S(2)}) collective-permute-start(bf16[4,1024,128]{2,1,0:T(8,128)(2,1)} %broadcast_select_fusion), channel_id=1, source_target_pairs={{0,32},{32,64},{64,96},{96,0},{1,33},{33,65},{65,97},{97,1},{2,34}... | collective-permute-start | bytes 3145736 | tf_op jit(solution)/shard_map/ppermute | solution.py:29
  87.6 1.0 copy-start.4
  90.1 9.4 %collective-permute-start.7 = (bf16[4,1024,64]{1,2,0:T(8,128)(2,1)}, bf16[4,1024,64]{1,2,0:T(8,128)(2,1)S(1)}, u32[]{:S(2)}, u32[]{:S(2)}) collective-permute-start(bf16[4,1024,64]{1,2,0:T(8,128)(2,1)} %copy.43), channel_id=1, source_target_pairs={{0,96},{32,0},{64,32},{96,64},{1,97},{33,1},{65,33},{97,65},{2,98}... | collective-permute-start | bytes 1572872 | tf_op jit(solution)/shard_map/ppermute | solution.py:35
  91.1 3.9 copy-start.5
  91.4 9.5 %collective-permute-start.6 = (bf16[4,1024,64]{1,2,0:T(8,128)(2,1)S(1)}, bf16[4,1024,64]{1,2,0:T(8,128)(2,1)}, u32[]{:S(2)}, u32[]{:S(2)}) collective-permute-start(bf16[4,1024,64]{1,2,0:T(8,128)(2,1)S(1)} %copy.42), channel_id=1, source_target_pairs={{0,32},{32,64},{64,96},{96,0},{1,33},{33,65},{65,97},{97,1},{2,34}... | collective-permute-start | bytes 1572872 | tf_op jit(solution)/shard_map/ppermute | solution.py:34
  116.4 6.4 %copy-start.6 = (bf16[2,2,128,1024]{3,2,1,0:T(8,128)(2,1)S(1)}, bf16[2,2,128,1024]{3,2,1,0:T(8,128)(2,1)}, u32[]{:S(2)}) copy-start(bf16[2,2,128,1024]{3,2,1,0:T(8,128)(2,1)} %copy.41) | copy-start | bytes 3145732
  129.3 4.7 copy-start.3
  137.8 0.7 copy-start.8
  161.7 25.3 %collective-permute-start.8 = (bf16[128,4096]{1,0:T(8,128)(2,1)S(1)}, bf16[128,4096]{1,0:T(8,128)(2,1)S(1)}, u32[]{:S(2)}, u32[]{:S(2)}) collective-permute-start(bf16[128,4096]{1,0:T(8,128)(2,1)S(1)} %fusion.15), channel_id=1, source_target_pairs={{0,2},{2,0},{1,3},{3,1},{4,6},{6,4},{5,7},{7,5},{8,10},{10,8},{9,1... | collective-permute-start | bytes 3145736 | tf_op jit(solution)/shard_map/ppermute | solution.py:69
  191.6 5.3 %copy-start = (bf16[128,4096]{1,0:T(8,128)(2,1)S(1)}, bf16[128,4096]{1,0:T(8,128)(2,1)}, u32[]{:S(2)}) copy-start(bf16[128,4096]{1,0:T(8,128)(2,1)} %param.8) | copy-start | bytes 3145732
  194.8 2.5 copy-start.7
  201.7 62.0 %all-to-all-start = ((bf16[128,128,128]{2,1,0:T(8,128)(2,1)}), bf16[128,128,128]{2,1,0:T(8,128)(2,1)}, u32[]{:S(2)}, u32[]{:S(2)}) async-start(bf16[128,128,128]{2,1,0:T(8,128)(2,1)} %bitcast.90), calls=%async_computation.1 | async-start | bytes 8388608 | tf_op jit(solution)/shard_map/all_to_all | solution.py:111
  263.7 72.7 %all-to-all-start.2 = ((bf16[128,160,128]{2,1,0:T(8,128)(2,1)}), bf16[128,160,128]{2,1,0:T(8,128)(2,1)}, u32[]{:S(2)}, u32[]{:S(2)}) async-start(bf16[128,160,128]{2,1,0:T(8,128)(2,1)} %bitcast.89), calls=%async_computation.3 | async-start | bytes 10485760 | tf_op jit(solution)/shard_map/all_to_all | solution.py:111
  336.4 61.0 %all-to-all-start.1 = ((bf16[128,128,128]{2,1,0:T(8,128)(2,1)}), bf16[128,128,128]{2,1,0:T(8,128)(2,1)}, u32[]{:S(2)}, u32[]{:S(2)}) async-start(bf16[128,128,128]{2,1,0:T(8,128)(2,1)} %reshape.326), calls=%async_computation.2 | async-start | bytes 8388608 | tf_op jit(solution)/shard_map/all_to_all | solution.py:114
  384.5 21.2 %copy-start.9 = (f32[128,8]{0,1:T(8,128)S(1)}, f32[128,8]{0,1:T(8,128)}, u32[]{:S(2)}) copy-start(f32[128,8]{0,1:T(8,128)} %param.13) | copy-start | bytes 12292
  397.4 72.7 %all-to-all-start.3 = ((bf16[128,160,128]{2,1,0:T(8,128)(2,1)}), bf16[128,160,128]{2,1,0:T(8,128)(2,1)}, u32[]{:S(2)}, u32[]{:S(2)}) async-start(bf16[128,160,128]{2,1,0:T(8,128)(2,1)} %reshape.330), calls=%async_computation.4 | async-start | bytes 10485760 | tf_op jit(solution)/shard_map/all_to_all | solution.py:114
  482.4 5.8 %copy-start.2 = (f32[128,32,128]{2,1,0:T(8,128)S(1)}, f32[128,32,128]{2,1,0:T(8,128)}, u32[]{:S(2)}) copy-start(f32[128,32,128]{2,1,0:T(8,128)} %fusion.1) | copy-start | bytes 6291460
  488.2 1.2 copy-start.1
Sparse Core Ops, SparseCore 0:
  18.6 27.3 all-gather.7
  47.6 48.9 all-gather.9
  137.9 21.9 reduce-scatter.1

commit v13 on v11

--- a/solution.py
+++ b/solution.py
@@ -56,21 +56,23 @@
     rows = context.shape[0] // (n_x * n_c)
     context = context.reshape(n_x, n_c, rows, -1).transpose(1, 0, 2, 3).reshape(n_x * n_c * rows, -1)
     first, second = gather_columns(w_out)
-    partial_sums = jnp.dot(context, first, preferred_element_type=jnp.float32)
+    me = lax.axis_index("xlo")
+
+    def over_tensor(partial_sums):
+        chip_sums = lax.psum_scatter(partial_sums, "core", scatter_dimension=0, tiled=True)
+        chip_sums = chip_sums.reshape(n_x, rows, -1)
+        own = lax.dynamic_index_in_dim(chip_sums, me, axis=0, keepdims=False)
+        other = lax.dynamic_index_in_dim(chip_sums, 1 - me, axis=0, keepdims=False)
+        arrived = lax.ppermute(other.astype(jnp.bfloat16), "xlo", perm=[(0, 1), (1, 0)])
+        return own + arrived.astype(jnp.float32)
+
+    by_gathers = over_tensor(jnp.dot(context, first, preferred_element_type=jnp.float32))
     other = jnp.einsum("th,yzhl->tyzl", context, second, preferred_element_type=jnp.float32)
-    partial_sums = jnp.concatenate([partial_sums, other.reshape(other.shape[0], -1)], axis=1)
-    width = partial_sums.shape[1]
-    chip_sums = lax.psum_scatter(partial_sums, "core", scatter_dimension=0, tiled=True)
-    chip_sums = chip_sums.reshape(n_x, rows, width)
-    me = lax.axis_index("xlo")
-    own = lax.dynamic_index_in_dim(chip_sums, me, axis=0, keepdims=False)
-    other = lax.dynamic_index_in_dim(chip_sums, 1 - me, axis=0, keepdims=False)
-    arrived = lax.ppermute(other.astype(jnp.bfloat16), "xlo", perm=[(0, 1), (1, 0)])
-    summed = own + arrived.astype(jnp.float32)
+    by_rings = over_tensor(other.reshape(other.shape[0], -1))
     n_y, n_z = lax.axis_size("y"), lax.axis_size("z")
-    first = summed[:, : width // 2].reshape(rows, n_z, n_y, -1).transpose(0, 2, 1, 3)
-    second = summed[:, width // 2 :].reshape(rows, n_y, n_z, -1)
-    return jnp.stack([first, second], axis=2).reshape(rows, width)
+    by_gathers = by_gathers.reshape(rows, n_z, n_y, -1).transpose(0, 2, 1, 3)
+    by_rings = by_rings.reshape(rows, n_y, n_z, -1)
+    return jnp.stack([by_gathers, by_rings], axis=2).reshape(rows, -1)
 
 
 def on_device(hidden_in, context, w_out, norm_gain, expert_ids, route_weight, w_gate_up, w_down):

time: 496 us -> 484 us (0.976)
  waiting for transfers between devices: 242 us -> 233 us
  other arithmetic: 31.9 us -> 26.4 us
    ppermute x1 -> x2, waiting for transfers between devices: 18.4 us -> 10.6 us  [over_tensor(): lax.ppermute(other.astype(jnp.bfloat16), 'xlo', perm=[(0, 1), (1, 0)])]
    reshape x4 -> x3, local copies, waits for them, and re-layouts: 9.48 us -> 3.1 us  [the longest x1 2.12 us: project(): return jnp.stack([by_gathers, by_rings], axis=2).reshape(rows, -1)]
    reduce_scatter x1 -> x2, waiting for transfers between devices: 20.8 us -> 19.1 us  [over_tensor(): lax.psum_scatter(partial_sums, 'core', scatter_dimension=0, tiled=True)]
  transfers between devices with their start and end apart: 16 -> 18, of which waited for: 14 -> 15; matrix products, arithmetic and copies ran while one was open for 27% -> 29% of each run, Pallas kernels for 0% -> 0%
where the time goes in v13:
time: 484 us; the launch traced here: 481 us
  waiting for transfers between devices  233 us (48%)
  local copies, waits for them, and re-layouts  97.4 us (20%)
  matrix products  53 us (11%)
  starting transfers between devices  45.5 us (9%)
  other arithmetic  26.4 us (5%)
  between operations  15.9 us (3%)
  blocking collectives  10.4 us (2%)
    all_to_all x2, waiting for transfers between devices, on_device(): lax.all_to_all(send, ALL, split_axis=0, concat_axis=0, tiled=True)  79 us
    all_to_all x2, waiting for transfers between devices, on_device(): lax.all_to_all(outputs, ALL, split_axis=0, concat_axis=0, tiled=True)  58.2 us
    all_gather x1, waiting for transfers between devices, gather_columns(): first = lax.all_gather(staged[0], 'y', axis=1, tiled=True)  27.4 us
    gather x2, local copies, waits for them, and re-layouts, on_device(): picked = jnp.take(returned, chosen * size + slots - lo, axis=0, mode='clip')  24.3 us
    dot_general x2, matrix products, expert_block(): jnp.dot(received, w_gate_up[0], preferred_element_type=jnp.float32)  22.9 us
    ppermute x2, waiting for transfers between devices, ring_gather(): from_right = lax.ppermute(block, axis, perm=minus)  22.8 us
    reduce_scatter x2, waiting for transfers between devices, over_tensor(): lax.psum_scatter(partial_sums, 'core', scatter_dimension=0, tiled=True)  19.1 us
    all_to_all x2, starting transfers between devices, on_device(): lax.all_to_all(send, ALL, split_axis=0, concat_axis=0, tiled=True)  18.2 us
  transfers between devices with their start and end apart: 18, of which 15 were waited for; matrix products, arithmetic and copies ran while one was open for 29% of the time, Pallas kernels for 0%

profile of v13, /device:TPU:54, one launch (start us, length us, event | category | flops | bytes accessed | tf_op | source)
XLA Modules:
  0.0 481.3 jit_solution(13220142901218884974)
XLA Ops:
  8.0 10.4 %all-gather = bf16[2048,128]{1,0:T(8,128)(2,1)S(1)} all-gather(bf16[1024,128]{1,0:T(8,128)(2,1)} %param.10), channel_id=2, replica_groups=mesh['y'=4,'xhi'=2,'z'=4,'xlo'=2,'core'=2] {'xhi'}, dimensions={0}, use_global_device_ids=true | all-gather | bytes 786432 | tf_op jit(solution)/shard_map/all_gather | solution.py:45
  18.5 0.8 fusion.46
  19.3 27.4 %all-gather.8.cloned.1.call-done = bf16[1024,512]{1,0:T(8,128)(2,1)} async-done(((bf16[1024,128]{1,0:T(8,128)(2,1)}), bf16[1024,512]{1,0:T(8,128)(2,1)}) %all-gather.8.cloned.1.call-update) | async-done | bytes 1048592 | tf_op jit(solution)/shard_map/all_gather | solution.py:46
  47.4 1.6 collective-permute-start.2
  49.0 5.1 %collective-permute-done.1 = bf16[1024,128]{1,0:T(8,128)(2,1)S(1)} collective-permute-done((bf16[1024,128]{1,0:T(8,128)(2,1)S(1)}, bf16[1024,128]{1,0:T(8,128)(2,1)S(1)}, u32[]{:S(2)}, u32[]{:S(2)}) %collective-permute-start.1) | collective-permute-done | bytes 262176 | tf_op jit(solution)/shard_map/ppermute | solution.py:30
  54.3 1.0 collective-permute-start.4
  55.5 0.8 collective-permute-start.3
  56.4 4.3 collective-permute-done.4
  60.7 5.6 %collective-permute-done.3 = bf16[1024,64]{1,0:T(8,128)(2,1)S(1)} collective-permute-done((bf16[1024,64]{1,0:T(8,128)(2,1)S(1)}, bf16[1024,64]{1,0:T(8,128)(2,1)S(1)}, u32[]{:S(2)}, u32[]{:S(2)}) %collective-permute-start.3) | collective-permute-done | bytes 131104 | tf_op jit(solution)/shard_map/ppermute | solution.py:34
  66.6 0.7 gather_fusion
  67.4 1.1 broadcast_select_fusion
  68.5 2.0 collective-permute-start.6
  70.5 17.6 %collective-permute-done.5 = bf16[4,1024,128]{2,1,0:T(8,128)(2,1)S(1)} collective-permute-done((bf16[4,1024,128]{2,1,0:T(8,128)(2,1)}, bf16[4,1024,128]{2,1,0:T(8,128)(2,1)S(1)}, u32[]{:S(2)}, u32[]{:S(2)}) %collective-permute-start.5) | collective-permute-done | bytes 1048608 | tf_op jit(solution)/shard_map/ppermute | solution.py:30
  88.2 1.1 copy-done.4
  89.6 1.1 copy.46
  90.7 1.0 collective-permute-start.8
  92.1 1.1 collective-permute-start.7
  93.1 2.3 copy.43
  95.6 4.5 collective-permute-done.8
  100.6 0.8 collective-permute-done.7
  101.4 1.5 copy.47
  103.5 3.4 pad_maximum_fusion
  107.0 5.3 %gather_fusion.1 = bf16[4,4,1024,128]{3,2,1,0:T(8,128)(2,1)} fusion(bf16[4,4,1024,128]{3,2,1,0:T(8,128)(2,1)} %pad_maximum_fusion, s32[1024]{0:T(1024)S(1)} %pad_clamp_fusion.2), kind=kCustom, calls=%fused_computation.1 | custom fusion | bytes 8388624 | tf_op jit(solution)/shard_map/jit(_take)/gather | solution.py:41
  112.3 6.8 %fusion.12 = f32[4,4,128,512]{3,2,1,0:T(8,128)} fusion(bf16[512,1024,1,1]{1,0,3,2:T(8,128)(2,1)S(1)} %bitcast.108, bf16[4,4,1024,128]{3,2,1,0:T(8,128)(2,1)} %gather_fusion.1, pred[4]{0:T(512)(128)(4,1)S(1)} %get-tuple-element.18), kind=kOutput, calls=%fused_computation.21 | convolution fusion | flops 2149580800 | bytes 9437188 | tf_op jit(solution)/shard_map/th,yzhl->tyzl/dot_general | solution.py:70
  119.4 6.5 %fusion.47 = f32[512,2048]{1,0:T(8,128)} fusion(bf16[512,1024]{1,0:T(8,128)(2,1)S(1)} %bitcast.109, bf16[1024,2048]{1,0:T(8,128)(2,1)} %all-gather.10.cloned.1.call-done), kind=kOutput, calls=%fused_computation.115 | convolution fusion | flops 2147483648 | bytes 9437184 | tf_op jit(solution)/shard_map/dot_general | solution.py:69
  125.9 0.7 copy-done.8
  128.3 8.1 %reduce-scatter.5.cloned.1.call-done = f32[256,2048]{0,1:T(8,128)} async-done(((f32[512,2048]{0,1:T(8,128)}), f32[256,2048]{0,1:T(8,128)}) %reduce-scatter.5.cloned.1.call-update) | async-done | bytes 2097168 | tf_op jit(solution)/shard_map/reduce_scatter | solution.py:62
  136.4 1.9 copy.50
  138.5 0.9 collective-permute-start.9
  139.4 4.3 scatter_custom_fusion
  144.0 11.0 %reduce-scatter.3.cloned.1.call-done = f32[256,2048]{1,0:T(8,128)} async-done(((f32[512,2048]{1,0:T(8,128)}), f32[256,2048]{1,0:T(8,128)}) %reduce-scatter.3.cloned.1.call-update) | async-done | bytes 2097168 | tf_op jit(solution)/shard_map/reduce_scatter | solution.py:62
  155.0 2.1 fusion.24
  157.1 0.8 collective-permute-start
  158.0 1.2 bitcast_add_fusion.1
  159.1 1.7 stack_reshape.3
  160.8 10.6 %collective-permute-done = bf16[128,2048]{1,0:T(8,128)(2,1)} collective-permute-done((bf16[128,2048]{1,0:T(8,128)(2,1)}, bf16[128,2048]{1,0:T(8,128)(2,1)}, u32[]{:S(2)}, u32[]{:S(2)}) %collective-permute-start) | collective-permute-done | bytes 524320 | tf_op jit(solution)/shard_map/ppermute | solution.py:66
  171.4 1.5 bitcast_add_fusion.2
  172.9 0.7 reshape.322
  174.5 2.0 copy.51
  176.5 2.1 reshape.325
  179.9 3.5 gather_fusion.2
  183.3 10.1 %all-to-all-start = ((bf16[128,128,128]{2,1,0:T(8,128)(2,1)}), bf16[128,128,128]{2,1,0:T(8,128)(2,1)}, u32[]{:S(2)}, u32[]{:S(2)}) async-start(bf16[128,128,128]{2,1,0:T(8,128)(2,1)} %bitcast.95), calls=%async_computation.2 | async-start | bytes 8388608 | tf_op jit(solution)/shard_map/all_to_all | solution.py:112
  193.7 4.1 gather_fusion.4
  197.8 47.5 %all-to-all-done = bf16[128,128,128]{2,1,0:T(8,128)(2,1)} async-done(((bf16[128,128,128]{2,1,0:T(8,128)(2,1)}), bf16[128,128,128]{2,1,0:T(8,128)(2,1)}, u32[]{:S(2)}, u32[]{:S(2)}) %all-to-all-start) | async-done | bytes 4194336 | tf_op jit(solution)/shard_map/all_to_all | solution.py:112
  245.4 8.1 %all-to-all-start.2 = ((bf16[128,160,128]{2,1,0:T(8,128)(2,1)}), bf16[128,160,128]{2,1,0:T(8,128)(2,1)}, u32[]{:S(2)}, u32[]{:S(2)}) async-start(bf16[128,160,128]{2,1,0:T(8,128)(2,1)} %bitcast.94), calls=%async_computation.4 | async-start | bytes 10485760 | tf_op jit(solution)/shard_map/all_to_all | solution.py:112
  253.5 7.3 %reshape.330 = bf16[512,4096]{1,0:T(8,128)(2,1)} reshape(bf16[128,128,128]{2,1,0:T(8,128)(2,1)} %all-to-all-done) | data formatting | bytes 8388608 | tf_op jit(solution)/shard_map/reshape | solution.py:113
  260.8 10.5 %fusion.4 = f32[512,1536]{1,0:T(8,128)S(1)} fusion(bf16[512,4096]{1,0:T(8,128)(2,1)} %reshape.330, bf16[1,4096,1536]{2,1,0:T(8,128)(2,1)} %param.14), kind=kOutput, calls=%fused_computation.13 | convolution fusion | flops 6442450944 | bytes 19922944 | tf_op jit(solution)/shard_map/dot_general | solution.py:17
  271.3 7.9 %fusion.9 = bf16[512,4096]{1,0:T(8,128)(2,1)} fusion(bf16[1,768,4096]{2,1,0:T(8,128)(2,1)} %param.15, f32[512,1536]{1,0:T(8,128)S(1)} %fusion.4), kind=kOutput, calls=%fused_computation.19 | convolution fusion | flops 3225681920 | bytes 13631488 | tf_op jit(solution)/shard_map/dot_general | solution.py:21
  279.2 7.4 %reshape.331 = bf16[128,128,128]{2,1,0:T(8,128)(2,1)} reshape(bf16[512,4096]{1,0:T(8,128)(2,1)} %fusion.9) | data formatting | bytes 8388608 | tf_op jit(solution)/shard_map/reshape | solution.py:114
  286.6 31.5 %all-to-all-done.2 = bf16[128,160,128]{2,1,0:T(8,128)(2,1)} async-done(((bf16[128,160,128]{2,1,0:T(8,128)(2,1)}), bf16[128,160,128]{2,1,0:T(8,128)(2,1)}, u32[]{:S(2)}, u32[]{:S(2)}) %all-to-all-start.2) | async-done | bytes 5242912 | tf_op jit(solution)/shard_map/all_to_all | solution.py:112
  318.1 9.0 %all-to-all-start.1 = ((bf16[128,128,128]{2,1,0:T(8,128)(2,1)}), bf16[128,128,128]{2,1,0:T(8,128)(2,1)}, u32[]{:S(2)}, u32[]{:S(2)}) async-start(bf16[128,128,128]{2,1,0:T(8,128)(2,1)} %reshape.331), calls=%async_computation.3 | async-start | bytes 8388608 | tf_op jit(solution)/shard_map/all_to_all | solution.py:115
  327.1 8.9 %reshape.334 = bf16[640,4096]{1,0:T(8,128)(2,1)} reshape(bf16[128,160,128]{2,1,0:T(8,128)(2,1)} %all-to-all-done.2) | data formatting | bytes 10485760 | tf_op jit(solution)/shard_map/reshape | solution.py:113
  336.0 12.4 %fusion.2 = f32[640,1536]{1,0:T(8,128)S(1)} fusion(bf16[640,4096]{1,0:T(8,128)(2,1)} %reshape.334, bf16[1,4096,1536]{2,1,0:T(8,128)(2,1)} %param.14), kind=kOutput, calls=%fused_computation.11 | convolution fusion | flops 8053063680 | bytes 21757952 | tf_op jit(solution)/shard_map/dot_general | solution.py:17
  348.4 8.9 %convolution_convert_fusion = bf16[640,4096]{1,0:T(8,128)(2,1)} fusion(bf16[1,768,4096]{2,1,0:T(8,128)(2,1)} %param.15, f32[640,1536]{1,0:T(8,128)S(1)} %fusion.2), kind=kOutput, calls=%fused_computation.15 | convolution fusion | flops 4032102400 | bytes 15466496 | tf_op jit(solution)/shard_map/dot_general | solution.py:21
  357.2 8.9 %reshape.335 = bf16[128,160,128]{2,1,0:T(8,128)(2,1)} reshape(bf16[640,4096]{1,0:T(8,128)(2,1)} %convolution_convert_fusion) | data formatting | bytes 10485760 | tf_op jit(solution)/shard_map/reshape | solution.py:114
  366.1 12.9 %all-to-all-done.1 = bf16[128,128,128]{2,1,0:T(8,128)(2,1)} async-done(((bf16[128,128,128]{2,1,0:T(8,128)(2,1)}), bf16[128,128,128]{2,1,0:T(8,128)(2,1)}, u32[]{:S(2)}, u32[]{:S(2)}) %all-to-all-start.1) | async-done | bytes 4194336 | tf_op jit(solution)/shard_map/all_to_all | solution.py:115
  379.1 8.1 %all-to-all-start.3 = ((bf16[128,160,128]{2,1,0:T(8,128)(2,1)}), bf16[128,160,128]{2,1,0:T(8,128)(2,1)}, u32[]{:S(2)}, u32[]{:S(2)}) async-start(bf16[128,160,128]{2,1,0:T(8,128)(2,1)} %reshape.335), calls=%async_computation.5 | async-start | bytes 10485760 | tf_op jit(solution)/shard_map/all_to_all | solution.py:115
  387.6 12.0 %gather_fusion.3 = bf16[1024,32,128]{2,1,0:T(8,128)(2,1)} fusion(bf16[512,32,128]{2,1,0:T(8,128)(2,1)} %bitcast.33, s32[1024]{0:T(1024)S(1)} %broadcast_clamp_fusion.1), kind=kCustom, calls=%fused_computation.3 | custom fusion | bytes 16781312 | tf_op jit(solution)/shard_map/jit(_take)/gather | solution.py:118
  399.6 6.9 %fusion.1 = f32[128,32,128]{2,1,0:T(8,128)} fusion(f32[128,8]{1,0:T(8,128)S(1)} %get-tuple-element.8, bf16[1024,32,128]{2,1,0:T(8,128)(2,1)} %gather_fusion.3), kind=kLoop, calls=%fused_computation.10 | loop fusion | flops 12058624 | bytes 10489856 | tf_op jit(solution)/shard_map/reduce_sum | solution.py:120
  406.5 45.2 %all-to-all-done.3 = bf16[128,160,128]{2,1,0:T(8,128)(2,1)} async-done(((bf16[128,160,128]{2,1,0:T(8,128)(2,1)}), bf16[128,160,128]{2,1,0:T(8,128)(2,1)}, u32[]{:S(2)}, u32[]{:S(2)}) %all-to-all-start.3) | async-done | bytes 5242912 | tf_op jit(solution)/shard_map/all_to_all | solution.py:115
  451.8 12.3 %gather_fusion.5 = bf16[1024,32,128]{2,1,0:T(8,128)(2,1)} fusion(bf16[640,32,128]{2,1,0:T(8,128)(2,1)} %bitcast.37, s32[1024]{0:T(1024)S(1)} %broadcast_clamp_fusion), kind=kCustom, calls=%fused_computation.5 | custom fusion | bytes 16781312 | tf_op jit(solution)/shard_map/jit(_take)/gather | solution.py:118
  464.1 5.8 %fusion = f32[128,32,128]{2,1,0:T(8,128)S(1)} fusion(f32[128,8]{1,0:T(8,128)S(1)} %get-tuple-element.7, bf16[1024,32,128]{2,1,0:T(8,128)(2,1)} %gather_fusion.5), kind=kLoop, calls=%fused_computation.8 | loop fusion | flops 12058624 | bytes 10489856 | tf_op jit(solution)/shard_map/reduce_sum | solution.py:120
  470.4 0.7 copy-done.1
  471.1 2.8 fusion.15
  (86 shorter events, 9.0 us)
Async XLA Ops:
  8.0 38.8 %all-gather.8.cloned.1.call-start = ((), (), s32[]{:S(2)}) async-start(), calls=%async_computation.8 | async-start | bytes 1310720 | tf_op jit(solution)/shard_map/all_gather | solution.py:46
  19.3 100.1 %all-gather.10.cloned.1.call-start = ((), (), s32[]{:S(2)}) async-start(), calls=%async_computation.9 | async-start | bytes 5242880 | tf_op jit(solution)/shard_map/all_gather | solution.py:47
  46.8 89.6 %reduce-scatter.5.cloned.1.call-start = ((), (), s32[]{:S(2)}) async-start(), calls=%async_computation.7 | async-start | bytes 6291456 | tf_op jit(solution)/shard_map/reduce_scatter | solution.py:62
  46.9 7.2 %collective-permute-start.1 = (bf16[1024,128]{1,0:T(8,128)(2,1)S(1)}, bf16[1024,128]{1,0:T(8,128)(2,1)S(1)}, u32[]{:S(2)}, u32[]{:S(2)}) collective-permute-start(bf16[1024,128]{1,0:T(8,128)(2,1)S(1)} %get-tuple-element.6), channel_id=1, source_target_pairs={{0,12},{4,0},{8,4},{12,8},{1,13},{5,1},{9,5},{13,9},{2,14},{6,2},{... | collective-permute-start | bytes 786440 | tf_op jit(solution)/shard_map/ppermute | solution.py:30
  47.4 8.1 %collective-permute-start.2 = (bf16[1024,128]{1,0:T(8,128)(2,1)S(1)}, bf16[1024,128]{1,0:T(8,128)(2,1)S(1)}, u32[]{:S(2)}, u32[]{:S(2)}) collective-permute-start(bf16[1024,128]{1,0:T(8,128)(2,1)S(1)} %get-tuple-element.6), channel_id=1, source_target_pairs={{0,4},{4,8},{8,12},{12,0},{1,5},{5,9},{9,13},{13,1},{2,6},{6,10},{... | collective-permute-start | bytes 786440 | tf_op jit(solution)/shard_map/ppermute | solution.py:29
  54.3 6.4 %collective-permute-start.4 = (bf16[1024,64]{1,0:T(8,128)(2,1)S(1)}, bf16[1024,64]{1,0:T(8,128)(2,1)S(1)}, u32[]{:S(2)}, u32[]{:S(2)}) collective-permute-start(bf16[1024,64]{1,0:T(8,128)(2,1)S(1)} %slice.73), channel_id=1, source_target_pairs={{0,12},{4,0},{8,4},{12,8},{1,13},{5,1},{9,5},{13,9},{2,14},{6,2},{... | collective-permute-start | bytes 393224 | tf_op jit(solution)/shard_map/ppermute | solution.py:35
  55.5 10.8 %collective-permute-start.3 = (bf16[1024,64]{1,0:T(8,128)(2,1)S(1)}, bf16[1024,64]{1,0:T(8,128)(2,1)S(1)}, u32[]{:S(2)}, u32[]{:S(2)}) collective-permute-start(bf16[1024,64]{1,0:T(8,128)(2,1)S(1)} %bitcast.112), channel_id=1, source_target_pairs={{0,4},{4,8},{8,12},{12,0},{1,5},{5,9},{9,13},{13,1},{2,6},{6,10},{... | collective-permute-start | bytes 393224 | tf_op jit(solution)/shard_map/ppermute | solution.py:34
  68.5 19.7 %collective-permute-start.5 = (bf16[4,1024,128]{2,1,0:T(8,128)(2,1)}, bf16[4,1024,128]{2,1,0:T(8,128)(2,1)S(1)}, u32[]{:S(2)}, u32[]{:S(2)}) collective-permute-start(bf16[4,1024,128]{2,1,0:T(8,128)(2,1)} %broadcast_select_fusion), channel_id=1, source_target_pairs={{0,96},{32,0},{64,32},{96,64},{1,97},{33,1},{65,33},{97,65},{2,98}... | collective-permute-start | bytes 3145736 | tf_op jit(solution)/shard_map/ppermute | solution.py:30
  68.5 23.2 %collective-permute-start.6 = (bf16[4,1024,128]{2,1,0:T(8,128)(2,1)}, bf16[4,1024,128]{2,1,0:T(8,128)(2,1)S(1)}, u32[]{:S(2)}, u32[]{:S(2)}) collective-permute-start(bf16[4,1024,128]{2,1,0:T(8,128)(2,1)} %broadcast_select_fusion), channel_id=1, source_target_pairs={{0,32},{32,64},{64,96},{96,0},{1,33},{33,65},{65,97},{97,1},{2,34}... | collective-permute-start | bytes 3145736 | tf_op jit(solution)/shard_map/ppermute | solution.py:29
  88.2 1.1 copy-start.4
  90.7 9.4 %collective-permute-start.8 = (bf16[4,1024,64]{1,2,0:T(8,128)(2,1)}, bf16[4,1024,64]{1,2,0:T(8,128)(2,1)S(1)}, u32[]{:S(2)}, u32[]{:S(2)}) collective-permute-start(bf16[4,1024,64]{1,2,0:T(8,128)(2,1)} %copy.46), channel_id=1, source_target_pairs={{0,96},{32,0},{64,32},{96,64},{1,97},{33,1},{65,33},{97,65},{2,98}... | collective-permute-start | bytes 1572872 | tf_op jit(solution)/shard_map/ppermute | solution.py:35
  91.7 3.7 copy-start.5
  92.1 9.4 %collective-permute-start.7 = (bf16[4,1024,64]{1,2,0:T(8,128)(2,1)S(1)}, bf16[4,1024,64]{1,2,0:T(8,128)(2,1)}, u32[]{:S(2)}, u32[]{:S(2)}) collective-permute-start(bf16[4,1024,64]{1,2,0:T(8,128)(2,1)S(1)} %copy.45), channel_id=1, source_target_pairs={{0,32},{32,64},{64,96},{96,0},{1,33},{33,65},{65,97},{97,1},{2,34}... | collective-permute-start | bytes 1572872 | tf_op jit(solution)/shard_map/ppermute | solution.py:34
  107.0 5.3 %copy-start.6 = (bf16[2,2,128,1024]{3,2,1,0:T(8,128)(2,1)S(1)}, bf16[2,2,128,1024]{3,2,1,0:T(8,128)(2,1)}, u32[]{:S(2)}) copy-start(bf16[2,2,128,1024]{3,2,1,0:T(8,128)(2,1)} %copy.43) | copy-start | bytes 3145732
  119.1 35.9 %reduce-scatter.3.cloned.1.call-start = ((), (), s32[]{:S(2)}) async-start(), calls=%async_computation.6 | async-start | bytes 6291456 | tf_op jit(solution)/shard_map/reduce_scatter | solution.py:62
  125.9 0.7 copy-start.8
  138.5 19.5 %collective-permute-start.9 = (bf16[128,2048]{1,0:T(8,128)(2,1)S(1)}, bf16[128,2048]{1,0:T(8,128)(2,1)}, u32[]{:S(2)}, u32[]{:S(2)}) collective-permute-start(bf16[128,2048]{1,0:T(8,128)(2,1)S(1)} %fusion.25), channel_id=1, source_target_pairs={{0,2},{2,0},{1,3},{3,1},{4,6},{6,4},{5,7},{7,5},{8,10},{10,8},{9,1... | collective-permute-start | bytes 1572872 | tf_op jit(solution)/shard_map/ppermute | solution.py:66
  157.1 14.3 %collective-permute-start = (bf16[128,2048]{1,0:T(8,128)(2,1)}, bf16[128,2048]{1,0:T(8,128)(2,1)}, u32[]{:S(2)}, u32[]{:S(2)}) collective-permute-start(bf16[128,2048]{1,0:T(8,128)(2,1)} %fusion.24), channel_id=1, source_target_pairs={{0,2},{2,0},{1,3},{3,1},{4,6},{6,4},{5,7},{7,5},{8,10},{10,8},{9,1... | collective-permute-start | bytes 1572872 | tf_op jit(solution)/shard_map/ppermute | solution.py:66
  160.8 13.1 %copy-start.3 = (f32[128,4,1,4,128]{4,3,1,0,2:T(4,128)S(1)}, f32[128,4,1,4,128]{4,3,1,0,2:T(4,128)}, u32[]{:S(2)}) copy-start(f32[128,4,1,4,128]{4,3,1,0,2:T(4,128)} %stack_reshape.3) | copy-start | bytes 3145732
  174.5 4.1 copy-start
  176.5 2.5 copy-start.7
  183.3 62.0 %all-to-all-start = ((bf16[128,128,128]{2,1,0:T(8,128)(2,1)}), bf16[128,128,128]{2,1,0:T(8,128)(2,1)}, u32[]{:S(2)}, u32[]{:S(2)}) async-start(bf16[128,128,128]{2,1,0:T(8,128)(2,1)} %bitcast.95), calls=%async_computation.2 | async-start | bytes 8388608 | tf_op jit(solution)/shard_map/all_to_all | solution.py:112
  245.4 72.7 %all-to-all-start.2 = ((bf16[128,160,128]{2,1,0:T(8,128)(2,1)}), bf16[128,160,128]{2,1,0:T(8,128)(2,1)}, u32[]{:S(2)}, u32[]{:S(2)}) async-start(bf16[128,160,128]{2,1,0:T(8,128)(2,1)} %bitcast.94), calls=%async_computation.4 | async-start | bytes 10485760 | tf_op jit(solution)/shard_map/all_to_all | solution.py:112
  318.1 61.0 %all-to-all-start.1 = ((bf16[128,128,128]{2,1,0:T(8,128)(2,1)}), bf16[128,128,128]{2,1,0:T(8,128)(2,1)}, u32[]{:S(2)}, u32[]{:S(2)}) async-start(bf16[128,128,128]{2,1,0:T(8,128)(2,1)} %reshape.331), calls=%async_computation.3 | async-start | bytes 8388608 | tf_op jit(solution)/shard_map/all_to_all | solution.py:115
  366.1 21.3 %copy-start.9 = (f32[128,8]{0,1:T(8,128)S(1)}, f32[128,8]{0,1:T(8,128)}, u32[]{:S(2)}) copy-start(f32[128,8]{0,1:T(8,128)} %param.13) | copy-start | bytes 12292
  379.1 72.7 %all-to-all-start.3 = ((bf16[128,160,128]{2,1,0:T(8,128)(2,1)}), bf16[128,160,128]{2,1,0:T(8,128)(2,1)}, u32[]{:S(2)}, u32[]{:S(2)}) async-start(bf16[128,160,128]{2,1,0:T(8,128)(2,1)} %reshape.335), calls=%async_computation.5 | async-start | bytes 10485760 | tf_op jit(solution)/shard_map/all_to_all | solution.py:115
  464.1 5.8 %copy-start.2 = (f32[128,32,128]{2,1,0:T(8,128)S(1)}, f32[128,32,128]{2,1,0:T(8,128)}, u32[]{:S(2)}) copy-start(f32[128,32,128]{2,1,0:T(8,128)} %fusion.1) | copy-start | bytes 6291460
  469.9 1.2 copy-start.1
Sparse Core Ops, SparseCore 0:
  19.4 27.3 all-gather.7
  48.6 48.9 all-gather.9
Sparse Core Ops, SparseCore 1:
  119.2 17.2 reduce-scatter.4
  138.8 16.1 reduce-scatter.2

commit v14 on v13

--- a/solution.py
+++ b/solution.py
@@ -42,10 +42,10 @@
 
 
 def gather_columns(w_out):
-    staged = lax.all_gather(w_out, "xhi", axis=0)
-    first = lax.all_gather(staged[0], "y", axis=1, tiled=True)
+    partner = lax.ppermute(w_out, "xhi", perm=[(0, 1), (1, 0)])
+    first = lax.all_gather(w_out, "y", axis=1, tiled=True)
     first = lax.all_gather(first, "z", axis=1, tiled=True)
-    second = ring_gather(staged[1], "z")
+    second = ring_gather(partner, "z")
     second = ring_gather(second, "y")
     return first, second
 
@@ -72,7 +72,10 @@
     n_y, n_z = lax.axis_size("y"), lax.axis_size("z")
     by_gathers = by_gathers.reshape(rows, n_z, n_y, -1).transpose(0, 2, 1, 3)
     by_rings = by_rings.reshape(rows, n_y, n_z, -1)
-    return jnp.stack([by_gathers, by_rings], axis=2).reshape(rows, -1)
+    low_first = lax.axis_index("xhi") == 0
+    low = jnp.where(low_first, by_gathers, by_rings)
+    high = jnp.where(low_first, by_rings, by_gathers)
+    return jnp.stack([low, high], axis=2).reshape(rows, -1)
 
 
 def on_device(hidden_in, context, w_out, norm_gain, expert_ids, route_weight, w_gate_up, w_down):

time: 484 us -> 490 us (1.012)
  waiting for transfers between devices: 233 us -> 248 us
  blocking collectives: 10.4 us -> 0 us
    all_gather x1 -> x0, blocking collectives: 10.4 us -> none  [gather_columns(): staged = lax.all_gather(w_out, 'xhi', axis=0)]
    ppermute x0 -> x1, waiting for transfers between devices: none -> 7.44 us  [gather_columns(): partner = lax.ppermute(w_out, 'xhi', perm=[(0, 1), (1, 0)])]
  transfers between devices with their start and end apart: 18 -> 19, of which waited for: 15 -> 16; matrix products, arithmetic and copies ran while one was open for 29% -> 29% of each run, Pallas kernels for 0% -> 0%
where the time goes in v14:
time: 490 us; the launch traced here: 488 us
  waiting for transfers between devices  248 us (51%)
  local copies, waits for them, and re-layouts  95.4 us (19%)
  matrix products  53 us (11%)
  starting transfers between devices  48.7 us (10%)
  other arithmetic  26.7 us (5%)
  between operations  15.9 us (3%)
    all_to_all x2, waiting for transfers between devices, on_device(): lax.all_to_all(send, ALL, split_axis=0, concat_axis=0, tiled=True)  79 us
    all_to_all x2, waiting for transfers between devices, on_device(): lax.all_to_all(outputs, ALL, split_axis=0, concat_axis=0, tiled=True)  58.2 us
    all_gather x1, waiting for transfers between devices, gather_columns(): first = lax.all_gather(w_out, 'y', axis=1, tiled=True)  29.2 us
    gather x2, local copies, waits for them, and re-layouts, on_device(): picked = jnp.take(returned, chosen * size + slots - lo, axis=0, mode='clip')  24.3 us
    dot_general x2, matrix products, expert_block(): jnp.dot(received, w_gate_up[0], preferred_element_type=jnp.float32)  22.9 us
    ppermute x2, waiting for transfers between devices, ring_gather(): from_right = lax.ppermute(block, axis, perm=minus)  22.2 us
    reduce_scatter x2, waiting for transfers between devices, over_tensor(): lax.psum_scatter(partial_sums, 'core', scatter_dimension=0, tiled=True)  18.4 us
    all_to_all x2, starting transfers between devices, on_device(): lax.all_to_all(send, ALL, split_axis=0, concat_axis=0, tiled=True)  18.2 us
  transfers between devices with their start and end apart: 19, of which 16 were waited for; matrix products, arithmetic and copies ran while one was open for 29% of the time, Pallas kernels for 0%

profile of v14, /device:TPU:54, one launch (start us, length us, event | category | flops | bytes accessed | tf_op | source)
XLA Modules:
  0.0 487.9 jit_solution(11444951843729095752)
XLA Ops:
  8.0 0.7 all-gather.3.cloned.1.call-update
  8.8 29.2 %all-gather.3.cloned.1.call-done = bf16[1024,512]{1,0:T(8,128)(2,1)} async-done(((bf16[1024,128]{1,0:T(8,128)(2,1)}), bf16[1024,512]{1,0:T(8,128)(2,1)}) %all-gather.3.cloned.1.call-update) | async-done | bytes 1048592 | tf_op jit(solution)/shard_map/all_gather | solution.py:46
  38.0 1.5 collective-permute-start.1
  39.6 7.4 %collective-permute-done.1 = bf16[1024,128]{1,0:T(8,128)(2,1)S(1)} collective-permute-done((bf16[1024,128]{1,0:T(8,128)(2,1)}, bf16[1024,128]{1,0:T(8,128)(2,1)S(1)}, u32[]{:S(2)}, u32[]{:S(2)}) %collective-permute-start.1) | collective-permute-done | bytes 262176 | tf_op jit(solution)/shard_map/ppermute | solution.py:45
  47.5 1.6 collective-permute-start.3
  49.1 4.6 collective-permute-done.2
  53.8 3.6 collective-permute-start.5
  57.3 2.1 collective-permute-done.3
  59.4 7.5 %collective-permute-done.5 = bf16[1024,64]{1,0:T(8,128)(2,1)S(1)} collective-permute-done((bf16[1024,64]{1,0:T(8,128)(2,1)S(1)}, bf16[1024,64]{1,0:T(8,128)(2,1)S(1)}, u32[]{:S(2)}, u32[]{:S(2)}) %collective-permute-start.5) | collective-permute-done | bytes 131104 | tf_op jit(solution)/shard_map/ppermute | solution.py:35
  66.9 6.6 %collective-permute-done.4 = bf16[1024,64]{1,0:T(8,128)(2,1)S(1)} collective-permute-done((bf16[1024,64]{1,0:T(8,128)(2,1)S(1)}, bf16[1024,64]{1,0:T(8,128)(2,1)S(1)}, u32[]{:S(2)}, u32[]{:S(2)}) %collective-permute-start.4) | collective-permute-done | bytes 131104 | tf_op jit(solution)/shard_map/ppermute | solution.py:34
  73.8 0.7 gather_fusion
  74.5 1.1 broadcast_select_fusion
  75.7 2.0 collective-permute-start.7
  77.7 17.6 %collective-permute-done.6 = bf16[4,1024,128]{2,1,0:T(8,128)(2,1)S(1)} collective-permute-done((bf16[4,1024,128]{2,1,0:T(8,128)(2,1)}, bf16[4,1024,128]{2,1,0:T(8,128)(2,1)S(1)}, u32[]{:S(2)}, u32[]{:S(2)}) %collective-permute-start.6) | collective-permute-done | bytes 1048608 | tf_op jit(solution)/shard_map/ppermute | solution.py:30
  95.3 1.1 copy-done.3
  96.8 1.1 copy.47
  97.9 1.0 collective-permute-start.9
  99.2 1.1 collective-permute-start.8
  100.3 2.3 copy.44
  102.8 4.5 collective-permute-done.9
  107.8 0.8 collective-permute-done.8
  108.6 1.5 copy.48
  110.7 3.4 pad_maximum_fusion
  114.1 5.3 %gather_fusion.1 = bf16[4,4,1024,128]{3,2,1,0:T(8,128)(2,1)} fusion(bf16[4,4,1024,128]{3,2,1,0:T(8,128)(2,1)} %pad_maximum_fusion, s32[1024]{0:T(1024)S(1)} %pad_clamp_fusion.2), kind=kCustom, calls=%fused_computation.1 | custom fusion | bytes 8388624 | tf_op jit(solution)/shard_map/jit(_take)/gather | solution.py:41
  119.5 6.8 %fusion.12 = f32[4,4,128,512]{3,2,1,0:T(8,128)} fusion(bf16[512,1024,1,1]{1,0,3,2:T(8,128)(2,1)S(1)} %bitcast.112, bf16[4,4,1024,128]{3,2,1,0:T(8,128)(2,1)} %gather_fusion.1, pred[4]{0:T(512)(128)(4,1)S(1)} %get-tuple-element.17), kind=kOutput, calls=%fused_computation.21 | convolution fusion | flops 2149580800 | bytes 9437188 | tf_op jit(solution)/shard_map/th,yzhl->tyzl/dot_general | solution.py:70
  126.6 6.5 %fusion.48 = f32[512,2048]{1,0:T(8,128)} fusion(bf16[512,1024]{1,0:T(8,128)(2,1)S(1)} %bitcast.113, bf16[1024,2048]{1,0:T(8,128)(2,1)} %all-gather.5.cloned.1.call-done), kind=kOutput, calls=%fused_computation.116 | convolution fusion | flops 2147483648 | bytes 9437184 | tf_op jit(solution)/shard_map/dot_general | solution.py:69
  135.5 7.4 %reduce-scatter.5.cloned.1.call-done = f32[256,2048]{0,1:T(8,128)} async-done(((f32[512,2048]{0,1:T(8,128)}), f32[256,2048]{0,1:T(8,128)}) %reduce-scatter.5.cloned.1.call-update) | async-done | bytes 2097168 | tf_op jit(solution)/shard_map/reduce_scatter | solution.py:62
  143.0 1.9 copy.51
  145.0 1.0 collective-permute-start.10
  145.9 4.3 scatter_custom_fusion
  150.6 11.0 %reduce-scatter.3.cloned.1.call-done = f32[256,2048]{1,0:T(8,128)} async-done(((f32[512,2048]{1,0:T(8,128)}), f32[256,2048]{1,0:T(8,128)}) %reduce-scatter.3.cloned.1.call-update) | async-done | bytes 2097168 | tf_op jit(solution)/shard_map/reduce_scatter | solution.py:62
  161.6 2.1 fusion.26
  163.7 0.9 collective-permute-start
  164.5 1.2 bitcast_add_fusion.1
  165.7 0.7 reshape.328
  166.4 11.5 %collective-permute-done = bf16[128,2048]{1,0:T(8,128)(2,1)} collective-permute-done((bf16[128,2048]{1,0:T(8,128)(2,1)}, bf16[128,2048]{1,0:T(8,128)(2,1)}, u32[]{:S(2)}, u32[]{:S(2)}) %collective-permute-start) | collective-permute-done | bytes 524320 | tf_op jit(solution)/shard_map/ppermute | solution.py:66
  177.9 1.5 bitcast_add_fusion.2
  179.4 0.7 reshape.325
  181.1 2.0 copy.52
  183.0 2.1 reshape.329
  186.4 3.5 gather_fusion.2
  189.9 10.1 %all-to-all-start = ((bf16[128,128,128]{2,1,0:T(8,128)(2,1)}), bf16[128,128,128]{2,1,0:T(8,128)(2,1)}, u32[]{:S(2)}, u32[]{:S(2)}) async-start(bf16[128,128,128]{2,1,0:T(8,128)(2,1)} %bitcast.100), calls=%async_computation.2 | async-start | bytes 8388608 | tf_op jit(solution)/shard_map/all_to_all | solution.py:115
  200.2 4.1 gather_fusion.4
  204.4 47.5 %all-to-all-done = bf16[128,128,128]{2,1,0:T(8,128)(2,1)} async-done(((bf16[128,128,128]{2,1,0:T(8,128)(2,1)}), bf16[128,128,128]{2,1,0:T(8,128)(2,1)}, u32[]{:S(2)}, u32[]{:S(2)}) %all-to-all-start) | async-done | bytes 4194336 | tf_op jit(solution)/shard_map/all_to_all | solution.py:115
  251.9 8.1 %all-to-all-start.2 = ((bf16[128,160,128]{2,1,0:T(8,128)(2,1)}), bf16[128,160,128]{2,1,0:T(8,128)(2,1)}, u32[]{:S(2)}, u32[]{:S(2)}) async-start(bf16[128,160,128]{2,1,0:T(8,128)(2,1)} %bitcast.99), calls=%async_computation.4 | async-start | bytes 10485760 | tf_op jit(solution)/shard_map/all_to_all | solution.py:115
  260.0 7.3 %reshape.334 = bf16[512,4096]{1,0:T(8,128)(2,1)} reshape(bf16[128,128,128]{2,1,0:T(8,128)(2,1)} %all-to-all-done) | data formatting | bytes 8388608 | tf_op jit(solution)/shard_map/reshape | solution.py:116
  267.3 10.5 %fusion.4 = f32[512,1536]{1,0:T(8,128)S(1)} fusion(bf16[512,4096]{1,0:T(8,128)(2,1)} %reshape.334, bf16[1,4096,1536]{2,1,0:T(8,128)(2,1)} %param.14), kind=kOutput, calls=%fused_computation.13 | convolution fusion | flops 6442450944 | bytes 19922944 | tf_op jit(solution)/shard_map/dot_general | solution.py:17
  277.8 7.9 %fusion.9 = bf16[512,4096]{1,0:T(8,128)(2,1)} fusion(bf16[1,768,4096]{2,1,0:T(8,128)(2,1)} %param.15, f32[512,1536]{1,0:T(8,128)S(1)} %fusion.4), kind=kOutput, calls=%fused_computation.19 | convolution fusion | flops 3225681920 | bytes 13631488 | tf_op jit(solution)/shard_map/dot_general | solution.py:21
  285.7 7.4 %reshape.335 = bf16[128,128,128]{2,1,0:T(8,128)(2,1)} reshape(bf16[512,4096]{1,0:T(8,128)(2,1)} %fusion.9) | data formatting | bytes 8388608 | tf_op jit(solution)/shard_map/reshape | solution.py:117
  293.1 31.5 %all-to-all-done.2 = bf16[128,160,128]{2,1,0:T(8,128)(2,1)} async-done(((bf16[128,160,128]{2,1,0:T(8,128)(2,1)}), bf16[128,160,128]{2,1,0:T(8,128)(2,1)}, u32[]{:S(2)}, u32[]{:S(2)}) %all-to-all-start.2) | async-done | bytes 5242912 | tf_op jit(solution)/shard_map/all_to_all | solution.py:115
  324.6 9.0 %all-to-all-start.1 = ((bf16[128,128,128]{2,1,0:T(8,128)(2,1)}), bf16[128,128,128]{2,1,0:T(8,128)(2,1)}, u32[]{:S(2)}, u32[]{:S(2)}) async-start(bf16[128,128,128]{2,1,0:T(8,128)(2,1)} %reshape.335), calls=%async_computation.3 | async-start | bytes 8388608 | tf_op jit(solution)/shard_map/all_to_all | solution.py:118
  333.6 8.9 %reshape.338 = bf16[640,4096]{1,0:T(8,128)(2,1)} reshape(bf16[128,160,128]{2,1,0:T(8,128)(2,1)} %all-to-all-done.2) | data formatting | bytes 10485760 | tf_op jit(solution)/shard_map/reshape | solution.py:116
  342.5 12.4 %fusion.2 = f32[640,1536]{1,0:T(8,128)S(1)} fusion(bf16[640,4096]{1,0:T(8,128)(2,1)} %reshape.338, bf16[1,4096,1536]{2,1,0:T(8,128)(2,1)} %param.14), kind=kOutput, calls=%fused_computation.11 | convolution fusion | flops 8053063680 | bytes 21757952 | tf_op jit(solution)/shard_map/dot_general | solution.py:17
  354.9 8.9 %convolution_convert_fusion = bf16[640,4096]{1,0:T(8,128)(2,1)} fusion(bf16[1,768,4096]{2,1,0:T(8,128)(2,1)} %param.15, f32[640,1536]{1,0:T(8,128)S(1)} %fusion.2), kind=kOutput, calls=%fused_computation.15 | convolution fusion | flops 4032102400 | bytes 15466496 | tf_op jit(solution)/shard_map/dot_general | solution.py:21
  363.8 8.9 %reshape.339 = bf16[128,160,128]{2,1,0:T(8,128)(2,1)} reshape(bf16[640,4096]{1,0:T(8,128)(2,1)} %convolution_convert_fusion) | data formatting | bytes 10485760 | tf_op jit(solution)/shard_map/reshape | solution.py:117
  372.7 12.9 %all-to-all-done.1 = bf16[128,128,128]{2,1,0:T(8,128)(2,1)} async-done(((bf16[128,128,128]{2,1,0:T(8,128)(2,1)}), bf16[128,128,128]{2,1,0:T(8,128)(2,1)}, u32[]{:S(2)}, u32[]{:S(2)}) %all-to-all-start.1) | async-done | bytes 4194336 | tf_op jit(solution)/shard_map/all_to_all | solution.py:118
  385.6 8.1 %all-to-all-start.3 = ((bf16[128,160,128]{2,1,0:T(8,128)(2,1)}), bf16[128,160,128]{2,1,0:T(8,128)(2,1)}, u32[]{:S(2)}, u32[]{:S(2)}) async-start(bf16[128,160,128]{2,1,0:T(8,128)(2,1)} %reshape.339), calls=%async_computation.5 | async-start | bytes 10485760 | tf_op jit(solution)/shard_map/all_to_all | solution.py:118
  394.1 12.0 %gather_fusion.3 = bf16[1024,32,128]{2,1,0:T(8,128)(2,1)} fusion(bf16[512,32,128]{2,1,0:T(8,128)(2,1)} %bitcast.34, s32[1024]{0:T(1024)S(1)} %broadcast_clamp_fusion.1), kind=kCustom, calls=%fused_computation.3 | custom fusion | bytes 16781312 | tf_op jit(solution)/shard_map/jit(_take)/gather | solution.py:121
  406.1 6.9 %fusion.1 = f32[128,32,128]{2,1,0:T(8,128)} fusion(f32[128,8]{1,0:T(8,128)S(1)} %get-tuple-element.7, bf16[1024,32,128]{2,1,0:T(8,128)(2,1)} %gather_fusion.3), kind=kLoop, calls=%fused_computation.10 | loop fusion | flops 12058624 | bytes 10489856 | tf_op jit(solution)/shard_map/reduce_sum | solution.py:123
  413.0 45.2 %all-to-all-done.3 = bf16[128,160,128]{2,1,0:T(8,128)(2,1)} async-done(((bf16[128,160,128]{2,1,0:T(8,128)(2,1)}), bf16[128,160,128]{2,1,0:T(8,128)(2,1)}, u32[]{:S(2)}, u32[]{:S(2)}) %all-to-all-start.3) | async-done | bytes 5242912 | tf_op jit(solution)/shard_map/all_to_all | solution.py:118
  458.3 12.3 %gather_fusion.5 = bf16[1024,32,128]{2,1,0:T(8,128)(2,1)} fusion(bf16[640,32,128]{2,1,0:T(8,128)(2,1)} %bitcast.38, s32[1024]{0:T(1024)S(1)} %broadcast_clamp_fusion), kind=kCustom, calls=%fused_computation.5 | custom fusion | bytes 16781312 | tf_op jit(solution)/shard_map/jit(_take)/gather | solution.py:121
  470.6 5.8 %fusion = f32[128,32,128]{2,1,0:T(8,128)S(1)} fusion(f32[128,8]{1,0:T(8,128)S(1)} %get-tuple-element.6, bf16[1024,32,128]{2,1,0:T(8,128)(2,1)} %gather_fusion.5), kind=kLoop, calls=%fused_computation.8 | loop fusion | flops 12058624 | bytes 10489856 | tf_op jit(solution)/shard_map/reduce_sum | solution.py:123
  476.9 0.7 copy-done.1
  477.7 2.8 fusion.15
  (84 shorter events, 9.3 us)
Async XLA Ops:
  8.0 30.0 %all-gather.3.cloned.1.call-start = ((), (), s32[]{:S(2)}) async-start(), calls=%async_computation.6 | async-start | bytes 1310720 | tf_op jit(solution)/shard_map/all_gather | solution.py:46
  8.7 117.8 %all-gather.5.cloned.1.call-start = ((), (), s32[]{:S(2)}) async-start(), calls=%async_computation.7 | async-start | bytes 5242880 | tf_op jit(solution)/shard_map/all_gather | solution.py:47
  38.0 105.0 %reduce-scatter.5.cloned.1.call-start = ((), (), s32[]{:S(2)}) async-start(), calls=%async_computation.9 | async-start | bytes 6291456 | tf_op jit(solution)/shard_map/reduce_scatter | solution.py:62
  38.0 9.0 %collective-permute-start.1 = (bf16[1024,128]{1,0:T(8,128)(2,1)}, bf16[1024,128]{1,0:T(8,128)(2,1)S(1)}, u32[]{:S(2)}, u32[]{:S(2)}) collective-permute-start(bf16[1024,128]{1,0:T(8,128)(2,1)} %param.10), channel_id=1, source_target_pairs={{0,16},{16,0},{1,17},{17,1},{2,18},{18,2},{3,19},{19,3},{4,20},{20... | collective-permute-start | bytes 786440 | tf_op jit(solution)/shard_map/ppermute | solution.py:45
  47.0 6.6 %collective-permute-start.2 = (bf16[1024,128]{1,0:T(8,128)(2,1)S(1)}, bf16[1024,128]{1,0:T(8,128)(2,1)S(1)}, u32[]{:S(2)}, u32[]{:S(2)}) collective-permute-start(bf16[1024,128]{1,0:T(8,128)(2,1)S(1)} %collective-permute-done.1), channel_id=1, source_target_pairs={{0,12},{4,0},{8,4},{12,8},{1,13},{5,1},{9,5},{13,9},{2,14},{6,2},{... | collective-permute-start | bytes 786440 | tf_op jit(solution)/shard_map/ppermute | solution.py:30
  47.5 11.9 %collective-permute-start.3 = (bf16[1024,128]{1,0:T(8,128)(2,1)S(1)}, bf16[1024,128]{1,0:T(8,128)(2,1)S(1)}, u32[]{:S(2)}, u32[]{:S(2)}) collective-permute-start(bf16[1024,128]{1,0:T(8,128)(2,1)S(1)} %collective-permute-done.1), channel_id=1, source_target_pairs={{0,4},{4,8},{8,12},{12,0},{1,5},{5,9},{9,13},{13,1},{2,6},{6,10},{... | collective-permute-start | bytes 786440 | tf_op jit(solution)/shard_map/ppermute | solution.py:29
  53.8 13.1 %collective-permute-start.5 = (bf16[1024,64]{1,0:T(8,128)(2,1)S(1)}, bf16[1024,64]{1,0:T(8,128)(2,1)S(1)}, u32[]{:S(2)}, u32[]{:S(2)}) collective-permute-start(bf16[1024,64]{1,0:T(8,128)(2,1)S(1)} %slice.61), channel_id=1, source_target_pairs={{0,12},{4,0},{8,4},{12,8},{1,13},{5,1},{9,5},{13,9},{2,14},{6,2},{... | collective-permute-start | bytes 393224 | tf_op jit(solution)/shard_map/ppermute | solution.py:35
  59.4 14.1 %collective-permute-start.4 = (bf16[1024,64]{1,0:T(8,128)(2,1)S(1)}, bf16[1024,64]{1,0:T(8,128)(2,1)S(1)}, u32[]{:S(2)}, u32[]{:S(2)}) collective-permute-start(bf16[1024,64]{1,0:T(8,128)(2,1)S(1)} %bitcast.117), channel_id=1, source_target_pairs={{0,4},{4,8},{8,12},{12,0},{1,5},{5,9},{9,13},{13,1},{2,6},{6,10},{... | collective-permute-start | bytes 393224 | tf_op jit(solution)/shard_map/ppermute | solution.py:34
  75.7 19.6 %collective-permute-start.6 = (bf16[4,1024,128]{2,1,0:T(8,128)(2,1)}, bf16[4,1024,128]{2,1,0:T(8,128)(2,1)S(1)}, u32[]{:S(2)}, u32[]{:S(2)}) collective-permute-start(bf16[4,1024,128]{2,1,0:T(8,128)(2,1)} %broadcast_select_fusion), channel_id=1, source_target_pairs={{0,96},{32,0},{64,32},{96,64},{1,97},{33,1},{65,33},{97,65},{2,98}... | collective-permute-start | bytes 3145736 | tf_op jit(solution)/shard_map/ppermute | solution.py:30
  75.7 23.2 %collective-permute-start.7 = (bf16[4,1024,128]{2,1,0:T(8,128)(2,1)}, bf16[4,1024,128]{2,1,0:T(8,128)(2,1)S(1)}, u32[]{:S(2)}, u32[]{:S(2)}) collective-permute-start(bf16[4,1024,128]{2,1,0:T(8,128)(2,1)} %broadcast_select_fusion), channel_id=1, source_target_pairs={{0,32},{32,64},{64,96},{96,0},{1,33},{33,65},{65,97},{97,1},{2,34}... | collective-permute-start | bytes 3145736 | tf_op jit(solution)/shard_map/ppermute | solution.py:29
  95.3 1.1 copy-start.3
  97.9 9.4 %collective-permute-start.9 = (bf16[4,1024,64]{1,2,0:T(8,128)(2,1)}, bf16[4,1024,64]{1,2,0:T(8,128)(2,1)S(1)}, u32[]{:S(2)}, u32[]{:S(2)}) collective-permute-start(bf16[4,1024,64]{1,2,0:T(8,128)(2,1)} %copy.47), channel_id=1, source_target_pairs={{0,96},{32,0},{64,32},{96,64},{1,97},{33,1},{65,33},{97,65},{2,98}... | collective-permute-start | bytes 1572872 | tf_op jit(solution)/shard_map/ppermute | solution.py:35
  98.9 3.7 copy-start.4
  99.2 9.4 %collective-permute-start.8 = (bf16[4,1024,64]{1,2,0:T(8,128)(2,1)S(1)}, bf16[4,1024,64]{1,2,0:T(8,128)(2,1)}, u32[]{:S(2)}, u32[]{:S(2)}) collective-permute-start(bf16[4,1024,64]{1,2,0:T(8,128)(2,1)S(1)} %copy.46), channel_id=1, source_target_pairs={{0,32},{32,64},{64,96},{96,0},{1,33},{33,65},{65,97},{97,1},{2,34}... | collective-permute-start | bytes 1572872 | tf_op jit(solution)/shard_map/ppermute | solution.py:34
  114.1 5.3 %copy-start.5 = (bf16[2,2,128,1024]{3,2,1,0:T(8,128)(2,1)S(1)}, bf16[2,2,128,1024]{3,2,1,0:T(8,128)(2,1)}, u32[]{:S(2)}) copy-start(bf16[2,2,128,1024]{3,2,1,0:T(8,128)(2,1)} %copy.44) | copy-start | bytes 3145732
  126.3 35.3 %reduce-scatter.3.cloned.1.call-start = ((), (), s32[]{:S(2)}) async-start(), calls=%async_computation.8 | async-start | bytes 6291456 | tf_op jit(solution)/shard_map/reduce_scatter | solution.py:62
  133.0 0.7 copy-start.7
  145.0 19.6 %collective-permute-start.10 = (bf16[128,2048]{1,0:T(8,128)(2,1)S(1)}, bf16[128,2048]{1,0:T(8,128)(2,1)}, u32[]{:S(2)}, u32[]{:S(2)}) collective-permute-start(bf16[128,2048]{1,0:T(8,128)(2,1)S(1)} %fusion.27), channel_id=1, source_target_pairs={{0,2},{2,0},{1,3},{3,1},{4,6},{6,4},{5,7},{7,5},{8,10},{10,8},{9,1... | collective-permute-start | bytes 1572872 | tf_op jit(solution)/shard_map/ppermute | solution.py:66
  163.7 14.3 %collective-permute-start = (bf16[128,2048]{1,0:T(8,128)(2,1)}, bf16[128,2048]{1,0:T(8,128)(2,1)}, u32[]{:S(2)}, u32[]{:S(2)}) collective-permute-start(bf16[128,2048]{1,0:T(8,128)(2,1)} %fusion.26), channel_id=1, source_target_pairs={{0,2},{2,0},{1,3},{3,1},{4,6},{6,4},{5,7},{7,5},{8,10},{10,8},{9,1... | collective-permute-start | bytes 1572872 | tf_op jit(solution)/shard_map/ppermute | solution.py:66
  181.1 4.1 copy-start
  183.0 2.5 copy-start.6
  189.9 62.0 %all-to-all-start = ((bf16[128,128,128]{2,1,0:T(8,128)(2,1)}), bf16[128,128,128]{2,1,0:T(8,128)(2,1)}, u32[]{:S(2)}, u32[]{:S(2)}) async-start(bf16[128,128,128]{2,1,0:T(8,128)(2,1)} %bitcast.100), calls=%async_computation.2 | async-start | bytes 8388608 | tf_op jit(solution)/shard_map/all_to_all | solution.py:115
  251.9 72.7 %all-to-all-start.2 = ((bf16[128,160,128]{2,1,0:T(8,128)(2,1)}), bf16[128,160,128]{2,1,0:T(8,128)(2,1)}, u32[]{:S(2)}, u32[]{:S(2)}) async-start(bf16[128,160,128]{2,1,0:T(8,128)(2,1)} %bitcast.99), calls=%async_computation.4 | async-start | bytes 10485760 | tf_op jit(solution)/shard_map/all_to_all | solution.py:115
  324.6 61.0 %all-to-all-start.1 = ((bf16[128,128,128]{2,1,0:T(8,128)(2,1)}), bf16[128,128,128]{2,1,0:T(8,128)(2,1)}, u32[]{:S(2)}, u32[]{:S(2)}) async-start(bf16[128,128,128]{2,1,0:T(8,128)(2,1)} %reshape.335), calls=%async_computation.3 | async-start | bytes 8388608 | tf_op jit(solution)/shard_map/all_to_all | solution.py:118
  372.7 21.3 %copy-start.8 = (f32[128,8]{0,1:T(8,128)S(1)}, f32[128,8]{0,1:T(8,128)}, u32[]{:S(2)}) copy-start(f32[128,8]{0,1:T(8,128)} %param.13) | copy-start | bytes 12292
  385.6 72.7 %all-to-all-start.3 = ((bf16[128,160,128]{2,1,0:T(8,128)(2,1)}), bf16[128,160,128]{2,1,0:T(8,128)(2,1)}, u32[]{:S(2)}, u32[]{:S(2)}) async-start(bf16[128,160,128]{2,1,0:T(8,128)(2,1)} %reshape.339), calls=%async_computation.5 | async-start | bytes 10485760 | tf_op jit(solution)/shard_map/all_to_all | solution.py:118
  470.6 5.8 %copy-start.2 = (f32[128,32,128]{2,1,0:T(8,128)S(1)}, f32[128,32,128]{2,1,0:T(8,128)}, u32[]{:S(2)}) copy-start(f32[128,32,128]{2,1,0:T(8,128)} %fusion.1) | copy-start | bytes 6291460
  476.4 1.2 copy-start.1
Sparse Core Ops, SparseCore 0:
  10.6 27.3 all-gather.2
  39.7 54.7 all-gather.4
Sparse Core Ops, SparseCore 1:
  126.4 16.5 reduce-scatter.4
  145.4 16.2 reduce-scatter.2

commit v15 on v13

--- a/solution.py
+++ b/solution.py
@@ -21,7 +21,7 @@
     return jnp.dot(activated, w_down[0], preferred_element_type=jnp.float32).astype(jnp.bfloat16)
 
 
-def ring_gather(block, axis):
+def ring_gather(block, axis, natural=True):
     n = lax.axis_size(axis)
     me = lax.axis_index(axis)
     plus = [(i, (i + 1) % n) for i in range(n)]
@@ -37,6 +37,8 @@
         axis=-1,
     )
     by_step = jnp.stack([block, from_right, far, from_left])
+    if not natural:
+        return by_step
     order = (jnp.arange(n, dtype=jnp.int32) - me) % n
     return jnp.take(by_step, order, axis=0)
 
@@ -46,7 +48,7 @@
     first = lax.all_gather(staged[0], "y", axis=1, tiled=True)
     first = lax.all_gather(first, "z", axis=1, tiled=True)
     second = ring_gather(staged[1], "z")
-    second = ring_gather(second, "y")
+    second = ring_gather(second, "y", natural=False)
     return first, second
 
 
@@ -71,7 +73,7 @@
     by_rings = over_tensor(other.reshape(other.shape[0], -1))
     n_y, n_z = lax.axis_size("y"), lax.axis_size("z")
     by_gathers = by_gathers.reshape(rows, n_z, n_y, -1).transpose(0, 2, 1, 3)
-    by_rings = by_rings.reshape(rows, n_y, n_z, -1)
+    by_rings = jnp.roll(by_rings.reshape(rows, n_y, n_z, -1), lax.axis_index("y"), axis=1)
     return jnp.stack([by_gathers, by_rings], axis=2).reshape(rows, -1)
 
 

time: 484 us -> 476 us (0.983)
  local copies, waits for them, and re-layouts: 97.4 us -> 82.9 us
  waiting for transfers between devices: 233 us -> 247 us
    ppermute x2, waiting for transfers between devices: 0.25 us -> 21.3 us  [ring_gather(): from_left = lax.ppermute(block, axis, perm=plus)]
    ppermute x2, waiting for transfers between devices: 22.8 us -> 5.14 us  [ring_gather(): from_right = lax.ppermute(block, axis, perm=minus)]
    all_to_all x2, waiting for transfers between devices: 58.2 us -> 65.1 us  [on_device(): lax.all_to_all(outputs, ALL, split_axis=0, concat_axis=0, tiled=True)]
    ppermute x2, waiting for transfers between devices: 6.44 us -> 12.4 us  [ring_gather(): lax.ppermute(from_left[..., :half], axis, perm=plus)]
    reduce_sum x2 -> x1, other arithmetic: 12.8 us -> 9.01 us  [on_device(): part = jnp.sum(scaled.reshape(tok_count, top_count, chunks, LANES), axis=1)]
  transfers between devices with their start and end apart: 18 -> 18, of which waited for: 15 -> 15; matrix products, arithmetic and copies ran while one was open for 29% -> 24% of each run, Pallas kernels for 0% -> 0%
where the time goes in v15:
time: 476 us; the launch traced here: 473 us
  waiting for transfers between devices  247 us (52%)
  local copies, waits for them, and re-layouts  82.9 us (17%)
  matrix products  50.3 us (11%)
  starting transfers between devices  45.5 us (10%)
  other arithmetic  21.7 us (5%)
  between operations  16 us (3%)
  blocking collectives  10.4 us (2%)
    all_to_all x2, waiting for transfers between devices, on_device(): lax.all_to_all(send, ALL, split_axis=0, concat_axis=0, tiled=True)  79 us
    all_to_all x2, waiting for transfers between devices, on_device(): lax.all_to_all(outputs, ALL, split_axis=0, concat_axis=0, tiled=True)  65.1 us
    all_gather x1, waiting for transfers between devices, gather_columns(): first = lax.all_gather(staged[0], 'y', axis=1, tiled=True)  27.4 us
    gather x2, local copies, waits for them, and re-layouts, on_device(): picked = jnp.take(returned, chosen * size + slots - lo, axis=0, mode='clip')  24.4 us
    dot_general x2, matrix products, expert_block(): jnp.dot(received, w_gate_up[0], preferred_element_type=jnp.float32)  22.9 us
    ppermute x2, waiting for transfers between devices, ring_gather(): from_left = lax.ppermute(block, axis, perm=plus)  21.3 us
    reduce_scatter x2, waiting for transfers between devices, over_tensor(): lax.psum_scatter(partial_sums, 'core', scatter_dimension=0, tiled=True)  20.6 us
    all_to_all x2, starting transfers between devices, on_device(): lax.all_to_all(send, ALL, split_axis=0, concat_axis=0, tiled=True)  18.2 us
  transfers between devices with their start and end apart: 18, of which 15 were waited for; matrix products, arithmetic and copies ran while one was open for 24% of the time, Pallas kernels for 0%

profile of v15, /device:TPU:54, one launch (start us, length us, event | category | flops | bytes accessed | tf_op | source)
XLA Modules:
  0.0 473.2 jit_solution(11966462215134811360)
XLA Ops:
  8.0 10.4 %all-gather = bf16[2048,128]{1,0:T(8,128)(2,1)S(1)} all-gather(bf16[1024,128]{1,0:T(8,128)(2,1)} %param.10), channel_id=2, replica_groups=mesh['y'=4,'xhi'=2,'z'=4,'xlo'=2,'core'=2] {'xhi'}, dimensions={0}, use_global_device_ids=true | all-gather | bytes 786432 | tf_op jit(solution)/shard_map/all_gather | solution.py:47
  18.5 0.8 fusion.49
  19.3 27.4 %all-gather.8.cloned.1.call-done = bf16[1024,512]{1,0:T(8,128)(2,1)} async-done(((bf16[1024,128]{1,0:T(8,128)(2,1)}), bf16[1024,512]{1,0:T(8,128)(2,1)}) %all-gather.8.cloned.1.call-update) | async-done | bytes 1048592 | tf_op jit(solution)/shard_map/all_gather | solution.py:48
  46.9 0.5 collective-permute-start.1
  47.4 1.6 collective-permute-start.2
  49.0 5.1 %collective-permute-done.1 = bf16[1024,128]{1,0:T(8,128)(2,1)S(1)} collective-permute-done((bf16[1024,128]{1,0:T(8,128)(2,1)S(1)}, bf16[1024,128]{1,0:T(8,128)(2,1)S(1)}, u32[]{:S(2)}, u32[]{:S(2)}) %collective-permute-start.1) | collective-permute-done | bytes 262176 | tf_op jit(solution)/shard_map/ppermute | solution.py:30
  54.3 1.0 collective-permute-start.4
  55.3 0.2 collective-permute-done.2
  55.5 0.8 collective-permute-start.3
  56.4 4.3 collective-permute-done.4
  60.7 5.6 %collective-permute-done.3 = bf16[1024,64]{1,0:T(8,128)(2,1)S(1)} collective-permute-done((bf16[1024,64]{1,0:T(8,128)(2,1)S(1)}, bf16[1024,64]{1,0:T(8,128)(2,1)S(1)}, u32[]{:S(2)}, u32[]{:S(2)}) %collective-permute-start.3) | collective-permute-done | bytes 131104 | tf_op jit(solution)/shard_map/ppermute | solution.py:34
  66.6 0.7 gather_fusion
  67.4 0.5 copy.18
  68.2 2.0 collective-permute-start.5
  70.2 21.1 %collective-permute-done.6 = bf16[4,1024,128]{1,2,0:T(8,128)(2,1)S(1)} collective-permute-done((bf16[4,1024,128]{1,2,0:T(8,128)(2,1)S(1)}, bf16[4,1024,128]{1,2,0:T(8,128)(2,1)S(1)}, u32[]{:S(2)}, u32[]{:S(2)}) %collective-permute-start.6) | collective-permute-done | bytes 1048608 | tf_op jit(solution)/shard_map/ppermute | solution.py:29
  91.4 2.1 collective-permute-start.8
  93.7 6.8 %collective-permute-done.7 = bf16[4,1024,64]{1,2,0:T(8,128)(2,1)S(1)} collective-permute-done((bf16[4,1024,64]{1,2,0:T(8,128)(2,1)S(1)}, bf16[4,1024,64]{1,2,0:T(8,128)(2,1)S(1)}, u32[]{:S(2)}, u32[]{:S(2)}) %collective-permute-start.7) | collective-permute-done | bytes 524320 | tf_op jit(solution)/shard_map/ppermute | solution.py:34
  100.5 0.8 collective-permute-done.8
  101.5 4.0 fusion.12
  105.6 6.6 %fusion.50 = f32[512,2048]{1,0:T(8,128)} fusion(bf16[512,1024]{1,0:T(8,128)(2,1)S(1)} %bitcast.105, bf16[1024,2048]{1,0:T(8,128)(2,1)} %all-gather.10.cloned.1.call-done), kind=kOutput, calls=%fused_computation.108 | convolution fusion | flops 2147483648 | bytes 9437184 | tf_op jit(solution)/shard_map/dot_general | solution.py:71
  112.2 0.6 copy-done.4
  114.3 0.4 fusion.33
  114.6 9.6 %reduce-scatter.5.cloned.1.call-done = f32[256,2048]{0,1:T(8,128)} async-done(((f32[512,2048]{0,1:T(8,128)}), f32[256,2048]{0,1:T(8,128)}) %reduce-scatter.5.cloned.1.call-update) | async-done | bytes 2097168 | tf_op jit(solution)/shard_map/reduce_scatter | solution.py:64
  124.3 1.9 copy.20
  126.3 0.9 collective-permute-start.9
  127.2 4.3 scatter_custom_fusion
  131.9 11.0 %reduce-scatter.3.cloned.1.call-done = f32[256,2048]{1,0:T(8,128)} async-done(((f32[512,2048]{1,0:T(8,128)}), f32[256,2048]{1,0:T(8,128)}) %reduce-scatter.3.cloned.1.call-update) | async-done | bytes 2097168 | tf_op jit(solution)/shard_map/reduce_scatter | solution.py:64
  142.9 2.1 fusion.30
  145.0 0.9 collective-permute-start
  145.8 1.1 bitcast_add_fusion.1
  147.0 0.7 reshape.274
  147.7 1.4 fusion.25
  149.0 10.2 %collective-permute-done = bf16[128,2048]{1,0:T(8,128)(2,1)} collective-permute-done((bf16[128,2048]{1,0:T(8,128)(2,1)}, bf16[128,2048]{1,0:T(8,128)(2,1)}, u32[]{:S(2)}, u32[]{:S(2)}) %collective-permute-start) | collective-permute-done | bytes 524320 | tf_op jit(solution)/shard_map/ppermute | solution.py:68
  159.2 1.5 bitcast_add_fusion.2
  160.7 0.7 reshape.271
  161.5 0.3 copy.35
  161.8 3.2 pad_maximum_fusion
  165.0 2.1 reshape.275
  167.1 0.4 multiply_reduce_fusion
  167.5 0.4 fusion.23
  168.4 3.6 gather_fusion.1
  172.0 10.1 %all-to-all-start = ((bf16[128,128,128]{2,1,0:T(8,128)(2,1)}), bf16[128,128,128]{2,1,0:T(8,128)(2,1)}, u32[]{:S(2)}, u32[]{:S(2)}) async-start(bf16[128,128,128]{2,1,0:T(8,128)(2,1)} %bitcast.94), calls=%async_computation.2 | async-start | bytes 8388608 | tf_op jit(solution)/shard_map/all_to_all | solution.py:114
  182.4 4.1 gather_fusion.3
  186.4 47.6 %all-to-all-done = bf16[128,128,128]{2,1,0:T(8,128)(2,1)} async-done(((bf16[128,128,128]{2,1,0:T(8,128)(2,1)}), bf16[128,128,128]{2,1,0:T(8,128)(2,1)}, u32[]{:S(2)}, u32[]{:S(2)}) %all-to-all-start) | async-done | bytes 4194336 | tf_op jit(solution)/shard_map/all_to_all | solution.py:114
  234.0 8.1 %all-to-all-start.2 = ((bf16[128,160,128]{2,1,0:T(8,128)(2,1)}), bf16[128,160,128]{2,1,0:T(8,128)(2,1)}, u32[]{:S(2)}, u32[]{:S(2)}) async-start(bf16[128,160,128]{2,1,0:T(8,128)(2,1)} %bitcast.93), calls=%async_computation.4 | async-start | bytes 10485760 | tf_op jit(solution)/shard_map/all_to_all | solution.py:114
  242.1 7.3 %reshape.280 = bf16[512,4096]{1,0:T(8,128)(2,1)} reshape(bf16[128,128,128]{2,1,0:T(8,128)(2,1)} %all-to-all-done) | data formatting | bytes 8388608 | tf_op jit(solution)/shard_map/reshape | solution.py:115
  249.4 10.5 %fusion.4 = f32[512,1536]{1,0:T(8,128)S(1)} fusion(bf16[512,4096]{1,0:T(8,128)(2,1)} %reshape.280, bf16[1,4096,1536]{2,1,0:T(8,128)(2,1)} %param.14), kind=kOutput, calls=%fused_computation.12 | convolution fusion | flops 6442450944 | bytes 19922944 | tf_op jit(solution)/shard_map/dot_general | solution.py:17
  259.9 7.9 %fusion.9 = bf16[512,4096]{1,0:T(8,128)(2,1)} fusion(bf16[1,768,4096]{2,1,0:T(8,128)(2,1)} %param.15, f32[512,1536]{1,0:T(8,128)S(1)} %fusion.4), kind=kOutput, calls=%fused_computation.18 | convolution fusion | flops 3225681920 | bytes 13631488 | tf_op jit(solution)/shard_map/dot_general | solution.py:21
  267.8 7.4 %reshape.281 = bf16[128,128,128]{2,1,0:T(8,128)(2,1)} reshape(bf16[512,4096]{1,0:T(8,128)(2,1)} %fusion.9) | data formatting | bytes 8388608 | tf_op jit(solution)/shard_map/reshape | solution.py:116
  275.2 31.5 %all-to-all-done.2 = bf16[128,160,128]{2,1,0:T(8,128)(2,1)} async-done(((bf16[128,160,128]{2,1,0:T(8,128)(2,1)}), bf16[128,160,128]{2,1,0:T(8,128)(2,1)}, u32[]{:S(2)}, u32[]{:S(2)}) %all-to-all-start.2) | async-done | bytes 5242912 | tf_op jit(solution)/shard_map/all_to_all | solution.py:114
  306.7 9.0 %all-to-all-start.1 = ((bf16[128,128,128]{2,1,0:T(8,128)(2,1)}), bf16[128,128,128]{2,1,0:T(8,128)(2,1)}, u32[]{:S(2)}, u32[]{:S(2)}) async-start(bf16[128,128,128]{2,1,0:T(8,128)(2,1)} %reshape.281), calls=%async_computation.3 | async-start | bytes 8388608 | tf_op jit(solution)/shard_map/all_to_all | solution.py:117
  315.7 8.8 %reshape.284 = bf16[640,4096]{1,0:T(8,128)(2,1)} reshape(bf16[128,160,128]{2,1,0:T(8,128)(2,1)} %all-to-all-done.2) | data formatting | bytes 10485760 | tf_op jit(solution)/shard_map/reshape | solution.py:115
  324.6 12.4 %fusion.2 = f32[640,1536]{1,0:T(8,128)S(1)} fusion(bf16[640,4096]{1,0:T(8,128)(2,1)} %reshape.284, bf16[1,4096,1536]{2,1,0:T(8,128)(2,1)} %param.14), kind=kOutput, calls=%fused_computation.10 | convolution fusion | flops 8053063680 | bytes 21757952 | tf_op jit(solution)/shard_map/dot_general | solution.py:17
  337.0 8.8 %convolution_convert_fusion = bf16[640,4096]{1,0:T(8,128)(2,1)} fusion(bf16[1,768,4096]{2,1,0:T(8,128)(2,1)} %param.15, f32[640,1536]{1,0:T(8,128)S(1)} %fusion.2), kind=kOutput, calls=%fused_computation.14 | convolution fusion | flops 4032102400 | bytes 15466496 | tf_op jit(solution)/shard_map/dot_general | solution.py:21
  345.8 8.9 %reshape.285 = bf16[128,160,128]{2,1,0:T(8,128)(2,1)} reshape(bf16[640,4096]{1,0:T(8,128)(2,1)} %convolution_convert_fusion) | data formatting | bytes 10485760 | tf_op jit(solution)/shard_map/reshape | solution.py:116
  354.8 12.9 %all-to-all-done.1 = bf16[128,128,128]{2,1,0:T(8,128)(2,1)} async-done(((bf16[128,128,128]{2,1,0:T(8,128)(2,1)}), bf16[128,128,128]{2,1,0:T(8,128)(2,1)}, u32[]{:S(2)}, u32[]{:S(2)}) %all-to-all-start.1) | async-done | bytes 4194336 | tf_op jit(solution)/shard_map/all_to_all | solution.py:117
  367.7 8.1 %all-to-all-start.3 = ((bf16[128,160,128]{2,1,0:T(8,128)(2,1)}), bf16[128,160,128]{2,1,0:T(8,128)(2,1)}, u32[]{:S(2)}, u32[]{:S(2)}) async-start(bf16[128,160,128]{2,1,0:T(8,128)(2,1)} %reshape.285), calls=%async_computation.5 | async-start | bytes 10485760 | tf_op jit(solution)/shard_map/all_to_all | solution.py:117
  376.1 12.0 %gather_fusion.2 = bf16[1024,32,128]{2,1,0:T(8,128)(2,1)} fusion(bf16[512,32,128]{2,1,0:T(8,128)(2,1)} %bitcast.33, s32[1024]{0:T(1024)S(1)} %broadcast_clamp_fusion.1), kind=kCustom, calls=%fused_computation.2 | custom fusion | bytes 16781312 | tf_op jit(solution)/shard_map/jit(_take)/gather | solution.py:120
  388.2 52.2 %all-to-all-done.3 = bf16[128,160,128]{2,1,0:T(8,128)(2,1)} async-done(((bf16[128,160,128]{2,1,0:T(8,128)(2,1)}), bf16[128,160,128]{2,1,0:T(8,128)(2,1)}, u32[]{:S(2)}, u32[]{:S(2)}) %all-to-all-start.3) | async-done | bytes 5242912 | tf_op jit(solution)/shard_map/all_to_all | solution.py:117
  440.4 12.4 %gather_fusion.4 = bf16[1024,32,128]{2,1,0:T(8,128)(2,1)} fusion(bf16[640,32,128]{2,1,0:T(8,128)(2,1)} %bitcast.37, s32[1024]{0:T(1024)S(1)} %broadcast_clamp_fusion), kind=kCustom, calls=%fused_computation.4 | custom fusion | bytes 16781312 | tf_op jit(solution)/shard_map/jit(_take)/gather | solution.py:120
  452.7 9.0 %fusion = (f32[128,32,128]{2,1,0:T(8,128)S(1)}, f32[128,32,128]{2,1,0:T(8,128)S(1)}) fusion(f32[128,8]{1,0:T(8,128)S(1)} %get-tuple-element.7, bf16[1024,32,128]{2,1,0:T(8,128)(2,1)} %gather_fusion.4, bf16[1024,32,128]{2,1,0:T(8,128)(2,1)} %gather_fusion.2, f32[128,8]{1,0:T(8,128)S(1)} %get-tuple-element.8), kind=kLoop, calls=%fused_computation.7 | loop fusion | flops 24117248 | bytes 20979712 | tf_op jit(solution)/shard_map/reduce_sum | solution.py:122
  461.8 0.5 add.168
  462.3 0.7 copy-done.1
  463.0 2.8 fusion.20
  (71 shorter events, 4.2 us)
Async XLA Ops:
  8.0 38.8 %all-gather.8.cloned.1.call-start = ((), (), s32[]{:S(2)}) async-start(), calls=%async_computation.8 | async-start | bytes 1310720 | tf_op jit(solution)/shard_map/all_gather | solution.py:48
  19.3 86.3 %all-gather.10.cloned.1.call-start = ((), (), s32[]{:S(2)}) async-start(), calls=%async_computation.9 | async-start | bytes 5242880 | tf_op jit(solution)/shard_map/all_gather | solution.py:49
  46.8 77.5 %reduce-scatter.5.cloned.1.call-start = ((), (), s32[]{:S(2)}) async-start(), calls=%async_computation.7 | async-start | bytes 6291456 | tf_op jit(solution)/shard_map/reduce_scatter | solution.py:64
  46.9 7.2 %collective-permute-start.1 = (bf16[1024,128]{1,0:T(8,128)(2,1)S(1)}, bf16[1024,128]{1,0:T(8,128)(2,1)S(1)}, u32[]{:S(2)}, u32[]{:S(2)}) collective-permute-start(bf16[1024,128]{1,0:T(8,128)(2,1)S(1)} %get-tuple-element.6), channel_id=1, source_target_pairs={{0,12},{4,0},{8,4},{12,8},{1,13},{5,1},{9,5},{13,9},{2,14},{6,2},{... | collective-permute-start | bytes 786440 | tf_op jit(solution)/shard_map/ppermute | solution.py:30
  47.4 8.1 %collective-permute-start.2 = (bf16[1024,128]{1,0:T(8,128)(2,1)S(1)}, bf16[1024,128]{1,0:T(8,128)(2,1)S(1)}, u32[]{:S(2)}, u32[]{:S(2)}) collective-permute-start(bf16[1024,128]{1,0:T(8,128)(2,1)S(1)} %get-tuple-element.6), channel_id=1, source_target_pairs={{0,4},{4,8},{8,12},{12,0},{1,5},{5,9},{9,13},{13,1},{2,6},{6,10},{... | collective-permute-start | bytes 786440 | tf_op jit(solution)/shard_map/ppermute | solution.py:29
  54.3 6.4 %collective-permute-start.4 = (bf16[1024,64]{1,0:T(8,128)(2,1)S(1)}, bf16[1024,64]{1,0:T(8,128)(2,1)S(1)}, u32[]{:S(2)}, u32[]{:S(2)}) collective-permute-start(bf16[1024,64]{1,0:T(8,128)(2,1)S(1)} %slice.71), channel_id=1, source_target_pairs={{0,12},{4,0},{8,4},{12,8},{1,13},{5,1},{9,5},{13,9},{2,14},{6,2},{... | collective-permute-start | bytes 393224 | tf_op jit(solution)/shard_map/ppermute | solution.py:35
  55.5 10.8 %collective-permute-start.3 = (bf16[1024,64]{1,0:T(8,128)(2,1)S(1)}, bf16[1024,64]{1,0:T(8,128)(2,1)S(1)}, u32[]{:S(2)}, u32[]{:S(2)}) collective-permute-start(bf16[1024,64]{1,0:T(8,128)(2,1)S(1)} %bitcast.110), channel_id=1, source_target_pairs={{0,4},{4,8},{8,12},{12,0},{1,5},{5,9},{9,13},{13,1},{2,6},{6,10},{... | collective-permute-start | bytes 393224 | tf_op jit(solution)/shard_map/ppermute | solution.py:34
  66.6 26.9 %copy-start.2 = (bf16[512,1024]{1,0:T(8,128)(2,1)S(1)}, bf16[512,1024]{1,0:T(8,128)(2,1)}, u32[]{:S(2)}) copy-start(bf16[512,1024]{1,0:T(8,128)(2,1)} %param.9) | copy-start | bytes 3145732
  68.1 23.2 %collective-permute-start.6 = (bf16[4,1024,128]{1,2,0:T(8,128)(2,1)S(1)}, bf16[4,1024,128]{1,2,0:T(8,128)(2,1)S(1)}, u32[]{:S(2)}, u32[]{:S(2)}) collective-permute-start(bf16[4,1024,128]{1,2,0:T(8,128)(2,1)S(1)} %broadcast_select_fusion), channel_id=1, source_target_pairs={{0,32},{32,64},{64,96},{96,0},{1,33},{33,65},{65,97},{97,1},{2,34}... | collective-permute-start | bytes 3145736 | tf_op jit(solution)/shard_map/ppermute | solution.py:29
  68.2 23.2 %collective-permute-start.5 = (bf16[4,1024,128]{1,2,0:T(8,128)(2,1)S(1)}, bf16[4,1024,128]{1,2,0:T(8,128)(2,1)S(1)}, u32[]{:S(2)}, u32[]{:S(2)}) collective-permute-start(bf16[4,1024,128]{1,2,0:T(8,128)(2,1)S(1)} %broadcast_select_fusion), channel_id=1, source_target_pairs={{0,96},{32,0},{64,32},{96,64},{1,97},{33,1},{65,33},{97,65},{2,98}... | collective-permute-start | bytes 3145736 | tf_op jit(solution)/shard_map/ppermute | solution.py:30
  91.3 9.2 %collective-permute-start.7 = (bf16[4,1024,64]{1,2,0:T(8,128)(2,1)S(1)}, bf16[4,1024,64]{1,2,0:T(8,128)(2,1)S(1)}, u32[]{:S(2)}, u32[]{:S(2)}) collective-permute-start(bf16[4,1024,64]{1,2,0:T(8,128)(2,1)S(1)} %slice.72), channel_id=1, source_target_pairs={{0,32},{32,64},{64,96},{96,0},{1,33},{33,65},{65,97},{97,1},{2,34}... | collective-permute-start | bytes 1572872 | tf_op jit(solution)/shard_map/ppermute | solution.py:34
  91.4 10.0 %collective-permute-start.8 = (bf16[4,1024,64]{1,2,0:T(8,128)(2,1)S(1)}, bf16[4,1024,64]{1,2,0:T(8,128)(2,1)S(1)}, u32[]{:S(2)}, u32[]{:S(2)}) collective-permute-start(bf16[4,1024,64]{1,2,0:T(8,128)(2,1)S(1)} %slice.73), channel_id=1, source_target_pairs={{0,96},{32,0},{64,32},{96,64},{1,97},{33,1},{65,33},{97,65},{2,98}... | collective-permute-start | bytes 1572872 | tf_op jit(solution)/shard_map/ppermute | solution.py:35
  105.5 37.4 %reduce-scatter.3.cloned.1.call-start = ((), (), s32[]{:S(2)}) async-start(), calls=%async_computation.6 | async-start | bytes 6291456 | tf_op jit(solution)/shard_map/reduce_scatter | solution.py:64
  112.2 0.7 copy-start.4
  126.3 19.5 %collective-permute-start.9 = (bf16[128,2048]{1,0:T(8,128)(2,1)S(1)}, bf16[128,2048]{1,0:T(8,128)(2,1)}, u32[]{:S(2)}, u32[]{:S(2)}) collective-permute-start(bf16[128,2048]{1,0:T(8,128)(2,1)S(1)} %fusion.31), channel_id=1, source_target_pairs={{0,2},{2,0},{1,3},{3,1},{4,6},{6,4},{5,7},{7,5},{8,10},{10,8},{9,1... | collective-permute-start | bytes 1572872 | tf_op jit(solution)/shard_map/ppermute | solution.py:68
  145.0 14.3 %collective-permute-start = (bf16[128,2048]{1,0:T(8,128)(2,1)}, bf16[128,2048]{1,0:T(8,128)(2,1)}, u32[]{:S(2)}, u32[]{:S(2)}) collective-permute-start(bf16[128,2048]{1,0:T(8,128)(2,1)} %fusion.30), channel_id=1, source_target_pairs={{0,2},{2,0},{1,3},{3,1},{4,6},{6,4},{5,7},{7,5},{8,10},{10,8},{9,1... | collective-permute-start | bytes 1572872 | tf_op jit(solution)/shard_map/ppermute | solution.py:68
  161.7 5.4 %copy-start = (bf16[128,4096]{1,0:T(8,128)(2,1)S(1)}, bf16[128,4096]{1,0:T(8,128)(2,1)}, u32[]{:S(2)}) copy-start(bf16[128,4096]{1,0:T(8,128)(2,1)} %param.8) | copy-start | bytes 3145732
  165.0 2.5 copy-start.3
  172.0 62.0 %all-to-all-start = ((bf16[128,128,128]{2,1,0:T(8,128)(2,1)}), bf16[128,128,128]{2,1,0:T(8,128)(2,1)}, u32[]{:S(2)}, u32[]{:S(2)}) async-start(bf16[128,128,128]{2,1,0:T(8,128)(2,1)} %bitcast.94), calls=%async_computation.2 | async-start | bytes 8388608 | tf_op jit(solution)/shard_map/all_to_all | solution.py:114
  234.0 72.7 %all-to-all-start.2 = ((bf16[128,160,128]{2,1,0:T(8,128)(2,1)}), bf16[128,160,128]{2,1,0:T(8,128)(2,1)}, u32[]{:S(2)}, u32[]{:S(2)}) async-start(bf16[128,160,128]{2,1,0:T(8,128)(2,1)} %bitcast.93), calls=%async_computation.4 | async-start | bytes 10485760 | tf_op jit(solution)/shard_map/all_to_all | solution.py:114
  306.7 61.0 %all-to-all-start.1 = ((bf16[128,128,128]{2,1,0:T(8,128)(2,1)}), bf16[128,128,128]{2,1,0:T(8,128)(2,1)}, u32[]{:S(2)}, u32[]{:S(2)}) async-start(bf16[128,128,128]{2,1,0:T(8,128)(2,1)} %reshape.281), calls=%async_computation.3 | async-start | bytes 8388608 | tf_op jit(solution)/shard_map/all_to_all | solution.py:117
  354.8 21.2 %copy-start.5 = (f32[128,8]{0,1:T(8,128)S(1)}, f32[128,8]{0,1:T(8,128)}, u32[]{:S(2)}) copy-start(f32[128,8]{0,1:T(8,128)} %param.13) | copy-start | bytes 12292
  367.7 72.7 %all-to-all-start.3 = ((bf16[128,160,128]{2,1,0:T(8,128)(2,1)}), bf16[128,160,128]{2,1,0:T(8,128)(2,1)}, u32[]{:S(2)}, u32[]{:S(2)}) async-start(bf16[128,160,128]{2,1,0:T(8,128)(2,1)} %reshape.285), calls=%async_computation.5 | async-start | bytes 10485760 | tf_op jit(solution)/shard_map/all_to_all | solution.py:117
  461.8 1.2 copy-start.1
Sparse Core Ops, SparseCore 0:
  19.4 27.3 all-gather.7
  48.6 48.9 all-gather.9
Sparse Core Ops, SparseCore 1:
  105.6 18.6 reduce-scatter.4
  126.7 16.1 reduce-scatter.2

commit v16 on v15

--- a/solution.py
+++ b/solution.py
@@ -47,7 +47,7 @@
     staged = lax.all_gather(w_out, "xhi", axis=0)
     first = lax.all_gather(staged[0], "y", axis=1, tiled=True)
     first = lax.all_gather(first, "z", axis=1, tiled=True)
-    second = ring_gather(staged[1], "z")
+    second = ring_gather(staged[1], "z", natural=False)
     second = ring_gather(second, "y", natural=False)
     return first, second
 
@@ -74,6 +74,7 @@
     n_y, n_z = lax.axis_size("y"), lax.axis_size("z")
     by_gathers = by_gathers.reshape(rows, n_z, n_y, -1).transpose(0, 2, 1, 3)
     by_rings = jnp.roll(by_rings.reshape(rows, n_y, n_z, -1), lax.axis_index("y"), axis=1)
+    by_rings = jnp.roll(by_rings, lax.axis_index("z"), axis=2)
     return jnp.stack([by_gathers, by_rings], axis=2).reshape(rows, -1)
 
 

time: 476 us -> 468 us (0.983)
  waiting for transfers between devices: 247 us -> 239 us
    ppermute x2, waiting for transfers between devices: 5.14 us -> 0.01 us  [ring_gather(): from_right = lax.ppermute(block, axis, perm=minus)]
    ppermute x2, waiting for transfers between devices: 21.3 us -> 26.3 us  [ring_gather(): from_left = lax.ppermute(block, axis, perm=plus)]
  transfers between devices with their start and end apart: 18 -> 18, of which waited for: 15 -> 14; matrix products, arithmetic and copies ran while one was open for 24% -> 25% of each run, Pallas kernels for 0% -> 0%
where the time goes in v16:
time: 468 us; the launch traced here: 466 us
  waiting for transfers between devices  239 us (51%)
  local copies, waits for them, and re-layouts  82.4 us (18%)
  matrix products  50.3 us (11%)
  starting transfers between devices  45.8 us (10%)
  other arithmetic  21.7 us (5%)
  between operations  16 us (3%)
  blocking collectives  10.2 us (2%)
    all_to_all x2, waiting for transfers between devices, on_device(): lax.all_to_all(send, ALL, split_axis=0, concat_axis=0, tiled=True)  79.1 us
    all_to_all x2, waiting for transfers between devices, on_device(): lax.all_to_all(outputs, ALL, split_axis=0, concat_axis=0, tiled=True)  65.2 us
    ppermute x2, waiting for transfers between devices, ring_gather(): from_left = lax.ppermute(block, axis, perm=plus)  26.3 us
    all_gather x1, waiting for transfers between devices, gather_columns(): first = lax.all_gather(staged[0], 'y', axis=1, tiled=True)  24.9 us
    gather x2, local copies, waits for them, and re-layouts, on_device(): picked = jnp.take(returned, chosen * size + slots - lo, axis=0, mode='clip')  24.3 us
    dot_general x2, matrix products, expert_block(): jnp.dot(received, w_gate_up[0], preferred_element_type=jnp.float32)  22.9 us
    reduce_scatter x2, waiting for transfers between devices, over_tensor(): lax.psum_scatter(partial_sums, 'core', scatter_dimension=0, tiled=True)  21.8 us
    all_to_all x2, starting transfers between devices, on_device(): lax.all_to_all(send, ALL, split_axis=0, concat_axis=0, tiled=True)  18.2 us
  transfers between devices with their start and end apart: 18, of which 14 were waited for; matrix products, arithmetic and copies ran while one was open for 25% of the time, Pallas kernels for 0%

profile of v16, /device:TPU:54, one launch (start us, length us, event | category | flops | bytes accessed | tf_op | source)
XLA Modules:
  0.0 465.6 jit_solution(13476516137991773978)
XLA Ops:
  8.0 1.1 copy.18
  9.1 10.2 %all-gather = bf16[2048,128]{0,1:T(8,128)(2,1)S(1)} all-gather(bf16[1024,128]{0,1:T(8,128)(2,1)S(1)} %copy.18), channel_id=2, replica_groups=mesh['y'=4,'xhi'=2,'z'=4,'xlo'=2,'core'=2] {'xhi'}, dimensions={0}, use_global_device_ids=true | all-gather | bytes 786432 | tf_op jit(solution)/shard_map/all_gather | solution.py:47
  19.4 0.8 fusion.48
  20.2 24.9 %all-gather.8.cloned.1.call-done = bf16[1024,512]{0,1:T(8,128)(2,1)} async-done(((bf16[1024,128]{0,1:T(8,128)(2,1)}), bf16[1024,512]{0,1:T(8,128)(2,1)}) %all-gather.8.cloned.1.call-update) | async-done | bytes 1048592 | tf_op jit(solution)/shard_map/all_gather | solution.py:48
  45.2 1.6 collective-permute-start.2
  46.8 0.5 collective-permute-start.1
  47.3 5.2 %collective-permute-done.2 = bf16[1024,128]{0,1:T(8,128)(2,1)S(1)} collective-permute-done((bf16[1024,128]{0,1:T(8,128)(2,1)S(1)}, bf16[1024,128]{0,1:T(8,128)(2,1)S(1)}, u32[]{:S(2)}, u32[]{:S(2)}) %collective-permute-start.2) | collective-permute-done | bytes 262176 | tf_op jit(solution)/shard_map/ppermute | solution.py:29
  52.5 1.6 collective-permute-start.3
  54.1 0.5 collective-permute-start.4
  54.7 2.9 collective-permute-done.3
  57.5 1.6 collective-permute-done.4
  59.4 0.9 collective-permute-start.6
  60.3 1.2 collective-permute-start.5
  61.5 21.1 %collective-permute-done.6 = bf16[4,1024,128]{1,2,0:T(8,128)(2,1)S(1)} collective-permute-done((bf16[4,1024,128]{1,2,0:T(8,128)(2,1)S(1)}, bf16[4,1024,128]{1,2,0:T(8,128)(2,1)S(1)}, u32[]{:S(2)}, u32[]{:S(2)}) %collective-permute-start.6) | collective-permute-done | bytes 1048608 | tf_op jit(solution)/shard_map/ppermute | solution.py:29
  82.6 0.8 collective-permute-start.7
  83.4 1.4 collective-permute-start.8
  84.9 7.5 %collective-permute-done.7 = bf16[4,1024,64]{1,2,0:T(8,128)(2,1)S(1)} collective-permute-done((bf16[4,1024,64]{1,2,0:T(8,128)(2,1)S(1)}, bf16[4,1024,64]{1,2,0:T(8,128)(2,1)S(1)}, u32[]{:S(2)}, u32[]{:S(2)}) %collective-permute-start.7) | collective-permute-done | bytes 524320 | tf_op jit(solution)/shard_map/ppermute | solution.py:34
  92.4 0.5 collective-permute-done.8
  93.0 4.0 fusion.12
  97.1 6.6 %fusion.49 = f32[512,2048]{1,0:T(8,128)} fusion(bf16[512,1024]{1,0:T(8,128)(2,1)S(1)} %bitcast.102, bf16[1024,2048]{0,1:T(8,128)(2,1)} %all-gather.10.cloned.1.call-done), kind=kOutput, calls=%fused_computation.96 | convolution fusion | flops 2147483648 | bytes 9437184 | tf_op jit(solution)/shard_map/dot_general | solution.py:71
  103.7 0.6 copy-done.5
  105.8 0.4 fusion.34
  106.1 10.9 %reduce-scatter.5.cloned.1.call-done = f32[256,2048]{0,1:T(8,128)} async-done(((f32[512,2048]{0,1:T(8,128)}), f32[256,2048]{0,1:T(8,128)}) %reduce-scatter.5.cloned.1.call-update) | async-done | bytes 2097168 | tf_op jit(solution)/shard_map/reduce_scatter | solution.py:64
  117.0 1.9 copy.20
  119.0 1.0 collective-permute-start.9
  120.0 4.3 scatter_custom_fusion
  124.7 11.0 %reduce-scatter.3.cloned.1.call-done = f32[256,2048]{1,0:T(8,128)} async-done(((f32[512,2048]{1,0:T(8,128)}), f32[256,2048]{1,0:T(8,128)}) %reduce-scatter.3.cloned.1.call-update) | async-done | bytes 2097168 | tf_op jit(solution)/shard_map/reduce_scatter | solution.py:64
  135.6 2.1 fusion.31
  137.7 0.8 collective-permute-start
  138.6 1.1 bitcast_add_fusion.1
  139.7 0.7 reshape.213
  140.4 0.4 fusion.26
  140.8 1.7 fusion.25
  142.6 9.4 %collective-permute-done = bf16[128,2048]{1,0:T(8,128)(2,1)} collective-permute-done((bf16[128,2048]{1,0:T(8,128)(2,1)}, bf16[128,2048]{1,0:T(8,128)(2,1)}, u32[]{:S(2)}, u32[]{:S(2)}) %collective-permute-start) | collective-permute-done | bytes 524320 | tf_op jit(solution)/shard_map/ppermute | solution.py:68
  152.0 1.2 bitcast_add_fusion.2
  153.2 0.7 reshape.210
  154.2 3.2 pad_maximum_fusion
  157.4 2.1 reshape.214
  159.5 0.4 multiply_reduce_fusion
  159.9 0.4 fusion.23
  160.8 3.6 gather_fusion
  164.4 10.1 %all-to-all-start = ((bf16[128,128,128]{2,1,0:T(8,128)(2,1)}), bf16[128,128,128]{2,1,0:T(8,128)(2,1)}, u32[]{:S(2)}, u32[]{:S(2)}) async-start(bf16[128,128,128]{2,1,0:T(8,128)(2,1)} %bitcast.91), calls=%async_computation.2 | async-start | bytes 8388608 | tf_op jit(solution)/shard_map/all_to_all | solution.py:115
  174.8 4.1 gather_fusion.2
  178.9 47.6 %all-to-all-done = bf16[128,128,128]{2,1,0:T(8,128)(2,1)} async-done(((bf16[128,128,128]{2,1,0:T(8,128)(2,1)}), bf16[128,128,128]{2,1,0:T(8,128)(2,1)}, u32[]{:S(2)}, u32[]{:S(2)}) %all-to-all-start) | async-done | bytes 4194336 | tf_op jit(solution)/shard_map/all_to_all | solution.py:115
  226.4 8.1 %all-to-all-start.2 = ((bf16[128,160,128]{2,1,0:T(8,128)(2,1)}), bf16[128,160,128]{2,1,0:T(8,128)(2,1)}, u32[]{:S(2)}, u32[]{:S(2)}) async-start(bf16[128,160,128]{2,1,0:T(8,128)(2,1)} %bitcast.90), calls=%async_computation.4 | async-start | bytes 10485760 | tf_op jit(solution)/shard_map/all_to_all | solution.py:115
  234.6 7.3 %reshape.219 = bf16[512,4096]{1,0:T(8,128)(2,1)} reshape(bf16[128,128,128]{2,1,0:T(8,128)(2,1)} %all-to-all-done) | data formatting | bytes 8388608 | tf_op jit(solution)/shard_map/reshape | solution.py:116
  241.9 10.5 %fusion.4 = f32[512,1536]{1,0:T(8,128)S(1)} fusion(bf16[512,4096]{1,0:T(8,128)(2,1)} %reshape.219, bf16[1,4096,1536]{2,1,0:T(8,128)(2,1)} %param.14), kind=kOutput, calls=%fused_computation.11 | convolution fusion | flops 6442450944 | bytes 19922944 | tf_op jit(solution)/shard_map/dot_general | solution.py:17
  252.4 7.9 %fusion.9 = bf16[512,4096]{1,0:T(8,128)(2,1)} fusion(bf16[1,768,4096]{2,1,0:T(8,128)(2,1)} %param.15, f32[512,1536]{1,0:T(8,128)S(1)} %fusion.4), kind=kOutput, calls=%fused_computation.17 | convolution fusion | flops 3225681920 | bytes 13631488 | tf_op jit(solution)/shard_map/dot_general | solution.py:21
  260.3 7.4 %reshape.220 = bf16[128,128,128]{2,1,0:T(8,128)(2,1)} reshape(bf16[512,4096]{1,0:T(8,128)(2,1)} %fusion.9) | data formatting | bytes 8388608 | tf_op jit(solution)/shard_map/reshape | solution.py:117
  267.7 31.5 %all-to-all-done.2 = bf16[128,160,128]{2,1,0:T(8,128)(2,1)} async-done(((bf16[128,160,128]{2,1,0:T(8,128)(2,1)}), bf16[128,160,128]{2,1,0:T(8,128)(2,1)}, u32[]{:S(2)}, u32[]{:S(2)}) %all-to-all-start.2) | async-done | bytes 5242912 | tf_op jit(solution)/shard_map/all_to_all | solution.py:115
  299.1 9.0 %all-to-all-start.1 = ((bf16[128,128,128]{2,1,0:T(8,128)(2,1)}), bf16[128,128,128]{2,1,0:T(8,128)(2,1)}, u32[]{:S(2)}, u32[]{:S(2)}) async-start(bf16[128,128,128]{2,1,0:T(8,128)(2,1)} %reshape.220), calls=%async_computation.3 | async-start | bytes 8388608 | tf_op jit(solution)/shard_map/all_to_all | solution.py:118
  308.2 8.8 %reshape.223 = bf16[640,4096]{1,0:T(8,128)(2,1)} reshape(bf16[128,160,128]{2,1,0:T(8,128)(2,1)} %all-to-all-done.2) | data formatting | bytes 10485760 | tf_op jit(solution)/shard_map/reshape | solution.py:116
  317.0 12.4 %fusion.2 = f32[640,1536]{1,0:T(8,128)S(1)} fusion(bf16[640,4096]{1,0:T(8,128)(2,1)} %reshape.223, bf16[1,4096,1536]{2,1,0:T(8,128)(2,1)} %param.14), kind=kOutput, calls=%fused_computation.9 | convolution fusion | flops 8053063680 | bytes 21757952 | tf_op jit(solution)/shard_map/dot_general | solution.py:17
  329.4 8.8 %convolution_convert_fusion = bf16[640,4096]{1,0:T(8,128)(2,1)} fusion(bf16[1,768,4096]{2,1,0:T(8,128)(2,1)} %param.15, f32[640,1536]{1,0:T(8,128)S(1)} %fusion.2), kind=kOutput, calls=%fused_computation.13 | convolution fusion | flops 4032102400 | bytes 15466496 | tf_op jit(solution)/shard_map/dot_general | solution.py:21
  338.3 8.9 %reshape.224 = bf16[128,160,128]{2,1,0:T(8,128)(2,1)} reshape(bf16[640,4096]{1,0:T(8,128)(2,1)} %convolution_convert_fusion) | data formatting | bytes 10485760 | tf_op jit(solution)/shard_map/reshape | solution.py:117
  347.2 13.0 %all-to-all-done.1 = bf16[128,128,128]{2,1,0:T(8,128)(2,1)} async-done(((bf16[128,128,128]{2,1,0:T(8,128)(2,1)}), bf16[128,128,128]{2,1,0:T(8,128)(2,1)}, u32[]{:S(2)}, u32[]{:S(2)}) %all-to-all-start.1) | async-done | bytes 4194336 | tf_op jit(solution)/shard_map/all_to_all | solution.py:118
  360.1 8.1 %all-to-all-start.3 = ((bf16[128,160,128]{2,1,0:T(8,128)(2,1)}), bf16[128,160,128]{2,1,0:T(8,128)(2,1)}, u32[]{:S(2)}, u32[]{:S(2)}) async-start(bf16[128,160,128]{2,1,0:T(8,128)(2,1)} %reshape.224), calls=%async_computation.5 | async-start | bytes 10485760 | tf_op jit(solution)/shard_map/all_to_all | solution.py:118
  368.6 12.0 %gather_fusion.1 = bf16[1024,32,128]{2,1,0:T(8,128)(2,1)} fusion(bf16[512,32,128]{2,1,0:T(8,128)(2,1)} %bitcast.32, s32[1024]{0:T(1024)S(1)} %broadcast_clamp_fusion.1), kind=kCustom, calls=%fused_computation.1 | custom fusion | bytes 16781312 | tf_op jit(solution)/shard_map/jit(_take)/gather | solution.py:121
  380.6 52.2 %all-to-all-done.3 = bf16[128,160,128]{2,1,0:T(8,128)(2,1)} async-done(((bf16[128,160,128]{2,1,0:T(8,128)(2,1)}), bf16[128,160,128]{2,1,0:T(8,128)(2,1)}, u32[]{:S(2)}, u32[]{:S(2)}) %all-to-all-start.3) | async-done | bytes 5242912 | tf_op jit(solution)/shard_map/all_to_all | solution.py:118
  432.8 12.3 %gather_fusion.3 = bf16[1024,32,128]{2,1,0:T(8,128)(2,1)} fusion(bf16[640,32,128]{2,1,0:T(8,128)(2,1)} %bitcast.36, s32[1024]{0:T(1024)S(1)} %broadcast_clamp_fusion), kind=kCustom, calls=%fused_computation.3 | custom fusion | bytes 16781312 | tf_op jit(solution)/shard_map/jit(_take)/gather | solution.py:121
  445.2 9.0 %fusion = (f32[128,32,128]{2,1,0:T(8,128)S(1)}, f32[128,32,128]{2,1,0:T(8,128)S(1)}) fusion(f32[128,8]{1,0:T(8,128)S(1)} %get-tuple-element.9, bf16[1024,32,128]{2,1,0:T(8,128)(2,1)} %gather_fusion.3, bf16[1024,32,128]{2,1,0:T(8,128)(2,1)} %gather_fusion.1, f32[128,8]{1,0:T(8,128)S(1)} %get-tuple-element.10), kind=kLoop, calls=%fused_computation.6 | loop fusion | flops 24117248 | bytes 20979712 | tf_op jit(solution)/shard_map/reduce_sum | solution.py:123
  454.2 0.5 add.143
  454.7 0.7 copy-done.1
  455.4 2.8 fusion.20
  (69 shorter events, 3.8 us)
Async XLA Ops:
  8.0 37.1 %all-gather.8.cloned.1.call-start = ((), (), s32[]{:S(2)}) async-start(), calls=%async_computation.8 | async-start | bytes 1310720 | tf_op jit(solution)/shard_map/all_gather | solution.py:48
  19.4 65.4 %copy-start.3 = (bf16[512,1024]{1,0:T(8,128)(2,1)S(1)}, bf16[512,1024]{1,0:T(8,128)(2,1)}, u32[]{:S(2)}) copy-start(bf16[512,1024]{1,0:T(8,128)(2,1)} %param.9) | copy-start | bytes 3145732
  20.2 76.9 %all-gather.10.cloned.1.call-start = ((), (), s32[]{:S(2)}) async-start(), calls=%async_computation.9 | async-start | bytes 5242880 | tf_op jit(solution)/shard_map/all_gather | solution.py:49
  45.2 71.9 %reduce-scatter.5.cloned.1.call-start = ((), (), s32[]{:S(2)}) async-start(), calls=%async_computation.7 | async-start | bytes 6291456 | tf_op jit(solution)/shard_map/reduce_scatter | solution.py:64
  45.2 7.3 %collective-permute-start.2 = (bf16[1024,128]{0,1:T(8,128)(2,1)S(1)}, bf16[1024,128]{0,1:T(8,128)(2,1)S(1)}, u32[]{:S(2)}, u32[]{:S(2)}) collective-permute-start(bf16[1024,128]{0,1:T(8,128)(2,1)S(1)} %get-tuple-element.8), channel_id=1, source_target_pairs={{0,4},{4,8},{8,12},{12,0},{1,5},{5,9},{9,13},{13,1},{2,6},{6,10},{... | collective-permute-start | bytes 786440 | tf_op jit(solution)/shard_map/ppermute | solution.py:29
  46.8 7.3 %collective-permute-start.1 = (bf16[1024,128]{0,1:T(8,128)(2,1)S(1)}, bf16[1024,128]{0,1:T(8,128)(2,1)S(1)}, u32[]{:S(2)}, u32[]{:S(2)}) collective-permute-start(bf16[1024,128]{0,1:T(8,128)(2,1)S(1)} %get-tuple-element.8), channel_id=1, source_target_pairs={{0,12},{4,0},{8,4},{12,8},{1,13},{5,1},{9,5},{13,9},{2,14},{6,2},{... | collective-permute-start | bytes 786440 | tf_op jit(solution)/shard_map/ppermute | solution.py:30
  52.5 5.0 %collective-permute-start.3 = (bf16[1024,64]{0,1:T(8,128)(2,1)S(1)}, bf16[1024,64]{0,1:T(8,128)(2,1)S(1)}, u32[]{:S(2)}, u32[]{:S(2)}) collective-permute-start(bf16[1024,64]{0,1:T(8,128)(2,1)S(1)} %slice.68), channel_id=1, source_target_pairs={{0,4},{4,8},{8,12},{12,0},{1,5},{5,9},{9,13},{13,1},{2,6},{6,10},{... | collective-permute-start | bytes 393224 | tf_op jit(solution)/shard_map/ppermute | solution.py:34
  54.1 5.0 %collective-permute-start.4 = (bf16[1024,64]{0,1:T(8,128)(2,1)S(1)}, bf16[1024,64]{0,1:T(8,128)(2,1)S(1)}, u32[]{:S(2)}, u32[]{:S(2)}) collective-permute-start(bf16[1024,64]{0,1:T(8,128)(2,1)S(1)} %slice.69), channel_id=1, source_target_pairs={{0,12},{4,0},{8,4},{12,8},{1,13},{5,1},{9,5},{13,9},{2,14},{6,2},{... | collective-permute-start | bytes 393224 | tf_op jit(solution)/shard_map/ppermute | solution.py:35
  59.4 23.2 %collective-permute-start.6 = (bf16[4,1024,128]{1,2,0:T(8,128)(2,1)S(1)}, bf16[4,1024,128]{1,2,0:T(8,128)(2,1)S(1)}, u32[]{:S(2)}, u32[]{:S(2)}) collective-permute-start(bf16[4,1024,128]{1,2,0:T(8,128)(2,1)S(1)} %get-tuple-element.5), channel_id=1, source_target_pairs={{0,32},{32,64},{64,96},{96,0},{1,33},{33,65},{65,97},{97,1},{2,34}... | collective-permute-start | bytes 3145736 | tf_op jit(solution)/shard_map/ppermute | solution.py:29
  60.3 23.1 %collective-permute-start.5 = (bf16[4,1024,128]{1,2,0:T(8,128)(2,1)S(1)}, bf16[4,1024,128]{1,2,0:T(8,128)(2,1)S(1)}, u32[]{:S(2)}, u32[]{:S(2)}) collective-permute-start(bf16[4,1024,128]{1,2,0:T(8,128)(2,1)S(1)} %get-tuple-element.5), channel_id=1, source_target_pairs={{0,96},{32,0},{64,32},{96,64},{1,97},{33,1},{65,33},{97,65},{2,98}... | collective-permute-start | bytes 3145736 | tf_op jit(solution)/shard_map/ppermute | solution.py:30
  82.6 9.8 %collective-permute-start.7 = (bf16[4,1024,64]{1,2,0:T(8,128)(2,1)S(1)}, bf16[4,1024,64]{1,2,0:T(8,128)(2,1)S(1)}, u32[]{:S(2)}, u32[]{:S(2)}) collective-permute-start(bf16[4,1024,64]{1,2,0:T(8,128)(2,1)S(1)} %slice.70), channel_id=1, source_target_pairs={{0,32},{32,64},{64,96},{96,0},{1,33},{33,65},{65,97},{97,1},{2,34}... | collective-permute-start | bytes 1572872 | tf_op jit(solution)/shard_map/ppermute | solution.py:34
  83.4 9.5 %collective-permute-start.8 = (bf16[4,1024,64]{1,2,0:T(8,128)(2,1)S(1)}, bf16[4,1024,64]{1,2,0:T(8,128)(2,1)S(1)}, u32[]{:S(2)}, u32[]{:S(2)}) collective-permute-start(bf16[4,1024,64]{1,2,0:T(8,128)(2,1)S(1)} %slice.71), channel_id=1, source_target_pairs={{0,96},{32,0},{64,32},{96,64},{1,97},{33,1},{65,33},{97,65},{2,98}... | collective-permute-start | bytes 1572872 | tf_op jit(solution)/shard_map/ppermute | solution.py:35
  97.0 38.6 %reduce-scatter.3.cloned.1.call-start = ((), (), s32[]{:S(2)}) async-start(), calls=%async_computation.6 | async-start | bytes 6291456 | tf_op jit(solution)/shard_map/reduce_scatter | solution.py:64
  103.7 0.7 copy-start.5
  119.0 19.5 %collective-permute-start.9 = (bf16[128,2048]{1,0:T(8,128)(2,1)S(1)}, bf16[128,2048]{1,0:T(8,128)(2,1)}, u32[]{:S(2)}, u32[]{:S(2)}) collective-permute-start(bf16[128,2048]{1,0:T(8,128)(2,1)S(1)} %fusion.32), channel_id=1, source_target_pairs={{0,2},{2,0},{1,3},{3,1},{4,6},{6,4},{5,7},{7,5},{8,10},{10,8},{9,1... | collective-permute-start | bytes 1572872 | tf_op jit(solution)/shard_map/ppermute | solution.py:68
  137.7 14.3 %collective-permute-start = (bf16[128,2048]{1,0:T(8,128)(2,1)}, bf16[128,2048]{1,0:T(8,128)(2,1)}, u32[]{:S(2)}, u32[]{:S(2)}) collective-permute-start(bf16[128,2048]{1,0:T(8,128)(2,1)} %fusion.31), channel_id=1, source_target_pairs={{0,2},{2,0},{1,3},{3,1},{4,6},{6,4},{5,7},{7,5},{8,10},{10,8},{9,1... | collective-permute-start | bytes 1572872 | tf_op jit(solution)/shard_map/ppermute | solution.py:68
  140.4 11.5 %copy-start.2 = (f32[256,2048]{1,0:T(8,128)S(1)}, f32[256,2048]{1,0:T(8,128)}, u32[]{:S(2)}) copy-start(f32[256,2048]{1,0:T(8,128)} %reduce-scatter.3.cloned.1.call-done) | copy-start | bytes 6291460
  154.2 5.4 %copy-start = (bf16[128,4096]{1,0:T(8,128)(2,1)S(1)}, bf16[128,4096]{1,0:T(8,128)(2,1)}, u32[]{:S(2)}) copy-start(bf16[128,4096]{1,0:T(8,128)(2,1)} %param.8) | copy-start | bytes 3145732
  157.4 2.5 copy-start.4
  164.4 62.1 %all-to-all-start = ((bf16[128,128,128]{2,1,0:T(8,128)(2,1)}), bf16[128,128,128]{2,1,0:T(8,128)(2,1)}, u32[]{:S(2)}, u32[]{:S(2)}) async-start(bf16[128,128,128]{2,1,0:T(8,128)(2,1)} %bitcast.91), calls=%async_computation.2 | async-start | bytes 8388608 | tf_op jit(solution)/shard_map/all_to_all | solution.py:115
  226.4 72.7 %all-to-all-start.2 = ((bf16[128,160,128]{2,1,0:T(8,128)(2,1)}), bf16[128,160,128]{2,1,0:T(8,128)(2,1)}, u32[]{:S(2)}, u32[]{:S(2)}) async-start(bf16[128,160,128]{2,1,0:T(8,128)(2,1)} %bitcast.90), calls=%async_computation.4 | async-start | bytes 10485760 | tf_op jit(solution)/shard_map/all_to_all | solution.py:115
  299.1 61.0 %all-to-all-start.1 = ((bf16[128,128,128]{2,1,0:T(8,128)(2,1)}), bf16[128,128,128]{2,1,0:T(8,128)(2,1)}, u32[]{:S(2)}, u32[]{:S(2)}) async-start(bf16[128,128,128]{2,1,0:T(8,128)(2,1)} %reshape.220), calls=%async_computation.3 | async-start | bytes 8388608 | tf_op jit(solution)/shard_map/all_to_all | solution.py:118
  347.2 21.3 %copy-start.6 = (f32[128,8]{0,1:T(8,128)S(1)}, f32[128,8]{0,1:T(8,128)}, u32[]{:S(2)}) copy-start(f32[128,8]{0,1:T(8,128)} %param.13) | copy-start | bytes 12292
  360.1 72.7 %all-to-all-start.3 = ((bf16[128,160,128]{2,1,0:T(8,128)(2,1)}), bf16[128,160,128]{2,1,0:T(8,128)(2,1)}, u32[]{:S(2)}, u32[]{:S(2)}) async-start(bf16[128,160,128]{2,1,0:T(8,128)(2,1)} %reshape.224), calls=%async_computation.5 | async-start | bytes 10485760 | tf_op jit(solution)/shard_map/all_to_all | solution.py:118
  454.2 1.2 copy-start.1
Sparse Core Ops, SparseCore 0:
  20.3 24.7 all-gather.7
  46.9 48.9 all-gather.9
Sparse Core Ops, SparseCore 1:
  97.1 19.9 reduce-scatter.4
  119.4 16.2 reduce-scatter.2

commit v17 on v16

--- a/solution.py
+++ b/solution.py
@@ -106,7 +106,7 @@
     )
     weights = route_weight.reshape(-1)
     groups = 2
-    bounds = [capacity * g // groups for g in range(groups + 1)]
+    bounds = [-(-capacity * g // groups) for g in range(groups + 1)]
     moe_sum = None
     for lo, hi in zip(bounds[:-1], bounds[1:]):
         size = hi - lo

time: 468 us -> 468 us (level)
  no operation moved by 1% of the time
where the time goes in v17:
time: 468 us; the launch traced here: 466 us
  waiting for transfers between devices  239 us (51%)
  local copies, waits for them, and re-layouts  82.4 us (18%)
  matrix products  50.3 us (11%)
  starting transfers between devices  45.8 us (10%)
  other arithmetic  21.7 us (5%)
  between operations  16 us (3%)
  blocking collectives  10.2 us (2%)
    all_to_all x2, waiting for transfers between devices, on_device(): lax.all_to_all(send, ALL, split_axis=0, concat_axis=0, tiled=True)  79.2 us
    all_to_all x2, waiting for transfers between devices, on_device(): lax.all_to_all(outputs, ALL, split_axis=0, concat_axis=0, tiled=True)  65.2 us
    ppermute x2, waiting for transfers between devices, ring_gather(): from_left = lax.ppermute(block, axis, perm=plus)  26.3 us
    all_gather x1, waiting for transfers between devices, gather_columns(): first = lax.all_gather(staged[0], 'y', axis=1, tiled=True)  24.9 us
    gather x2, local copies, waits for them, and re-layouts, on_device(): picked = jnp.take(returned, chosen * size + slots - lo, axis=0, mode='clip')  24.3 us
    dot_general x2, matrix products, expert_block(): jnp.dot(received, w_gate_up[0], preferred_element_type=jnp.float32)  22.9 us
    reduce_scatter x2, waiting for transfers between devices, over_tensor(): lax.psum_scatter(partial_sums, 'core', scatter_dimension=0, tiled=True)  21.7 us
    all_to_all x2, starting transfers between devices, on_device(): lax.all_to_all(send, ALL, split_axis=0, concat_axis=0, tiled=True)  18.2 us
  transfers between devices with their start and end apart: 18, of which 14 were waited for; matrix products, arithmetic and copies ran while one was open for 25% of the time, Pallas kernels for 0%

profile of v17, /device:TPU:54, one launch (start us, length us, event | category | flops | bytes accessed | tf_op | source)
XLA Modules:
  0.0 465.6 jit_solution(15875254211229871607)
XLA Ops:
  8.0 1.1 copy.18
  9.1 10.2 %all-gather = bf16[2048,128]{0,1:T(8,128)(2,1)S(1)} all-gather(bf16[1024,128]{0,1:T(8,128)(2,1)S(1)} %copy.18), channel_id=2, replica_groups=mesh['y'=4,'xhi'=2,'z'=4,'xlo'=2,'core'=2] {'xhi'}, dimensions={0}, use_global_device_ids=true | all-gather | bytes 786432 | tf_op jit(solution)/shard_map/all_gather | solution.py:47
  19.4 0.8 fusion.48
  20.2 24.9 %all-gather.8.cloned.1.call-done = bf16[1024,512]{0,1:T(8,128)(2,1)} async-done(((bf16[1024,128]{0,1:T(8,128)(2,1)}), bf16[1024,512]{0,1:T(8,128)(2,1)}) %all-gather.8.cloned.1.call-update) | async-done | bytes 1048592 | tf_op jit(solution)/shard_map/all_gather | solution.py:48
  45.2 1.6 collective-permute-start.2
  46.8 0.5 collective-permute-start.1
  47.3 5.2 %collective-permute-done.2 = bf16[1024,128]{0,1:T(8,128)(2,1)S(1)} collective-permute-done((bf16[1024,128]{0,1:T(8,128)(2,1)S(1)}, bf16[1024,128]{0,1:T(8,128)(2,1)S(1)}, u32[]{:S(2)}, u32[]{:S(2)}) %collective-permute-start.2) | collective-permute-done | bytes 262176 | tf_op jit(solution)/shard_map/ppermute | solution.py:29
  52.5 1.6 collective-permute-start.3
  54.1 0.5 collective-permute-start.4
  54.7 2.9 collective-permute-done.3
  57.5 1.6 collective-permute-done.4
  59.4 0.9 collective-permute-start.6
  60.3 1.2 collective-permute-start.5
  61.5 21.1 %collective-permute-done.6 = bf16[4,1024,128]{1,2,0:T(8,128)(2,1)S(1)} collective-permute-done((bf16[4,1024,128]{1,2,0:T(8,128)(2,1)S(1)}, bf16[4,1024,128]{1,2,0:T(8,128)(2,1)S(1)}, u32[]{:S(2)}, u32[]{:S(2)}) %collective-permute-start.6) | collective-permute-done | bytes 1048608 | tf_op jit(solution)/shard_map/ppermute | solution.py:29
  82.6 0.8 collective-permute-start.7
  83.4 1.4 collective-permute-start.8
  84.9 7.5 %collective-permute-done.7 = bf16[4,1024,64]{1,2,0:T(8,128)(2,1)S(1)} collective-permute-done((bf16[4,1024,64]{1,2,0:T(8,128)(2,1)S(1)}, bf16[4,1024,64]{1,2,0:T(8,128)(2,1)S(1)}, u32[]{:S(2)}, u32[]{:S(2)}) %collective-permute-start.7) | collective-permute-done | bytes 524320 | tf_op jit(solution)/shard_map/ppermute | solution.py:34
  92.4 0.5 collective-permute-done.8
  93.0 4.0 fusion.12
  97.1 6.6 %fusion.49 = f32[512,2048]{1,0:T(8,128)} fusion(bf16[512,1024]{1,0:T(8,128)(2,1)S(1)} %bitcast.102, bf16[1024,2048]{0,1:T(8,128)(2,1)} %all-gather.10.cloned.1.call-done), kind=kOutput, calls=%fused_computation.96 | convolution fusion | flops 2147483648 | bytes 9437184 | tf_op jit(solution)/shard_map/dot_general | solution.py:71
  103.7 0.6 copy-done.5
  105.8 0.4 fusion.34
  106.1 10.9 %reduce-scatter.5.cloned.1.call-done = f32[256,2048]{0,1:T(8,128)} async-done(((f32[512,2048]{0,1:T(8,128)}), f32[256,2048]{0,1:T(8,128)}) %reduce-scatter.5.cloned.1.call-update) | async-done | bytes 2097168 | tf_op jit(solution)/shard_map/reduce_scatter | solution.py:64
  117.0 1.9 copy.20
  119.0 1.0 collective-permute-start.9
  120.0 4.3 scatter_custom_fusion
  124.7 10.9 %reduce-scatter.3.cloned.1.call-done = f32[256,2048]{1,0:T(8,128)} async-done(((f32[512,2048]{1,0:T(8,128)}), f32[256,2048]{1,0:T(8,128)}) %reduce-scatter.3.cloned.1.call-update) | async-done | bytes 2097168 | tf_op jit(solution)/shard_map/reduce_scatter | solution.py:64
  135.6 2.1 fusion.31
  137.7 0.8 collective-permute-start
  138.6 1.1 bitcast_add_fusion.1
  139.7 0.7 reshape.213
  140.4 0.4 fusion.26
  140.8 1.7 fusion.25
  142.6 9.4 %collective-permute-done = bf16[128,2048]{1,0:T(8,128)(2,1)} collective-permute-done((bf16[128,2048]{1,0:T(8,128)(2,1)}, bf16[128,2048]{1,0:T(8,128)(2,1)}, u32[]{:S(2)}, u32[]{:S(2)}) %collective-permute-start) | collective-permute-done | bytes 524320 | tf_op jit(solution)/shard_map/ppermute | solution.py:68
  152.0 1.2 bitcast_add_fusion.2
  153.2 0.7 reshape.210
  154.2 3.2 pad_maximum_fusion
  157.4 2.1 reshape.214
  159.5 0.4 multiply_reduce_fusion
  159.9 0.4 fusion.23
  160.8 3.6 gather_fusion.2
  164.4 10.1 %all-to-all-start.2 = ((bf16[128,128,128]{2,1,0:T(8,128)(2,1)}), bf16[128,128,128]{2,1,0:T(8,128)(2,1)}, u32[]{:S(2)}, u32[]{:S(2)}) async-start(bf16[128,128,128]{2,1,0:T(8,128)(2,1)} %bitcast.91), calls=%async_computation.4 | async-start | bytes 8388608 | tf_op jit(solution)/shard_map/all_to_all | solution.py:115
  174.7 4.1 gather_fusion
  178.8 47.7 %all-to-all-done.2 = bf16[128,128,128]{2,1,0:T(8,128)(2,1)} async-done(((bf16[128,128,128]{2,1,0:T(8,128)(2,1)}), bf16[128,128,128]{2,1,0:T(8,128)(2,1)}, u32[]{:S(2)}, u32[]{:S(2)}) %all-to-all-start.2) | async-done | bytes 4194336 | tf_op jit(solution)/shard_map/all_to_all | solution.py:115
  226.4 8.1 %all-to-all-start = ((bf16[128,160,128]{2,1,0:T(8,128)(2,1)}), bf16[128,160,128]{2,1,0:T(8,128)(2,1)}, u32[]{:S(2)}, u32[]{:S(2)}) async-start(bf16[128,160,128]{2,1,0:T(8,128)(2,1)} %bitcast.90), calls=%async_computation.2 | async-start | bytes 10485760 | tf_op jit(solution)/shard_map/all_to_all | solution.py:115
  234.6 7.3 %reshape.223 = bf16[512,4096]{1,0:T(8,128)(2,1)} reshape(bf16[128,128,128]{2,1,0:T(8,128)(2,1)} %all-to-all-done.2) | data formatting | bytes 8388608 | tf_op jit(solution)/shard_map/reshape | solution.py:116
  241.9 10.5 %fusion.2 = f32[512,1536]{1,0:T(8,128)S(1)} fusion(bf16[512,4096]{1,0:T(8,128)(2,1)} %reshape.223, bf16[1,4096,1536]{2,1,0:T(8,128)(2,1)} %param.14), kind=kOutput, calls=%fused_computation.9 | convolution fusion | flops 6442450944 | bytes 19922944 | tf_op jit(solution)/shard_map/dot_general | solution.py:17
  252.4 7.9 %fusion.9 = bf16[512,4096]{1,0:T(8,128)(2,1)} fusion(bf16[1,768,4096]{2,1,0:T(8,128)(2,1)} %param.15, f32[512,1536]{1,0:T(8,128)S(1)} %fusion.2), kind=kOutput, calls=%fused_computation.17 | convolution fusion | flops 3225681920 | bytes 13631488 | tf_op jit(solution)/shard_map/dot_general | solution.py:21
  260.3 7.4 %reshape.224 = bf16[128,128,128]{2,1,0:T(8,128)(2,1)} reshape(bf16[512,4096]{1,0:T(8,128)(2,1)} %fusion.9) | data formatting | bytes 8388608 | tf_op jit(solution)/shard_map/reshape | solution.py:117
  267.7 31.5 %all-to-all-done = bf16[128,160,128]{2,1,0:T(8,128)(2,1)} async-done(((bf16[128,160,128]{2,1,0:T(8,128)(2,1)}), bf16[128,160,128]{2,1,0:T(8,128)(2,1)}, u32[]{:S(2)}, u32[]{:S(2)}) %all-to-all-start) | async-done | bytes 5242912 | tf_op jit(solution)/shard_map/all_to_all | solution.py:115
  299.1 9.0 %all-to-all-start.3 = ((bf16[128,128,128]{2,1,0:T(8,128)(2,1)}), bf16[128,128,128]{2,1,0:T(8,128)(2,1)}, u32[]{:S(2)}, u32[]{:S(2)}) async-start(bf16[128,128,128]{2,1,0:T(8,128)(2,1)} %reshape.224), calls=%async_computation.5 | async-start | bytes 8388608 | tf_op jit(solution)/shard_map/all_to_all | solution.py:118
  308.2 8.8 %reshape.219 = bf16[640,4096]{1,0:T(8,128)(2,1)} reshape(bf16[128,160,128]{2,1,0:T(8,128)(2,1)} %all-to-all-done) | data formatting | bytes 10485760 | tf_op jit(solution)/shard_map/reshape | solution.py:116
  317.0 12.4 %fusion.4 = f32[640,1536]{1,0:T(8,128)S(1)} fusion(bf16[640,4096]{1,0:T(8,128)(2,1)} %reshape.219, bf16[1,4096,1536]{2,1,0:T(8,128)(2,1)} %param.14), kind=kOutput, calls=%fused_computation.11 | convolution fusion | flops 8053063680 | bytes 21757952 | tf_op jit(solution)/shard_map/dot_general | solution.py:17
  329.4 8.8 %convolution_convert_fusion = bf16[640,4096]{1,0:T(8,128)(2,1)} fusion(bf16[1,768,4096]{2,1,0:T(8,128)(2,1)} %param.15, f32[640,1536]{1,0:T(8,128)S(1)} %fusion.4), kind=kOutput, calls=%fused_computation.13 | convolution fusion | flops 4032102400 | bytes 15466496 | tf_op jit(solution)/shard_map/dot_general | solution.py:21
  338.3 8.9 %reshape.220 = bf16[128,160,128]{2,1,0:T(8,128)(2,1)} reshape(bf16[640,4096]{1,0:T(8,128)(2,1)} %convolution_convert_fusion) | data formatting | bytes 10485760 | tf_op jit(solution)/shard_map/reshape | solution.py:117
  347.2 13.0 %all-to-all-done.3 = bf16[128,128,128]{2,1,0:T(8,128)(2,1)} async-done(((bf16[128,128,128]{2,1,0:T(8,128)(2,1)}), bf16[128,128,128]{2,1,0:T(8,128)(2,1)}, u32[]{:S(2)}, u32[]{:S(2)}) %all-to-all-start.3) | async-done | bytes 4194336 | tf_op jit(solution)/shard_map/all_to_all | solution.py:118
  360.1 8.1 %all-to-all-start.1 = ((bf16[128,160,128]{2,1,0:T(8,128)(2,1)}), bf16[128,160,128]{2,1,0:T(8,128)(2,1)}, u32[]{:S(2)}, u32[]{:S(2)}) async-start(bf16[128,160,128]{2,1,0:T(8,128)(2,1)} %reshape.220), calls=%async_computation.3 | async-start | bytes 10485760 | tf_op jit(solution)/shard_map/all_to_all | solution.py:118
  368.6 12.0 %gather_fusion.3 = bf16[1024,32,128]{2,1,0:T(8,128)(2,1)} fusion(bf16[512,32,128]{2,1,0:T(8,128)(2,1)} %bitcast.36, s32[1024]{0:T(1024)S(1)} %broadcast_clamp_fusion), kind=kCustom, calls=%fused_computation.3 | custom fusion | bytes 16781312 | tf_op jit(solution)/shard_map/jit(_take)/gather | solution.py:121
  380.6 52.2 %all-to-all-done.1 = bf16[128,160,128]{2,1,0:T(8,128)(2,1)} async-done(((bf16[128,160,128]{2,1,0:T(8,128)(2,1)}), bf16[128,160,128]{2,1,0:T(8,128)(2,1)}, u32[]{:S(2)}, u32[]{:S(2)}) %all-to-all-start.1) | async-done | bytes 5242912 | tf_op jit(solution)/shard_map/all_to_all | solution.py:118
  432.8 12.3 %gather_fusion.1 = bf16[1024,32,128]{2,1,0:T(8,128)(2,1)} fusion(bf16[640,32,128]{2,1,0:T(8,128)(2,1)} %bitcast.32, s32[1024]{0:T(1024)S(1)} %broadcast_clamp_fusion.1), kind=kCustom, calls=%fused_computation.1 | custom fusion | bytes 16781312 | tf_op jit(solution)/shard_map/jit(_take)/gather | solution.py:121
  445.2 9.0 %fusion = (f32[128,32,128]{2,1,0:T(8,128)S(1)}, f32[128,32,128]{2,1,0:T(8,128)S(1)}) fusion(f32[128,8]{1,0:T(8,128)S(1)} %get-tuple-element.9, bf16[1024,32,128]{2,1,0:T(8,128)(2,1)} %gather_fusion.3, bf16[1024,32,128]{2,1,0:T(8,128)(2,1)} %gather_fusion.1, f32[128,8]{1,0:T(8,128)S(1)} %get-tuple-element.10), kind=kLoop, calls=%fused_computation.6 | loop fusion | flops 24117248 | bytes 20979712 | tf_op jit(solution)/shard_map/reduce_sum | solution.py:123
  454.2 0.5 add.143
  454.7 0.7 copy-done.1
  455.4 2.8 fusion.20
  (69 shorter events, 3.8 us)
Async XLA Ops:
  8.0 37.1 %all-gather.8.cloned.1.call-start = ((), (), s32[]{:S(2)}) async-start(), calls=%async_computation.8 | async-start | bytes 1310720 | tf_op jit(solution)/shard_map/all_gather | solution.py:48
  19.4 65.4 %copy-start.3 = (bf16[512,1024]{1,0:T(8,128)(2,1)S(1)}, bf16[512,1024]{1,0:T(8,128)(2,1)}, u32[]{:S(2)}) copy-start(bf16[512,1024]{1,0:T(8,128)(2,1)} %param.9) | copy-start | bytes 3145732
  20.2 76.9 %all-gather.10.cloned.1.call-start = ((), (), s32[]{:S(2)}) async-start(), calls=%async_computation.9 | async-start | bytes 5242880 | tf_op jit(solution)/shard_map/all_gather | solution.py:49
  45.2 71.9 %reduce-scatter.5.cloned.1.call-start = ((), (), s32[]{:S(2)}) async-start(), calls=%async_computation.7 | async-start | bytes 6291456 | tf_op jit(solution)/shard_map/reduce_scatter | solution.py:64
  45.2 7.3 %collective-permute-start.2 = (bf16[1024,128]{0,1:T(8,128)(2,1)S(1)}, bf16[1024,128]{0,1:T(8,128)(2,1)S(1)}, u32[]{:S(2)}, u32[]{:S(2)}) collective-permute-start(bf16[1024,128]{0,1:T(8,128)(2,1)S(1)} %get-tuple-element.8), channel_id=1, source_target_pairs={{0,4},{4,8},{8,12},{12,0},{1,5},{5,9},{9,13},{13,1},{2,6},{6,10},{... | collective-permute-start | bytes 786440 | tf_op jit(solution)/shard_map/ppermute | solution.py:29
  46.8 7.3 %collective-permute-start.1 = (bf16[1024,128]{0,1:T(8,128)(2,1)S(1)}, bf16[1024,128]{0,1:T(8,128)(2,1)S(1)}, u32[]{:S(2)}, u32[]{:S(2)}) collective-permute-start(bf16[1024,128]{0,1:T(8,128)(2,1)S(1)} %get-tuple-element.8), channel_id=1, source_target_pairs={{0,12},{4,0},{8,4},{12,8},{1,13},{5,1},{9,5},{13,9},{2,14},{6,2},{... | collective-permute-start | bytes 786440 | tf_op jit(solution)/shard_map/ppermute | solution.py:30
  52.5 5.0 %collective-permute-start.3 = (bf16[1024,64]{0,1:T(8,128)(2,1)S(1)}, bf16[1024,64]{0,1:T(8,128)(2,1)S(1)}, u32[]{:S(2)}, u32[]{:S(2)}) collective-permute-start(bf16[1024,64]{0,1:T(8,128)(2,1)S(1)} %slice.68), channel_id=1, source_target_pairs={{0,4},{4,8},{8,12},{12,0},{1,5},{5,9},{9,13},{13,1},{2,6},{6,10},{... | collective-permute-start | bytes 393224 | tf_op jit(solution)/shard_map/ppermute | solution.py:34
  54.1 5.0 %collective-permute-start.4 = (bf16[1024,64]{0,1:T(8,128)(2,1)S(1)}, bf16[1024,64]{0,1:T(8,128)(2,1)S(1)}, u32[]{:S(2)}, u32[]{:S(2)}) collective-permute-start(bf16[1024,64]{0,1:T(8,128)(2,1)S(1)} %slice.69), channel_id=1, source_target_pairs={{0,12},{4,0},{8,4},{12,8},{1,13},{5,1},{9,5},{13,9},{2,14},{6,2},{... | collective-permute-start | bytes 393224 | tf_op jit(solution)/shard_map/ppermute | solution.py:35
  59.4 23.2 %collective-permute-start.6 = (bf16[4,1024,128]{1,2,0:T(8,128)(2,1)S(1)}, bf16[4,1024,128]{1,2,0:T(8,128)(2,1)S(1)}, u32[]{:S(2)}, u32[]{:S(2)}) collective-permute-start(bf16[4,1024,128]{1,2,0:T(8,128)(2,1)S(1)} %get-tuple-element.5), channel_id=1, source_target_pairs={{0,32},{32,64},{64,96},{96,0},{1,33},{33,65},{65,97},{97,1},{2,34}... | collective-permute-start | bytes 3145736 | tf_op jit(solution)/shard_map/ppermute | solution.py:29
  60.3 23.1 %collective-permute-start.5 = (bf16[4,1024,128]{1,2,0:T(8,128)(2,1)S(1)}, bf16[4,1024,128]{1,2,0:T(8,128)(2,1)S(1)}, u32[]{:S(2)}, u32[]{:S(2)}) collective-permute-start(bf16[4,1024,128]{1,2,0:T(8,128)(2,1)S(1)} %get-tuple-element.5), channel_id=1, source_target_pairs={{0,96},{32,0},{64,32},{96,64},{1,97},{33,1},{65,33},{97,65},{2,98}... | collective-permute-start | bytes 3145736 | tf_op jit(solution)/shard_map/ppermute | solution.py:30
  82.6 9.8 %collective-permute-start.7 = (bf16[4,1024,64]{1,2,0:T(8,128)(2,1)S(1)}, bf16[4,1024,64]{1,2,0:T(8,128)(2,1)S(1)}, u32[]{:S(2)}, u32[]{:S(2)}) collective-permute-start(bf16[4,1024,64]{1,2,0:T(8,128)(2,1)S(1)} %slice.70), channel_id=1, source_target_pairs={{0,32},{32,64},{64,96},{96,0},{1,33},{33,65},{65,97},{97,1},{2,34}... | collective-permute-start | bytes 1572872 | tf_op jit(solution)/shard_map/ppermute | solution.py:34
  83.4 9.5 %collective-permute-start.8 = (bf16[4,1024,64]{1,2,0:T(8,128)(2,1)S(1)}, bf16[4,1024,64]{1,2,0:T(8,128)(2,1)S(1)}, u32[]{:S(2)}, u32[]{:S(2)}) collective-permute-start(bf16[4,1024,64]{1,2,0:T(8,128)(2,1)S(1)} %slice.71), channel_id=1, source_target_pairs={{0,96},{32,0},{64,32},{96,64},{1,97},{33,1},{65,33},{97,65},{2,98}... | collective-permute-start | bytes 1572872 | tf_op jit(solution)/shard_map/ppermute | solution.py:35
  97.0 38.6 %reduce-scatter.3.cloned.1.call-start = ((), (), s32[]{:S(2)}) async-start(), calls=%async_computation.6 | async-start | bytes 6291456 | tf_op jit(solution)/shard_map/reduce_scatter | solution.py:64
  103.7 0.7 copy-start.5
  119.0 19.5 %collective-permute-start.9 = (bf16[128,2048]{1,0:T(8,128)(2,1)S(1)}, bf16[128,2048]{1,0:T(8,128)(2,1)}, u32[]{:S(2)}, u32[]{:S(2)}) collective-permute-start(bf16[128,2048]{1,0:T(8,128)(2,1)S(1)} %fusion.32), channel_id=1, source_target_pairs={{0,2},{2,0},{1,3},{3,1},{4,6},{6,4},{5,7},{7,5},{8,10},{10,8},{9,1... | collective-permute-start | bytes 1572872 | tf_op jit(solution)/shard_map/ppermute | solution.py:68
  137.7 14.3 %collective-permute-start = (bf16[128,2048]{1,0:T(8,128)(2,1)}, bf16[128,2048]{1,0:T(8,128)(2,1)}, u32[]{:S(2)}, u32[]{:S(2)}) collective-permute-start(bf16[128,2048]{1,0:T(8,128)(2,1)} %fusion.31), channel_id=1, source_target_pairs={{0,2},{2,0},{1,3},{3,1},{4,6},{6,4},{5,7},{7,5},{8,10},{10,8},{9,1... | collective-permute-start | bytes 1572872 | tf_op jit(solution)/shard_map/ppermute | solution.py:68
  140.4 11.5 %copy-start.2 = (f32[256,2048]{1,0:T(8,128)S(1)}, f32[256,2048]{1,0:T(8,128)}, u32[]{:S(2)}) copy-start(f32[256,2048]{1,0:T(8,128)} %reduce-scatter.3.cloned.1.call-done) | copy-start | bytes 6291460
  154.2 5.4 %copy-start = (bf16[128,4096]{1,0:T(8,128)(2,1)S(1)}, bf16[128,4096]{1,0:T(8,128)(2,1)}, u32[]{:S(2)}) copy-start(bf16[128,4096]{1,0:T(8,128)(2,1)} %param.8) | copy-start | bytes 3145732
  157.4 2.5 copy-start.4
  164.4 62.1 %all-to-all-start.2 = ((bf16[128,128,128]{2,1,0:T(8,128)(2,1)}), bf16[128,128,128]{2,1,0:T(8,128)(2,1)}, u32[]{:S(2)}, u32[]{:S(2)}) async-start(bf16[128,128,128]{2,1,0:T(8,128)(2,1)} %bitcast.91), calls=%async_computation.4 | async-start | bytes 8388608 | tf_op jit(solution)/shard_map/all_to_all | solution.py:115
  226.4 72.7 %all-to-all-start = ((bf16[128,160,128]{2,1,0:T(8,128)(2,1)}), bf16[128,160,128]{2,1,0:T(8,128)(2,1)}, u32[]{:S(2)}, u32[]{:S(2)}) async-start(bf16[128,160,128]{2,1,0:T(8,128)(2,1)} %bitcast.90), calls=%async_computation.2 | async-start | bytes 10485760 | tf_op jit(solution)/shard_map/all_to_all | solution.py:115
  299.1 61.0 %all-to-all-start.3 = ((bf16[128,128,128]{2,1,0:T(8,128)(2,1)}), bf16[128,128,128]{2,1,0:T(8,128)(2,1)}, u32[]{:S(2)}, u32[]{:S(2)}) async-start(bf16[128,128,128]{2,1,0:T(8,128)(2,1)} %reshape.224), calls=%async_computation.5 | async-start | bytes 8388608 | tf_op jit(solution)/shard_map/all_to_all | solution.py:118
  347.2 21.3 %copy-start.6 = (f32[128,8]{0,1:T(8,128)S(1)}, f32[128,8]{0,1:T(8,128)}, u32[]{:S(2)}) copy-start(f32[128,8]{0,1:T(8,128)} %param.13) | copy-start | bytes 12292
  360.1 72.7 %all-to-all-start.1 = ((bf16[128,160,128]{2,1,0:T(8,128)(2,1)}), bf16[128,160,128]{2,1,0:T(8,128)(2,1)}, u32[]{:S(2)}, u32[]{:S(2)}) async-start(bf16[128,160,128]{2,1,0:T(8,128)(2,1)} %reshape.220), calls=%async_computation.3 | async-start | bytes 10485760 | tf_op jit(solution)/shard_map/all_to_all | solution.py:118
  454.2 1.2 copy-start.1
Sparse Core Ops, SparseCore 0:
  20.3 24.7 all-gather.7
  46.9 48.9 all-gather.9
Sparse Core Ops, SparseCore 1:
  97.1 19.9 reduce-scatter.4
  119.4 16.2 reduce-scatter.2

commit v18 on v17

--- a/solution.py
+++ b/solution.py
@@ -110,7 +110,7 @@
     moe_sum = None
     for lo, hi in zip(bounds[:-1], bounds[1:]):
         size = hi - lo
-        send = jnp.take(normed3, source[:, lo:hi].reshape(-1), axis=0, mode="clip")
+        send = normed3.at[source[:, lo:hi].reshape(-1)].get(mode="promise_in_bounds")
         send = send.reshape(experts_all, size * chunks, LANES)
         received = lax.all_to_all(send, ALL, split_axis=0, concat_axis=0, tiled=True)
         outputs = expert_block(received.reshape(experts_all * size, width), w_gate_up, w_down)

time: 468 us -> 469 us (level)
  no operation moved by 1% of the time
where the time goes in v18:
time: 469 us; the launch traced here: 466 us
  waiting for transfers between devices  239 us (51%)
  local copies, waits for them, and re-layouts  82.6 us (18%)
  matrix products  50.4 us (11%)
  starting transfers between devices  45.8 us (10%)
  other arithmetic  21.7 us (5%)
  between operations  16 us (3%)
  blocking collectives  10.2 us (2%)
    all_to_all x2, waiting for transfers between devices, on_device(): lax.all_to_all(send, ALL, split_axis=0, concat_axis=0, tiled=True)  79.1 us
    all_to_all x2, waiting for transfers between devices, on_device(): lax.all_to_all(outputs, ALL, split_axis=0, concat_axis=0, tiled=True)  65.2 us
    ppermute x2, waiting for transfers between devices, ring_gather(): from_left = lax.ppermute(block, axis, perm=plus)  26.3 us
    all_gather x1, waiting for transfers between devices, gather_columns(): first = lax.all_gather(staged[0], 'y', axis=1, tiled=True)  24.9 us
    gather x2, local copies, waits for them, and re-layouts, on_device(): picked = jnp.take(returned, chosen * size + slots - lo, axis=0, mode='clip')  24.4 us
    dot_general x2, matrix products, expert_block(): jnp.dot(received, w_gate_up[0], preferred_element_type=jnp.float32)  22.9 us
    reduce_scatter x2, waiting for transfers between devices, over_tensor(): lax.psum_scatter(partial_sums, 'core', scatter_dimension=0, tiled=True)  21.8 us
    all_to_all x2, starting transfers between devices, on_device(): lax.all_to_all(send, ALL, split_axis=0, concat_axis=0, tiled=True)  18.2 us
  transfers between devices with their start and end apart: 18, of which 14 were waited for; matrix products, arithmetic and copies ran while one was open for 25% of the time, Pallas kernels for 0%

profile of v18, /device:TPU:54, one launch (start us, length us, event | category | flops | bytes accessed | tf_op | source)
XLA Modules:
  0.0 465.8 jit_solution(9786127943368146725)
XLA Ops:
  8.0 1.1 copy.18
  9.1 10.2 %all-gather = bf16[2048,128]{0,1:T(8,128)(2,1)S(1)} all-gather(bf16[1024,128]{0,1:T(8,128)(2,1)S(1)} %copy.18), channel_id=2, replica_groups=mesh['y'=4,'xhi'=2,'z'=4,'xlo'=2,'core'=2] {'xhi'}, dimensions={0}, use_global_device_ids=true | all-gather | bytes 786432 | tf_op jit(solution)/shard_map/all_gather | solution.py:47
  19.4 0.8 fusion.49
  20.2 24.9 %all-gather.8.cloned.1.call-done = bf16[1024,512]{0,1:T(8,128)(2,1)} async-done(((bf16[1024,128]{0,1:T(8,128)(2,1)}), bf16[1024,512]{0,1:T(8,128)(2,1)}) %all-gather.8.cloned.1.call-update) | async-done | bytes 1048592 | tf_op jit(solution)/shard_map/all_gather | solution.py:48
  45.2 1.6 collective-permute-start.2
  46.8 0.5 collective-permute-start.1
  47.3 5.2 %collective-permute-done.2 = bf16[1024,128]{0,1:T(8,128)(2,1)S(1)} collective-permute-done((bf16[1024,128]{0,1:T(8,128)(2,1)S(1)}, bf16[1024,128]{0,1:T(8,128)(2,1)S(1)}, u32[]{:S(2)}, u32[]{:S(2)}) %collective-permute-start.2) | collective-permute-done | bytes 262176 | tf_op jit(solution)/shard_map/ppermute | solution.py:29
  52.5 1.6 collective-permute-start.3
  54.1 0.5 collective-permute-start.4
  54.7 2.9 collective-permute-done.3
  57.5 1.6 collective-permute-done.4
  59.4 0.9 collective-permute-start.6
  60.3 1.2 collective-permute-start.5
  61.5 21.1 %collective-permute-done.6 = bf16[4,1024,128]{1,2,0:T(8,128)(2,1)S(1)} collective-permute-done((bf16[4,1024,128]{1,2,0:T(8,128)(2,1)S(1)}, bf16[4,1024,128]{1,2,0:T(8,128)(2,1)S(1)}, u32[]{:S(2)}, u32[]{:S(2)}) %collective-permute-start.6) | collective-permute-done | bytes 1048608 | tf_op jit(solution)/shard_map/ppermute | solution.py:29
  82.6 0.8 collective-permute-start.7
  83.4 1.4 collective-permute-start.8
  84.9 7.5 %collective-permute-done.7 = bf16[4,1024,64]{1,2,0:T(8,128)(2,1)S(1)} collective-permute-done((bf16[4,1024,64]{1,2,0:T(8,128)(2,1)S(1)}, bf16[4,1024,64]{1,2,0:T(8,128)(2,1)S(1)}, u32[]{:S(2)}, u32[]{:S(2)}) %collective-permute-start.7) | collective-permute-done | bytes 524320 | tf_op jit(solution)/shard_map/ppermute | solution.py:34
  92.4 0.5 collective-permute-done.8
  93.0 4.1 fusion.12
  97.2 6.6 %fusion.50 = f32[512,2048]{1,0:T(8,128)} fusion(bf16[512,1024]{1,0:T(8,128)(2,1)S(1)} %bitcast.103, bf16[1024,2048]{0,1:T(8,128)(2,1)} %all-gather.10.cloned.1.call-done), kind=kOutput, calls=%fused_computation.99 | convolution fusion | flops 2147483648 | bytes 9437184 | tf_op jit(solution)/shard_map/dot_general | solution.py:71
  103.8 0.6 copy-done.5
  105.9 0.4 fusion.34
  106.3 4.3 scatter_custom_fusion
  111.0 6.1 %reduce-scatter.5.cloned.1.call-done = f32[256,2048]{0,1:T(8,128)} async-done(((f32[512,2048]{0,1:T(8,128)}), f32[256,2048]{0,1:T(8,128)}) %reduce-scatter.5.cloned.1.call-update) | async-done | bytes 2097168 | tf_op jit(solution)/shard_map/reduce_scatter | solution.py:64
  117.1 1.9 copy.20
  119.1 1.0 collective-permute-start.9
  120.1 15.6 %reduce-scatter.3.cloned.1.call-done = f32[256,2048]{1,0:T(8,128)} async-done(((f32[512,2048]{1,0:T(8,128)}), f32[256,2048]{1,0:T(8,128)}) %reduce-scatter.3.cloned.1.call-update) | async-done | bytes 2097168 | tf_op jit(solution)/shard_map/reduce_scatter | solution.py:64
  135.7 2.1 fusion.31
  137.8 0.8 collective-permute-start
  138.7 1.1 bitcast_add_fusion.1
  139.8 0.7 reshape.271
  140.6 0.4 fusion.26
  141.0 1.7 fusion.25
  142.7 9.4 %collective-permute-done = bf16[128,2048]{1,0:T(8,128)(2,1)} collective-permute-done((bf16[128,2048]{1,0:T(8,128)(2,1)}, bf16[128,2048]{1,0:T(8,128)(2,1)}, u32[]{:S(2)}, u32[]{:S(2)}) %collective-permute-start) | collective-permute-done | bytes 524320 | tf_op jit(solution)/shard_map/ppermute | solution.py:68
  152.1 1.2 bitcast_add_fusion.2
  153.3 0.7 reshape.268
  154.3 3.2 pad_maximum_fusion
  157.5 2.1 reshape.272
  159.7 0.4 multiply_reduce_fusion
  160.1 0.4 fusion.23
  160.9 3.6 gather_fusion.2
  164.5 10.1 %all-to-all-start.2 = ((bf16[128,128,128]{2,1,0:T(8,128)(2,1)}), bf16[128,128,128]{2,1,0:T(8,128)(2,1)}, u32[]{:S(2)}, u32[]{:S(2)}) async-start(bf16[128,128,128]{2,1,0:T(8,128)(2,1)} %bitcast.92), calls=%async_computation.4 | async-start | bytes 8388608 | tf_op jit(solution)/shard_map/all_to_all | solution.py:115
  174.8 4.1 gather_fusion
  178.9 47.7 %all-to-all-done.2 = bf16[128,128,128]{2,1,0:T(8,128)(2,1)} async-done(((bf16[128,128,128]{2,1,0:T(8,128)(2,1)}), bf16[128,128,128]{2,1,0:T(8,128)(2,1)}, u32[]{:S(2)}, u32[]{:S(2)}) %all-to-all-start.2) | async-done | bytes 4194336 | tf_op jit(solution)/shard_map/all_to_all | solution.py:115
  226.5 8.1 %all-to-all-start = ((bf16[128,160,128]{2,1,0:T(8,128)(2,1)}), bf16[128,160,128]{2,1,0:T(8,128)(2,1)}, u32[]{:S(2)}, u32[]{:S(2)}) async-start(bf16[128,160,128]{2,1,0:T(8,128)(2,1)} %bitcast.91), calls=%async_computation.2 | async-start | bytes 10485760 | tf_op jit(solution)/shard_map/all_to_all | solution.py:115
  234.7 7.3 %reshape.283 = bf16[512,4096]{1,0:T(8,128)(2,1)} reshape(bf16[128,128,128]{2,1,0:T(8,128)(2,1)} %all-to-all-done.2) | data formatting | bytes 8388608 | tf_op jit(solution)/shard_map/reshape | solution.py:116
  242.0 10.5 %fusion.2 = f32[512,1536]{1,0:T(8,128)S(1)} fusion(bf16[512,4096]{1,0:T(8,128)(2,1)} %reshape.283, bf16[1,4096,1536]{2,1,0:T(8,128)(2,1)} %param.14), kind=kOutput, calls=%fused_computation.9 | convolution fusion | flops 6442450944 | bytes 19922944 | tf_op jit(solution)/shard_map/dot_general | solution.py:17
  252.5 7.9 %fusion.9 = bf16[512,4096]{1,0:T(8,128)(2,1)} fusion(bf16[1,768,4096]{2,1,0:T(8,128)(2,1)} %param.15, f32[512,1536]{1,0:T(8,128)S(1)} %fusion.2), kind=kOutput, calls=%fused_computation.17 | convolution fusion | flops 3225681920 | bytes 13631488 | tf_op jit(solution)/shard_map/dot_general | solution.py:21
  260.4 7.4 %reshape.284 = bf16[128,128,128]{2,1,0:T(8,128)(2,1)} reshape(bf16[512,4096]{1,0:T(8,128)(2,1)} %fusion.9) | data formatting | bytes 8388608 | tf_op jit(solution)/shard_map/reshape | solution.py:117
  267.8 31.4 %all-to-all-done = bf16[128,160,128]{2,1,0:T(8,128)(2,1)} async-done(((bf16[128,160,128]{2,1,0:T(8,128)(2,1)}), bf16[128,160,128]{2,1,0:T(8,128)(2,1)}, u32[]{:S(2)}, u32[]{:S(2)}) %all-to-all-start) | async-done | bytes 5242912 | tf_op jit(solution)/shard_map/all_to_all | solution.py:115
  299.2 9.0 %all-to-all-start.3 = ((bf16[128,128,128]{2,1,0:T(8,128)(2,1)}), bf16[128,128,128]{2,1,0:T(8,128)(2,1)}, u32[]{:S(2)}, u32[]{:S(2)}) async-start(bf16[128,128,128]{2,1,0:T(8,128)(2,1)} %reshape.284), calls=%async_computation.5 | async-start | bytes 8388608 | tf_op jit(solution)/shard_map/all_to_all | solution.py:118
  308.3 8.8 %reshape.278 = bf16[640,4096]{1,0:T(8,128)(2,1)} reshape(bf16[128,160,128]{2,1,0:T(8,128)(2,1)} %all-to-all-done) | data formatting | bytes 10485760 | tf_op jit(solution)/shard_map/reshape | solution.py:116
  317.1 12.4 %fusion.4 = f32[640,1536]{1,0:T(8,128)S(1)} fusion(bf16[640,4096]{1,0:T(8,128)(2,1)} %reshape.278, bf16[1,4096,1536]{2,1,0:T(8,128)(2,1)} %param.14), kind=kOutput, calls=%fused_computation.11 | convolution fusion | flops 8053063680 | bytes 21757952 | tf_op jit(solution)/shard_map/dot_general | solution.py:17
  329.5 8.8 %convolution_convert_fusion = bf16[640,4096]{1,0:T(8,128)(2,1)} fusion(bf16[1,768,4096]{2,1,0:T(8,128)(2,1)} %param.15, f32[640,1536]{1,0:T(8,128)S(1)} %fusion.4), kind=kOutput, calls=%fused_computation.13 | convolution fusion | flops 4032102400 | bytes 15466496 | tf_op jit(solution)/shard_map/dot_general | solution.py:21
  338.3 8.9 %reshape.279 = bf16[128,160,128]{2,1,0:T(8,128)(2,1)} reshape(bf16[640,4096]{1,0:T(8,128)(2,1)} %convolution_convert_fusion) | data formatting | bytes 10485760 | tf_op jit(solution)/shard_map/reshape | solution.py:117
  347.3 13.0 %all-to-all-done.3 = bf16[128,128,128]{2,1,0:T(8,128)(2,1)} async-done(((bf16[128,128,128]{2,1,0:T(8,128)(2,1)}), bf16[128,128,128]{2,1,0:T(8,128)(2,1)}, u32[]{:S(2)}, u32[]{:S(2)}) %all-to-all-start.3) | async-done | bytes 4194336 | tf_op jit(solution)/shard_map/all_to_all | solution.py:118
  360.2 8.1 %all-to-all-start.1 = ((bf16[128,160,128]{2,1,0:T(8,128)(2,1)}), bf16[128,160,128]{2,1,0:T(8,128)(2,1)}, u32[]{:S(2)}, u32[]{:S(2)}) async-start(bf16[128,160,128]{2,1,0:T(8,128)(2,1)} %reshape.279), calls=%async_computation.3 | async-start | bytes 10485760 | tf_op jit(solution)/shard_map/all_to_all | solution.py:118
  368.7 12.0 %gather_fusion.3 = bf16[1024,32,128]{2,1,0:T(8,128)(2,1)} fusion(bf16[512,32,128]{2,1,0:T(8,128)(2,1)} %bitcast.37, s32[1024]{0:T(1024)S(1)} %broadcast_clamp_fusion), kind=kCustom, calls=%fused_computation.3 | custom fusion | bytes 16781312 | tf_op jit(solution)/shard_map/jit(_take)/gather | solution.py:121
  380.7 52.2 %all-to-all-done.1 = bf16[128,160,128]{2,1,0:T(8,128)(2,1)} async-done(((bf16[128,160,128]{2,1,0:T(8,128)(2,1)}), bf16[128,160,128]{2,1,0:T(8,128)(2,1)}, u32[]{:S(2)}, u32[]{:S(2)}) %all-to-all-start.1) | async-done | bytes 5242912 | tf_op jit(solution)/shard_map/all_to_all | solution.py:118
  432.9 12.4 %gather_fusion.1 = bf16[1024,32,128]{2,1,0:T(8,128)(2,1)} fusion(bf16[640,32,128]{2,1,0:T(8,128)(2,1)} %bitcast.32, s32[1024]{0:T(1024)S(1)} %broadcast_clamp_fusion.1), kind=kCustom, calls=%fused_computation.1 | custom fusion | bytes 16781312 | tf_op jit(solution)/shard_map/jit(_take)/gather | solution.py:121
  445.3 9.0 %fusion = (f32[128,32,128]{2,1,0:T(8,128)S(1)}, f32[128,32,128]{2,1,0:T(8,128)S(1)}) fusion(f32[128,8]{1,0:T(8,128)S(1)} %get-tuple-element.9, bf16[1024,32,128]{2,1,0:T(8,128)(2,1)} %gather_fusion.3, bf16[1024,32,128]{2,1,0:T(8,128)(2,1)} %gather_fusion.1, f32[128,8]{1,0:T(8,128)S(1)} %get-tuple-element.10), kind=kLoop, calls=%fused_computation.6 | loop fusion | flops 24117248 | bytes 20979712 | tf_op jit(solution)/shard_map/reduce_sum | solution.py:123
  454.3 0.5 add.173
  454.8 0.7 copy-done.1
  455.6 2.8 fusion.20
  (71 shorter events, 3.8 us)
Async XLA Ops:
  8.0 37.1 %all-gather.8.cloned.1.call-start = ((), (), s32[]{:S(2)}) async-start(), calls=%async_computation.8 | async-start | bytes 1310720 | tf_op jit(solution)/shard_map/all_gather | solution.py:48
  19.4 65.4 %copy-start.3 = (bf16[512,1024]{1,0:T(8,128)(2,1)S(1)}, bf16[512,1024]{1,0:T(8,128)(2,1)}, u32[]{:S(2)}) copy-start(bf16[512,1024]{1,0:T(8,128)(2,1)} %param.9) | copy-start | bytes 3145732
  20.2 77.0 %all-gather.10.cloned.1.call-start = ((), (), s32[]{:S(2)}) async-start(), calls=%async_computation.9 | async-start | bytes 5242880 | tf_op jit(solution)/shard_map/all_gather | solution.py:49
  45.2 72.0 %reduce-scatter.5.cloned.1.call-start = ((), (), s32[]{:S(2)}) async-start(), calls=%async_computation.7 | async-start | bytes 6291456 | tf_op jit(solution)/shard_map/reduce_scatter | solution.py:64
  45.2 7.3 %collective-permute-start.2 = (bf16[1024,128]{0,1:T(8,128)(2,1)S(1)}, bf16[1024,128]{0,1:T(8,128)(2,1)S(1)}, u32[]{:S(2)}, u32[]{:S(2)}) collective-permute-start(bf16[1024,128]{0,1:T(8,128)(2,1)S(1)} %get-tuple-element.8), channel_id=1, source_target_pairs={{0,4},{4,8},{8,12},{12,0},{1,5},{5,9},{9,13},{13,1},{2,6},{6,10},{... | collective-permute-start | bytes 786440 | tf_op jit(solution)/shard_map/ppermute | solution.py:29
  46.8 7.3 %collective-permute-start.1 = (bf16[1024,128]{0,1:T(8,128)(2,1)S(1)}, bf16[1024,128]{0,1:T(8,128)(2,1)S(1)}, u32[]{:S(2)}, u32[]{:S(2)}) collective-permute-start(bf16[1024,128]{0,1:T(8,128)(2,1)S(1)} %get-tuple-element.8), channel_id=1, source_target_pairs={{0,12},{4,0},{8,4},{12,8},{1,13},{5,1},{9,5},{13,9},{2,14},{6,2},{... | collective-permute-start | bytes 786440 | tf_op jit(solution)/shard_map/ppermute | solution.py:30
  52.5 5.0 %collective-permute-start.3 = (bf16[1024,64]{0,1:T(8,128)(2,1)S(1)}, bf16[1024,64]{0,1:T(8,128)(2,1)S(1)}, u32[]{:S(2)}, u32[]{:S(2)}) collective-permute-start(bf16[1024,64]{0,1:T(8,128)(2,1)S(1)} %slice.68), channel_id=1, source_target_pairs={{0,4},{4,8},{8,12},{12,0},{1,5},{5,9},{9,13},{13,1},{2,6},{6,10},{... | collective-permute-start | bytes 393224 | tf_op jit(solution)/shard_map/ppermute | solution.py:34
  54.1 5.0 %collective-permute-start.4 = (bf16[1024,64]{0,1:T(8,128)(2,1)S(1)}, bf16[1024,64]{0,1:T(8,128)(2,1)S(1)}, u32[]{:S(2)}, u32[]{:S(2)}) collective-permute-start(bf16[1024,64]{0,1:T(8,128)(2,1)S(1)} %slice.69), channel_id=1, source_target_pairs={{0,12},{4,0},{8,4},{12,8},{1,13},{5,1},{9,5},{13,9},{2,14},{6,2},{... | collective-permute-start | bytes 393224 | tf_op jit(solution)/shard_map/ppermute | solution.py:35
  59.4 23.2 %collective-permute-start.6 = (bf16[4,1024,128]{1,2,0:T(8,128)(2,1)S(1)}, bf16[4,1024,128]{1,2,0:T(8,128)(2,1)S(1)}, u32[]{:S(2)}, u32[]{:S(2)}) collective-permute-start(bf16[4,1024,128]{1,2,0:T(8,128)(2,1)S(1)} %get-tuple-element.5), channel_id=1, source_target_pairs={{0,32},{32,64},{64,96},{96,0},{1,33},{33,65},{65,97},{97,1},{2,34}... | collective-permute-start | bytes 3145736 | tf_op jit(solution)/shard_map/ppermute | solution.py:29
  60.3 23.1 %collective-permute-start.5 = (bf16[4,1024,128]{1,2,0:T(8,128)(2,1)S(1)}, bf16[4,1024,128]{1,2,0:T(8,128)(2,1)S(1)}, u32[]{:S(2)}, u32[]{:S(2)}) collective-permute-start(bf16[4,1024,128]{1,2,0:T(8,128)(2,1)S(1)} %get-tuple-element.5), channel_id=1, source_target_pairs={{0,96},{32,0},{64,32},{96,64},{1,97},{33,1},{65,33},{97,65},{2,98}... | collective-permute-start | bytes 3145736 | tf_op jit(solution)/shard_map/ppermute | solution.py:30
  82.6 9.8 %collective-permute-start.7 = (bf16[4,1024,64]{1,2,0:T(8,128)(2,1)S(1)}, bf16[4,1024,64]{1,2,0:T(8,128)(2,1)S(1)}, u32[]{:S(2)}, u32[]{:S(2)}) collective-permute-start(bf16[4,1024,64]{1,2,0:T(8,128)(2,1)S(1)} %slice.70), channel_id=1, source_target_pairs={{0,32},{32,64},{64,96},{96,0},{1,33},{33,65},{65,97},{97,1},{2,34}... | collective-permute-start | bytes 1572872 | tf_op jit(solution)/shard_map/ppermute | solution.py:34
  83.4 9.5 %collective-permute-start.8 = (bf16[4,1024,64]{1,2,0:T(8,128)(2,1)S(1)}, bf16[4,1024,64]{1,2,0:T(8,128)(2,1)S(1)}, u32[]{:S(2)}, u32[]{:S(2)}) collective-permute-start(bf16[4,1024,64]{1,2,0:T(8,128)(2,1)S(1)} %slice.71), channel_id=1, source_target_pairs={{0,96},{32,0},{64,32},{96,64},{1,97},{33,1},{65,33},{97,65},{2,98}... | collective-permute-start | bytes 1572872 | tf_op jit(solution)/shard_map/ppermute | solution.py:35
  97.1 38.6 %reduce-scatter.3.cloned.1.call-start = ((), (), s32[]{:S(2)}) async-start(), calls=%async_computation.6 | async-start | bytes 6291456 | tf_op jit(solution)/shard_map/reduce_scatter | solution.py:64
  103.8 0.7 copy-start.5
  119.1 19.5 %collective-permute-start.9 = (bf16[128,2048]{1,0:T(8,128)(2,1)S(1)}, bf16[128,2048]{1,0:T(8,128)(2,1)}, u32[]{:S(2)}, u32[]{:S(2)}) collective-permute-start(bf16[128,2048]{1,0:T(8,128)(2,1)S(1)} %fusion.32), channel_id=1, source_target_pairs={{0,2},{2,0},{1,3},{3,1},{4,6},{6,4},{5,7},{7,5},{8,10},{10,8},{9,1... | collective-permute-start | bytes 1572872 | tf_op jit(solution)/shard_map/ppermute | solution.py:68
  137.8 14.3 %collective-permute-start = (bf16[128,2048]{1,0:T(8,128)(2,1)}, bf16[128,2048]{1,0:T(8,128)(2,1)}, u32[]{:S(2)}, u32[]{:S(2)}) collective-permute-start(bf16[128,2048]{1,0:T(8,128)(2,1)} %fusion.31), channel_id=1, source_target_pairs={{0,2},{2,0},{1,3},{3,1},{4,6},{6,4},{5,7},{7,5},{8,10},{10,8},{9,1... | collective-permute-start | bytes 1572872 | tf_op jit(solution)/shard_map/ppermute | solution.py:68
  140.5 11.6 %copy-start.2 = (f32[256,2048]{1,0:T(8,128)S(1)}, f32[256,2048]{1,0:T(8,128)}, u32[]{:S(2)}) copy-start(f32[256,2048]{1,0:T(8,128)} %reduce-scatter.3.cloned.1.call-done) | copy-start | bytes 6291460
  154.3 5.3 %copy-start = (bf16[128,4096]{1,0:T(8,128)(2,1)S(1)}, bf16[128,4096]{1,0:T(8,128)(2,1)}, u32[]{:S(2)}) copy-start(bf16[128,4096]{1,0:T(8,128)(2,1)} %param.8) | copy-start | bytes 3145732
  157.5 2.5 copy-start.4
  164.5 62.0 %all-to-all-start.2 = ((bf16[128,128,128]{2,1,0:T(8,128)(2,1)}), bf16[128,128,128]{2,1,0:T(8,128)(2,1)}, u32[]{:S(2)}, u32[]{:S(2)}) async-start(bf16[128,128,128]{2,1,0:T(8,128)(2,1)} %bitcast.92), calls=%async_computation.4 | async-start | bytes 8388608 | tf_op jit(solution)/shard_map/all_to_all | solution.py:115
  226.5 72.7 %all-to-all-start = ((bf16[128,160,128]{2,1,0:T(8,128)(2,1)}), bf16[128,160,128]{2,1,0:T(8,128)(2,1)}, u32[]{:S(2)}, u32[]{:S(2)}) async-start(bf16[128,160,128]{2,1,0:T(8,128)(2,1)} %bitcast.91), calls=%async_computation.2 | async-start | bytes 10485760 | tf_op jit(solution)/shard_map/all_to_all | solution.py:115
  299.2 61.0 %all-to-all-start.3 = ((bf16[128,128,128]{2,1,0:T(8,128)(2,1)}), bf16[128,128,128]{2,1,0:T(8,128)(2,1)}, u32[]{:S(2)}, u32[]{:S(2)}) async-start(bf16[128,128,128]{2,1,0:T(8,128)(2,1)} %reshape.284), calls=%async_computation.5 | async-start | bytes 8388608 | tf_op jit(solution)/shard_map/all_to_all | solution.py:118
  347.3 21.3 %copy-start.6 = (f32[128,8]{0,1:T(8,128)S(1)}, f32[128,8]{0,1:T(8,128)}, u32[]{:S(2)}) copy-start(f32[128,8]{0,1:T(8,128)} %param.13) | copy-start | bytes 12292
  360.2 72.7 %all-to-all-start.1 = ((bf16[128,160,128]{2,1,0:T(8,128)(2,1)}), bf16[128,160,128]{2,1,0:T(8,128)(2,1)}, u32[]{:S(2)}, u32[]{:S(2)}) async-start(bf16[128,160,128]{2,1,0:T(8,128)(2,1)} %reshape.279), calls=%async_computation.3 | async-start | bytes 10485760 | tf_op jit(solution)/shard_map/all_to_all | solution.py:118
  454.3 1.2 copy-start.1
Sparse Core Ops, SparseCore 0:
  20.3 24.7 all-gather.7
  46.9 48.9 all-gather.9
Sparse Core Ops, SparseCore 1:
  97.2 19.9 reduce-scatter.4
  119.5 16.2 reduce-scatter.2
